TPU v7x, 128 devices: a whole 4x4x4 slice. The times are simulated.
128 devices in a mesh: ctx: 4 (over x_hi, core), dp: 32 (over y, x_lo, z).
Axes of the slice: x: 4 (x_hi: 2, x_lo: 2; x = x_hi * 2 + x_lo), y: 4, z: 4, core: 2. Of those that a mesh axis runs over, the one named last changes fastest.
Arguments:
- query_in: bfloat16 [32, 1024, 256], P('dp', 'ctx'), may hold values from -6 to 6
- key_in: bfloat16 [32, 1024, 256], P('dp', 'ctx'), may hold values from -6 to 6
- value_in: bfloat16 [32, 1024, 256], P('dp', 'ctx'), may hold values from -6 to 6
- short_taps: float32 [3, 3, 256], replicated, may hold values from -3 to 3
- long_filter: bfloat16 [16, 1024], replicated, may hold values from -1 to 1
- skip_gain: float32 [256], replicated, may hold values from 0.5 to 1.5
- out_weight: bfloat16 [8192, 256], replicated, may hold values from -0.375 to 0.375
- out_cotangent: bfloat16 [32, 1024, 8192], P('dp', 'ctx'), may hold values from -6 to 6
Outputs:
- gated_out: bfloat16 [32, 1024, 256], P('dp', 'ctx')
- grad_query: bfloat16 [32, 1024, 256], P('dp', 'ctx')
- grad_key: bfloat16 [32, 1024, 256], P('dp', 'ctx')
- grad_value: bfloat16 [32, 1024, 256], P('dp', 'ctx')
- grad_taps: float32 [3, 3, 256], replicated
- grad_filter: float32 [16, 1024], replicated
- grad_skip: float32 [256], replicated
- grad_weight: float32 [8192, 256], P('ctx')
All inputs are finite; a program needn't handle non-finite values.
Results may differ from a plain program's by a relative error of at most 0.015.
Values may be sent and summed in bfloat16 or wider, within the bound.
No kernel may reach another device: no remote copies, remote signals or barrier semaphores. Data moves between devices by JAX's collectives and lax.ppermute only.
A program may use at most 128 MiB of HBM per device.

v0:
```python
import math

import jax
import jax.numpy as jnp
from jax import lax
from jax.sharding import PartitionSpec as P


def passed_along(block, axis, distance):
    devices = range(lax.axis_size(axis))
    route = [(i - distance, i) for i in devices if i - distance in devices]
    return lax.ppermute(block, axis, route)


def toeplitz(padded, delta, count_rows, count_cols, length):
    row_ids = lax.broadcasted_iota(jnp.int32, (count_rows, count_cols), 0)
    col_ids = lax.broadcasted_iota(jnp.int32, (count_rows, count_cols), 1)
    lag_index = jnp.clip(delta + length + col_ids - row_ids, 0, 2 * length - 1)
    return jnp.take(padded, lag_index, axis=1, mode="clip")


def diagonal_sums(flipped_outer, count, row_count):
    groups = flipped_outer.shape[0]
    span = count + row_count - 1
    padded = jnp.pad(flipped_outer, ((0, 0), (0, 0), (0, count)))
    flat = padded.reshape(groups, count * (row_count + count))[:, : count * span]
    skewed = flat.reshape(groups, count, span)
    return jnp.sum(skewed, axis=1)


def shards(
    query_in, key_in, value_in, short_taps, long_filter, skip_gain, out_weight, out_cotangent
):
    inputs = jnp.stack([query_in[0], key_in[0], value_in[0]])
    row_count = inputs.shape[1]
    chans = inputs.shape[2]
    groups = long_filter.shape[0]
    length = long_filter.shape[1]
    width = chans // groups
    ctx_count = lax.axis_size("ctx")
    own_start = lax.axis_index("ctx") * row_count
    tokens = row_count * ctx_count * lax.axis_size("dp") * query_in.shape[0]
    scale = 1.0 / math.sqrt(tokens)
    prior = passed_along(inputs[:, row_count - 2 :], "ctx", 1)
    extended = jnp.concatenate([prior, inputs], axis=1).astype(jnp.float32)
    shorts = (
        short_taps[:, 0, None, :] * extended[:, 2:]
        + short_taps[:, 1, None, :] * extended[:, 1:-1]
        + short_taps[:, 2, None, :] * extended[:, :-2]
    )
    q_short = shorts[0]
    k_short = shorts[1]
    v_short = shorts[2]
    mixed = (k_short * v_short).astype(jnp.bfloat16)
    mixed_grp = mixed.T.reshape(groups, width, row_count)
    mixed_flipped = mixed_grp[:, :, ::-1]
    padded_filter = jnp.concatenate(
        [jnp.zeros((groups, length), long_filter.dtype), long_filter], axis=1
    )
    piece = lax.all_gather(mixed, "ctx", axis=0, tiled=True)
    blocks = piece.shape[0] // row_count

    def conv_one_block(index, acc):
        sub = lax.dynamic_slice_in_dim(piece, index * row_count, row_count, 0)
        sub_start = index * row_count

        def conv_compute(inner_acc):
            sub_grp = sub.T.reshape(groups, width, row_count)
            matrix = toeplitz(padded_filter, own_start - sub_start, row_count, row_count, length)
            return inner_acc + jnp.einsum(
                "gwc,gcr->gwr", sub_grp, matrix, preferred_element_type=jnp.float32
            )

        return lax.cond(
            sub_start < own_start + row_count, conv_compute, lambda inner_acc: inner_acc, acc
        )

    convolved_grp = lax.fori_loop(
        0, blocks, conv_one_block, jnp.zeros((groups, width, row_count), jnp.float32)
    )
    convolved = convolved_grp.reshape(chans, row_count).T
    mixed_f = mixed.astype(jnp.float32)
    inner = convolved + skip_gain * mixed_f
    gated = (q_short * inner).astype(jnp.bfloat16)
    cotangent = out_cotangent[0]
    share = out_weight.shape[0] // ctx_count
    full_terms = lax.dot_general(
        cotangent, gated, (((0,), (0,)), ((), ())), preferred_element_type=jnp.float32
    )
    summed = lax.psum(full_terms, ("ctx", "dp"))
    grad_weight = lax.dynamic_slice_in_dim(summed, lax.axis_index("ctx") * share, share, 0) * scale
    d_gated = jnp.dot(cotangent, out_weight, preferred_element_type=jnp.float32).astype(
        jnp.bfloat16
    )
    d_gated_f = d_gated.astype(jnp.float32)
    d_inner = (d_gated_f * q_short).astype(jnp.bfloat16)
    d_qs = d_gated_f * inner
    start_state = (
        jnp.zeros((groups, width, row_count), jnp.float32),
        jnp.zeros((groups, 2 * length), jnp.float32),
    )
    back_piece = lax.all_gather(d_inner, "ctx", axis=0, tiled=True)
    blocks = back_piece.shape[0] // row_count

    def back_one_block(index, state):
        sub = lax.dynamic_slice_in_dim(back_piece, index * row_count, row_count, 0)
        sub_start = index * row_count

        def back_compute(inner_state):
            grad_mixed, lag_sums = inner_state
            sub_grp = sub.T.reshape(groups, width, row_count)
            delta = sub_start - own_start
            matrix = toeplitz(padded_filter, delta, row_count, row_count, length)
            back_parts = jnp.einsum(
                "gwc,grc->gwr", sub_grp, matrix, preferred_element_type=jnp.float32
            )
            outer = jnp.einsum(
                "gwc,gwr->gcr", sub_grp, mixed_flipped, preferred_element_type=jnp.float32
            )
            diagonals = diagonal_sums(outer, row_count, row_count)
            offset = delta - row_count + 1 + length
            window = lax.dynamic_slice_in_dim(lag_sums, offset, 2 * row_count - 1, 1)
            lag_sums = lax.dynamic_update_slice_in_dim(lag_sums, window + diagonals, offset, 1)
            return (grad_mixed + back_parts, lag_sums)

        return lax.cond(
            sub_start + row_count > own_start, back_compute, lambda inner_state: inner_state, state
        )

    back_grp, lag_sums = lax.fori_loop(0, blocks, back_one_block, start_state)
    d_inner_f = d_inner.astype(jnp.float32)
    d_mixed = back_grp.reshape(chans, row_count).T + skip_gain * d_inner_f
    d_ks = d_mixed * v_short
    d_vs = d_mixed * k_short
    d_shorts = jnp.stack([d_qs, d_ks, d_vs])
    taps_local = jnp.stack(
        [
            jnp.sum(d_shorts * extended[:, 2:], axis=1),
            jnp.sum(d_shorts * extended[:, 1:-1], axis=1),
            jnp.sum(d_shorts * extended[:, :-2], axis=1),
        ],
        axis=1,
    )
    filter_local = lag_sums[:, length:]
    skip_local = jnp.sum(d_inner_f * mixed_f, axis=0)
    taps_sum, filter_sum, skip_sum = lax.psum((taps_local, filter_local, skip_local), ("ctx", "dp"))
    following = passed_along(d_shorts[:, :2], "ctx", -1)
    ahead = jnp.concatenate([d_shorts, following], axis=1)
    input_grads = (
        short_taps[:, 0, None, :] * ahead[:, :-2]
        + short_taps[:, 1, None, :] * ahead[:, 1:-1]
        + short_taps[:, 2, None, :] * ahead[:, 2:]
    ).astype(jnp.bfloat16)
    return (
        gated[None],
        input_grads[0][None],
        input_grads[1][None],
        input_grads[2][None],
        taps_sum * scale,
        filter_sum * scale,
        skip_sum * scale,
        grad_weight,
    )


def solution(mesh):
    in_specs = (
        P("dp", "ctx", None),
        P("dp", "ctx", None),
        P("dp", "ctx", None),
        P(),
        P(),
        P(),
        P(),
        P("dp", "ctx", None),
    )
    out_specs = (
        P("dp", "ctx", None),
        P("dp", "ctx", None),
        P("dp", "ctx", None),
        P("dp", "ctx", None),
        P(),
        P(),
        P(),
        P("ctx", None),
    )
    return jax.shard_map(shards, mesh=mesh, in_specs=in_specs, out_specs=out_specs, check_vma=False)
```

profile of v0, /device:TPU:1, one launch (start us, length us, event | category | flops | bytes accessed | tf_op | source)
XLA Modules:
  0.0 1556.1 jit_solution(3772879815758970291)
XLA Ops:
  7.2 0.9 constant_dynamic-update-slice_fusion.2
  8.1 0.9 constant_dynamic-update-slice_fusion.1
  9.0 0.9 constant_dynamic-update-slice_fusion
  10.0 6.0 collective-permute-start
  16.0 0.8 fusion.26
  16.9 0.9 copy.27
  18.1 0.9 copy-done
  19.2 1.2 copy-done.2
  20.4 5.1 fusion.24
  25.5 7.5 all_gather.6
  33.3 8.8 all_gather.7
  42.1 1.0 copy.31
  43.2 814.3 %while.33 = (s32[]{:T(128)}, f32[16,16,256]{2,1,0:T(8,128)S(1)}, f32[16,2048]{1,0:T(8,128)S(1)}, s32[]{:T(128)}, bf16[1024,256]{0,1:T(8,128)(2,1)}, /*index=5*/b...) while((s32[]{:T(128)}, f32[16,16,256]{2,1,0:T(8,128)S(1)}, ...), condition=%wide.region_8.9_spmd, body=%wide.region_4.8_spmd.sunk | while | flops 69464328 | bytes 88852448 | solution.py:130
  43.4 271.3 %conditional.5 = ((f32[16,16,256]{2,1,0:T(8,128)S(1)}, f32[16,2048]{1,0:T(8,128)S(1)})) conditional(s32[]{:T(128)} %convert_element_type.87, (f32[16,16,256]{2,1,0:T(8,128)S(1)}, f32[16,2048]{1,0:T(8,128)S(1)}) %tuple.113, (s32[]{:T(128)}, bf16[1024,256]{0,1:T(8,128)(2,1)}, s32[]{:T(128)}, bf16[16,2048]{0,1:T(8,128)(2,1)S(1)}, ...), branch_computations={%region_5.5_spmd, %region_6.7_spmd} | conditional | flops 69464320 | bytes 88852248 | solution.py:126
  43.5 0.9 constant_dynamic-slice_fusion.1
  44.4 0.7 fusion.27
  45.1 1.1 pad.6
  46.2 4.9 copy.40
  51.1 3.8 slice.83
  54.8 11.8 reshape.94
  66.6 4.5 reduce_sum.42
  72.0 229.0 %gather_fusion.1 = bf16[65536,16]{1,0:T(8,128)(2,1)} fusion(bf16[16,2048]{0,1:T(8,128)(2,1)S(1)} %get-tuple-element.374, s32[65536]{0:T(1024)S(1)} %broadcast_clamp_fusion.1), kind=kCustom, calls=%fused_computation.1 | custom fusion | bytes 4456448 | tf_op jit(solution)/shard_map/while/body/eval_jaxpr/cond/branch_1_fun/jit(_take)/gather | solution.py:19
  301.0 13.1 copy.26
  314.1 0.6 fusion.7
  314.7 271.3 %conditional.5 = ((f32[16,16,256]{2,1,0:T(8,128)S(1)}, f32[16,2048]{1,0:T(8,128)S(1)})) conditional(s32[]{:T(128)} %convert_element_type.87, (f32[16,16,256]{2,1,0:T(8,128)S(1)}, f32[16,2048]{1,0:T(8,128)S(1)}) %tuple.113, (s32[]{:T(128)}, bf16[1024,256]{0,1:T(8,128)(2,1)}, s32[]{:T(128)}, bf16[16,2048]{0,1:T(8,128)(2,1)S(1)}, ...), branch_computations={%region_5.5_spmd, %region_6.7_spmd} | conditional | flops 69464320 | bytes 88852248 | solution.py:126
  314.8 0.9 constant_dynamic-slice_fusion.1
  315.7 0.7 fusion.27
  316.4 1.1 pad.6
  317.5 4.9 copy.40
  322.4 3.8 slice.83
  326.2 11.8 reshape.94
  337.9 4.5 reduce_sum.42
  343.3 229.0 %gather_fusion.1 = bf16[65536,16]{1,0:T(8,128)(2,1)} fusion(bf16[16,2048]{0,1:T(8,128)(2,1)S(1)} %get-tuple-element.374, s32[65536]{0:T(1024)S(1)} %broadcast_clamp_fusion.1), kind=kCustom, calls=%fused_computation.1 | custom fusion | bytes 4456448 | tf_op jit(solution)/shard_map/while/body/eval_jaxpr/cond/branch_1_fun/jit(_take)/gather | solution.py:19
  572.3 13.1 copy.26
  585.4 0.6 fusion.7
  586.1 271.3 %conditional.5 = ((f32[16,16,256]{2,1,0:T(8,128)S(1)}, f32[16,2048]{1,0:T(8,128)S(1)})) conditional(s32[]{:T(128)} %convert_element_type.87, (f32[16,16,256]{2,1,0:T(8,128)S(1)}, f32[16,2048]{1,0:T(8,128)S(1)}) %tuple.113, (s32[]{:T(128)}, bf16[1024,256]{0,1:T(8,128)(2,1)}, s32[]{:T(128)}, bf16[16,2048]{0,1:T(8,128)(2,1)S(1)}, ...), branch_computations={%region_5.5_spmd, %region_6.7_spmd} | conditional | flops 69464320 | bytes 88852248 | solution.py:126
  586.1 0.9 constant_dynamic-slice_fusion.1
  587.0 0.7 fusion.27
  587.7 1.1 pad.6
  588.8 4.9 copy.40
  593.7 3.8 slice.83
  597.5 11.8 reshape.94
  609.2 4.5 reduce_sum.42
  614.6 229.0 %gather_fusion.1 = bf16[65536,16]{1,0:T(8,128)(2,1)} fusion(bf16[16,2048]{0,1:T(8,128)(2,1)S(1)} %get-tuple-element.374, s32[65536]{0:T(1024)S(1)} %broadcast_clamp_fusion.1), kind=kCustom, calls=%fused_computation.1 | custom fusion | bytes 4456448 | tf_op jit(solution)/shard_map/while/body/eval_jaxpr/cond/branch_1_fun/jit(_take)/gather | solution.py:19
  843.6 13.1 copy.26
  856.7 0.6 fusion.7
  858.2 0.8 copy.32
  859.0 1.2 copy.28
  860.3 485.6 %while.32 = (s32[]{:T(128)}, f32[16,16,256]{2,1,0:T(8,128)S(1)}, s32[]{:T(128)}, bf16[1024,256]{0,1:T(8,128)(2,1)S(1)}, s32[]{:T(128)}, /*index=5*/bf16[16,2048]{0,1:T(8,128)(2,1)S(1)}, s32[]{:T(128)}, s32[]{:T(128)}) while((s32[]{:T(128)}, f32[16,16,256]{2,1,0:T(8,128)S(1)}, s32[]{:T(128)}, bf16[1024,256]{0,1:T(8,128)(2,1)S(1)}, s32[]{:T(128)}, ...), condition=%wide.region_3.4_spmd, body=%wide.region_0.3_spmd.sunk | while | flops 33816840 | bytes 12978401 | solution.py:78
  860.3 242.8 %conditional.4 = (f32[16,16,256]{2,1,0:T(8,128)S(1)}) conditional(s32[]{:T(128)} %convert_element_type.86, f32[16,16,256]{2,1,0:T(8,128)S(1)} %get-tuple-element.618, (s32[]{:T(128)}, bf16[1024,256]{0,1:T(8,128)(2,1)S(1)}, s32[]{:T(128)}, bf16[16,2048]{0,1:T(8,128)(2,1)S(1)}, f32[16,16,256]{2,1,0:T(8,128)S(1)}) %tuple.111), branch_computations={%region_1.0_spmd, %region_2.2_spmd} | conditional | flops 33816836 | bytes 12978250 | solution.py:74
  860.6 229.0 %gather_fusion = bf16[65536,16]{1,0:T(8,128)(2,1)} fusion(bf16[16,2048]{0,1:T(8,128)(2,1)S(1)} %get-tuple-element.362, s32[65536]{0:T(1024)S(1)} %broadcast_clamp_fusion), kind=kCustom, calls=%fused_computation | custom fusion | bytes 4456448 | tf_op jit(solution)/shard_map/while/body/eval_jaxpr/cond/branch_1_fun/jit(_take)/gather | solution.py:19
  1089.6 13.1 copy.25
  1103.1 242.8 %conditional.4 = (f32[16,16,256]{2,1,0:T(8,128)S(1)}) conditional(s32[]{:T(128)} %convert_element_type.86, f32[16,16,256]{2,1,0:T(8,128)S(1)} %get-tuple-element.618, (s32[]{:T(128)}, bf16[1024,256]{0,1:T(8,128)(2,1)S(1)}, s32[]{:T(128)}, bf16[16,2048]{0,1:T(8,128)(2,1)S(1)}, f32[16,16,256]{2,1,0:T(8,128)S(1)}) %tuple.111), branch_computations={%region_1.0_spmd, %region_2.2_spmd} | conditional | flops 33816836 | bytes 12978250 | solution.py:74
  1103.4 229.0 %gather_fusion = bf16[65536,16]{1,0:T(8,128)(2,1)} fusion(bf16[16,2048]{0,1:T(8,128)(2,1)S(1)} %get-tuple-element.362, s32[65536]{0:T(1024)S(1)} %broadcast_clamp_fusion), kind=kCustom, calls=%fused_computation | custom fusion | bytes 4456448 | tf_op jit(solution)/shard_map/while/body/eval_jaxpr/cond/branch_1_fun/jit(_take)/gather | solution.py:19
  1332.4 13.1 copy.25
  1346.1 1.5 multiply_bitcast_fusion.1
  1347.6 6.8 convolution_bitcast_fusion
  1355.2 30.6 %collective-permute-start.1 = (f32[3,2,256]{2,1,0:T(2,128)S(1)}, f32[3,2,256]{2,1,0:T(2,128)S(1)}, u32[]{:S(2)}, u32[]{:S(2)}) collective-permute-start(f32[3,2,256]{2,1,0:T(2,128)S(1)} %slice.91), channel_id=1, source_target_pairs={{32,0},{64,32},{96,64},{33,1},{65,33},{97,65},{34,2},{66,34},{98,6... | collective-permute-start | bytes 18440 | tf_op jit(solution)/shard_map/ppermute | solution.py:12
  1385.8 0.8 collective-permute-done.1
  1387.3 66.8 %all-reduce.2 = (f32[3,3,256]{2,0,1:T(4,128)S(1)}, f32[256]{0:T(256)S(1)}) all-reduce(f32[3,3,256]{2,0,1:T(4,128)S(1)} %pad_maximum_fusion.2, f32[256]{0:T(256)S(1)} %copy-done.17), channel_id=1, replica_groups=mesh['ctx'=4,'dp'=32] {'ctx','dp'}, use_global_device_ids=true, to_apply=%region_12.13 | all-reduce | flops 2560 | bytes 20480 | tf_op jit(solution)/shard_map/psum | solution.py:146
  1455.3 0.7 fusion.25
  1456.0 88.9 %all-reduce.6.cloned.1.call-done = (f32[16,1024]{1,0:T(8,128)}, f32[8192,256]{0,1:T(8,128)}) async-done(((f32[16,1024]{1,0:T(8,128)}, f32[8192,256]{0,1:T(8,128)}), (f32[16,1024]{1,0:T(8,128)}, f32[8192,256]{0,1:T(8,128)})) %all-reduce.6.cloned.1.call-update) | async-done | bytes 8454160 | tf_op jit(solution)/shard_map/psum | solution.py:146
  1545.0 1.8 dynamic-slice_multiply_fusion
  1546.8 1.8 copy.34
  (92 shorter events, 8.8 us)
Async XLA Ops:
  7.2 1537.8 %all-reduce.6.cloned.1.call-start = ((), (), s32[]{:S(2)}) async-start(), calls=%async_computation | async-start | bytes 16908288 | tf_op jit(solution)/shard_map/psum | solution.py:146
  10.0 8.0 collective-permute-start
  16.9 8.6 copy-start.10
  16.9 8.5 copy-start.12
  16.9 8.5 copy-start.14
  17.9 2.5 copy-start.2
  18.1 0.9 copy-start
  20.4 5.1 copy-start.3
  25.4 7.9 copy-start.4
  25.5 17.7 %copy-start.8 = (bf16[256,256]{1,0:T(8,128)(2,1)}, bf16[256,256]{1,0:T(8,128)(2,1)S(1)}, u32[]{:S(2)}) copy-start(bf16[256,256]{1,0:T(8,128)(2,1)S(1)} %get-tuple-element.478) | copy-start | bytes 393220
  857.5 0.7 copy-start.5
  860.3 485.8 %copy-start.16 = (f32[256]{0:T(256)S(1)}, f32[256]{0:T(256)}, u32[]{:S(2)}) copy-start(f32[256]{0:T(256)} %param.21) | copy-start | bytes 3076
  1347.6 6.8 copy-start.7
  1347.6 6.8 copy-start.6
  1355.1 31.6 %copy-start.1 = (f32[3,258,256]{2,1,0:T(8,128)S(1)}, f32[3,258,256]{2,1,0:T(8,128)}, u32[]{:S(2)}) copy-start(f32[3,258,256]{2,1,0:T(8,128)} %copy-done) | copy-start | bytes 2377732
  1355.1 31.6 %copy-start.11 = (f32[3,256]{1,0:T(4,128)S(1)}, f32[3,256]{1,0:T(4,128)}, u32[]{:S(2)}) copy-start(f32[3,256]{1,0:T(4,128)} %copy-done.10) | copy-start | bytes 9220
  1355.1 31.6 %copy-start.13 = (f32[3,256]{1,0:T(4,128)S(1)}, f32[3,256]{1,0:T(4,128)}, u32[]{:S(2)}) copy-start(f32[3,256]{1,0:T(4,128)} %copy-done.12) | copy-start | bytes 9220
  1355.1 31.6 %copy-start.15 = (f32[3,1,256]{2,0,1:T(4,128)S(1)}, f32[3,1,256]{2,0,1:T(4,128)}, u32[]{:S(2)}) copy-start(f32[3,1,256]{2,0,1:T(4,128)} %copy-done.14) | copy-start | bytes 9220
  1355.1 32.2 %copy-start.17 = (f32[256]{0:T(256)S(1)}, f32[256]{0:T(256)}, u32[]{:S(2)}) copy-start(f32[256]{0:T(256)} %get-tuple-element.477) | copy-start | bytes 3076
  1355.2 31.4 %collective-permute-start.1 = (f32[3,2,256]{2,1,0:T(2,128)S(1)}, f32[3,2,256]{2,1,0:T(2,128)S(1)}, u32[]{:S(2)}, u32[]{:S(2)}) collective-permute-start(f32[3,2,256]{2,1,0:T(2,128)S(1)} %slice.91), channel_id=1, source_target_pairs={{32,0},{64,32},{96,64},{33,1},{65,33},{97,65},{34,2},{66,34},{98,6... | collective-permute-start | bytes 18440 | tf_op jit(solution)/shard_map/ppermute | solution.py:12
  1545.0 3.6 copy-start.9
Sparse Core Ops, SparseCore 0:
  1355.2 189.7 all-reduce.5
where the time goes:
time: 1560 us
  local copies, waits for them, and re-layouts  1290 us (83%)
  waiting for transfers between devices  89.8 us (6%)
  blocking collectives  83.1 us (5%)
  starting transfers between devices  36.7 us (2%)
  other arithmetic  19.7 us (1%)
  matrix products  16.8 us (1%)
    gather x10, local copies, waits for them, and re-layouts, toeplitz(): return jnp.take(padded, lag_index, axis=1, mode='clip')  1210 us
    psum x1, waiting for transfers between devices, shards(): lax.psum((taps_local, filter_local, skip_local), ('ctx', 'dp'))  88.9 us
    psum x1, blocking collectives, shards(): lax.psum((taps_local, filter_local, skip_local), ('ctx', 'dp'))  66.8 us
    ppermute x2, starting transfers between devices, passed_along(): return lax.ppermute(block, axis, route)  36.6 us
    reshape x3, local copies, waits for them, and re-layouts, diagonal_sums(): skewed = flat.reshape(groups, count, span)  35.3 us
  transfers between devices with their start and end apart: 3, of which 2 were waited for; matrix products, arithmetic and copies ran while one was open for 0% of the time, Pallas kernels for 0%

commit v1 on v0

v1 whole, which is shorter than its diff:
```python
import math

import jax
import jax.numpy as jnp
from jax import lax
from jax.experimental import pallas as pl
from jax.experimental.pallas import tpu as pltpu
from jax.sharding import Mesh
from jax.sharding import PartitionSpec as P

F32 = jnp.float32
BF16 = jnp.bfloat16
CTX = ("xh", "co")
DP = ("y", "xl", "z")
CHIPS = ("xh", "y", "xl", "z")
ALL = ("xh", "co", "y", "xl", "z")

ROWS = 256
CHANS = 256
GROUPS = 16
LENGTH = 1024
STRIP = 128
WIDE = LENGTH + STRIP
FEATS = 8192
TILE = 1024
SMALL = 64
TAIL = 16
VMEM_LIMIT = 56 * 1024 * 1024


def params(*semantics):
    return pltpu.CompilerParams(vmem_limit_bytes=VMEM_LIMIT)


def lane_groups(rows):
    return lax.broadcasted_iota(jnp.int32, (rows, CHANS), 1) // (CHANS // GROUPS)


def later(x, count):
    row = lax.broadcasted_iota(jnp.int32, x.shape, 0)
    return jnp.where(row >= count, pltpu.roll(x, count, 0), 0.0)


def strip_of(line):
    wide = jnp.broadcast_to(line, (STRIP, WIDE))
    return pltpu.roll(wide, 0, 1, stride=1, stride_axis=0)[:, :LENGTH].astype(BF16)


def pick_groups(result):
    ids = lane_groups(STRIP)
    out = jnp.zeros((STRIP, CHANS), F32)
    for g in range(GROUPS):
        out = jnp.where(ids == g, result[g * STRIP : (g + 1) * STRIP], out)
    return out


def with_tail(tail, block):
    joined = jnp.concatenate([tail, block], axis=0).astype(F32)
    return joined[TAIL:], pltpu.roll(joined, 1, 0)[TAIL:], pltpu.roll(joined, 2, 0)[TAIL:]


def short_sum(taps_ref, i, parts):
    return sum(taps_ref[3 * i + j : 3 * i + j + 1, :] * parts[j] for j in range(3))


def pre_kernel(cot_ref, weight_ref, line_ref, d_gated_ref, strips_ref, acc_ref):
    step = pl.program_id(0)

    @pl.when(step == 0)
    def _():
        acc_ref[...] = jnp.zeros_like(acc_ref)

    acc_ref[...] += jnp.dot(cot_ref[...], weight_ref[...], preferred_element_type=F32)
    for g in range(2):
        strips_ref[g * STRIP : (g + 1) * STRIP, :] = strip_of(line_ref[g])

    @pl.when(step == pl.num_programs(0) - 1)
    def _():
        d_gated_ref[...] = acc_ref[...].astype(BF16)


def pre_call(cot, weight, lines):
    steps = FEATS // TILE
    return pl.pallas_call(
        pre_kernel,
        grid=(steps,),
        in_specs=[
            pl.BlockSpec((ROWS, TILE), lambda i: (0, i)),
            pl.BlockSpec((TILE, CHANS), lambda i: (i, 0)),
            pl.BlockSpec((2, 1, WIDE), lambda i: (i, 0, 0)),
        ],
        out_specs=[
            pl.BlockSpec((ROWS, CHANS), lambda i: (0, 0)),
            pl.BlockSpec((2 * STRIP, LENGTH), lambda i: (i, 0)),
        ],
        out_shape=[
            jax.ShapeDtypeStruct((ROWS, CHANS), BF16),
            jax.ShapeDtypeStruct((GROUPS * STRIP, LENGTH), BF16),
        ],
        scratch_shapes=[pltpu.VMEM((ROWS, CHANS), F32)],
        compiler_params=params(),
        cost_estimate=pl.CostEstimate(
            flops=2 * ROWS * FEATS * CHANS, bytes_accessed=14 << 20, transcendentals=0
        ),
        name="pre",
    )(cot, weight, lines)


def d_inner_kernel(d_gated_ref, query_ref, tail_ref, taps_ref, out_ref):
    q_short = short_sum(taps_ref, 0, with_tail(tail_ref[...], query_ref[...]))
    out_ref[...] = (d_gated_ref[...].astype(F32) * q_short).astype(BF16)


def d_inner_call(d_gated, query, tail, taps):
    return pl.pallas_call(
        d_inner_kernel,
        out_shape=jax.ShapeDtypeStruct((ROWS, CHANS), BF16),
        compiler_params=params(),
        cost_estimate=pl.CostEstimate(flops=1 << 20, bytes_accessed=1 << 19, transcendentals=0),
        name="d_inner",
    )(d_gated, query, tail, taps)


def fwd_kernel(
    strips_ref, far_ref, mid_ref, near_ref, own_ref, query_ref, tail_ref, taps_ref, skip_ref,
    gated_ref, inner_ref, mixed_ref,
):
    both = jnp.concatenate([far_ref[...], mid_ref[...], near_ref[...], own_ref[...]], axis=0)
    both = both.astype(F32)
    shifted = (both, later(both, 1), later(both, 2))
    k_short = short_sum(taps_ref, 1, [part[:, :CHANS] for part in shifted])
    v_short = short_sum(taps_ref, 2, [part[:, CHANS:] for part in shifted])
    mixed = (k_short * v_short).astype(BF16)
    mixed_ref[...] = mixed[LENGTH - ROWS :]
    low = jnp.dot(strips_ref[:, STRIP:], mixed[: LENGTH - STRIP], preferred_element_type=F32)
    high = jnp.dot(strips_ref[...], mixed, preferred_element_type=F32)
    convolved = jnp.concatenate([pick_groups(low), pick_groups(high)], axis=0)
    inner = convolved + skip_ref[...] * mixed[LENGTH - ROWS :].astype(F32)
    inner_ref[...] = inner
    q_short = short_sum(taps_ref, 0, with_tail(tail_ref[...], query_ref[...]))
    gated_ref[...] = (q_short * inner).astype(BF16)


def fwd_call(strips, far, mid, near, own, query, tail, taps, skip):
    return pl.pallas_call(
        fwd_kernel,
        out_shape=[
            jax.ShapeDtypeStruct((ROWS, CHANS), BF16),
            jax.ShapeDtypeStruct((ROWS, CHANS), F32),
            jax.ShapeDtypeStruct((ROWS, CHANS), BF16),
        ],
        compiler_params=params(),
        cost_estimate=pl.CostEstimate(flops=4 << 30, bytes_accessed=6 << 20, transcendentals=0),
        name="fwd",
    )(strips, far, mid, near, own, query, tail, taps, skip)


def weight_kernel(core_ref, own_cot_ref, other_cot_ref, gated_ref, other_gated_ref, out_ref):
    dims = (((0,), (0,)), ((), ()))
    total = lax.dot_general(own_cot_ref[...], gated_ref[...], dims, preferred_element_type=F32)
    total += lax.dot_general(
        other_cot_ref[...], other_gated_ref[...], dims, preferred_element_type=F32
    )
    out_ref[...] = total.astype(BF16)


def weight_call(core, own_cot, other_cot, gated, other_gated):
    share = FEATS // 4 // TILE

    def column(i, core_ref):
        return (0, (i // share) * 2 * share + core_ref[0] * share + i % share)

    return pl.pallas_call(
        weight_kernel,
        grid_spec=pltpu.PrefetchScalarGridSpec(
            num_scalar_prefetch=1,
            grid=(2 * share,),
            in_specs=[
                pl.BlockSpec((ROWS, TILE), column),
                pl.BlockSpec((ROWS, TILE), column),
                pl.BlockSpec((ROWS, CHANS), lambda i, core_ref: (0, 0)),
                pl.BlockSpec((ROWS, CHANS), lambda i, core_ref: (0, 0)),
            ],
            out_specs=pl.BlockSpec((TILE, CHANS), lambda i, core_ref: (i, 0)),
        ),
        out_shape=jax.ShapeDtypeStruct((FEATS // 2, CHANS), BF16),
        compiler_params=params(),
        cost_estimate=pl.CostEstimate(
            flops=2 * ROWS * FEATS * CHANS, bytes_accessed=6 << 20, transcendentals=0
        ),
        name="weight_terms",
    )(core, own_cot, other_cot, gated, other_gated)


def bwd_kernel(
    d0_ref, d1_ref, d2_ref, d3_ref, line_ref, mixed_ref, own_ref, near_ref, query_ref, tail_ref,
    inner_ref, d_gated_ref, taps_ref, skip_ref,
    d_short_ref, filter_ref, small_ref,
    strips_ref, ahead_ref, outer_ref, stack_ref,
):
    for n, ref in enumerate((d0_ref, d1_ref, d2_ref, d3_ref)):
        ahead_ref[n * ROWS : (n + 1) * ROWS, :] = ref[...]
    ahead_ref[LENGTH:, :] = jnp.zeros((ROWS, CHANS), BF16)
    for g in range(GROUPS):
        strips_ref[g * STRIP : (g + 1) * STRIP, :] = strip_of(line_ref[g])
    low = jnp.dot(strips_ref[...], ahead_ref[:LENGTH, :], preferred_element_type=F32)
    d_mixed_low = pick_groups(low)
    high = jnp.dot(
        strips_ref[:, : LENGTH - STRIP], ahead_ref[STRIP:LENGTH, :], preferred_element_type=F32
    )
    d_mixed_high = pick_groups(high)
    d_inner = d0_ref[...].astype(F32)
    mixed = mixed_ref[...]
    d_mixed = jnp.concatenate([d_mixed_low, d_mixed_high], axis=0) + skip_ref[...] * d_inner

    k_parts = with_tail(near_ref[:, :CHANS], own_ref[:, :CHANS])
    v_parts = with_tail(near_ref[:, CHANS:], own_ref[:, CHANS:])
    q_parts = with_tail(tail_ref[...], query_ref[...])
    d_qs = d_gated_ref[...].astype(F32) * inner_ref[...]
    d_ks = d_mixed * short_sum(taps_ref, 2, v_parts)
    d_vs = d_mixed * short_sum(taps_ref, 1, k_parts)
    for i, (grad, parts) in enumerate(((d_qs, q_parts), (d_ks, k_parts), (d_vs, v_parts))):
        d_short_ref[i] = grad
        for j in range(3):
            small_ref[3 * i + j : 3 * i + j + 1, :] = jnp.sum(grad * parts[j], axis=0, keepdims=True)
    small_ref[9:10, :] = jnp.sum(d_inner * mixed.astype(F32), axis=0, keepdims=True)
    small_ref[10:, :] = jnp.zeros((6, CHANS), F32)

    row = lax.broadcasted_iota(jnp.int32, (ROWS, ROWS), 0)
    col = lax.broadcasted_iota(jnp.int32, (ROWS, ROWS), 1)
    turn = ((row // SMALL) * SMALL + (SMALL - 1 - row % SMALL) == col).astype(F32).astype(BF16)
    turned = jnp.dot(turn, mixed, preferred_element_type=F32)
    ids = lane_groups(SMALL)
    for part in range(ROWS // SMALL):
        piece = turned[part * SMALL : (part + 1) * SMALL]
        for g in range(GROUPS):
            stack_ref[g * SMALL : (g + 1) * SMALL, :] = jnp.where(ids == g, piece, 0.0).astype(BF16)
        term = lax.dot_general(
            stack_ref[...],
            ahead_ref[part * SMALL : part * SMALL + LENGTH, :],
            (((1,), (1,)), ((), ())),
            preferred_element_type=F32,
        )
        if part == 0:
            outer_ref[:, :LENGTH] = term
        else:
            outer_ref[:, :LENGTH] += term
    outer_ref[:, LENGTH:] = jnp.zeros((GROUPS * SMALL, STRIP), F32)
    for g in range(GROUPS):
        skewed = pltpu.roll(
            outer_ref[g * SMALL : (g + 1) * SMALL, :], WIDE - (SMALL - 1), 1, stride=1, stride_axis=0
        )
        filter_ref[g : g + 1, :] = jnp.sum(skewed[:, :LENGTH], axis=0, keepdims=True)


def bwd_call(blocks, lines, mixed, own, near, query, tail, inner, d_gated, taps, skip):
    whole = lambda shape: pl.BlockSpec(shape, lambda i: (0,) * len(shape))
    operands = (*blocks, lines, mixed, own, near, query, tail, inner, d_gated, taps, skip)
    specs = [whole(x.shape) for x in operands]
    specs[7] = pl.BlockSpec((TAIL, 2 * CHANS), lambda i: (ROWS // TAIL - 1, 0))
    return pl.pallas_call(
        bwd_kernel,
        grid=(1,),
        in_specs=specs,
        out_specs=[whole((3, ROWS, CHANS)), whole((GROUPS, LENGTH)), whole((16, CHANS))],
        out_shape=[
            jax.ShapeDtypeStruct((3, ROWS, CHANS), F32),
            jax.ShapeDtypeStruct((GROUPS, LENGTH), F32),
            jax.ShapeDtypeStruct((16, CHANS), F32),
        ],
        scratch_shapes=[
            pltpu.VMEM((GROUPS * STRIP, LENGTH), BF16),
            pltpu.VMEM((LENGTH + ROWS, CHANS), BF16),
            pltpu.VMEM((GROUPS * SMALL, WIDE), F32),
            pltpu.VMEM((GROUPS * SMALL, CHANS), BF16),
        ],
        compiler_params=params(),
        cost_estimate=pl.CostEstimate(flops=12 << 30, bytes_accessed=4 << 20, transcendentals=0),
        name="bwd",
    )(*operands)


def input_grad_kernel(d_short_ref, next_ref, taps_ref, query_ref, key_ref, value_ref):
    for i, out_ref in enumerate((query_ref, key_ref, value_ref)):
        joined = jnp.concatenate([d_short_ref[i], next_ref[i]], axis=0)
        rows = joined.shape[0]
        parts = (
            joined[:ROWS],
            pltpu.roll(joined, rows - 1, 0)[:ROWS],
            pltpu.roll(joined, rows - 2, 0)[:ROWS],
        )
        out_ref[...] = short_sum(taps_ref, i, parts).astype(BF16)


def input_grad_call(d_short, following, taps):
    return pl.pallas_call(
        input_grad_kernel,
        out_shape=[jax.ShapeDtypeStruct((ROWS, CHANS), BF16)] * 3,
        compiler_params=params(),
        cost_estimate=pl.CostEstimate(flops=1 << 20, bytes_accessed=2 << 20, transcendentals=0),
        name="input_grads",
    )(d_short, following, taps)


def total_kernel(scale, terms_ref, out_ref):
    total = (jnp.sum(terms_ref[...].astype(F32), axis=0) * scale).astype(BF16)
    out_ref[...] = jnp.broadcast_to(total[None], out_ref.shape)


def total_call(terms, copies, scale):
    return pl.pallas_call(
        lambda *refs: total_kernel(scale, *refs),
        out_shape=jax.ShapeDtypeStruct((copies, *terms.shape[1:]), BF16),
        compiler_params=params(),
        cost_estimate=pl.CostEstimate(flops=1 << 20, bytes_accessed=3 << 20, transcendentals=0),
        name="weight_total",
    )(terms)


def sent(block, distance):
    count = 4
    route = [(i, i + distance) for i in range(count) if 0 <= i + distance < count]
    return lax.ppermute(block, CTX, route)


def shards(
    query_in, key_in, value_in, short_taps, long_filter, skip_gain, out_weight, out_cotangent
):
    query = query_in[0]
    cot = out_cotangent[0]
    taps = short_taps.reshape(9, CHANS)
    skip = skip_gain.reshape(1, CHANS)
    devices = lax.axis_size(ALL)
    tokens = ROWS * devices
    scale = 1.0 / math.sqrt(tokens)
    core = lax.axis_index("co").astype(jnp.int32).reshape(1)

    own = jnp.concatenate([key_in[0], value_in[0]], axis=1)
    near, mid, far = (sent(own, distance) for distance in (1, 2, 3))
    tail = sent(query[ROWS - TAIL :], 1)
    swap = [(0, 1), (1, 0)]
    other_cot = lax.ppermute(cot, "co", swap)

    lags = long_filter.astype(F32)
    pad = jnp.zeros((GROUPS, STRIP), F32)
    back_lines = jnp.concatenate([lags, pad], axis=1)[:, None, :]
    turned = lags[:, ::-1]
    lines = jnp.concatenate([turned[:, STRIP - 1 :], pad, turned[:, : STRIP - 1]], axis=1)[:, None, :]

    d_gated, strips = pre_call(cot, out_weight, lines)
    d_inner = d_inner_call(d_gated, query, tail, taps)
    blocks = [d_inner] + [sent(d_inner, -distance) for distance in (1, 2, 3)]

    gated, inner, mixed = fwd_call(strips, far, mid, near, own, query, tail, taps, skip)
    other_gated = lax.ppermute(gated, "co", swap)
    terms = weight_call(core, cot, other_cot, gated, other_gated)
    chips = devices // 2
    terms = terms.reshape(chips, FEATS // 2 // chips, CHANS)
    terms = lax.all_to_all(terms, CHIPS, 0, 0)

    d_short, filter_part, small_part = bwd_call(
        blocks, back_lines, mixed, own, near, query, tail, inner, d_gated, taps, skip
    )
    following = sent(d_short[:, :8], -1)
    grad_query, grad_key, grad_value = input_grad_call(d_short, following, taps)

    filter_rows = GROUPS * LENGTH // CHANS
    rows = jnp.concatenate([filter_part.reshape(filter_rows, CHANS), small_part], axis=0)
    rows = jnp.pad(rows, ((0, devices - rows.shape[0]), (0, 0)))
    rows = lax.all_to_all(rows.reshape(devices, 1, CHANS), ALL, 0, 0)
    total = jnp.sum(rows, axis=0, keepdims=True) * scale
    rows = lax.all_to_all(jnp.broadcast_to(total, (devices, 1, CHANS)), ALL, 0, 0)
    rows = rows.reshape(devices, CHANS)
    grad_filter = rows[:filter_rows].reshape(GROUPS, LENGTH)
    grad_taps = rows[filter_rows : filter_rows + 9].reshape(3, 3, CHANS)
    grad_skip = rows[filter_rows + 9]

    copies = lax.axis_size(DP)
    shares = lax.all_to_all(total_call(terms, copies, scale), DP, 0, 0)
    grad_weight = shares.reshape(FEATS // 4, CHANS).astype(F32)
    return (
        gated[None],
        grad_query[None],
        grad_key[None],
        grad_value[None],
        grad_taps,
        grad_filter,
        grad_skip,
        grad_weight,
    )


def solution(mesh):
    fine = Mesh(mesh.devices.reshape(2, 2, 4, 2, 4), ALL)
    tokens = P(DP, CTX, None)
    in_specs = (tokens, tokens, tokens, P(), P(), P(), P(), tokens)
    out_specs = (tokens, tokens, tokens, tokens, P(), P(), P(), P(CTX, None))
    return jax.shard_map(
        shards, mesh=fine, in_specs=in_specs, out_specs=out_specs, check_vma=False
    )
```

time: 1560 us -> 151 us (0.10)
  local copies, waits for them, and re-layouts: 1290 us -> 13.5 us
  blocking collectives: 83.1 us -> 0 us
  waiting for transfers between devices: 89.8 us -> 50.6 us
  Pallas kernels: 0 us -> 34.3 us
  matrix products: 16.8 us -> 0 us
  other arithmetic: 19.7 us -> 3.42 us
    gather x10 -> x0, local copies, waits for them, and re-layouts: 1210 us -> none  [toeplitz(): return jnp.take(padded, lag_index, axis=1, mode='clip')]
    psum x1 -> x0, waiting for transfers between devices: 88.9 us -> none  [shards(): lax.psum((taps_local, filter_local, skip_local), ('ctx', 'dp'))]
    psum x1 -> x0, blocking collectives: 66.8 us -> none  [shards(): lax.psum((taps_local, filter_local, skip_local), ('ctx', 'dp'))]
    all_to_all x0 -> x4, waiting for transfers between devices: none -> 39.7 us  [the longest x1 28.5 us: shards(): terms = lax.all_to_all(terms, CHIPS, 0, 0)]
    pallas_call x0 -> x7, Pallas kernels: none -> 34.3 us  [the longest x1 8.57 us: pre_call(): pl.pallas_call(pre_kernel, grid=(steps,), in_specs=[pl.BlockSpec((ROWS, T...]
    reshape x5, local copies, waits for them, and re-layouts: 36.3 us -> 3.47 us  [the longest x1 0.86 us: shards(): filter_part.reshape(filter_rows, CHANS)]
    all_to_all x0 -> x4, starting transfers between devices: none -> 27.8 us  [the longest x1 9.92 us: shards(): rows = lax.all_to_all(rows.reshape(devices, 1, CHANS), ALL, 0, 0)]
    ppermute x2 -> x10, starting transfers between devices: 36.6 us -> 19.4 us  [the longest x8 15.9 us: sent(): return lax.ppermute(block, CTX, route)]
  transfers between devices with their start and end apart: 3 -> 14, of which waited for: 2 -> 5; matrix products, arithmetic and copies ran while one was open for 0% -> 8% of each run, Pallas kernels for 0% -> 23%
where the time goes in v1:
time: 151 us; the launch traced here: 150 us
  waiting for transfers between devices  50.6 us (34%)
  starting transfers between devices  47.2 us (31%)
  Pallas kernels  34.3 us (23%)
  local copies, waits for them, and re-layouts  13.5 us (9%)
  other arithmetic  3.42 us (2%)
    all_to_all x1, waiting for transfers between devices, shards(): terms = lax.all_to_all(terms, CHIPS, 0, 0)  28.5 us
    ppermute x8, starting transfers between devices, sent(): return lax.ppermute(block, CTX, route)  15.9 us
    ppermute x8, waiting for transfers between devices, sent(): return lax.ppermute(block, CTX, route)  10.9 us
    all_to_all x1, starting transfers between devices, shards(): rows = lax.all_to_all(rows.reshape(devices, 1, CHANS), ALL, 0, 0)  9.92 us
    pallas_call x1, Pallas kernels, pre_call(): pl.pallas_call(pre_kernel, grid=(steps,), in_specs=[pl.BlockSpec((ROWS, T...  8.57 us
    pallas_call x1, Pallas kernels, bwd_call(): pl.pallas_call(bwd_kernel, grid=(1,), in_specs=specs, out_specs=[whole((3...  7.84 us
    all_to_all x1, starting transfers between devices, shards(): lax.all_to_all(jnp.broadcast_to(total, (devices, 1, CHANS)), ALL, 0, 0)  7.34 us
    all_to_all x1, waiting for transfers between devices, shards(): lax.all_to_all(jnp.broadcast_to(total, (devices, 1, CHANS)), ALL, 0, 0)  7 us
  transfers between devices with their start and end apart: 14, of which 5 were waited for; matrix products, arithmetic and copies ran while one was open for 8% of the time, Pallas kernels for 23%

profile of v1, /device:TPU:1, one launch (start us, length us, event | category | flops | bytes accessed | tf_op | source)
XLA Modules:
  0.0 149.8 jit_solution(5773312067009648462)
XLA Ops:
  0.6 1.5 %collective-permute-start.8 = (bf16[256,8192]{1,0:T(8,128)(2,1)}, bf16[256,8192]{1,0:T(8,128)(2,1)}, u32[]{:S(2)}, u32[]{:S(2)}) collective-permute-start(bf16[256,8192]{1,0:T(8,128)(2,1)} %bitcast.19), channel_id=1, source_target_pairs={{0,32},{32,0},{1,33},{33,1},{2,34},{34,2},{3,35},{35,3},{4,36},{36... | collective-permute-start | bytes 12582920 | tf_op jit(solution)/shard_map/ppermute | solution.py:342
  2.1 1.0 pad_maximum_fusion.own_ref
  3.1 4.6 %collective-permute-start.2 = (bf16[256,512]{1,0:T(8,128)(2,1)S(1)}, bf16[256,512]{1,0:T(8,128)(2,1)S(1)}, u32[]{:S(2)}, u32[]{:S(2)}) collective-permute-start(bf16[256,512]{1,0:T(8,128)(2,1)S(1)} %pad_maximum_fusion.own_ref), channel_id=1, source_target_pairs={{0,32},{32,64},{64,96},{1,33},{33,65},{65,97},{2,34},{34,66},{66,9... | collective-permute-start | bytes 786440 | tf_op jit(solution)/shard_map/ppermute | solution.py:323
  7.8 0.7 collective-permute-start
  8.5 2.0 %collective-permute-start.1 = (bf16[256,512]{1,0:T(8,128)(2,1)S(1)}, bf16[256,512]{1,0:T(8,128)(2,1)S(1)}, u32[]{:S(2)}, u32[]{:S(2)}) collective-permute-start(bf16[256,512]{1,0:T(8,128)(2,1)S(1)} %pad_maximum_fusion.own_ref), channel_id=1, source_target_pairs={{0,64},{32,96},{1,65},{33,97},{2,66},{34,98},{3,67},{35,99},{4,68}... | collective-permute-start | bytes 786440 | tf_op jit(solution)/shard_map/ppermute | solution.py:323
  10.5 0.7 slice_bitcast_fusion
  11.2 1.9 %collective-permute-start.3 = (bf16[16,256]{1,0:T(8,128)(2,1)S(1)}, bf16[16,256]{1,0:T(8,128)(2,1)S(1)}, u32[]{:S(2)}, u32[]{:S(2)}) collective-permute-start(bf16[16,256]{1,0:T(8,128)(2,1)S(1)} %slice_bitcast_fusion), channel_id=1, source_target_pairs={{0,32},{32,64},{64,96},{1,33},{33,65},{65,97},{2,34},{34,66},{66,9... | collective-permute-start | bytes 24584 | tf_op jit(solution)/shard_map/ppermute | solution.py:323
  13.1 0.8 slice.43
  13.9 0.8 slice.44
  14.6 0.6 reverse.2
  15.2 0.1 slice.51
  15.3 0.1 slice.36
  15.4 0.1 concatenate.12
  15.5 0.7 copy.18.line_ref
  16.2 8.6 %pre.1 = (bf16[256,256]{1,0:T(8,128)(2,1)}, bf16[2048,1024]{1,0:T(8,128)(2,1)}) custom-call(bf16[256,8192]{1,0:T(8,128)(2,1)} %bitcast.20, bf16[8192,256]{1,0:T(8,128)(2,1)} %weight_ref.1, f32[16,1,1152]{2,1,0:T(1,128)} %copy.18.line_ref), custom_call_target="tpu_custom_call" | custom-call | flops 1073741824 | bytes 14680064 | tf_op jit(solution)/shard_map/pre/pallas_call | solution.py:84
  24.8 0.6 reshape.60.taps_ref
  25.4 0.7 broadcast_in_dim.30.line_ref
  26.1 0.0 collective-permute-done.3.tail_ref
  26.1 0.6 copy-done.7
  26.7 1.7 %d_inner.1.d0_ref = bf16[256,256]{1,0:T(8,128)(2,1)} custom-call(bf16[256,256]{1,0:T(8,128)(2,1)} %get-tuple-element.21.d_gated_ref, bf16[256,256]{1,0:T(8,128)(2,1)} %bitcast.25, bf16[16,256]{1,0:T(8,128)(2,1)} %copy-done.7, f32[9,256]{1,0:T(8,128)} %reshape.60.taps_ref), custom_call_target="tpu_custom_call" | custom-call | flops 1048576 | bytes 524288 | tf_op jit(solution)/shard_map/d_inner/pallas_call | solution.py:115
  28.4 2.4 %collective-permute-start.4 = (bf16[256,256]{1,0:T(8,128)(2,1)}, bf16[256,256]{1,0:T(8,128)(2,1)S(1)}, u32[]{:S(2)}, u32[]{:S(2)}) collective-permute-start(bf16[256,256]{1,0:T(8,128)(2,1)} %d_inner.1.d0_ref), channel_id=1, source_target_pairs={{32,0},{64,32},{96,64},{33,1},{65,33},{97,65},{34,2},{66,34},{98,6... | collective-permute-start | bytes 393224 | tf_op jit(solution)/shard_map/ppermute | solution.py:323
  30.8 0.0 collective-permute-done.2.near_ref
  30.8 1.3 collective-permute-start.5
  32.1 0.0 collective-permute-done.far_ref
  32.1 0.0 copy-start.9
  32.1 0.7 collective-permute-start.6
  32.9 0.7 copy-done.10
  33.5 5.9 %fwd.1 = (bf16[256,256]{1,0:T(8,128)(2,1)}, f32[256,256]{1,0:T(8,128)}, bf16[256,256]{1,0:T(8,128)(2,1)}) custom-call(bf16[2048,1024]{1,0:T(8,128)(2,1)} %get-tuple-element.19.strips_ref, bf16[256,512]{1,0:T(8,128)(2,1)} %copy-done.9, bf16[256,512]{1,0:T(8,128)(2,1)} %copy-done.10, bf16[256,512]{1,0:T(8,128)(2,1)} %copy-done.8, bf16[256,512]{1,0:T(8,128)(2,1)} %copy-done.2, ...), custom_call_target="tpu_custom_call" | custom-call | flops 4294967296 | bytes 6291456 | tf_op jit(solution)/shard_map/fwd/pallas_call | solution.py:145
  39.4 0.0 collective-permute-done.4.d1_ref
  39.4 0.2 collective-permute-done.5.d2_ref
  39.6 0.0 collective-permute-done.6.d3_ref
  39.6 0.5 copy-done.11
  40.1 0.2 copy-done.12
  40.3 0.0 copy-done.13
  40.3 7.8 %bwd.1 = (f32[3,256,256]{2,1,0:T(8,128)}, f32[16,1024]{1,0:T(8,128)}, f32[16,256]{1,0:T(8,128)}) custom-call(bf16[256,256]{1,0:T(8,128)(2,1)} %d_inner.1.d0_ref, bf16[256,256]{1,0:T(8,128)(2,1)} %copy-done.11, bf16[256,256]{1,0:T(8,128)(2,1)} %copy-done.12, bf16[256,256]{1,0:T(8,128)(2,1)} %copy-done.13, f32[16,1,1152]{2,1,0:T(1,128)} %broadcast_in_dim.30.line_ref, ...), custom_call_target="tpu_custom_call" | custom-call | flops 12884901888 | bytes 4194304 | tf_op jit(solution)/shard_map/bwd/pallas_call | solution.py:261
  48.2 0.9 reshape.62
  49.0 2.0 %collective-permute-start.9 = (bf16[256,256]{1,0:T(8,128)(2,1)S(1)}, bf16[256,256]{1,0:T(8,128)(2,1)S(1)}, u32[]{:S(2)}, u32[]{:S(2)}) collective-permute-start(bf16[256,256]{1,0:T(8,128)(2,1)S(1)} %copy-done.3), channel_id=1, source_target_pairs={{0,32},{32,0},{1,33},{33,1},{2,34},{34,2},{3,35},{35,3},{4,36},{36... | collective-permute-start | bytes 393224 | tf_op jit(solution)/shard_map/ppermute | solution.py:355
  51.0 0.7 select_maximum_fusion
  51.8 0.7 reshape.63
  52.5 9.9 %all-to-all-start = ((f32[128,1,256]{2,1,0:T(1,128)}), f32[128,1,256]{2,1,0:T(1,128)S(1)}, u32[]{:S(2)}, u32[]{:S(2)}) async-start(f32[128,1,256]{2,1,0:T(1,128)} %reshape.63), calls=%async_computation | async-start | bytes 262144 | tf_op jit(solution)/shard_map/all_to_all | solution.py:370
  62.4 0.0 collective-permute-done.9.other_gated_ref
  62.4 0.0 copy-start.4
  62.5 0.6 copy-done.4
  63.1 5.2 %weight_terms.1 = bf16[4096,256]{1,0:T(8,128)(2,1)} custom-call(s32[1]{0:T(128)} %bitcast.12.core_ref, bf16[256,8192]{1,0:T(8,128)(2,1)} %bitcast.21, bf16[256,8192]{1,0:T(8,128)(2,1)} %collective-permute-done.8.other_cot_ref, bf16[256,256]{1,0:T(8,128)(2,1)} %get-tuple-element.20.gated_ref, bf16[256,256]{1,0:T(8,128)(2,1)} %copy-done.4), custom_call_target="tpu_custom_call" | custom-call | flops 1073741824 | bytes 6291456 | tf_op jit(solution)/shard_map/weight_terms/pallas_call | solution.py:173
  68.3 4.1 %all-to-all-done = f32[128,1,256]{2,1,0:T(1,128)S(1)} async-done(((f32[128,1,256]{2,1,0:T(1,128)}), f32[128,1,256]{2,1,0:T(1,128)S(1)}, u32[]{:S(2)}, u32[]{:S(2)}) %all-to-all-start) | async-done | bytes 131104 | tf_op jit(solution)/shard_map/all_to_all | solution.py:370
  72.4 6.6 %all-to-all-start.2 = ((bf16[64,64,256]{2,1,0:T(8,128)(2,1)}), bf16[64,64,256]{2,1,0:T(8,128)(2,1)S(1)}, u32[]{:S(2)}, u32[]{:S(2)}) async-start(bf16[64,64,256]{2,1,0:T(8,128)(2,1)} %bitcast.22), calls=%async_computation.2 | async-start | bytes 4194304 | tf_op jit(solution)/shard_map/all_to_all | solution.py:359
  79.1 0.2 reduce_sum.9
  79.2 28.5 %all-to-all-done.2.refs_0_ = bf16[64,64,256]{2,1,0:T(8,128)(2,1)S(1)} async-done(((bf16[64,64,256]{2,1,0:T(8,128)(2,1)}), bf16[64,64,256]{2,1,0:T(8,128)(2,1)S(1)}, u32[]{:S(2)}, u32[]{:S(2)}) %all-to-all-start.2) | async-done | bytes 2097184 | tf_op jit(solution)/shard_map/all_to_all | solution.py:359
  107.8 0.8 broadcast_in_dim.34
  108.6 7.3 %all-to-all-start.1 = ((f32[128,1,256]{2,1,0:T(1,128)}), f32[128,1,256]{2,1,0:T(1,128)S(1)}, u32[]{:S(2)}, u32[]{:S(2)}) async-start(f32[128,1,256]{2,1,0:T(1,128)} %broadcast_in_dim.34), calls=%async_computation.1 | async-start | bytes 262144 | tf_op jit(solution)/shard_map/all_to_all | solution.py:372
  115.9 3.0 %weight_total.1 = bf16[32,64,256]{2,1,0:T(8,128)(2,1)} custom-call(bf16[64,64,256]{2,1,0:T(8,128)(2,1)} %copy-done), custom_call_target="tpu_custom_call" | custom-call | flops 1048576 | bytes 3145728 | tf_op jit(solution)/shard_map/weight_total/pallas_call | solution.py:311
  118.9 7.0 %all-to-all-done.1 = f32[128,1,256]{2,1,0:T(1,128)S(1)} async-done(((f32[128,1,256]{2,1,0:T(1,128)}), f32[128,1,256]{2,1,0:T(1,128)S(1)}, u32[]{:S(2)}, u32[]{:S(2)}) %all-to-all-start.1) | async-done | bytes 131104 | tf_op jit(solution)/shard_map/all_to_all | solution.py:372
  125.9 3.9 %all-to-all-start.3 = ((bf16[32,64,256]{2,1,0:T(8,128)(2,1)}), bf16[32,64,256]{2,1,0:T(8,128)(2,1)S(1)}, u32[]{:S(2)}, u32[]{:S(2)}) async-start(bf16[32,64,256]{2,1,0:T(8,128)(2,1)} %weight_total.1), calls=%async_computation.3 | async-start | bytes 2097152 | tf_op jit(solution)/shard_map/all_to_all | solution.py:379
  129.8 0.7 slice.39
  130.6 2.3 %collective-permute-start.7 = (f32[3,8,256]{2,1,0:T(8,128)S(1)}, f32[3,8,256]{2,1,0:T(8,128)S(1)}, u32[]{:S(2)}, u32[]{:S(2)}) collective-permute-start(f32[3,8,256]{2,1,0:T(8,128)S(1)} %slice.39), channel_id=1, source_target_pairs={{32,0},{64,32},{96,64},{33,1},{65,33},{97,65},{34,2},{66,34},{98,6... | collective-permute-start | bytes 73736 | tf_op jit(solution)/shard_map/ppermute | solution.py:323
  132.9 10.7 %collective-permute-done.7.next_ref = f32[3,8,256]{2,1,0:T(8,128)S(1)} collective-permute-done((f32[3,8,256]{2,1,0:T(8,128)S(1)}, f32[3,8,256]{2,1,0:T(8,128)S(1)}, u32[]{:S(2)}, u32[]{:S(2)}) %collective-permute-start.7) | collective-permute-done | bytes 24608 | tf_op jit(solution)/shard_map/ppermute | solution.py:323
  143.6 0.6 copy-done.5
  144.2 2.1 %input_grads.1 = (bf16[256,256]{1,0:T(8,128)(2,1)}, bf16[256,256]{1,0:T(8,128)(2,1)}, bf16[256,256]{1,0:T(8,128)(2,1)}) custom-call(f32[3,256,256]{2,1,0:T(8,128)} %get-tuple-element.24.d_short_ref, f32[3,8,256]{2,1,0:T(8,128)} %copy-done.5, f32[9,256]{1,0:T(8,128)} %reshape.60.taps_ref), custom_call_target="tpu_custom_call" | custom-call | flops 1048576 | bytes 2097152 | tf_op jit(solution)/shard_map/input_grads/pallas_call | solution.py:296
  146.3 0.2 slice_reduce_fusion
  146.4 0.6 reshape.65
  147.1 0.6 reshape.64
  147.7 0.6 slice.47
  148.3 0.0 all-to-all-done.3
  148.3 1.5 %bitcast_convert_fusion = f32[2048,256]{1,0:T(8,128)} fusion(bf16[32,64,256]{2,1,0:T(8,128)(2,1)S(1)} %all-to-all-done.3), kind=kLoop, calls=%fused_computation | loop fusion | flops 524288 | bytes 3145728 | tf_op jit(solution)/shard_map/convert_element_type | solution.py:380
  (25 shorter events, 0.1 us)
Async XLA Ops:
  0.6 61.8 %collective-permute-start.8 = (bf16[256,8192]{1,0:T(8,128)(2,1)}, bf16[256,8192]{1,0:T(8,128)(2,1)}, u32[]{:S(2)}, u32[]{:S(2)}) collective-permute-start(bf16[256,8192]{1,0:T(8,128)(2,1)} %bitcast.19), channel_id=1, source_target_pairs={{0,32},{32,0},{1,33},{33,1},{2,34},{34,2},{3,35},{35,3},{4,36},{36... | collective-permute-start | bytes 12582920 | tf_op jit(solution)/shard_map/ppermute | solution.py:342
  3.1 21.6 %copy-start.2 = (bf16[256,512]{1,0:T(8,128)(2,1)}, bf16[256,512]{1,0:T(8,128)(2,1)S(1)}, u32[]{:S(2)}) copy-start(bf16[256,512]{1,0:T(8,128)(2,1)S(1)} %pad_maximum_fusion.own_ref) | copy-start | bytes 786436
  3.1 27.7 %collective-permute-start.2 = (bf16[256,512]{1,0:T(8,128)(2,1)S(1)}, bf16[256,512]{1,0:T(8,128)(2,1)S(1)}, u32[]{:S(2)}, u32[]{:S(2)}) collective-permute-start(bf16[256,512]{1,0:T(8,128)(2,1)S(1)} %pad_maximum_fusion.own_ref), channel_id=1, source_target_pairs={{0,32},{32,64},{64,96},{1,33},{33,65},{65,97},{2,34},{34,66},{66,9... | collective-permute-start | bytes 786440 | tf_op jit(solution)/shard_map/ppermute | solution.py:323
  7.8 24.3 %collective-permute-start = (bf16[256,512]{1,0:T(8,128)(2,1)S(1)}, bf16[256,512]{1,0:T(8,128)(2,1)S(1)}, u32[]{:S(2)}, u32[]{:S(2)}) collective-permute-start(bf16[256,512]{1,0:T(8,128)(2,1)S(1)} %pad_maximum_fusion.own_ref), channel_id=1, source_target_pairs={{0,96},{1,97},{2,98},{3,99},{4,100},{5,101},{6,102},{7,103},{8,104... | collective-permute-start | bytes 786440 | tf_op jit(solution)/shard_map/ppermute | solution.py:323
  8.5 24.3 %collective-permute-start.1 = (bf16[256,512]{1,0:T(8,128)(2,1)S(1)}, bf16[256,512]{1,0:T(8,128)(2,1)S(1)}, u32[]{:S(2)}, u32[]{:S(2)}) collective-permute-start(bf16[256,512]{1,0:T(8,128)(2,1)S(1)} %pad_maximum_fusion.own_ref), channel_id=1, source_target_pairs={{0,64},{32,96},{1,65},{33,97},{2,66},{34,98},{3,67},{35,99},{4,68}... | collective-permute-start | bytes 786440 | tf_op jit(solution)/shard_map/ppermute | solution.py:323
  11.2 14.9 %collective-permute-start.3 = (bf16[16,256]{1,0:T(8,128)(2,1)S(1)}, bf16[16,256]{1,0:T(8,128)(2,1)S(1)}, u32[]{:S(2)}, u32[]{:S(2)}) collective-permute-start(bf16[16,256]{1,0:T(8,128)(2,1)S(1)} %slice_bitcast_fusion), channel_id=1, source_target_pairs={{0,32},{32,64},{64,96},{1,33},{33,65},{65,97},{2,34},{34,66},{66,9... | collective-permute-start | bytes 24584 | tf_op jit(solution)/shard_map/ppermute | solution.py:323
  16.2 8.6 %copy-start.1 = (bf16[16,1024]{1,0:T(8,128)(2,1)S(1)}, bf16[16,1024]{1,0:T(8,128)(2,1)}, u32[]{:S(2)}) copy-start(bf16[16,1024]{1,0:T(8,128)(2,1)} %param.12) | copy-start | bytes 98308
  16.2 8.6 %copy-start.6 = (f32[3,3,256]{2,1,0:T(4,128)S(1)}, f32[3,3,256]{2,1,0:T(4,128)}, u32[]{:S(2)}) copy-start(f32[3,3,256]{2,1,0:T(4,128)} %param.11) | copy-start | bytes 27652
  26.1 0.6 copy-start.7
  28.4 11.0 %collective-permute-start.4 = (bf16[256,256]{1,0:T(8,128)(2,1)}, bf16[256,256]{1,0:T(8,128)(2,1)S(1)}, u32[]{:S(2)}, u32[]{:S(2)}) collective-permute-start(bf16[256,256]{1,0:T(8,128)(2,1)} %d_inner.1.d0_ref), channel_id=1, source_target_pairs={{32,0},{64,32},{96,64},{33,1},{65,33},{97,65},{34,2},{66,34},{98,6... | collective-permute-start | bytes 393224 | tf_op jit(solution)/shard_map/ppermute | solution.py:323
  30.8 2.0 %copy-start.8 = (bf16[256,512]{1,0:T(8,128)(2,1)}, bf16[256,512]{1,0:T(8,128)(2,1)S(1)}, u32[]{:S(2)}) copy-start(bf16[256,512]{1,0:T(8,128)(2,1)S(1)} %collective-permute-done.2.near_ref) | copy-start | bytes 786436
  30.8 8.8 %collective-permute-start.5 = (bf16[256,256]{1,0:T(8,128)(2,1)}, bf16[256,256]{1,0:T(8,128)(2,1)S(1)}, u32[]{:S(2)}, u32[]{:S(2)}) collective-permute-start(bf16[256,256]{1,0:T(8,128)(2,1)} %d_inner.1.d0_ref), channel_id=1, source_target_pairs={{64,0},{96,32},{65,1},{97,33},{66,2},{98,34},{67,3},{99,35},{68,4}... | collective-permute-start | bytes 393224 | tf_op jit(solution)/shard_map/ppermute | solution.py:323
  32.1 0.7 copy-start.9
  32.1 7.5 %collective-permute-start.6 = (bf16[256,256]{1,0:T(8,128)(2,1)}, bf16[256,256]{1,0:T(8,128)(2,1)S(1)}, u32[]{:S(2)}, u32[]{:S(2)}) collective-permute-start(bf16[256,256]{1,0:T(8,128)(2,1)} %d_inner.1.d0_ref), channel_id=1, source_target_pairs={{96,0},{97,1},{98,2},{99,3},{100,4},{101,5},{102,6},{103,7},{104,8... | collective-permute-start | bytes 393224 | tf_op jit(solution)/shard_map/ppermute | solution.py:323
  32.8 0.7 copy-start.10
  39.4 0.7 copy-start.11
  39.6 0.6 copy-start.12
  39.6 0.7 copy-start.13
  40.3 8.7 %copy-start.3 = (bf16[256,256]{1,0:T(8,128)(2,1)S(1)}, bf16[256,256]{1,0:T(8,128)(2,1)}, u32[]{:S(2)}) copy-start(bf16[256,256]{1,0:T(8,128)(2,1)} %get-tuple-element.20.gated_ref) | copy-start | bytes 393220
  49.0 13.4 %collective-permute-start.9 = (bf16[256,256]{1,0:T(8,128)(2,1)S(1)}, bf16[256,256]{1,0:T(8,128)(2,1)S(1)}, u32[]{:S(2)}, u32[]{:S(2)}) collective-permute-start(bf16[256,256]{1,0:T(8,128)(2,1)S(1)} %copy-done.3), channel_id=1, source_target_pairs={{0,32},{32,0},{1,33},{33,1},{2,34},{34,2},{3,35},{35,3},{4,36},{36... | collective-permute-start | bytes 393224 | tf_op jit(solution)/shard_map/ppermute | solution.py:355
  52.5 19.9 %all-to-all-start = ((f32[128,1,256]{2,1,0:T(1,128)}), f32[128,1,256]{2,1,0:T(1,128)S(1)}, u32[]{:S(2)}, u32[]{:S(2)}) async-start(f32[128,1,256]{2,1,0:T(1,128)} %reshape.63), calls=%async_computation | async-start | bytes 262144 | tf_op jit(solution)/shard_map/all_to_all | solution.py:370
  62.4 0.7 copy-start.4
  72.4 35.3 %all-to-all-start.2 = ((bf16[64,64,256]{2,1,0:T(8,128)(2,1)}), bf16[64,64,256]{2,1,0:T(8,128)(2,1)S(1)}, u32[]{:S(2)}, u32[]{:S(2)}) async-start(bf16[64,64,256]{2,1,0:T(8,128)(2,1)} %bitcast.22), calls=%async_computation.2 | async-start | bytes 4194304 | tf_op jit(solution)/shard_map/all_to_all | solution.py:359
  107.8 8.2 %copy-start = (bf16[64,64,256]{2,1,0:T(8,128)(2,1)}, bf16[64,64,256]{2,1,0:T(8,128)(2,1)S(1)}, u32[]{:S(2)}) copy-start(bf16[64,64,256]{2,1,0:T(8,128)(2,1)S(1)} %all-to-all-done.2.refs_0_) | copy-start | bytes 6291460
  108.6 17.3 %all-to-all-start.1 = ((f32[128,1,256]{2,1,0:T(1,128)}), f32[128,1,256]{2,1,0:T(1,128)S(1)}, u32[]{:S(2)}, u32[]{:S(2)}) async-start(f32[128,1,256]{2,1,0:T(1,128)} %broadcast_in_dim.34), calls=%async_computation.1 | async-start | bytes 262144 | tf_op jit(solution)/shard_map/all_to_all | solution.py:372
  125.9 22.4 %all-to-all-start.3 = ((bf16[32,64,256]{2,1,0:T(8,128)(2,1)}), bf16[32,64,256]{2,1,0:T(8,128)(2,1)S(1)}, u32[]{:S(2)}, u32[]{:S(2)}) async-start(bf16[32,64,256]{2,1,0:T(8,128)(2,1)} %weight_total.1), calls=%async_computation.3 | async-start | bytes 2097152 | tf_op jit(solution)/shard_map/all_to_all | solution.py:379
  130.6 13.0 %collective-permute-start.7 = (f32[3,8,256]{2,1,0:T(8,128)S(1)}, f32[3,8,256]{2,1,0:T(8,128)S(1)}, u32[]{:S(2)}, u32[]{:S(2)}) collective-permute-start(f32[3,8,256]{2,1,0:T(8,128)S(1)} %slice.39), channel_id=1, source_target_pairs={{32,0},{64,32},{96,64},{33,1},{65,33},{97,65},{34,2},{66,34},{98,6... | collective-permute-start | bytes 73736 | tf_op jit(solution)/shard_map/ppermute | solution.py:323
  143.6 0.6 copy-start.5

commit v2 on v1

v2 whole, which is shorter than its diff:
```python
import math

import jax
import jax.numpy as jnp
from jax import lax
from jax.experimental import pallas as pl
from jax.experimental.pallas import tpu as pltpu
from jax.sharding import Mesh
from jax.sharding import PartitionSpec as P

F32 = jnp.float32
BF16 = jnp.bfloat16
CTX = ("xh", "co")
DP = ("y", "xl", "z")
CHIPS = ("xh", "y", "xl", "z")
ALL = ("xh", "co", "y", "xl", "z")

ROWS = 256
CHANS = 256
GROUPS = 16
LENGTH = 1024
STRIP = 128
WIDE = LENGTH + STRIP
FEATS = 8192
TILE = 1024
SMALL = 64
TAIL = 16
SHARES = 32
FIRST = 48
SECOND = 16
SEGMENT = 8
FWD_GROUPS = 4
VMEM_LIMIT = 56 * 1024 * 1024


def params(*semantics):
    return pltpu.CompilerParams(vmem_limit_bytes=VMEM_LIMIT)


def lane_groups(rows):
    return lax.broadcasted_iota(jnp.int32, (rows, CHANS), 1) // (CHANS // GROUPS)


def later(x, count):
    row = lax.broadcasted_iota(jnp.int32, x.shape, 0)
    return jnp.where(row >= count, pltpu.roll(x, count, 0), 0.0)


def strip_of(line):
    wide = jnp.broadcast_to(line, (STRIP, WIDE))
    return pltpu.roll(wide, 0, 1, stride=1, stride_axis=0)[:, :LENGTH].astype(BF16)


def pick_groups(result, first=0, out=None):
    ids = lane_groups(STRIP)
    if out is None:
        out = jnp.zeros((STRIP, CHANS), F32)
    for g in range(result.shape[0] // STRIP):
        out = jnp.where(ids == first + g, result[g * STRIP : (g + 1) * STRIP], out)
    return out


def with_tail(tail, block):
    joined = jnp.concatenate([tail, block], axis=0).astype(F32)
    return joined[TAIL:], pltpu.roll(joined, 1, 0)[TAIL:], pltpu.roll(joined, 2, 0)[TAIL:]


def short_sum(taps_ref, i, parts):
    return sum(taps_ref[i, j : j + 1, :] * parts[j] for j in range(3))


def pack_kernel(key_ref, value_ref, query_ref, out_ref):
    out_ref[:ROWS, :CHANS] = key_ref[...]
    out_ref[:ROWS, CHANS:] = value_ref[...]
    out_ref[ROWS:, :CHANS] = query_ref[...]
    out_ref[ROWS:, CHANS:] = query_ref[...]


def pack_call(key, value, query):
    whole = pl.BlockSpec((ROWS, CHANS), lambda i: (0, 0))
    return pl.pallas_call(
        pack_kernel,
        grid=(1,),
        in_specs=[whole, whole, pl.BlockSpec((TAIL, CHANS), lambda i: (ROWS // TAIL - 1, 0))],
        out_specs=pl.BlockSpec((ROWS + TAIL, 2 * CHANS), lambda i: (0, 0)),
        out_shape=jax.ShapeDtypeStruct((ROWS + TAIL, 2 * CHANS), BF16),
        compiler_params=params(),
        name="pack",
    )(key, value, query)


def lines_of(filter_ref, turned):
    if not turned:
        return jnp.concatenate(
            [filter_ref[...].astype(F32), jnp.zeros((GROUPS, STRIP), F32)], axis=1
        )
    row = lax.broadcasted_iota(jnp.int32, (CHANS, CHANS), 0)
    col = lax.broadcasted_iota(jnp.int32, (CHANS, CHANS), 1)
    turn = (row + col == CHANS - 1).astype(F32).astype(BF16)
    pieces = [
        jnp.dot(filter_ref[:, n * CHANS : (n + 1) * CHANS], turn, preferred_element_type=F32)
        for n in reversed(range(LENGTH // CHANS))
    ]
    wide = jnp.concatenate([*pieces, jnp.zeros((GROUPS, STRIP), F32)], axis=1)
    return pltpu.roll(wide, WIDE - (STRIP - 1), 1)


def pre_kernel(cot_ref, weight_ref, filter_ref, d_gated_ref, strips_ref, acc_ref, line_ref):
    step = pl.program_id(0)

    @pl.when(step == 0)
    def _():
        acc_ref[...] = jnp.zeros_like(acc_ref)
        line_ref[...] = lines_of(filter_ref, True)

    acc_ref[...] += jnp.dot(cot_ref[...], weight_ref[...], preferred_element_type=F32)
    for g in range(2):
        line = line_ref[pl.ds(2 * step + g, 1), :]
        strips_ref[g * STRIP : (g + 1) * STRIP, :] = strip_of(line)

    @pl.when(step == pl.num_programs(0) - 1)
    def _():
        d_gated_ref[...] = acc_ref[...].astype(BF16)


def pre_call(cot, weight, lags):
    steps = FEATS // TILE
    return pl.pallas_call(
        pre_kernel,
        grid=(steps,),
        in_specs=[
            pl.BlockSpec((ROWS, TILE), lambda i: (0, i)),
            pl.BlockSpec((TILE, CHANS), lambda i: (i, 0)),
            pl.BlockSpec((GROUPS, LENGTH), lambda i: (0, 0)),
        ],
        out_specs=[
            pl.BlockSpec((ROWS, CHANS), lambda i: (0, 0)),
            pl.BlockSpec((2 * STRIP, LENGTH), lambda i: (i, 0)),
        ],
        out_shape=[
            jax.ShapeDtypeStruct((ROWS, CHANS), BF16),
            jax.ShapeDtypeStruct((GROUPS * STRIP, LENGTH), BF16),
        ],
        scratch_shapes=[pltpu.VMEM((ROWS, CHANS), F32), pltpu.VMEM((GROUPS, WIDE), F32)],
        compiler_params=params(),
        cost_estimate=pl.CostEstimate(
            flops=2 * ROWS * FEATS * CHANS, bytes_accessed=14 << 20, transcendentals=0
        ),
        name="pre",
    )(cot, weight, lags)


def d_inner_kernel(d_gated_ref, query_ref, tail_ref, taps_ref, out_ref):
    q_short = short_sum(taps_ref, 0, with_tail(tail_ref[...], query_ref[...]))
    out_ref[...] = (d_gated_ref[...].astype(F32) * q_short).astype(BF16)


def d_inner_call(d_gated, query, near, taps):
    whole = pl.BlockSpec((ROWS, CHANS), lambda i: (0, 0))
    return pl.pallas_call(
        d_inner_kernel,
        grid=(1,),
        in_specs=[
            whole,
            whole,
            pl.BlockSpec((TAIL, CHANS), lambda i: (ROWS // TAIL, 0)),
            pl.BlockSpec((3, 3, CHANS), lambda i: (0, 0, 0)),
        ],
        out_specs=whole,
        out_shape=jax.ShapeDtypeStruct((ROWS, CHANS), BF16),
        compiler_params=params(),
        cost_estimate=pl.CostEstimate(flops=1 << 20, bytes_accessed=1 << 19, transcendentals=0),
        name="d_inner",
    )(d_gated, query, near, taps)


def fwd_kernel(
    strips_ref, far_ref, mid_ref, near_ref, own_ref, query_ref, taps_ref, skip_ref,
    gated_ref, inner_ref, mixed_ref,
    signal_ref, conv_ref,
):
    step = pl.program_id(0)

    @pl.when(step == 0)
    def _():
        both = [ref[:ROWS, :] for ref in (far_ref, mid_ref, near_ref, own_ref)]
        both = jnp.concatenate(both, axis=0).astype(F32)
        shifted = (both, later(both, 1), later(both, 2))
        k_short = short_sum(taps_ref, 1, [part[:, :CHANS] for part in shifted])
        v_short = short_sum(taps_ref, 2, [part[:, CHANS:] for part in shifted])
        mixed = (k_short * v_short).astype(BF16)
        signal_ref[...] = mixed
        mixed_ref[...] = mixed[LENGTH - ROWS :]
        conv_ref[...] = jnp.zeros_like(conv_ref)

    low = jnp.dot(
        strips_ref[:, STRIP:], signal_ref[: LENGTH - STRIP, :], preferred_element_type=F32
    )
    high = jnp.dot(strips_ref[...], signal_ref[...], preferred_element_type=F32)
    conv_ref[:STRIP, :] = pick_groups(low, step * FWD_GROUPS, conv_ref[:STRIP, :])
    conv_ref[STRIP:, :] = pick_groups(high, step * FWD_GROUPS, conv_ref[STRIP:, :])

    @pl.when(step == pl.num_programs(0) - 1)
    def _():
        inner = conv_ref[...] + skip_ref[...] * mixed_ref[...].astype(F32)
        inner_ref[...] = inner
        q_short = short_sum(taps_ref, 0, with_tail(near_ref[ROWS:, :CHANS], query_ref[...]))
        gated_ref[...] = (q_short * inner).astype(BF16)


def fwd_call(strips, far, mid, near, own, query, taps, skip):
    whole = lambda x: pl.BlockSpec(x.shape, lambda i: (0,) * x.ndim)
    rest = (far, mid, near, own, query, taps, skip)
    out = pl.BlockSpec((ROWS, CHANS), lambda i: (0, 0))
    return pl.pallas_call(
        fwd_kernel,
        grid=(GROUPS // FWD_GROUPS,),
        in_specs=[
            pl.BlockSpec((FWD_GROUPS * STRIP, LENGTH), lambda i: (i, 0)),
            *(whole(x) for x in rest),
        ],
        out_specs=[out] * 3,
        out_shape=[
            jax.ShapeDtypeStruct((ROWS, CHANS), BF16),
            jax.ShapeDtypeStruct((ROWS, CHANS), F32),
            jax.ShapeDtypeStruct((ROWS, CHANS), BF16),
        ],
        scratch_shapes=[pltpu.VMEM((LENGTH, CHANS), BF16), pltpu.VMEM((ROWS, CHANS), F32)],
        compiler_params=params(),
        cost_estimate=pl.CostEstimate(flops=4 << 30, bytes_accessed=6 << 20, transcendentals=0),
        name="fwd",
    )(strips, *rest)


def term_tile(own_cot_ref, other_cot_ref, gated_ref, other_gated_ref):
    dims = (((0,), (0,)), ((), ()))
    total = lax.dot_general(own_cot_ref[...], gated_ref[...], dims, preferred_element_type=F32)
    total += lax.dot_general(
        other_cot_ref[...], other_gated_ref[...], dims, preferred_element_type=F32
    )
    return total.astype(BF16)


def first_kernel(core_ref, own_cot_ref, other_cot_ref, gated_ref, other_gated_ref, out_ref):
    out_ref[...] = term_tile(own_cot_ref, other_cot_ref, gated_ref, other_gated_ref)


def two_parts(total):
    rounded = total.astype(BF16).astype(F32)
    left = pltpu.roll(total - rounded, SEGMENT // 2, total.ndim - 2)
    return (rounded + left).astype(BF16)


def second_kernel(
    core_ref, own_cot_ref, other_cot_ref, gated_ref, other_gated_ref, small_ref, other_small_ref,
    out_ref,
):
    tile = term_tile(own_cot_ref, other_cot_ref, gated_ref, other_gated_ref)
    out_ref[:, :SECOND, :] = tile.reshape(SHARES, SECOND, CHANS)
    out_ref[:, SECOND:, :] = two_parts(small_ref[...] + other_small_ref[...])


def weight_call(core, own_cot, other_cot, gated, other_gated, small=None, other_small=None):
    tile = SHARES * SECOND
    share = FEATS // 4 // tile
    first = small is None
    steps = FIRST // SECOND if first else 1
    skipped = 0 if first else FIRST // SECOND

    def column(i, core_ref):
        return (0, (i // steps) * 2 * share + core_ref[0] * share + skipped + i % steps)

    signal = pl.BlockSpec((ROWS, CHANS), lambda i, core_ref: (0, 0))
    specs = [pl.BlockSpec((ROWS, tile), column)] * 2 + [signal] * 2
    operands = (core, own_cot, other_cot, gated, other_gated)
    if first:
        out_spec = pl.BlockSpec((tile, CHANS), lambda i, core_ref: (i, 0))
        out_shape = jax.ShapeDtypeStruct((2 * SHARES * FIRST, CHANS), BF16)
    else:
        specs += [pl.BlockSpec((SHARES, SEGMENT, CHANS), lambda i, core_ref: (0, 0, 0))] * 2
        operands += (small, other_small)
        out_spec = pl.BlockSpec((SHARES, SECOND + SEGMENT, CHANS), lambda i, core_ref: (i, 0, 0))
        out_shape = jax.ShapeDtypeStruct((2 * SHARES, SECOND + SEGMENT, CHANS), BF16)
    out = pl.pallas_call(
        first_kernel if first else second_kernel,
        grid_spec=pltpu.PrefetchScalarGridSpec(
            num_scalar_prefetch=1, grid=(2 * steps,), in_specs=specs, out_specs=out_spec
        ),
        out_shape=out_shape,
        compiler_params=params(),
        cost_estimate=pl.CostEstimate(flops=1 << 10, bytes_accessed=1 << 10, transcendentals=0),
        name="first_terms" if first else "second_terms",
    )(*operands)
    return out.reshape(2 * SHARES, FIRST, CHANS) if first else out


def place(g, n):
    row = g * (LENGTH // CHANS) + n
    return row % SHARES, row // SHARES


def bwd_kernel(
    d0_ref, d1_ref, d2_ref, d3_ref, lags_ref, mixed_ref, own_ref, near_ref, query_ref, inner_ref,
    d_gated_ref, taps_ref, skip_ref,
    d_short_ref, small_ref,
    strips_ref, ahead_ref, outer_ref, stack_ref,
):
    for n, ref in enumerate((d0_ref, d1_ref, d2_ref, d3_ref)):
        ahead_ref[n * ROWS : (n + 1) * ROWS, :] = ref[...]
    ahead_ref[LENGTH:, :] = jnp.zeros((ROWS, CHANS), BF16)
    lines = lines_of(lags_ref, False)
    for g in range(GROUPS):
        strips_ref[g * STRIP : (g + 1) * STRIP, :] = strip_of(lines[g : g + 1])
    low = jnp.dot(strips_ref[...], ahead_ref[:LENGTH, :], preferred_element_type=F32)
    d_mixed_low = pick_groups(low)
    high = jnp.dot(
        strips_ref[:, : LENGTH - STRIP], ahead_ref[STRIP:LENGTH, :], preferred_element_type=F32
    )
    d_mixed_high = pick_groups(high)
    d_inner = d0_ref[...].astype(F32)
    mixed = mixed_ref[...]
    d_mixed = jnp.concatenate([d_mixed_low, d_mixed_high], axis=0) + skip_ref[...] * d_inner

    last = near_ref[ROWS - TAIL : ROWS, :]
    k_parts = with_tail(last[:, :CHANS], own_ref[:ROWS, :CHANS])
    v_parts = with_tail(last[:, CHANS:], own_ref[:ROWS, CHANS:])
    q_parts = with_tail(near_ref[ROWS:, :CHANS], query_ref[...])
    small_ref[...] = jnp.zeros_like(small_ref)
    d_qs = d_gated_ref[...].astype(F32) * inner_ref[...]
    d_ks = d_mixed * short_sum(taps_ref, 2, v_parts)
    d_vs = d_mixed * short_sum(taps_ref, 1, k_parts)
    for i, (grad, parts) in enumerate(((d_qs, q_parts), (d_ks, k_parts), (d_vs, v_parts))):
        d_short_ref[i] = grad
        for j in range(3):
            small_ref[3 * i + j, 2:3, :] = jnp.sum(grad * parts[j], axis=0, keepdims=True)
    small_ref[9, 2:3, :] = jnp.sum(d_inner * mixed.astype(F32), axis=0, keepdims=True)

    row = lax.broadcasted_iota(jnp.int32, (ROWS, ROWS), 0)
    col = lax.broadcasted_iota(jnp.int32, (ROWS, ROWS), 1)
    turn = ((row // SMALL) * SMALL + (SMALL - 1 - row % SMALL) == col).astype(F32).astype(BF16)
    turned = jnp.dot(turn, mixed, preferred_element_type=F32)
    ids = lane_groups(SMALL)
    for part in range(ROWS // SMALL):
        piece = turned[part * SMALL : (part + 1) * SMALL]
        for g in range(GROUPS):
            stack_ref[g * SMALL : (g + 1) * SMALL, :] = jnp.where(ids == g, piece, 0.0).astype(BF16)
        term = lax.dot_general(
            stack_ref[...],
            ahead_ref[part * SMALL : part * SMALL + LENGTH, :],
            (((1,), (1,)), ((), ())),
            preferred_element_type=F32,
        )
        if part == 0:
            outer_ref[:, :LENGTH] = term
        else:
            outer_ref[:, :LENGTH] += term
    outer_ref[:, LENGTH:] = jnp.zeros((GROUPS * SMALL, STRIP), F32)
    for g in range(GROUPS):
        skewed = pltpu.roll(
            outer_ref[g * SMALL : (g + 1) * SMALL, :], WIDE - (SMALL - 1), 1, stride=1, stride_axis=0
        )
        sums = jnp.sum(skewed[:, :LENGTH], axis=0, keepdims=True)
        for n in range(LENGTH // CHANS):
            share, slot = place(g, n)
            small_ref[share, slot : slot + 1, :] = sums[:, n * CHANS : (n + 1) * CHANS]


def bwd_call(blocks, lags, mixed, own, near, query, inner, d_gated, taps, skip):
    whole = lambda shape: pl.BlockSpec(shape, lambda i: (0,) * len(shape))
    operands = (*blocks, lags, mixed, own, near, query, inner, d_gated, taps, skip)
    specs = [whole(x.shape) for x in operands]
    return pl.pallas_call(
        bwd_kernel,
        grid=(1,),
        in_specs=specs,
        out_specs=[whole((3, ROWS, CHANS)), whole((SHARES, SEGMENT, CHANS))],
        out_shape=[
            jax.ShapeDtypeStruct((3, ROWS, CHANS), F32),
            jax.ShapeDtypeStruct((SHARES, SEGMENT, CHANS), F32),
        ],
        scratch_shapes=[
            pltpu.VMEM((GROUPS * STRIP, LENGTH), BF16),
            pltpu.VMEM((LENGTH + ROWS, CHANS), BF16),
            pltpu.VMEM((GROUPS * SMALL, WIDE), F32),
            pltpu.VMEM((GROUPS * SMALL, CHANS), BF16),
        ],
        compiler_params=params(),
        cost_estimate=pl.CostEstimate(flops=1 << 10, bytes_accessed=1 << 10, transcendentals=0),
        name="bwd",
    )(*operands)


def input_grad_kernel(d_short_ref, next_ref, taps_ref, query_ref, key_ref, value_ref):
    for i, out_ref in enumerate((query_ref, key_ref, value_ref)):
        joined = jnp.concatenate([d_short_ref[i], next_ref[i]], axis=0)
        rows = joined.shape[0]
        parts = (
            joined[:ROWS],
            pltpu.roll(joined, rows - 1, 0)[:ROWS],
            pltpu.roll(joined, rows - 2, 0)[:ROWS],
        )
        out_ref[...] = short_sum(taps_ref, i, parts).astype(BF16)


def input_grad_call(d_short, following, taps):
    return pl.pallas_call(
        input_grad_kernel,
        out_shape=[jax.ShapeDtypeStruct((ROWS, CHANS), BF16)] * 3,
        compiler_params=params(),
        cost_estimate=pl.CostEstimate(flops=1 << 20, bytes_accessed=2 << 20, transcendentals=0),
        name="input_grads",
    )(d_short, following, taps)


def first_total_kernel(scale, terms_ref, out_ref):
    out_ref[...] = jnp.sum(terms_ref[...].astype(F32), axis=0) * scale


def first_total_call(terms, scale):
    return pl.pallas_call(
        lambda *refs: first_total_kernel(scale, *refs),
        out_shape=jax.ShapeDtypeStruct((FIRST, CHANS), F32),
        compiler_params=params(),
        cost_estimate=pl.CostEstimate(flops=1 << 10, bytes_accessed=1 << 10, transcendentals=0),
        name="first_total",
    )(terms)


def total_kernel(scale, first_ref, terms_ref, out_ref):
    total = jnp.sum(terms_ref[...].astype(F32), axis=0) * scale
    small = total[SECOND:]
    row = lax.broadcasted_iota(jnp.int32, small.shape, 0)
    small = jnp.where(row < SEGMENT // 2, small + pltpu.roll(small, SEGMENT // 2, 0), 0.0)
    total = jnp.concatenate(
        [first_ref[...].astype(BF16), total[:SECOND].astype(BF16), two_parts(small)], axis=0
    )
    out_ref[...] = jnp.broadcast_to(total[None], out_ref.shape)


def total_call(first, terms, scale):
    rows = FIRST + SECOND + SEGMENT
    return pl.pallas_call(
        lambda *refs: total_kernel(scale, *refs),
        out_shape=jax.ShapeDtypeStruct((SHARES, rows, CHANS), BF16),
        compiler_params=params(),
        cost_estimate=pl.CostEstimate(flops=1 << 20, bytes_accessed=3 << 20, transcendentals=0),
        name="second_total",
    )(first, terms)


def spread_kernel(shares_ref, weight_ref, taps_ref, filter_ref, skip_ref):
    for n in range(SHARES):
        weight_ref[n * FIRST : (n + 1) * FIRST, :] = shares_ref[n, :FIRST, :].astype(F32)
        start = SHARES * FIRST + n * SECOND
        weight_ref[start : start + SECOND, :] = shares_ref[n, FIRST : FIRST + SECOND, :].astype(F32)

    def small(share):
        segment = shares_ref[share, FIRST + SECOND :, :].astype(F32)
        return segment + pltpu.roll(segment, SEGMENT // 2, 0)

    for share in range(SHARES):
        segment = small(share)
        for g in range(GROUPS):
            for n in range(LENGTH // CHANS):
                if place(g, n)[0] == share:
                    slot = place(g, n)[1]
                    filter_ref[g : g + 1, n * CHANS : (n + 1) * CHANS] = segment[slot : slot + 1]
        if share < 9:
            taps_ref[share // 3, share % 3 : share % 3 + 1, :] = segment[2:3]
        if share == 9:
            skip_ref[...] = segment[2:3]


def spread_call(shares):
    return pl.pallas_call(
        spread_kernel,
        out_shape=[
            jax.ShapeDtypeStruct((FEATS // 4, CHANS), F32),
            jax.ShapeDtypeStruct((3, 3, CHANS), F32),
            jax.ShapeDtypeStruct((GROUPS, LENGTH), F32),
            jax.ShapeDtypeStruct((1, CHANS), F32),
        ],
        compiler_params=params(),
        name="spread",
    )(shares)


def sent(block, distance):
    count = 4
    route = [(i, i + distance) for i in range(count) if 0 <= i + distance < count]
    return lax.ppermute(block, CTX, route)


def shards(
    query_in, key_in, value_in, short_taps, long_filter, skip_gain, out_weight, out_cotangent
):
    query = query_in[0]
    cot = out_cotangent[0]
    taps = short_taps
    skip = skip_gain.reshape(1, CHANS)
    devices = lax.axis_size(ALL)
    tokens = ROWS * devices
    scale = 1.0 / math.sqrt(tokens)
    core = lax.axis_index("co").astype(jnp.int32).reshape(1)

    own = pack_call(key_in[0], value_in[0], query)
    near, mid, far = (sent(own, distance) for distance in (1, 2, 3))
    swap = [(0, 1), (1, 0)]
    other_cot = lax.ppermute(cot, "co", swap)

    d_gated, strips = pre_call(cot, out_weight, long_filter)
    gated, inner, mixed = fwd_call(strips, far, mid, near, own, query, taps, skip)
    gated, d_gated = lax.optimization_barrier((gated, d_gated))
    other_gated = lax.ppermute(gated, "co", swap)
    d_inner = d_inner_call(d_gated, query, near, taps)
    operands = (core, cot, other_cot, gated, other_gated)
    first = weight_call(*operands)
    first, d_inner = lax.optimization_barrier((first, d_inner))
    first = lax.all_to_all(first, CHIPS, 0, 0)
    blocks = [d_inner] + [sent(d_inner, -distance) for distance in (1, 2, 3)]
    d_short, small = bwd_call(
        blocks, long_filter, mixed, own, near, query, inner, d_gated, taps, skip
    )
    other_small = lax.ppermute(small, "co", swap)
    second = weight_call(*operands, small, other_small)
    second = lax.all_to_all(second, CHIPS, 0, 0)
    first = first_total_call(first, scale)
    following = sent(d_short[:, :8], -1)
    grad_query, grad_key, grad_value = input_grad_call(d_short, following, taps)

    shares = lax.all_to_all(total_call(first, second, scale), DP, 0, 0)
    grad_weight, grad_taps, grad_filter, grad_skip = spread_call(shares)
    return (
        gated[None],
        grad_query[None],
        grad_key[None],
        grad_value[None],
        grad_taps,
        grad_filter,
        grad_skip.reshape(CHANS),
        grad_weight,
    )


def solution(mesh):
    fine = Mesh(mesh.devices.reshape(2, 2, 4, 2, 4), ALL)
    tokens = P(DP, CTX, None)
    in_specs = (tokens, tokens, tokens, P(), P(), P(), P(), tokens)
    out_specs = (tokens, tokens, tokens, tokens, P(), P(), P(), P(CTX, None))
    return jax.shard_map(
        shards, mesh=fine, in_specs=in_specs, out_specs=out_specs, check_vma=False
    )
```

time: 151 us -> 142 us (0.940)
  Pallas kernels: 34.3 us -> 44.9 us
  local copies, waits for them, and re-layouts: 13.5 us -> 6.25 us
  waiting for transfers between devices: 50.6 us -> 44.6 us
  other arithmetic: 3.42 us -> 0 us
  starting transfers between devices: 47.2 us -> 44.4 us
    all_to_all x4 -> x3, waiting for transfers between devices: 39.7 us -> 12.7 us  [the longest x1 12.7 us: shards(): second = lax.all_to_all(second, CHIPS, 0, 0)]
    ppermute x8 -> x7, waiting for transfers between devices: 10.9 us -> 30.5 us  [sent(): return lax.ppermute(block, CTX, route)]
    pallas_call x3 -> x7, Pallas kernels: 12.8 us -> 23.9 us  [the longest x2 8.65 us: weight_call(): pl.pallas_call(first_kernel if first else second_kernel, grid_spec=pltpu....]
    all_to_all x4 -> x3, starting transfers between devices: 27.8 us -> 23.6 us  [the longest x1 12.1 us: shards(): first = lax.all_to_all(first, CHIPS, 0, 0)]
    reshape x5 -> x0, local copies, waits for them, and re-layouts: 3.47 us -> none  [the longest x1 0.86 us: shards(): filter_part.reshape(filter_rows, CHANS)]
    slice x7 -> x0, local copies, waits for them, and re-layouts: 3.07 us -> none  [the longest x2 0.84 us: shards(): turned[:, :STRIP - 1]]
    ppermute x0 -> x1, starting transfers between devices: none -> 2.45 us  [shards(): other_small = lax.ppermute(small, 'co', swap)]
    broadcast_in_dim x4 -> x0, local copies, waits for them, and re-layouts: 2.19 us -> none  [the longest x1 0.8 us: shards(): jnp.broadcast_to(total, (devices, 1, CHANS))]
  transfers between devices with their start and end apart: 14 -> 13, of which waited for: 5 -> 4; matrix products, arithmetic and copies ran while one was open for 8% -> 1% of each run, Pallas kernels for 23% -> 24%
where the time goes in v2:
time: 142 us; the launch traced here: 141 us
  Pallas kernels  44.9 us (32%)
  waiting for transfers between devices  44.6 us (31%)
  starting transfers between devices  44.4 us (31%)
  local copies, waits for them, and re-layouts  6.25 us (4%)
    ppermute x7, waiting for transfers between devices, sent(): return lax.ppermute(block, CTX, route)  30.5 us
    ppermute x7, starting transfers between devices, sent(): return lax.ppermute(block, CTX, route)  15.4 us
    all_to_all x1, waiting for transfers between devices, shards(): second = lax.all_to_all(second, CHIPS, 0, 0)  12.7 us
    all_to_all x1, starting transfers between devices, shards(): first = lax.all_to_all(first, CHIPS, 0, 0)  12.1 us
    pallas_call x1, Pallas kernels, pre_call(): pl.pallas_call(pre_kernel, grid=(steps,), in_specs=[pl.BlockSpec((ROWS, T...  8.85 us
    pallas_call x2, Pallas kernels, weight_call(): pl.pallas_call(first_kernel if first else second_kernel, grid_spec=pltpu....  8.65 us
    pallas_call x1, Pallas kernels, bwd_call(): pl.pallas_call(bwd_kernel, grid=(1,), in_specs=specs, out_specs=[whole((3...  7.76 us
    all_to_all x1, starting transfers between devices, shards(): second = lax.all_to_all(second, CHIPS, 0, 0)  7.54 us
  transfers between devices with their start and end apart: 13, of which 4 were waited for; matrix products, arithmetic and copies ran while one was open for 1% of the time, Pallas kernels for 24%

profile of v2, /device:TPU:1, one launch (start us, length us, event | category | flops | bytes accessed | tf_op | source)
XLA Modules:
  0.0 140.9 jit_solution(7294441623684542318)
XLA Ops:
  0.6 1.5 %collective-permute-start.3 = (bf16[256,8192]{1,0:T(8,128)(2,1)}, bf16[256,8192]{1,0:T(8,128)(2,1)}, u32[]{:S(2)}, u32[]{:S(2)}) collective-permute-start(bf16[256,8192]{1,0:T(8,128)(2,1)} %bitcast.12), channel_id=1, source_target_pairs={{0,32},{32,0},{1,33},{33,1},{2,34},{34,2},{3,35},{35,3},{4,36},{36... | collective-permute-start | bytes 12582920 | tf_op jit(solution)/shard_map/ppermute | solution.py:509
  2.1 1.7 %pack.1.own_ref = bf16[272,512]{1,0:T(8,128)(2,1)} custom-call(bf16[256,256]{1,0:T(8,128)(2,1)} %bitcast.22, bf16[256,256]{1,0:T(8,128)(2,1)} %bitcast.23, bf16[256,256]{1,0:T(8,128)(2,1)} %bitcast.17), custom_call_target="tpu_custom_call" | custom-call | tf_op jit(solution)/shard_map/pack/pallas_call | solution.py:81
  3.8 4.6 %collective-permute-start.2 = (bf16[272,512]{1,0:T(8,128)(2,1)}, bf16[272,512]{1,0:T(8,128)(2,1)S(1)}, u32[]{:S(2)}, u32[]{:S(2)}) collective-permute-start(bf16[272,512]{1,0:T(8,128)(2,1)} %pack.1.own_ref), channel_id=1, source_target_pairs={{0,32},{32,64},{64,96},{1,33},{33,65},{65,97},{2,34},{34,66},{66,9... | collective-permute-start | bytes 835592 | tf_op jit(solution)/shard_map/ppermute | solution.py:491
  8.5 0.7 collective-permute-start
  9.2 2.0 %collective-permute-start.1 = (bf16[272,512]{1,0:T(8,128)(2,1)}, bf16[272,512]{1,0:T(8,128)(2,1)S(1)}, u32[]{:S(2)}, u32[]{:S(2)}) collective-permute-start(bf16[272,512]{1,0:T(8,128)(2,1)} %pack.1.own_ref), channel_id=1, source_target_pairs={{0,64},{32,96},{1,65},{33,97},{2,66},{34,98},{3,67},{35,99},{4,68}... | collective-permute-start | bytes 835592 | tf_op jit(solution)/shard_map/ppermute | solution.py:491
  11.2 8.8 %pre.1 = (bf16[256,256]{1,0:T(8,128)(2,1)}, bf16[2048,1024]{1,0:T(8,128)(2,1)}) custom-call(bf16[256,8192]{1,0:T(8,128)(2,1)} %bitcast.13, bf16[8192,256]{1,0:T(8,128)(2,1)} %weight_ref.1, bf16[16,1024]{1,0:T(8,128)(2,1)} %lags_ref.1), custom_call_target="tpu_custom_call" | custom-call | flops 1073741824 | bytes 14680064 | tf_op jit(solution)/shard_map/pre/pallas_call | solution.py:128
  20.0 0.0 collective-permute-done.2.near_ref.tail_ref
  20.0 0.0 copy-start.3
  20.0 0.0 collective-permute-done.far_ref
  20.1 0.0 copy-start.11
  20.1 0.0 collective-permute-done.1.mid_ref
  20.1 0.0 copy-start.12
  20.1 0.7 copy-done.3
  20.8 0.1 copy-done.11
  20.8 0.1 copy-done.12
  20.9 6.8 %fwd.1 = (bf16[256,256]{1,0:T(8,128)(2,1)}, f32[256,256]{1,0:T(8,128)}, bf16[256,256]{1,0:T(8,128)(2,1)}) custom-call(bf16[2048,1024]{1,0:T(8,128)(2,1)} %get-tuple-element.26.strips_ref, bf16[272,512]{1,0:T(8,128)(2,1)} %copy-done.11, bf16[272,512]{1,0:T(8,128)(2,1)} %copy-done.12, bf16[272,512]{1,0:T(8,128)(2,1)} %copy-done.3, ...), custom_call_target="tpu_custom_call" | custom-call | flops 4294967296 | bytes 6291456 | tf_op jit(solution)/shard_map/fwd/pallas_call | solution.py:215
  27.7 1.4 collective-permute-start.4
  29.1 1.7 %d_inner.1.d0_ref = bf16[256,256]{1,0:T(8,128)(2,1)} custom-call(bf16[256,256]{1,0:T(8,128)(2,1)} %get-tuple-element.30.d_gated_ref, bf16[256,256]{1,0:T(8,128)(2,1)} %bitcast.19, bf16[272,512]{1,0:T(8,128)(2,1)} %copy-done.3, f32[3,3,256]{2,1,0:T(4,128)} %taps_ref.7), custom_call_target="tpu_custom_call" | custom-call | flops 1048576 | bytes 524288 | tf_op jit(solution)/shard_map/d_inner/pallas_call | solution.py:160
  30.8 0.0 collective-permute-done.4.other_gated_ref
  30.8 0.0 copy-start.4
  30.8 0.0 collective-permute-done.3.other_cot_ref
  30.8 0.6 copy-done.4
  31.5 5.8 %first_terms.1 = bf16[3072,256]{1,0:T(8,128)(2,1)} custom-call(s32[1]{0:T(128)} %bitcast.6.core_ref, bf16[256,8192]{1,0:T(8,128)(2,1)} %bitcast.14, bf16[256,8192]{1,0:T(8,128)(2,1)} %collective-permute-done.3.other_cot_ref, bf16[256,256]{1,0:T(8,128)(2,1)} %get-tuple-element.29.gated_ref, bf16[256,256]{1,0:T(8,128)(2,1)} %copy-done.4), custom_call_target="tpu_custom_call" | custom-call | flops 1024 | bytes 1024 | tf_op jit(solution)/shard_map/first_terms/pallas_call | solution.py:284
  37.3 0.0 copy-start.5
  37.3 12.1 %all-to-all-start = ((bf16[64,48,256]{2,1,0:T(8,128)(2,1)}), bf16[64,48,256]{2,1,0:T(8,128)(2,1)S(1)}, u32[]{:S(2)}, u32[]{:S(2)}) async-start(bf16[64,48,256]{2,1,0:T(8,128)(2,1)} %bitcast.16), calls=%async_computation | async-start | bytes 3145728 | tf_op jit(solution)/shard_map/all_to_all | solution.py:519
  49.4 0.0 copy-done.5
  49.4 2.2 %collective-permute-start.5 = (bf16[256,256]{1,0:T(8,128)(2,1)S(1)}, bf16[256,256]{1,0:T(8,128)(2,1)S(1)}, u32[]{:S(2)}, u32[]{:S(2)}) collective-permute-start(bf16[256,256]{1,0:T(8,128)(2,1)S(1)} %copy-done.5), channel_id=1, source_target_pairs={{32,0},{64,32},{96,64},{33,1},{65,33},{97,65},{34,2},{66,34},{98,6... | collective-permute-start | bytes 393224 | tf_op jit(solution)/shard_map/ppermute | solution.py:491
  51.6 1.3 collective-permute-start.6
  52.9 0.7 collective-permute-start.7
  53.6 19.9 %collective-permute-done.5.d1_ref = bf16[256,256]{1,0:T(8,128)(2,1)S(1)} collective-permute-done((bf16[256,256]{1,0:T(8,128)(2,1)S(1)}, bf16[256,256]{1,0:T(8,128)(2,1)S(1)}, u32[]{:S(2)}, u32[]{:S(2)}) %collective-permute-start.5) | collective-permute-done | bytes 131104 | tf_op jit(solution)/shard_map/ppermute | solution.py:491
  73.5 0.0 copy-start.7
  73.5 0.0 collective-permute-done.6.d2_ref
  73.5 0.0 copy-start.8
  73.5 0.0 collective-permute-done.7.d3_ref
  73.5 0.0 copy-start.9
  73.5 0.6 copy-done.7
  74.1 0.1 copy-done.8
  74.2 0.0 copy-done.9
  74.3 7.8 %bwd.1 = (f32[3,256,256]{2,1,0:T(8,128)}, f32[32,8,256]{2,1,0:T(8,128)}) custom-call(bf16[256,256]{1,0:T(8,128)(2,1)} %d_inner.1.d0_ref, bf16[256,256]{1,0:T(8,128)(2,1)} %copy-done.7, bf16[256,256]{1,0:T(8,128)(2,1)} %copy-done.8, bf16[256,256]{1,0:T(8,128)(2,1)} %copy-done.9, bf16[16,1024]{1,0:T(8,128)(2,1)} %lags_ref.1, ...), custom_call_target="tpu_custom_call" | custom-call | flops 1024 | bytes 1024 | tf_op jit(solution)/shard_map/bwd/pallas_call | solution.py:372
  82.0 2.4 %collective-permute-start.9 = (f32[32,8,256]{2,1,0:T(8,128)}, f32[32,8,256]{2,1,0:T(8,128)S(1)}, u32[]{:S(2)}, u32[]{:S(2)}) collective-permute-start(f32[32,8,256]{2,1,0:T(8,128)} %get-tuple-element.39.small_ref), channel_id=1, source_target_pairs={{0,32},{32,0},{1,33},{33,1},{2,34},{34,2},{3,35},{35,3},{4,36},{36... | collective-permute-start | bytes 786440 | tf_op jit(solution)/shard_map/ppermute | solution.py:524
  84.5 1.4 collective-permute-done.9.other_small_ref
  85.8 0.0 copy-start.6
  85.8 0.7 copy-done.6
  86.5 2.8 %second_terms.1 = bf16[64,24,256]{2,1,0:T(8,128)(2,1)} custom-call(s32[1]{0:T(128)} %bitcast.6.core_ref, bf16[256,8192]{1,0:T(8,128)(2,1)} %bitcast.15, bf16[256,8192]{1,0:T(8,128)(2,1)} %collective-permute-done.3.other_cot_ref, bf16[256,256]{1,0:T(8,128)(2,1)} %get-tuple-element.29.gated_ref, bf16[256,256]{1,0:T(8,128)(2,1)} %copy-done.4, ...), custom_call_target="tpu_custom_call" | custom-call | flops 1024 | bytes 1024 | tf_op jit(solution)/shard_map/second_terms/pallas_call | solution.py:284
  89.4 0.0 all-to-all-done.refs_0_
  89.4 0.0 copy-start
  89.4 7.5 %all-to-all-start.1 = ((bf16[64,24,256]{2,1,0:T(8,128)(2,1)}), bf16[64,24,256]{2,1,0:T(8,128)(2,1)S(1)}, u32[]{:S(2)}, u32[]{:S(2)}) async-start(bf16[64,24,256]{2,1,0:T(8,128)(2,1)} %second_terms.1), calls=%async_computation.1 | async-start | bytes 1572864 | tf_op jit(solution)/shard_map/all_to_all | solution.py:526
  97.0 0.0 copy-done
  97.0 2.3 %first_total.1.refs_0_ = f32[48,256]{1,0:T(8,128)} custom-call(bf16[64,48,256]{2,1,0:T(8,128)(2,1)} %copy-done), custom_call_target="tpu_custom_call" | custom-call | flops 1024 | bytes 1024 | tf_op jit(solution)/shard_map/first_total/pallas_call | solution.py:420
  99.2 12.7 %all-to-all-done.1.refs_1_ = bf16[64,24,256]{2,1,0:T(8,128)(2,1)S(1)} async-done(((bf16[64,24,256]{2,1,0:T(8,128)(2,1)}), bf16[64,24,256]{2,1,0:T(8,128)(2,1)S(1)}, u32[]{:S(2)}, u32[]{:S(2)}) %all-to-all-start.1) | async-done | bytes 786464 | tf_op jit(solution)/shard_map/all_to_all | solution.py:526
  112.0 0.0 copy-start.2
  112.0 0.9 copy-done.2
  112.9 2.4 %second_total.1 = bf16[32,72,256]{2,1,0:T(8,128)(2,1)} custom-call(f32[48,256]{1,0:T(8,128)} %first_total.1.refs_0_, bf16[64,24,256]{2,1,0:T(8,128)(2,1)} %copy-done.2), custom_call_target="tpu_custom_call" | custom-call | flops 1048576 | bytes 3145728 | tf_op jit(solution)/shard_map/second_total/pallas_call | solution.py:442
  115.2 3.9 %all-to-all-start.2 = ((bf16[32,72,256]{2,1,0:T(8,128)(2,1)}), bf16[32,72,256]{2,1,0:T(8,128)(2,1)S(1)}, u32[]{:S(2)}, u32[]{:S(2)}) async-start(bf16[32,72,256]{2,1,0:T(8,128)(2,1)} %second_total.1), calls=%async_computation.2 | async-start | bytes 2359296 | tf_op jit(solution)/shard_map/all_to_all | solution.py:531
  119.2 0.7 slice.3
  119.9 3.9 %collective-permute-start.8 = (f32[3,8,256]{2,1,0:T(8,128)S(1)}, f32[3,8,256]{2,1,0:T(8,128)S(1)}, u32[]{:S(2)}, u32[]{:S(2)}) collective-permute-start(f32[3,8,256]{2,1,0:T(8,128)S(1)} %slice.3), channel_id=1, source_target_pairs={{32,0},{64,32},{96,64},{33,1},{65,33},{97,65},{34,2},{66,34},{98,6... | collective-permute-start | bytes 73736 | tf_op jit(solution)/shard_map/ppermute | solution.py:491
  123.9 10.6 %collective-permute-done.8.next_ref = f32[3,8,256]{2,1,0:T(8,128)S(1)} collective-permute-done((f32[3,8,256]{2,1,0:T(8,128)S(1)}, f32[3,8,256]{2,1,0:T(8,128)S(1)}, u32[]{:S(2)}, u32[]{:S(2)}) %collective-permute-start.8) | collective-permute-done | bytes 24608 | tf_op jit(solution)/shard_map/ppermute | solution.py:491
  134.4 0.0 copy-start.10
  134.4 0.6 copy-done.10
  135.0 2.1 %input_grads.1 = (bf16[256,256]{1,0:T(8,128)(2,1)}, bf16[256,256]{1,0:T(8,128)(2,1)}, bf16[256,256]{1,0:T(8,128)(2,1)}) custom-call(f32[3,256,256]{2,1,0:T(8,128)} %get-tuple-element.34.d_short_ref, f32[3,8,256]{2,1,0:T(8,128)} %copy-done.10, f32[3,3,256]{2,1,0:T(4,128)} %taps_ref.7), custom_call_target="tpu_custom_call" | custom-call | flops 1048576 | bytes 2097152 | tf_op jit(solution)/shard_map/input_grads/pallas_call | solution.py:406
  137.1 0.0 all-to-all-done.2.shares_ref
  137.1 0.0 copy-start.1
  137.1 1.0 copy-done.1
  138.1 2.7 %spread.1 = (f32[2048,256]{1,0:T(8,128)}, f32[3,3,256]{2,1,0:T(4,128)}, f32[16,1024]{1,0:T(8,128)}, f32[1,256]{1,0:T(1,128)}) custom-call(bf16[32,72,256]{2,1,0:T(8,128)(2,1)} %copy-done.1), custom_call_target="tpu_custom_call" | custom-call | tf_op jit(solution)/shard_map/spread/pallas_call | solution.py:475
Async XLA Ops:
  0.6 30.2 %collective-permute-start.3 = (bf16[256,8192]{1,0:T(8,128)(2,1)}, bf16[256,8192]{1,0:T(8,128)(2,1)}, u32[]{:S(2)}, u32[]{:S(2)}) collective-permute-start(bf16[256,8192]{1,0:T(8,128)(2,1)} %bitcast.12), channel_id=1, source_target_pairs={{0,32},{32,0},{1,33},{33,1},{2,34},{34,2},{3,35},{35,3},{4,36},{36... | collective-permute-start | bytes 12582920 | tf_op jit(solution)/shard_map/ppermute | solution.py:509
  3.8 16.2 %collective-permute-start.2 = (bf16[272,512]{1,0:T(8,128)(2,1)}, bf16[272,512]{1,0:T(8,128)(2,1)S(1)}, u32[]{:S(2)}, u32[]{:S(2)}) collective-permute-start(bf16[272,512]{1,0:T(8,128)(2,1)} %pack.1.own_ref), channel_id=1, source_target_pairs={{0,32},{32,64},{64,96},{1,33},{33,65},{65,97},{2,34},{34,66},{66,9... | collective-permute-start | bytes 835592 | tf_op jit(solution)/shard_map/ppermute | solution.py:491
  8.5 11.6 %collective-permute-start = (bf16[272,512]{1,0:T(8,128)(2,1)}, bf16[272,512]{1,0:T(8,128)(2,1)S(1)}, u32[]{:S(2)}, u32[]{:S(2)}) collective-permute-start(bf16[272,512]{1,0:T(8,128)(2,1)} %pack.1.own_ref), channel_id=1, source_target_pairs={{0,96},{1,97},{2,98},{3,99},{4,100},{5,101},{6,102},{7,103},{8,104... | collective-permute-start | bytes 835592 | tf_op jit(solution)/shard_map/ppermute | solution.py:491
  9.2 10.9 %collective-permute-start.1 = (bf16[272,512]{1,0:T(8,128)(2,1)}, bf16[272,512]{1,0:T(8,128)(2,1)S(1)}, u32[]{:S(2)}, u32[]{:S(2)}) collective-permute-start(bf16[272,512]{1,0:T(8,128)(2,1)} %pack.1.own_ref), channel_id=1, source_target_pairs={{0,64},{32,96},{1,65},{33,97},{2,66},{34,98},{3,67},{35,99},{4,68}... | collective-permute-start | bytes 835592 | tf_op jit(solution)/shard_map/ppermute | solution.py:491
  20.0 0.7 copy-start.3
  20.1 0.8 copy-start.11
  20.1 0.9 copy-start.12
  27.7 3.1 %collective-permute-start.4 = (bf16[256,256]{1,0:T(8,128)(2,1)}, bf16[256,256]{1,0:T(8,128)(2,1)S(1)}, u32[]{:S(2)}, u32[]{:S(2)}) collective-permute-start(bf16[256,256]{1,0:T(8,128)(2,1)} %get-tuple-element.29.gated_ref), channel_id=1, source_target_pairs={{0,32},{32,0},{1,33},{33,1},{2,34},{34,2},{3,35},{35,3},{4,36},{36... | collective-permute-start | bytes 393224 | tf_op jit(solution)/shard_map/ppermute | solution.py:514
  30.8 0.7 copy-start.4
  37.3 12.1 %copy-start.5 = (bf16[256,256]{1,0:T(8,128)(2,1)S(1)}, bf16[256,256]{1,0:T(8,128)(2,1)}, u32[]{:S(2)}) copy-start(bf16[256,256]{1,0:T(8,128)(2,1)} %d_inner.1.d0_ref) | copy-start | bytes 393220
  37.3 52.1 %all-to-all-start = ((bf16[64,48,256]{2,1,0:T(8,128)(2,1)}), bf16[64,48,256]{2,1,0:T(8,128)(2,1)S(1)}, u32[]{:S(2)}, u32[]{:S(2)}) async-start(bf16[64,48,256]{2,1,0:T(8,128)(2,1)} %bitcast.16), calls=%async_computation | async-start | bytes 3145728 | tf_op jit(solution)/shard_map/all_to_all | solution.py:519
  49.4 24.1 %collective-permute-start.5 = (bf16[256,256]{1,0:T(8,128)(2,1)S(1)}, bf16[256,256]{1,0:T(8,128)(2,1)S(1)}, u32[]{:S(2)}, u32[]{:S(2)}) collective-permute-start(bf16[256,256]{1,0:T(8,128)(2,1)S(1)} %copy-done.5), channel_id=1, source_target_pairs={{32,0},{64,32},{96,64},{33,1},{65,33},{97,65},{34,2},{66,34},{98,6... | collective-permute-start | bytes 393224 | tf_op jit(solution)/shard_map/ppermute | solution.py:491
  51.6 21.9 %collective-permute-start.6 = (bf16[256,256]{1,0:T(8,128)(2,1)S(1)}, bf16[256,256]{1,0:T(8,128)(2,1)S(1)}, u32[]{:S(2)}, u32[]{:S(2)}) collective-permute-start(bf16[256,256]{1,0:T(8,128)(2,1)S(1)} %copy-done.5), channel_id=1, source_target_pairs={{64,0},{96,32},{65,1},{97,33},{66,2},{98,34},{67,3},{99,35},{68,4}... | collective-permute-start | bytes 393224 | tf_op jit(solution)/shard_map/ppermute | solution.py:491
  52.9 20.6 %collective-permute-start.7 = (bf16[256,256]{1,0:T(8,128)(2,1)S(1)}, bf16[256,256]{1,0:T(8,128)(2,1)S(1)}, u32[]{:S(2)}, u32[]{:S(2)}) collective-permute-start(bf16[256,256]{1,0:T(8,128)(2,1)S(1)} %copy-done.5), channel_id=1, source_target_pairs={{96,0},{97,1},{98,2},{99,3},{100,4},{101,5},{102,6},{103,7},{104,8... | collective-permute-start | bytes 393224 | tf_op jit(solution)/shard_map/ppermute | solution.py:491
  73.5 0.6 copy-start.7
  73.5 0.7 copy-start.8
  73.5 0.8 copy-start.9
  82.0 3.8 %collective-permute-start.9 = (f32[32,8,256]{2,1,0:T(8,128)}, f32[32,8,256]{2,1,0:T(8,128)S(1)}, u32[]{:S(2)}, u32[]{:S(2)}) collective-permute-start(f32[32,8,256]{2,1,0:T(8,128)} %get-tuple-element.39.small_ref), channel_id=1, source_target_pairs={{0,32},{32,0},{1,33},{33,1},{2,34},{34,2},{3,35},{35,3},{4,36},{36... | collective-permute-start | bytes 786440 | tf_op jit(solution)/shard_map/ppermute | solution.py:524
  85.8 0.7 copy-start.6
  89.4 7.6 %copy-start = (bf16[64,48,256]{2,1,0:T(8,128)(2,1)}, bf16[64,48,256]{2,1,0:T(8,128)(2,1)S(1)}, u32[]{:S(2)}) copy-start(bf16[64,48,256]{2,1,0:T(8,128)(2,1)S(1)} %all-to-all-done.refs_0_) | copy-start | bytes 4718596
  89.4 22.6 %all-to-all-start.1 = ((bf16[64,24,256]{2,1,0:T(8,128)(2,1)}), bf16[64,24,256]{2,1,0:T(8,128)(2,1)S(1)}, u32[]{:S(2)}, u32[]{:S(2)}) async-start(bf16[64,24,256]{2,1,0:T(8,128)(2,1)} %second_terms.1), calls=%async_computation.1 | async-start | bytes 1572864 | tf_op jit(solution)/shard_map/all_to_all | solution.py:526
  112.0 0.9 copy-start.2
  115.2 21.9 %all-to-all-start.2 = ((bf16[32,72,256]{2,1,0:T(8,128)(2,1)}), bf16[32,72,256]{2,1,0:T(8,128)(2,1)S(1)}, u32[]{:S(2)}, u32[]{:S(2)}) async-start(bf16[32,72,256]{2,1,0:T(8,128)(2,1)} %second_total.1), calls=%async_computation.2 | async-start | bytes 2359296 | tf_op jit(solution)/shard_map/all_to_all | solution.py:531
  119.9 14.5 %collective-permute-start.8 = (f32[3,8,256]{2,1,0:T(8,128)S(1)}, f32[3,8,256]{2,1,0:T(8,128)S(1)}, u32[]{:S(2)}, u32[]{:S(2)}) collective-permute-start(f32[3,8,256]{2,1,0:T(8,128)S(1)} %slice.3), channel_id=1, source_target_pairs={{32,0},{64,32},{96,64},{33,1},{65,33},{97,65},{34,2},{66,34},{98,6... | collective-permute-start | bytes 73736 | tf_op jit(solution)/shard_map/ppermute | solution.py:491
  134.4 0.6 copy-start.10
  137.1 1.0 copy-start.1

commit v3 on v1

v3 whole, which is shorter than its diff:
```python
import math

import jax
import jax.numpy as jnp
from jax import lax
from jax.experimental import pallas as pl
from jax.experimental.pallas import tpu as pltpu
from jax.sharding import Mesh
from jax.sharding import PartitionSpec as P

F32 = jnp.float32
BF16 = jnp.bfloat16
CTX = ("xh", "co")
DP = ("y", "xl", "z")
CHIPS = ("xh", "y", "xl", "z")
ALL = ("xh", "co", "y", "xl", "z")

ROWS = 256
CHANS = 256
GROUPS = 16
LENGTH = 1024
STRIP = 32
PAD = 128
WIDE = LENGTH + PAD
FEATS = 8192
TILE = 1024
SMALL = 32
TAIL = 16
SHARES = 32
SHARE = FEATS // 4
SEGMENT = 8
VMEM_LIMIT = 56 * 1024 * 1024


def params(*semantics):
    return pltpu.CompilerParams(vmem_limit_bytes=VMEM_LIMIT)


def lane_groups(rows):
    return lax.broadcasted_iota(jnp.int32, (rows, CHANS), 1) // (CHANS // GROUPS)


def later(x, count):
    row = lax.broadcasted_iota(jnp.int32, x.shape, 0)
    return jnp.where(row >= count, pltpu.roll(x, count, 0), 0.0)


def strip_of(line):
    wide = jnp.broadcast_to(line, (STRIP, WIDE))
    return pltpu.roll(wide, 0, 1, stride=1, stride_axis=0)[:, :LENGTH].astype(BF16)


def pick_groups(result):
    ids = lane_groups(STRIP)
    out = jnp.zeros((STRIP, CHANS), F32)
    for g in range(GROUPS):
        out = jnp.where(ids == g, result[g * STRIP : (g + 1) * STRIP], out)
    return out


def all_strips(strips_ref, signal_ref):
    parts = []
    for n in range(ROWS // STRIP):
        window = signal_ref[n * STRIP : n * STRIP + LENGTH, :]
        parts.append(pick_groups(jnp.dot(strips_ref[...], window, preferred_element_type=F32)))
    return jnp.concatenate(parts, axis=0)


def with_tail(tail, block):
    joined = jnp.concatenate([tail.astype(F32), block.astype(F32)], axis=0)
    return joined[TAIL:], pltpu.roll(joined, 1, 0)[TAIL:], pltpu.roll(joined, 2, 0)[TAIL:]


def short_sum(taps_ref, i, parts):
    return sum(taps_ref[i, j : j + 1, :] * parts[j] for j in range(3))


def lines_of(filter_ref, turned):
    if not turned:
        return jnp.concatenate(
            [filter_ref[...].astype(F32), jnp.zeros((GROUPS, PAD), F32)], axis=1
        )
    row = lax.broadcasted_iota(jnp.int32, (CHANS, CHANS), 0)
    col = lax.broadcasted_iota(jnp.int32, (CHANS, CHANS), 1)
    turn = (row + col == CHANS - 1).astype(F32).astype(BF16)
    pieces = [
        jnp.dot(filter_ref[:, n * CHANS : (n + 1) * CHANS], turn, preferred_element_type=F32)
        for n in reversed(range(LENGTH // CHANS))
    ]
    wide = jnp.concatenate([*pieces, jnp.zeros((GROUPS, PAD), F32)], axis=1)
    return pltpu.roll(wide, WIDE - (STRIP - 1), 1)


def pre_kernel(cot_ref, weight_ref, filter_ref, d_gated_ref, strips_ref, acc_ref, line_ref):
    step = pl.program_id(0)

    @pl.when(step == 0)
    def _():
        acc_ref[...] = jnp.zeros_like(acc_ref)
        line_ref[...] = lines_of(filter_ref, True)

    acc_ref[...] += jnp.dot(cot_ref[...], weight_ref[...], preferred_element_type=F32)
    for g in range(2):
        line = line_ref[pl.ds(2 * step + g, 1), :]
        strips_ref[g * STRIP : (g + 1) * STRIP, :] = strip_of(line)

    @pl.when(step == pl.num_programs(0) - 1)
    def _():
        d_gated_ref[...] = acc_ref[...].astype(BF16)


def pre_call(cot, weight, lags):
    steps = FEATS // TILE
    return pl.pallas_call(
        pre_kernel,
        grid=(steps,),
        in_specs=[
            pl.BlockSpec((ROWS, TILE), lambda i: (0, i)),
            pl.BlockSpec((TILE, CHANS), lambda i: (i, 0)),
            pl.BlockSpec((GROUPS, LENGTH), lambda i: (0, 0)),
        ],
        out_specs=[
            pl.BlockSpec((ROWS, CHANS), lambda i: (0, 0)),
            pl.BlockSpec((2 * STRIP, LENGTH), lambda i: (i, 0)),
        ],
        out_shape=[
            jax.ShapeDtypeStruct((ROWS, CHANS), BF16),
            jax.ShapeDtypeStruct((GROUPS * STRIP, LENGTH), BF16),
        ],
        scratch_shapes=[pltpu.VMEM((ROWS, CHANS), F32), pltpu.VMEM((GROUPS, WIDE), F32)],
        compiler_params=params(),
        cost_estimate=pl.CostEstimate(
            flops=2 * ROWS * FEATS * CHANS, bytes_accessed=14 << 20, transcendentals=0
        ),
        name="pre",
    )(cot, weight, lags)


def d_inner_kernel(d_gated_ref, query_ref, tail_ref, taps_ref, out_ref):
    q_short = short_sum(taps_ref, 0, with_tail(tail_ref[...], query_ref[...]))
    out_ref[...] = (d_gated_ref[...].astype(F32) * q_short).astype(BF16)


def d_inner_call(d_gated, query, tail, taps):
    return pl.pallas_call(
        d_inner_kernel,
        out_shape=jax.ShapeDtypeStruct((ROWS, CHANS), BF16),
        compiler_params=params(),
        cost_estimate=pl.CostEstimate(flops=1 << 20, bytes_accessed=1 << 19, transcendentals=0),
        name="d_inner",
    )(d_gated, query, tail, taps)


def fwd_kernel(
    core_ref, strips_ref, pair_ref, cross_ref, cross_pair_ref, key_ref, value_ref, query_ref,
    tail_ref, taps_ref, skip_ref,
    gated_ref, inner_ref, mixed_ref,
    signal_ref,
):
    upper = core_ref[0] == 1
    pair = pair_ref[...].astype(F32)
    cross_pair = cross_pair_ref[...].astype(F32)
    near = jnp.where(upper, pair, cross_pair)
    far = jnp.where(upper, cross_pair, 0.0)
    own = jnp.concatenate([key_ref[...], value_ref[...]], axis=1).astype(F32)
    both = jnp.concatenate([far, cross_ref[...].astype(F32), near, own], axis=0)
    shifted = (both, later(both, 1), later(both, 2))
    k_short = short_sum(taps_ref, 1, [part[:, :CHANS] for part in shifted])
    v_short = short_sum(taps_ref, 2, [part[:, CHANS:] for part in shifted])
    mixed = (k_short * v_short).astype(BF16)
    mixed_ref[...] = mixed[LENGTH - ROWS :]
    signal_ref[: ROWS - STRIP, :] = jnp.zeros((ROWS - STRIP, CHANS), BF16)
    signal_ref[ROWS - STRIP :, :] = mixed
    inner = all_strips(strips_ref, signal_ref) + skip_ref[...] * mixed[LENGTH - ROWS :].astype(F32)
    inner_ref[...] = inner
    q_short = short_sum(taps_ref, 0, with_tail(tail_ref[...], query_ref[...]))
    gated_ref[...] = (q_short * inner).astype(BF16)


def with_core(kernel, name, core, operands, out_shape, scratch, flops):
    whole = lambda x: pl.BlockSpec(x.shape, lambda i, core_ref: (0,) * len(x.shape))
    return pl.pallas_call(
        kernel,
        grid_spec=pltpu.PrefetchScalarGridSpec(
            num_scalar_prefetch=1,
            grid=(1,),
            in_specs=[whole(x) for x in operands],
            out_specs=[whole(x) for x in out_shape],
            scratch_shapes=scratch,
        ),
        out_shape=out_shape,
        compiler_params=params(),
        cost_estimate=pl.CostEstimate(flops=flops, bytes_accessed=1 << 10, transcendentals=0),
        name=name,
    )(core, *operands)


def fwd_call(core, *operands):
    return with_core(
        fwd_kernel,
        "fwd",
        core,
        operands,
        [
            jax.ShapeDtypeStruct((ROWS, CHANS), BF16),
            jax.ShapeDtypeStruct((ROWS, CHANS), F32),
            jax.ShapeDtypeStruct((ROWS, CHANS), BF16),
        ],
        [pltpu.VMEM((LENGTH + ROWS - STRIP, CHANS), BF16)],
        4 << 30,
    )


def terms_kernel(core_ref, own_cot_ref, other_cot_ref, gated_ref, other_gated_ref, out_ref):
    dims = (((0,), (0,)), ((), ()))
    total = lax.dot_general(gated_ref[...], own_cot_ref[...], dims, preferred_element_type=F32)
    total += lax.dot_general(
        other_gated_ref[...], other_cot_ref[...], dims, preferred_element_type=F32
    )
    out_ref[0] = total.astype(BF16)


def terms_call(core, own_cot, other_cot, gated, other_gated):
    column = pl.BlockSpec((ROWS, SHARE), lambda i, core_ref: (0, 2 * i + core_ref[0]))
    signal = pl.BlockSpec((ROWS, CHANS), lambda i, core_ref: (0, 0))
    return pl.pallas_call(
        terms_kernel,
        grid_spec=pltpu.PrefetchScalarGridSpec(
            num_scalar_prefetch=1,
            grid=(2,),
            in_specs=[column, column, signal, signal],
            out_specs=pl.BlockSpec((1, CHANS, SHARE), lambda i, core_ref: (i, 0, 0)),
        ),
        out_shape=jax.ShapeDtypeStruct((2, CHANS, SHARE + CHANS), BF16),
        compiler_params=params(),
        cost_estimate=pl.CostEstimate(
            flops=2 * ROWS * FEATS * CHANS, bytes_accessed=6 << 20, transcendentals=0
        ),
        name="terms",
    )(core, own_cot, other_cot, gated, other_gated)


def two_parts(total):
    rounded = total.astype(BF16).astype(F32)
    left = pltpu.roll(total - rounded, SEGMENT // 2, total.ndim - 2)
    return (rounded + left).astype(BF16)


def add_small_kernel(terms_ref, small_ref, other_small_ref, out_ref):
    parts = two_parts(small_ref[...] + other_small_ref[...]).astype(F32)
    out_ref[...] = jnp.broadcast_to(parts.reshape(1, CHANS, CHANS).astype(BF16), out_ref.shape)


def add_small_call(terms, small, other_small):
    whole = pl.BlockSpec((SHARES, SEGMENT, CHANS), lambda i: (0, 0, 0))
    return pl.pallas_call(
        add_small_kernel,
        grid=(1,),
        in_specs=[pl.BlockSpec(memory_space=pl.ANY), whole, whole],
        out_specs=pl.BlockSpec((2, CHANS, CHANS), lambda i: (0, 0, SHARE // CHANS)),
        out_shape=jax.ShapeDtypeStruct(terms.shape, BF16),
        input_output_aliases={0: 0},
        compiler_params=params(),
        name="add_small",
    )(terms, small, other_small)


def place(g, n):
    row = g * (LENGTH // CHANS) + n
    return row % SHARES, row // SHARES


def bwd_kernel(
    core_ref, d0_ref, d1_ref, d2_ref, d3_ref, lags_ref, mixed_ref, key_ref, value_ref, pair_ref,
    cross_pair_ref, query_ref, tail_ref, inner_ref, d_gated_ref, taps_ref, skip_ref,
    d_short_ref, small_ref,
    strips_ref, ahead_ref, outer_ref, stack_ref,
):
    for n, ref in enumerate((d0_ref, d1_ref, d2_ref, d3_ref)):
        ahead_ref[n * ROWS : (n + 1) * ROWS, :] = ref[...]
    ahead_ref[LENGTH:, :] = jnp.zeros((ROWS, CHANS), BF16)
    lines = lines_of(lags_ref, False)
    for g in range(GROUPS):
        strips_ref[g * STRIP : (g + 1) * STRIP, :] = strip_of(lines[g : g + 1])
    d_inner = d0_ref[...].astype(F32)
    mixed = mixed_ref[...]
    d_mixed = all_strips(strips_ref, ahead_ref) + skip_ref[...] * d_inner

    upper = core_ref[0] == 1
    last = slice(ROWS - TAIL, ROWS)
    near = jnp.where(upper, pair_ref[last, :].astype(F32), cross_pair_ref[last, :].astype(F32))
    k_parts = with_tail(near[:, :CHANS], key_ref[...])
    v_parts = with_tail(near[:, CHANS:], value_ref[...])
    q_parts = with_tail(tail_ref[...], query_ref[...])
    small_ref[...] = jnp.zeros_like(small_ref)
    d_qs = d_gated_ref[...].astype(F32) * inner_ref[...]
    d_ks = d_mixed * short_sum(taps_ref, 2, v_parts)
    d_vs = d_mixed * short_sum(taps_ref, 1, k_parts)
    for i, (grad, parts) in enumerate(((d_qs, q_parts), (d_ks, k_parts), (d_vs, v_parts))):
        d_short_ref[i] = grad
        for j in range(3):
            small_ref[3 * i + j, 2:3, :] = jnp.sum(grad * parts[j], axis=0, keepdims=True)
    small_ref[9, 2:3, :] = jnp.sum(d_inner * mixed.astype(F32), axis=0, keepdims=True)

    row = lax.broadcasted_iota(jnp.int32, (ROWS, ROWS), 0)
    col = lax.broadcasted_iota(jnp.int32, (ROWS, ROWS), 1)
    turn = ((row // SMALL) * SMALL + (SMALL - 1 - row % SMALL) == col).astype(F32).astype(BF16)
    turned = jnp.dot(turn, mixed, preferred_element_type=F32)
    ids = lane_groups(SMALL)
    for part in range(ROWS // SMALL):
        piece = turned[part * SMALL : (part + 1) * SMALL]
        for g in range(GROUPS):
            stack_ref[g * SMALL : (g + 1) * SMALL, :] = jnp.where(ids == g, piece, 0.0).astype(BF16)
        term = lax.dot_general(
            stack_ref[...],
            ahead_ref[part * SMALL : part * SMALL + LENGTH, :],
            (((1,), (1,)), ((), ())),
            preferred_element_type=F32,
        )
        if part == 0:
            outer_ref[:, :LENGTH] = term
        else:
            outer_ref[:, :LENGTH] += term
    outer_ref[:, LENGTH:] = jnp.zeros((GROUPS * SMALL, PAD), F32)
    for g in range(GROUPS):
        skewed = pltpu.roll(
            outer_ref[g * SMALL : (g + 1) * SMALL, :], WIDE - (SMALL - 1), 1, stride=1, stride_axis=0
        )
        sums = jnp.sum(skewed[:, :LENGTH], axis=0, keepdims=True)
        for n in range(LENGTH // CHANS):
            share, slot = place(g, n)
            small_ref[share, slot : slot + 1, :] = sums[:, n * CHANS : (n + 1) * CHANS]


def bwd_call(core, *operands):
    return with_core(
        bwd_kernel,
        "bwd",
        core,
        operands,
        [
            jax.ShapeDtypeStruct((3, ROWS, CHANS), F32),
            jax.ShapeDtypeStruct((SHARES, SEGMENT, CHANS), F32),
        ],
        [
            pltpu.VMEM((GROUPS * STRIP, LENGTH), BF16),
            pltpu.VMEM((LENGTH + ROWS, CHANS), BF16),
            pltpu.VMEM((GROUPS * SMALL, WIDE), F32),
            pltpu.VMEM((GROUPS * SMALL, CHANS), BF16),
        ],
        1 << 10,
    )


def input_grad_kernel(d_short_ref, next_ref, taps_ref, query_ref, key_ref, value_ref):
    for i, out_ref in enumerate((query_ref, key_ref, value_ref)):
        joined = jnp.concatenate([d_short_ref[i], next_ref[i]], axis=0)
        rows = joined.shape[0]
        parts = (
            joined[:ROWS],
            pltpu.roll(joined, rows - 1, 0)[:ROWS],
            pltpu.roll(joined, rows - 2, 0)[:ROWS],
        )
        out_ref[...] = short_sum(taps_ref, i, parts).astype(BF16)


def input_grad_call(d_short, following, taps):
    return pl.pallas_call(
        input_grad_kernel,
        out_shape=[jax.ShapeDtypeStruct((ROWS, CHANS), BF16)] * 3,
        compiler_params=params(),
        cost_estimate=pl.CostEstimate(flops=1 << 10, bytes_accessed=1 << 10, transcendentals=0),
        name="input_grads",
    )(d_short, following, taps)


def total_kernel(scale, terms_ref, out_ref):
    total = jnp.sum(terms_ref[...].astype(F32), axis=0) * scale
    small = total[:, SHARE:]
    row = lax.broadcasted_iota(jnp.int32, small.shape, 0)
    small = jnp.where(row < SEGMENT // 2, small + pltpu.roll(small, SEGMENT // 2, 0), 0.0)
    total = jnp.concatenate([total[:, :SHARE].astype(BF16), two_parts(small)], axis=1)
    out_ref[...] = jnp.broadcast_to(total[None], out_ref.shape)


def total_call(terms, scale):
    return pl.pallas_call(
        lambda *refs: total_kernel(scale, *refs),
        out_shape=jax.ShapeDtypeStruct((SHARES, *terms.shape[1:]), BF16),
        compiler_params=params(),
        cost_estimate=pl.CostEstimate(flops=1 << 20, bytes_accessed=3 << 20, transcendentals=0),
        name="total",
    )(terms)


def spread_kernel(shares_ref, small_ref, weight_ref, taps_ref, filter_ref, skip_ref):
    weight_ref[...] = shares_ref[...].astype(F32).T

    @pl.when(pl.program_id(0) == 0)
    def _():
        for share in range(SHARES):
            segment = small_ref[share * SEGMENT : (share + 1) * SEGMENT, :].astype(F32)
            segment = segment + pltpu.roll(segment, SEGMENT // 2, 0)
            for g in range(GROUPS):
                for n in range(LENGTH // CHANS):
                    if place(g, n)[0] == share:
                        slot = place(g, n)[1]
                        filter_ref[g : g + 1, n * CHANS : (n + 1) * CHANS] = segment[slot : slot + 1]
            if share < 9:
                taps_ref[share // 3, share % 3 : share % 3 + 1, :] = segment[2:3]
            if share == 9:
                skip_ref[...] = segment[2:3]


def spread_call(shares):
    shares = shares.reshape(CHANS, SHARE + CHANS)
    tile = 512
    return pl.pallas_call(
        spread_kernel,
        grid=(SHARE // tile,),
        in_specs=[
            pl.BlockSpec((CHANS, tile), lambda i: (0, i)),
            pl.BlockSpec((CHANS, CHANS), lambda i: (0, SHARE // CHANS)),
        ],
        out_specs=[
            pl.BlockSpec((tile, CHANS), lambda i: (i, 0)),
            pl.BlockSpec((3, 3, CHANS), lambda i: (0, 0, 0)),
            pl.BlockSpec((GROUPS, LENGTH), lambda i: (0, 0)),
            pl.BlockSpec((1, CHANS), lambda i: (0, 0)),
        ],
        out_shape=[
            jax.ShapeDtypeStruct((SHARE, CHANS), F32),
            jax.ShapeDtypeStruct((3, 3, CHANS), F32),
            jax.ShapeDtypeStruct((GROUPS, LENGTH), F32),
            jax.ShapeDtypeStruct((1, CHANS), F32),
        ],
        compiler_params=params(),
        name="spread",
    )(shares, shares)


def sent(block, distance):
    count = 4
    route = [(i, i + distance) for i in range(count) if 0 <= i + distance < count]
    return lax.ppermute(block, CTX, route)


def shards(
    query_in, key_in, value_in, short_taps, long_filter, skip_gain, out_weight, out_cotangent
):
    query = query_in[0]
    cot = out_cotangent[0]
    taps = short_taps
    skip = skip_gain.reshape(1, CHANS)
    devices = lax.axis_size(ALL)
    tokens = ROWS * devices
    scale = 1.0 / math.sqrt(tokens)
    core = lax.axis_index("co").astype(jnp.int32).reshape(1)

    key = key_in[0]
    value = value_in[0]
    swap = [(0, 1), (1, 0)]
    own = jnp.concatenate([key, value], axis=1)
    tail = sent(query[ROWS - TAIL :], 1)
    cross = lax.ppermute(own, "xh", [(0, 1)])
    pair = lax.ppermute(own, "co", swap)
    other_cot = lax.ppermute(cot, "co", swap)

    d_gated, strips = pre_call(cot, out_weight, long_filter)
    cross, tail, d_gated, strips = lax.optimization_barrier((cross, tail, d_gated, strips))
    cross_pair = lax.ppermute(cross, "co", swap)
    d_inner = d_inner_call(d_gated, query, tail, taps)
    blocks = [d_inner] + [sent(d_inner, -distance) for distance in (1, 2, 3)]
    gated, inner, mixed = fwd_call(
        core, strips, pair, cross, cross_pair, key, value, query, tail, taps, skip
    )
    other_gated = lax.ppermute(gated, "co", swap)
    d_short, small = bwd_call(
        core, *blocks, long_filter, mixed, key, value, pair, cross_pair, query, tail, inner,
        d_gated, taps, skip,
    )
    other_gated, d_short, small = lax.optimization_barrier((other_gated, d_short, small))
    other_small = lax.ppermute(small, "co", swap)
    following = sent(d_short[:, :8], -1)
    terms = terms_call(core, cot, other_cot, gated, other_gated)
    terms, other_small, following = lax.optimization_barrier((terms, other_small, following))
    terms = add_small_call(terms, small, other_small)
    terms = terms.reshape(2 * SHARES, CHANS // SHARES, SHARE + CHANS)
    terms = lax.all_to_all(terms, CHIPS, 0, 0)
    grad_query, grad_key, grad_value = input_grad_call(d_short, following, taps)

    shares = lax.all_to_all(total_call(terms, scale), DP, 0, 0)
    grad_weight, grad_taps, grad_filter, grad_skip = spread_call(shares)
    return (
        gated[None],
        grad_query[None],
        grad_key[None],
        grad_value[None],
        grad_taps,
        grad_filter,
        grad_skip.reshape(CHANS),
        grad_weight,
    )


def solution(mesh):
    fine = Mesh(mesh.devices.reshape(2, 2, 4, 2, 4), ALL)
    tokens = P(DP, CTX, None)
    in_specs = (tokens, tokens, tokens, P(), P(), P(), P(), tokens)
    out_specs = (tokens, tokens, tokens, tokens, P(), P(), P(), P(CTX, None))
    return jax.shard_map(
        shards, mesh=fine, in_specs=in_specs, out_specs=out_specs, check_vma=False
    )
```

time: 151 us -> 124 us (0.82)
  the two profiles are of different devices: /device:TPU:1 before, /device:TPU:4 now
where the time goes in v3:
time: 124 us; the launch traced here: 123 us
  blocking collectives  41.9 us (34%)
  Pallas kernels  37.1 us (30%)
  starting transfers between devices  21.9 us (18%)
  waiting for transfers between devices  15.1 us (12%)
  local copies, waits for them, and re-layouts  5.12 us (4%)
    all_to_all x1, blocking collectives, shards(): terms = lax.all_to_all(terms, CHIPS, 0, 0)  41.9 us
    all_to_all x1, waiting for transfers between devices, shards(): shares = lax.all_to_all(total_call(terms, scale), DP, 0, 0)  15.1 us
    ppermute x5, starting transfers between devices, sent(): return lax.ppermute(block, CTX, route)  13.4 us
    pallas_call x2, Pallas kernels, with_core(): pl.pallas_call(kernel, grid_spec=pltpu.PrefetchScalarGridSpec(num_scalar_...  12.4 us
    pallas_call x1, Pallas kernels, pre_call(): pl.pallas_call(pre_kernel, grid=(steps,), in_specs=[pl.BlockSpec((ROWS, T...  8.08 us
    all_to_all x1, starting transfers between devices, shards(): shares = lax.all_to_all(total_call(terms, scale), DP, 0, 0)  4.92 us
    pallas_call x1, Pallas kernels, terms_call(): pl.pallas_call(terms_kernel, grid_spec=pltpu.PrefetchScalarGridSpec(num_s...  4.09 us
    pallas_call x1, Pallas kernels, spread_call(): pl.pallas_call(spread_kernel, grid=(SHARE // tile,), in_specs=[pl.BlockSp...  3.88 us
  transfers between devices with their start and end apart: 12, of which 1 were waited for; matrix products, arithmetic and copies ran while one was open for 2% of the time, Pallas kernels for 23%

profile of v3, /device:TPU:4, one launch (start us, length us, event | category | flops | bytes accessed | tf_op | source)
XLA Modules:
  0.0 123.0 jit_solution(6102724181547352225)
XLA Ops:
  0.6 0.1 collective-permute-start.8
  0.7 1.0 pad_maximum_fusion
  1.7 1.3 %collective-permute-start = (bf16[256,512]{1,0:T(8,128)(2,1)S(1)}, bf16[256,512]{1,0:T(8,128)(2,1)S(1)}, u32[]{:S(2)}, u32[]{:S(2)}) collective-permute-start(bf16[256,512]{1,0:T(8,128)(2,1)S(1)} %pad_maximum_fusion), channel_id=1, source_target_pairs={{0,64},{1,65},{2,66},{3,67},{4,68},{5,69},{6,70},{7,71},{8,72},{9,... | collective-permute-start | bytes 786440 | tf_op jit(solution)/shard_map/ppermute | solution.py:465
  3.0 0.6 collective-permute-start.2
  3.6 0.7 slice_bitcast_fusion
  4.3 1.9 %collective-permute-start.1 = (bf16[16,256]{1,0:T(8,128)(2,1)S(1)}, bf16[16,256]{1,0:T(8,128)(2,1)S(1)}, u32[]{:S(2)}, u32[]{:S(2)}) collective-permute-start(bf16[16,256]{1,0:T(8,128)(2,1)S(1)} %slice_bitcast_fusion), channel_id=1, source_target_pairs={{0,32},{32,64},{64,96},{1,33},{33,65},{65,97},{2,34},{34,66},{66,9... | collective-permute-start | bytes 24584 | tf_op jit(solution)/shard_map/ppermute | solution.py:445
  6.2 8.1 %pre.1 = (bf16[256,256]{1,0:T(8,128)(2,1)}, bf16[512,1024]{1,0:T(8,128)(2,1)}) custom-call(bf16[256,8192]{1,0:T(8,128)(2,1)} %bitcast.17, bf16[8192,256]{1,0:T(8,128)(2,1)} %weight_ref.1, bf16[16,1024]{1,0:T(8,128)(2,1)} %lags_ref.1), custom_call_target="tpu_custom_call" | custom-call | flops 1073741824 | bytes 14680064 | tf_op jit(solution)/shard_map/pre/pallas_call | solution.py:114
  14.3 0.0 collective-permute-done.1.tail_ref
  14.3 0.0 copy-start.8
  14.3 0.0 collective-permute-done.cross_ref
  14.3 0.0 copy-start.10
  14.3 0.1 collective-permute-start.3
  14.4 0.5 copy-done.8
  14.9 1.7 %d_inner.1.d0_ref = bf16[256,256]{1,0:T(8,128)(2,1)} custom-call(bf16[256,256]{1,0:T(8,128)(2,1)} %get-tuple-element.38.d_gated_ref, bf16[256,256]{1,0:T(8,128)(2,1)} %bitcast.21, bf16[16,256]{1,0:T(8,128)(2,1)} %copy-done.8, f32[3,3,256]{2,1,0:T(4,128)} %taps_ref.7), custom_call_target="tpu_custom_call" | custom-call | flops 1048576 | bytes 524288 | tf_op jit(solution)/shard_map/d_inner/pallas_call | solution.py:145
  16.6 5.7 %collective-permute-start.5 = (bf16[256,256]{1,0:T(8,128)(2,1)}, bf16[256,256]{1,0:T(8,128)(2,1)S(1)}, u32[]{:S(2)}, u32[]{:S(2)}) collective-permute-start(bf16[256,256]{1,0:T(8,128)(2,1)} %d_inner.1.d0_ref), channel_id=1, source_target_pairs={{32,0},{64,32},{96,64},{33,1},{65,33},{97,65},{34,2},{66,34},{98,6... | collective-permute-start | bytes 393224 | tf_op jit(solution)/shard_map/ppermute | solution.py:445
  22.3 1.7 %collective-permute-start.6 = (bf16[256,256]{1,0:T(8,128)(2,1)}, bf16[256,256]{1,0:T(8,128)(2,1)S(1)}, u32[]{:S(2)}, u32[]{:S(2)}) collective-permute-start(bf16[256,256]{1,0:T(8,128)(2,1)} %d_inner.1.d0_ref), channel_id=1, source_target_pairs={{64,0},{96,32},{65,1},{97,33},{66,2},{98,34},{67,3},{99,35},{68,4}... | collective-permute-start | bytes 393224 | tf_op jit(solution)/shard_map/ppermute | solution.py:445
  24.0 0.0 collective-permute-done.2.pair_ref
  24.0 0.0 copy-start.2
  24.0 0.7 collective-permute-start.7
  24.7 0.0 collective-permute-done.3.cross_pair_ref
  24.7 0.0 copy-start.3
  24.7 0.0 copy-done.10
  24.7 0.0 copy-done.2
  24.7 0.7 copy-done.3
  25.4 5.0 %fwd.1 = (bf16[256,256]{1,0:T(8,128)(2,1)}, f32[256,256]{1,0:T(8,128)}, bf16[256,256]{1,0:T(8,128)(2,1)}) custom-call(s32[1]{0:T(128)} %bitcast.core_ref, bf16[512,1024]{1,0:T(8,128)(2,1)} %get-tuple-element.34.strips_ref, bf16[256,512]{1,0:T(8,128)(2,1)} %copy-done.2, bf16[256,512]{1,0:T(8,128)(2,1)} %copy-done.10, bf16[256,512]{1,0:T(8,128)(2,1)} %copy-done.3, ...), custom_call_target="tpu_custom_call" | custom-call | flops 4294967296 | bytes 1024 | tf_op jit(solution)/shard_map/fwd/pallas_call | solution.py:182
  30.4 1.5 %collective-permute-start.4 = (bf16[256,256]{1,0:T(8,128)(2,1)}, bf16[256,256]{1,0:T(8,128)(2,1)S(1)}, u32[]{:S(2)}, u32[]{:S(2)}) collective-permute-start(bf16[256,256]{1,0:T(8,128)(2,1)} %get-tuple-element.37.gated_ref), channel_id=1, source_target_pairs={{0,32},{32,0},{1,33},{33,1},{2,34},{34,2},{3,35},{35,3},{4,36},{36... | collective-permute-start | bytes 393224 | tf_op jit(solution)/shard_map/ppermute | solution.py:477
  31.9 0.0 collective-permute-done.5.d1_ref
  31.9 0.0 copy-start.5
  31.9 0.0 collective-permute-done.6.d2_ref
  31.9 0.0 copy-start.6
  31.9 0.0 collective-permute-done.7.d3_ref
  31.9 0.0 copy-start.7
  31.9 0.6 copy-done.5
  32.5 0.1 copy-done.6
  32.6 0.1 copy-done.7
  32.7 7.4 %bwd.1 = (f32[3,256,256]{2,1,0:T(8,128)}, f32[32,8,256]{2,1,0:T(8,128)}) custom-call(s32[1]{0:T(128)} %bitcast.core_ref, bf16[256,256]{1,0:T(8,128)(2,1)} %d_inner.1.d0_ref, bf16[256,256]{1,0:T(8,128)(2,1)} %copy-done.5, bf16[256,256]{1,0:T(8,128)(2,1)} %copy-done.6, bf16[256,256]{1,0:T(8,128)(2,1)} %copy-done.7, bf16[16,1024]{1,0:T(8,128)(2,1)} %lags_ref.1, ...), custom_call_target="tpu_custom_call" | custom-call | flops 1024 | bytes 1024 | tf_op jit(solution)/shard_map/bwd/pallas_call | solution.py:182
  40.1 0.0 collective-permute-done.4.other_gated_ref
  40.1 0.0 copy-start.4
  40.1 0.1 collective-permute-start.9
  40.2 0.7 slice.11
  40.9 3.4 %collective-permute-start.10 = (f32[3,8,256]{2,1,0:T(8,128)S(1)}, f32[3,8,256]{2,1,0:T(8,128)S(1)}, u32[]{:S(2)}, u32[]{:S(2)}) collective-permute-start(f32[3,8,256]{2,1,0:T(8,128)S(1)} %slice.11), channel_id=1, source_target_pairs={{32,0},{64,32},{96,64},{33,1},{65,33},{97,65},{34,2},{66,34},{98,6... | collective-permute-start | bytes 73736 | tf_op jit(solution)/shard_map/ppermute | solution.py:445
  44.4 0.0 collective-permute-done.8.other_cot_ref
  44.4 0.0 copy-done.4
  44.4 4.1 %terms.1.terms_ref = bf16[2,256,2304]{2,1,0:T(8,128)(2,1)} custom-call(s32[1]{0:T(128)} %bitcast.core_ref, bf16[256,8192]{1,0:T(8,128)(2,1)} %bitcast.18, bf16[256,8192]{1,0:T(8,128)(2,1)} %collective-permute-done.8.other_cot_ref, bf16[256,256]{1,0:T(8,128)(2,1)} %get-tuple-element.37.gated_ref, bf16[256,256]{1,0:T(8,128)(2,1)} %copy-done.4), custom_call_target="tpu_custom_call" | custom-call | flops 1073741824 | bytes 6291456 | tf_op jit(solution)/shard_map/terms/pallas_call | solution.py:226
  48.5 0.0 collective-permute-done.10.next_ref
  48.5 0.0 copy-start.9
  48.5 0.0 collective-permute-done.9.other_small_ref
  48.5 0.0 copy-start.1
  48.5 0.7 copy-done.1
  49.2 1.8 %add_small.1 = bf16[2,256,2304]{2,1,0:T(8,128)(2,1)} custom-call(bf16[2,256,2304]{2,1,0:T(8,128)(2,1)} %terms.1.terms_ref, f32[32,8,256]{2,1,0:T(8,128)} %get-tuple-element.45.small_ref, f32[32,8,256]{2,1,0:T(8,128)} %copy-done.1), custom_call_target="tpu_custom_call", output_to_operand_aliasing={{}: (0, {})} | custom-call | tf_op jit(solution)/shard_map/add_small/pallas_call | solution.py:256
  51.1 41.9 %all_to_all.10.refs_0_ = bf16[64,8,2304]{2,1,0:T(8,128)(2,1)} all-to-all(bf16[64,8,2304]{2,1,0:T(8,128)(2,1)} %bitcast.15), channel_id=1, replica_groups=mesh['xh'=2,'co'=2,'y'=4,'xl'=2,'z'=4] {'xh','y','xl','z'}, dimensions={0} | all-to-all | bytes 4718592 | tf_op jit(solution)/shard_map/all_to_all | solution.py:489
  93.0 3.0 %total.1 = bf16[32,8,2304]{2,1,0:T(8,128)(2,1)} custom-call(bf16[64,8,2304]{2,1,0:T(8,128)(2,1)} %all_to_all.10.refs_0_), custom_call_target="tpu_custom_call" | custom-call | flops 1048576 | bytes 3145728 | tf_op jit(solution)/shard_map/total/pallas_call | solution.py:387
  96.0 0.0 copy-done.9
  96.0 4.9 %all-to-all-start.1 = ((bf16[32,8,2304]{2,1,0:T(8,128)(2,1)}), bf16[32,8,2304]{2,1,0:T(8,128)(2,1)S(1)}, u32[]{:S(2)}, u32[]{:S(2)}) async-start(bf16[32,8,2304]{2,1,0:T(8,128)(2,1)} %total.1), calls=%async_computation.1 | async-start | bytes 2359296 | tf_op jit(solution)/shard_map/all_to_all | solution.py:492
  100.9 2.1 %input_grads.1 = (bf16[256,256]{1,0:T(8,128)(2,1)}, bf16[256,256]{1,0:T(8,128)(2,1)}, bf16[256,256]{1,0:T(8,128)(2,1)}) custom-call(f32[3,256,256]{2,1,0:T(8,128)} %get-tuple-element.43.d_short_ref, f32[3,8,256]{2,1,0:T(8,128)} %copy-done.9, f32[3,3,256]{2,1,0:T(4,128)} %taps_ref.7), custom_call_target="tpu_custom_call" | custom-call | flops 1024 | bytes 1024 | tf_op jit(solution)/shard_map/input_grads/pallas_call | solution.py:368
  103.0 15.1 %all-to-all-done.1 = bf16[32,8,2304]{2,1,0:T(8,128)(2,1)S(1)} async-done(((bf16[32,8,2304]{2,1,0:T(8,128)(2,1)}), bf16[32,8,2304]{2,1,0:T(8,128)(2,1)S(1)}, u32[]{:S(2)}, u32[]{:S(2)}) %all-to-all-start.1) | async-done | bytes 1179680 | tf_op jit(solution)/shard_map/all_to_all | solution.py:492
  118.1 0.0 copy-start
  118.1 1.0 copy-done
  119.2 3.9 %spread.1 = (f32[2048,256]{1,0:T(8,128)}, f32[3,3,256]{2,1,0:T(4,128)}, f32[16,1024]{1,0:T(8,128)}, f32[1,256]{1,0:T(1,128)}) custom-call(bf16[256,2304]{1,0:T(8,128)(2,1)} %bitcast.19, bf16[256,2304]{1,0:T(8,128)(2,1)} %bitcast.20), custom_call_target="tpu_custom_call" | custom-call | tf_op jit(solution)/shard_map/spread/pallas_call | solution.py:418
Async XLA Ops:
  0.6 43.8 %collective-permute-start.8 = (bf16[256,8192]{1,0:T(8,128)(2,1)}, bf16[256,8192]{1,0:T(8,128)(2,1)}, u32[]{:S(2)}, u32[]{:S(2)}) collective-permute-start(bf16[256,8192]{1,0:T(8,128)(2,1)} %bitcast.16), channel_id=1, source_target_pairs={{0,32},{32,0},{1,33},{33,1},{2,34},{34,2},{3,35},{35,3},{4,36},{36... | collective-permute-start | bytes 12582920 | tf_op jit(solution)/shard_map/ppermute | solution.py:467
  1.7 12.6 %collective-permute-start = (bf16[256,512]{1,0:T(8,128)(2,1)S(1)}, bf16[256,512]{1,0:T(8,128)(2,1)S(1)}, u32[]{:S(2)}, u32[]{:S(2)}) collective-permute-start(bf16[256,512]{1,0:T(8,128)(2,1)S(1)} %pad_maximum_fusion), channel_id=1, source_target_pairs={{0,64},{1,65},{2,66},{3,67},{4,68},{5,69},{6,70},{7,71},{8,72},{9,... | collective-permute-start | bytes 786440 | tf_op jit(solution)/shard_map/ppermute | solution.py:465
  3.0 21.0 %collective-permute-start.2 = (bf16[256,512]{1,0:T(8,128)(2,1)S(1)}, bf16[256,512]{1,0:T(8,128)(2,1)S(1)}, u32[]{:S(2)}, u32[]{:S(2)}) collective-permute-start(bf16[256,512]{1,0:T(8,128)(2,1)S(1)} %pad_maximum_fusion), channel_id=1, source_target_pairs={{0,32},{32,0},{1,33},{33,1},{2,34},{34,2},{3,35},{35,3},{4,36},{36... | collective-permute-start | bytes 786440 | tf_op jit(solution)/shard_map/ppermute | solution.py:466
  4.3 10.0 %collective-permute-start.1 = (bf16[16,256]{1,0:T(8,128)(2,1)S(1)}, bf16[16,256]{1,0:T(8,128)(2,1)S(1)}, u32[]{:S(2)}, u32[]{:S(2)}) collective-permute-start(bf16[16,256]{1,0:T(8,128)(2,1)S(1)} %slice_bitcast_fusion), channel_id=1, source_target_pairs={{0,32},{32,64},{64,96},{1,33},{33,65},{65,97},{2,34},{34,66},{66,9... | collective-permute-start | bytes 24584 | tf_op jit(solution)/shard_map/ppermute | solution.py:445
  14.3 0.6 copy-start.8
  14.3 10.4 %copy-start.10 = (bf16[256,512]{1,0:T(8,128)(2,1)}, bf16[256,512]{1,0:T(8,128)(2,1)S(1)}, u32[]{:S(2)}) copy-start(bf16[256,512]{1,0:T(8,128)(2,1)S(1)} %collective-permute-done.cross_ref) | copy-start | bytes 786436
  14.3 10.4 %collective-permute-start.3 = (bf16[256,512]{1,0:T(8,128)(2,1)S(1)}, bf16[256,512]{1,0:T(8,128)(2,1)S(1)}, u32[]{:S(2)}, u32[]{:S(2)}) collective-permute-start(bf16[256,512]{1,0:T(8,128)(2,1)S(1)} %collective-permute-done.cross_ref), channel_id=1, source_target_pairs={{0,32},{32,0},{1,33},{33,1},{2,34},{34,2},{3,35},{35,3},{4,36},{36... | collective-permute-start | bytes 786440 | tf_op jit(solution)/shard_map/ppermute | solution.py:471
  16.6 15.3 %collective-permute-start.5 = (bf16[256,256]{1,0:T(8,128)(2,1)}, bf16[256,256]{1,0:T(8,128)(2,1)S(1)}, u32[]{:S(2)}, u32[]{:S(2)}) collective-permute-start(bf16[256,256]{1,0:T(8,128)(2,1)} %d_inner.1.d0_ref), channel_id=1, source_target_pairs={{32,0},{64,32},{96,64},{33,1},{65,33},{97,65},{34,2},{66,34},{98,6... | collective-permute-start | bytes 393224 | tf_op jit(solution)/shard_map/ppermute | solution.py:445
  22.3 9.6 %collective-permute-start.6 = (bf16[256,256]{1,0:T(8,128)(2,1)}, bf16[256,256]{1,0:T(8,128)(2,1)S(1)}, u32[]{:S(2)}, u32[]{:S(2)}) collective-permute-start(bf16[256,256]{1,0:T(8,128)(2,1)} %d_inner.1.d0_ref), channel_id=1, source_target_pairs={{64,0},{96,32},{65,1},{97,33},{66,2},{98,34},{67,3},{99,35},{68,4}... | collective-permute-start | bytes 393224 | tf_op jit(solution)/shard_map/ppermute | solution.py:445
  24.0 0.7 copy-start.2
  24.0 7.9 %collective-permute-start.7 = (bf16[256,256]{1,0:T(8,128)(2,1)}, bf16[256,256]{1,0:T(8,128)(2,1)S(1)}, u32[]{:S(2)}, u32[]{:S(2)}) collective-permute-start(bf16[256,256]{1,0:T(8,128)(2,1)} %d_inner.1.d0_ref), channel_id=1, source_target_pairs={{96,0},{97,1},{98,2},{99,3},{100,4},{101,5},{102,6},{103,7},{104,8... | collective-permute-start | bytes 393224 | tf_op jit(solution)/shard_map/ppermute | solution.py:445
  24.7 0.7 copy-start.3
  30.4 9.7 %collective-permute-start.4 = (bf16[256,256]{1,0:T(8,128)(2,1)}, bf16[256,256]{1,0:T(8,128)(2,1)S(1)}, u32[]{:S(2)}, u32[]{:S(2)}) collective-permute-start(bf16[256,256]{1,0:T(8,128)(2,1)} %get-tuple-element.37.gated_ref), channel_id=1, source_target_pairs={{0,32},{32,0},{1,33},{33,1},{2,34},{34,2},{3,35},{35,3},{4,36},{36... | collective-permute-start | bytes 393224 | tf_op jit(solution)/shard_map/ppermute | solution.py:477
  31.9 0.6 copy-start.5
  31.9 0.7 copy-start.6
  31.9 0.7 copy-start.7
  40.1 4.3 %copy-start.4 = (bf16[256,256]{1,0:T(8,128)(2,1)}, bf16[256,256]{1,0:T(8,128)(2,1)S(1)}, u32[]{:S(2)}) copy-start(bf16[256,256]{1,0:T(8,128)(2,1)S(1)} %collective-permute-done.4.other_gated_ref) | copy-start | bytes 393220
  40.1 8.4 %collective-permute-start.9 = (f32[32,8,256]{2,1,0:T(8,128)}, f32[32,8,256]{2,1,0:T(8,128)S(1)}, u32[]{:S(2)}, u32[]{:S(2)}) collective-permute-start(f32[32,8,256]{2,1,0:T(8,128)} %get-tuple-element.45.small_ref), channel_id=1, source_target_pairs={{0,32},{32,0},{1,33},{33,1},{2,34},{34,2},{3,35},{35,3},{4,36},{36... | collective-permute-start | bytes 786440 | tf_op jit(solution)/shard_map/ppermute | solution.py:483
  40.9 7.6 %collective-permute-start.10 = (f32[3,8,256]{2,1,0:T(8,128)S(1)}, f32[3,8,256]{2,1,0:T(8,128)S(1)}, u32[]{:S(2)}, u32[]{:S(2)}) collective-permute-start(f32[3,8,256]{2,1,0:T(8,128)S(1)} %slice.11), channel_id=1, source_target_pairs={{32,0},{64,32},{96,64},{33,1},{65,33},{97,65},{34,2},{66,34},{98,6... | collective-permute-start | bytes 73736 | tf_op jit(solution)/shard_map/ppermute | solution.py:445
  48.5 47.5 %copy-start.9 = (f32[3,8,256]{2,1,0:T(8,128)}, f32[3,8,256]{2,1,0:T(8,128)S(1)}, u32[]{:S(2)}) copy-start(f32[3,8,256]{2,1,0:T(8,128)S(1)} %collective-permute-done.10.next_ref) | copy-start | bytes 73732
  48.5 0.7 copy-start.1
  96.0 22.1 %all-to-all-start.1 = ((bf16[32,8,2304]{2,1,0:T(8,128)(2,1)}), bf16[32,8,2304]{2,1,0:T(8,128)(2,1)S(1)}, u32[]{:S(2)}, u32[]{:S(2)}) async-start(bf16[32,8,2304]{2,1,0:T(8,128)(2,1)} %total.1), calls=%async_computation.1 | async-start | bytes 2359296 | tf_op jit(solution)/shard_map/all_to_all | solution.py:492
  118.1 1.0 copy-start

commit v4 on v3

--- a/solution.py
+++ b/solution.py
@@ -23,17 +23,35 @@
 PAD = 128
 WIDE = LENGTH + PAD
 FEATS = 8192
-TILE = 1024
 SMALL = 32
 TAIL = 16
 SHARES = 32
 SHARE = FEATS // 4
 SEGMENT = 8
-VMEM_LIMIT = 56 * 1024 * 1024
-
-
-def params(*semantics):
-    return pltpu.CompilerParams(vmem_limit_bytes=VMEM_LIMIT)
+SPREAD = 4
+PIECES = 8
+VMEM_LIMIT = 24 * 1024 * 1024
+
+
+def call(kernel, name, out_shape, operands, scratch=(), scalars=0, flops=1 << 10, **more):
+    spec = pl.BlockSpec(memory_space=pltpu.VMEM)
+    in_specs = [pl.BlockSpec(memory_space=pltpu.SMEM)] * scalars
+    in_specs += [spec] * (len(operands) - scalars)
+    defaults = {"in_specs": in_specs, "out_specs": jax.tree.map(lambda _: spec, out_shape)}
+    more = {**defaults, **more}
+    placed = [
+        pltpu.with_memory_space_constraint(x, pltpu.VMEM) if s.memory_space == pltpu.VMEM else x
+        for x, s in zip(operands, more["in_specs"])
+    ]
+    return pl.pallas_call(
+        kernel,
+        out_shape=out_shape,
+        scratch_shapes=list(scratch),
+        compiler_params=pltpu.CompilerParams(vmem_limit_bytes=VMEM_LIMIT),
+        cost_estimate=pl.CostEstimate(flops=flops, bytes_accessed=1 << 10, transcendentals=0),
+        name=name,
+        **more,
+    )(*placed)
 
 
 def lane_groups(rows):
@@ -91,49 +109,47 @@
     return pltpu.roll(wide, WIDE - (STRIP - 1), 1)
 
 
-def pre_kernel(cot_ref, weight_ref, filter_ref, d_gated_ref, strips_ref, acc_ref, line_ref):
-    step = pl.program_id(0)
-
-    @pl.when(step == 0)
-    def _():
-        acc_ref[...] = jnp.zeros_like(acc_ref)
-        line_ref[...] = lines_of(filter_ref, True)
-
-    acc_ref[...] += jnp.dot(cot_ref[...], weight_ref[...], preferred_element_type=F32)
-    for g in range(2):
-        line = line_ref[pl.ds(2 * step + g, 1), :]
-        strips_ref[g * STRIP : (g + 1) * STRIP, :] = strip_of(line)
-
-    @pl.when(step == pl.num_programs(0) - 1)
-    def _():
-        d_gated_ref[...] = acc_ref[...].astype(BF16)
+def pre_kernel(
+    cot_ref, weight_ref, filter_ref, d_gated_ref, strips_ref, cot_buffer, weight_buffer, sems
+):
+    tile = FEATS // PIECES
+    copies = []
+    for n in range(PIECES):
+        piece = slice(n * tile, (n + 1) * tile)
+        pair = (
+            pltpu.make_async_copy(cot_ref.at[:, piece], cot_buffer.at[n], sems.at[0, n]),
+            pltpu.make_async_copy(weight_ref.at[piece, :], weight_buffer.at[n], sems.at[1, n]),
+        )
+        for copy in pair:
+            copy.start()
+        copies.append(pair)
+    lines = lines_of(filter_ref, True)
+    for g in range(GROUPS):
+        strips_ref[g * STRIP : (g + 1) * STRIP, :] = strip_of(lines[g : g + 1])
+    total = jnp.zeros((ROWS, CHANS), F32)
+    for n in range(PIECES):
+        for copy in copies[n]:
+            copy.wait()
+        total += jnp.dot(cot_buffer[n], weight_buffer[n], preferred_element_type=F32)
+    d_gated_ref[...] = total.astype(BF16)
 
 
 def pre_call(cot, weight, lags):
-    steps = FEATS // TILE
-    return pl.pallas_call(
-        pre_kernel,
-        grid=(steps,),
-        in_specs=[
-            pl.BlockSpec((ROWS, TILE), lambda i: (0, i)),
-            pl.BlockSpec((TILE, CHANS), lambda i: (i, 0)),
-            pl.BlockSpec((GROUPS, LENGTH), lambda i: (0, 0)),
-        ],
-        out_specs=[
-            pl.BlockSpec((ROWS, CHANS), lambda i: (0, 0)),
-            pl.BlockSpec((2 * STRIP, LENGTH), lambda i: (i, 0)),
-        ],
-        out_shape=[
-            jax.ShapeDtypeStruct((ROWS, CHANS), BF16),
-            jax.ShapeDtypeStruct((GROUPS * STRIP, LENGTH), BF16),
-        ],
-        scratch_shapes=[pltpu.VMEM((ROWS, CHANS), F32), pltpu.VMEM((GROUPS, WIDE), F32)],
-        compiler_params=params(),
-        cost_estimate=pl.CostEstimate(
-            flops=2 * ROWS * FEATS * CHANS, bytes_accessed=14 << 20, transcendentals=0
-        ),
-        name="pre",
-    )(cot, weight, lags)
+    out_shape = [
+        pltpu.VMEM((ROWS, CHANS), BF16),
+        pltpu.VMEM((GROUPS * STRIP, LENGTH), BF16),
+    ]
+    tile = FEATS // PIECES
+    scratch = [
+        pltpu.VMEM((PIECES, ROWS, tile), BF16),
+        pltpu.VMEM((PIECES, tile, CHANS), BF16),
+        pltpu.SemaphoreType.DMA((2, PIECES)),
+    ]
+    far = pl.BlockSpec(memory_space=pl.ANY)
+    in_specs = [far, far, pl.BlockSpec(memory_space=pltpu.VMEM)]
+    return call(
+        pre_kernel, "pre", out_shape, (cot, weight, lags), scratch, in_specs=in_specs, flops=1 << 30
+    )
 
 
 def d_inner_kernel(d_gated_ref, query_ref, tail_ref, taps_ref, out_ref):
@@ -141,14 +157,8 @@
     out_ref[...] = (d_gated_ref[...].astype(F32) * q_short).astype(BF16)
 
 
-def d_inner_call(d_gated, query, tail, taps):
-    return pl.pallas_call(
-        d_inner_kernel,
-        out_shape=jax.ShapeDtypeStruct((ROWS, CHANS), BF16),
-        compiler_params=params(),
-        cost_estimate=pl.CostEstimate(flops=1 << 20, bytes_accessed=1 << 19, transcendentals=0),
-        name="d_inner",
-    )(d_gated, query, tail, taps)
+def d_inner_call(*operands):
+    return call(d_inner_kernel, "d_inner", pltpu.VMEM((ROWS, CHANS), BF16), operands)
 
 
 def fwd_kernel(
@@ -177,67 +187,30 @@
     gated_ref[...] = (q_short * inner).astype(BF16)
 
 
-def with_core(kernel, name, core, operands, out_shape, scratch, flops):
-    whole = lambda x: pl.BlockSpec(x.shape, lambda i, core_ref: (0,) * len(x.shape))
-    return pl.pallas_call(
-        kernel,
-        grid_spec=pltpu.PrefetchScalarGridSpec(
-            num_scalar_prefetch=1,
-            grid=(1,),
-            in_specs=[whole(x) for x in operands],
-            out_specs=[whole(x) for x in out_shape],
-            scratch_shapes=scratch,
-        ),
-        out_shape=out_shape,
-        compiler_params=params(),
-        cost_estimate=pl.CostEstimate(flops=flops, bytes_accessed=1 << 10, transcendentals=0),
-        name=name,
-    )(core, *operands)
-
-
-def fwd_call(core, *operands):
-    return with_core(
-        fwd_kernel,
-        "fwd",
-        core,
-        operands,
-        [
-            jax.ShapeDtypeStruct((ROWS, CHANS), BF16),
-            jax.ShapeDtypeStruct((ROWS, CHANS), F32),
-            jax.ShapeDtypeStruct((ROWS, CHANS), BF16),
-        ],
-        [pltpu.VMEM((LENGTH + ROWS - STRIP, CHANS), BF16)],
-        4 << 30,
-    )
+def fwd_call(*operands):
+    out_shape = [
+        pltpu.VMEM((ROWS, CHANS), BF16),
+        pltpu.VMEM((ROWS, CHANS), F32),
+        pltpu.VMEM((ROWS, CHANS), BF16),
+    ]
+    scratch = [pltpu.VMEM((LENGTH + ROWS - STRIP, CHANS), BF16)]
+    return call(fwd_kernel, "fwd", out_shape, operands, scratch, 1, 4 << 30)
 
 
 def terms_kernel(core_ref, own_cot_ref, other_cot_ref, gated_ref, other_gated_ref, out_ref):
     dims = (((0,), (0,)), ((), ()))
-    total = lax.dot_general(gated_ref[...], own_cot_ref[...], dims, preferred_element_type=F32)
-    total += lax.dot_general(
-        other_gated_ref[...], other_cot_ref[...], dims, preferred_element_type=F32
-    )
-    out_ref[0] = total.astype(BF16)
-
-
-def terms_call(core, own_cot, other_cot, gated, other_gated):
-    column = pl.BlockSpec((ROWS, SHARE), lambda i, core_ref: (0, 2 * i + core_ref[0]))
-    signal = pl.BlockSpec((ROWS, CHANS), lambda i, core_ref: (0, 0))
-    return pl.pallas_call(
-        terms_kernel,
-        grid_spec=pltpu.PrefetchScalarGridSpec(
-            num_scalar_prefetch=1,
-            grid=(2,),
-            in_specs=[column, column, signal, signal],
-            out_specs=pl.BlockSpec((1, CHANS, SHARE), lambda i, core_ref: (i, 0, 0)),
-        ),
-        out_shape=jax.ShapeDtypeStruct((2, CHANS, SHARE + CHANS), BF16),
-        compiler_params=params(),
-        cost_estimate=pl.CostEstimate(
-            flops=2 * ROWS * FEATS * CHANS, bytes_accessed=6 << 20, transcendentals=0
-        ),
-        name="terms",
-    )(core, own_cot, other_cot, gated, other_gated)
+    for half in range(2):
+        start = pl.multiple_of((2 * half + core_ref[0]) * SHARE, SHARE)
+        own_cot = own_cot_ref[:, pl.ds(start, SHARE)]
+        other_cot = other_cot_ref[:, pl.ds(start, SHARE)]
+        total = lax.dot_general(gated_ref[...], own_cot, dims, preferred_element_type=F32)
+        total += lax.dot_general(other_gated_ref[...], other_cot, dims, preferred_element_type=F32)
+        out_ref[half, :, :SHARE] = total.astype(BF16)
+
+
+def terms_call(*operands):
+    out_shape = pltpu.VMEM((2, CHANS, SHARE + CHANS), BF16)
+    return call(terms_kernel, "terms", out_shape, operands, scalars=1, flops=1 << 30)
 
 
 def two_parts(total):
@@ -248,21 +221,14 @@
 
 def add_small_kernel(terms_ref, small_ref, other_small_ref, out_ref):
     parts = two_parts(small_ref[...] + other_small_ref[...]).astype(F32)
-    out_ref[...] = jnp.broadcast_to(parts.reshape(1, CHANS, CHANS).astype(BF16), out_ref.shape)
-
-
-def add_small_call(terms, small, other_small):
-    whole = pl.BlockSpec((SHARES, SEGMENT, CHANS), lambda i: (0, 0, 0))
-    return pl.pallas_call(
-        add_small_kernel,
-        grid=(1,),
-        in_specs=[pl.BlockSpec(memory_space=pl.ANY), whole, whole],
-        out_specs=pl.BlockSpec((2, CHANS, CHANS), lambda i: (0, 0, SHARE // CHANS)),
-        out_shape=jax.ShapeDtypeStruct(terms.shape, BF16),
-        input_output_aliases={0: 0},
-        compiler_params=params(),
-        name="add_small",
-    )(terms, small, other_small)
+    parts = parts.reshape(CHANS, CHANS).astype(BF16)
+    for half in range(2):
+        out_ref[half, :, SHARE:] = parts
+
+
+def add_small_call(*operands):
+    out_shape = pltpu.VMEM(operands[0].shape, BF16)
+    return call(add_small_kernel, "add_small", out_shape, operands, input_output_aliases={0: 0})
 
 
 def place(g, n):
@@ -273,7 +239,7 @@
 def bwd_kernel(
     core_ref, d0_ref, d1_ref, d2_ref, d3_ref, lags_ref, mixed_ref, key_ref, value_ref, pair_ref,
     cross_pair_ref, query_ref, tail_ref, inner_ref, d_gated_ref, taps_ref, skip_ref,
-    d_short_ref, small_ref,
+    d_short_ref, head_ref, small_ref,
     strips_ref, ahead_ref, outer_ref, stack_ref,
 ):
     for n, ref in enumerate((d0_ref, d1_ref, d2_ref, d3_ref)):
@@ -298,6 +264,7 @@
     d_vs = d_mixed * short_sum(taps_ref, 1, k_parts)
     for i, (grad, parts) in enumerate(((d_qs, q_parts), (d_ks, k_parts), (d_vs, v_parts))):
         d_short_ref[i] = grad
+        head_ref[i] = grad[:8]
         for j in range(3):
             small_ref[3 * i + j, 2:3, :] = jnp.sum(grad * parts[j], axis=0, keepdims=True)
     small_ref[9, 2:3, :] = jnp.sum(d_inner * mixed.astype(F32), axis=0, keepdims=True)
@@ -332,24 +299,19 @@
             small_ref[share, slot : slot + 1, :] = sums[:, n * CHANS : (n + 1) * CHANS]
 
 
-def bwd_call(core, *operands):
-    return with_core(
-        bwd_kernel,
-        "bwd",
-        core,
-        operands,
-        [
-            jax.ShapeDtypeStruct((3, ROWS, CHANS), F32),
-            jax.ShapeDtypeStruct((SHARES, SEGMENT, CHANS), F32),
-        ],
-        [
-            pltpu.VMEM((GROUPS * STRIP, LENGTH), BF16),
-            pltpu.VMEM((LENGTH + ROWS, CHANS), BF16),
-            pltpu.VMEM((GROUPS * SMALL, WIDE), F32),
-            pltpu.VMEM((GROUPS * SMALL, CHANS), BF16),
-        ],
-        1 << 10,
-    )
+def bwd_call(*operands):
+    out_shape = [
+        pltpu.VMEM((3, ROWS, CHANS), F32),
+        pltpu.VMEM((3, 8, CHANS), F32),
+        pltpu.VMEM((SHARES, SEGMENT, CHANS), F32),
+    ]
+    scratch = [
+        pltpu.VMEM((GROUPS * STRIP, LENGTH), BF16),
+        pltpu.VMEM((LENGTH + ROWS, CHANS), BF16),
+        pltpu.VMEM((GROUPS * SMALL, WIDE), F32),
+        pltpu.VMEM((GROUPS * SMALL, CHANS), BF16),
+    ]
+    return call(bwd_kernel, "bwd", out_shape, operands, scratch, 1)
 
 
 def input_grad_kernel(d_short_ref, next_ref, taps_ref, query_ref, key_ref, value_ref):
@@ -364,14 +326,9 @@
         out_ref[...] = short_sum(taps_ref, i, parts).astype(BF16)
 
 
-def input_grad_call(d_short, following, taps):
-    return pl.pallas_call(
-        input_grad_kernel,
-        out_shape=[jax.ShapeDtypeStruct((ROWS, CHANS), BF16)] * 3,
-        compiler_params=params(),
-        cost_estimate=pl.CostEstimate(flops=1 << 10, bytes_accessed=1 << 10, transcendentals=0),
-        name="input_grads",
-    )(d_short, following, taps)
+def input_grad_call(*operands):
+    out_shape = [jax.ShapeDtypeStruct((ROWS, CHANS), BF16)] * 3
+    return call(input_grad_kernel, "input_grads", out_shape, operands)
 
 
 def total_kernel(scale, terms_ref, out_ref):
@@ -384,59 +341,50 @@
 
 
 def total_call(terms, scale):
-    return pl.pallas_call(
-        lambda *refs: total_kernel(scale, *refs),
-        out_shape=jax.ShapeDtypeStruct((SHARES, *terms.shape[1:]), BF16),
-        compiler_params=params(),
-        cost_estimate=pl.CostEstimate(flops=1 << 20, bytes_accessed=3 << 20, transcendentals=0),
-        name="total",
-    )(terms)
-
-
-def spread_kernel(shares_ref, small_ref, weight_ref, taps_ref, filter_ref, skip_ref):
-    weight_ref[...] = shares_ref[...].astype(F32).T
-
-    @pl.when(pl.program_id(0) == 0)
-    def _():
-        for share in range(SHARES):
-            segment = small_ref[share * SEGMENT : (share + 1) * SEGMENT, :].astype(F32)
-            segment = segment + pltpu.roll(segment, SEGMENT // 2, 0)
-            for g in range(GROUPS):
-                for n in range(LENGTH // CHANS):
-                    if place(g, n)[0] == share:
-                        slot = place(g, n)[1]
-                        filter_ref[g : g + 1, n * CHANS : (n + 1) * CHANS] = segment[slot : slot + 1]
-            if share < 9:
-                taps_ref[share // 3, share % 3 : share % 3 + 1, :] = segment[2:3]
-            if share == 9:
-                skip_ref[...] = segment[2:3]
+    out_shape = pltpu.VMEM((SHARES, *terms.shape[1:]), BF16)
+    return call(lambda *refs: total_kernel(scale, *refs), "total", out_shape, (terms,))
+
+
+def spread_kernel(
+    shares_ref, weight_ref, taps_ref, filter_ref, skip_ref, turned_ref, sems
+):
+    tile = SHARE // SPREAD
+    copies = []
+    for n in range(SPREAD):
+        piece = slice(n * tile, (n + 1) * tile)
+        turned_ref[piece, :] = shares_ref[:, piece].astype(F32).T
+        copies.append(
+            pltpu.make_async_copy(turned_ref.at[piece, :], weight_ref.at[piece, :], sems.at[n])
+        )
+        copies[-1].start()
+    for share in range(SHARES):
+        segment = shares_ref[share * SEGMENT : (share + 1) * SEGMENT, SHARE:].astype(F32)
+        segment = segment + pltpu.roll(segment, SEGMENT // 2, 0)
+        for g in range(GROUPS):
+            for n in range(LENGTH // CHANS):
+                if place(g, n)[0] == share:
+                    slot = place(g, n)[1]
+                    filter_ref[g : g + 1, n * CHANS : (n + 1) * CHANS] = segment[slot : slot + 1]
+        if share < 9:
+            taps_ref[share // 3, share % 3 : share % 3 + 1, :] = segment[2:3]
+        if share == 9:
+            skip_ref[...] = segment[2:3]
+    for copy in copies:
+        copy.wait()
 
 
 def spread_call(shares):
+    out_shape = [
+        jax.ShapeDtypeStruct((SHARE, CHANS), F32),
+        jax.ShapeDtypeStruct((3, 3, CHANS), F32),
+        jax.ShapeDtypeStruct((GROUPS, LENGTH), F32),
+        jax.ShapeDtypeStruct((1, CHANS), F32),
+    ]
+    scratch = [pltpu.VMEM((SHARE, CHANS), F32), pltpu.SemaphoreType.DMA((SPREAD,))]
+    out_specs = [pl.BlockSpec(memory_space=pl.ANY)]
+    out_specs += [pl.BlockSpec(memory_space=pltpu.VMEM)] * 3
     shares = shares.reshape(CHANS, SHARE + CHANS)
-    tile = 512
-    return pl.pallas_call(
-        spread_kernel,
-        grid=(SHARE // tile,),
-        in_specs=[
-            pl.BlockSpec((CHANS, tile), lambda i: (0, i)),
-            pl.BlockSpec((CHANS, CHANS), lambda i: (0, SHARE // CHANS)),
-        ],
-        out_specs=[
-            pl.BlockSpec((tile, CHANS), lambda i: (i, 0)),
-            pl.BlockSpec((3, 3, CHANS), lambda i: (0, 0, 0)),
-            pl.BlockSpec((GROUPS, LENGTH), lambda i: (0, 0)),
-            pl.BlockSpec((1, CHANS), lambda i: (0, 0)),
-        ],
-        out_shape=[
-            jax.ShapeDtypeStruct((SHARE, CHANS), F32),
-            jax.ShapeDtypeStruct((3, 3, CHANS), F32),
-            jax.ShapeDtypeStruct((GROUPS, LENGTH), F32),
-            jax.ShapeDtypeStruct((1, CHANS), F32),
-        ],
-        compiler_params=params(),
-        name="spread",
-    )(shares, shares)
+    return call(spread_kernel, "spread", out_shape, (shares,), scratch, out_specs=out_specs)
 
 
 def sent(block, distance):
@@ -475,13 +423,13 @@
         core, strips, pair, cross, cross_pair, key, value, query, tail, taps, skip
     )
     other_gated = lax.ppermute(gated, "co", swap)
-    d_short, small = bwd_call(
+    d_short, head, small = bwd_call(
         core, *blocks, long_filter, mixed, key, value, pair, cross_pair, query, tail, inner,
         d_gated, taps, skip,
     )
-    other_gated, d_short, small = lax.optimization_barrier((other_gated, d_short, small))
+    other_gated, head, small = lax.optimization_barrier((other_gated, head, small))
     other_small = lax.ppermute(small, "co", swap)
-    following = sent(d_short[:, :8], -1)
+    following = sent(head, -1)
     terms = terms_call(core, cot, other_cot, gated, other_gated)
     terms, other_small, following = lax.optimization_barrier((terms, other_small, following))
     terms = add_small_call(terms, small, other_small)

time: 124 us -> 111 us (0.90)
  the two profiles are of different devices: /device:TPU:4 before, /device:TPU:1 now
where the time goes in v4:
time: 111 us; the launch traced here: 109 us
  blocking collectives  39.3 us (35%)
  starting transfers between devices  21.3 us (19%)
  Pallas kernels  20 us (18%)
  waiting for transfers between devices  19.7 us (18%)
  local copies, waits for them, and re-layouts  6.52 us (6%)
    all_to_all x1, blocking collectives, shards(): terms = lax.all_to_all(terms, CHIPS, 0, 0)  39.3 us
    pallas_call x9, Pallas kernels, call(): pl.pallas_call(kernel, out_shape=out_shape, scratch_shapes=list(scratch),...  20 us
    all_to_all x1, waiting for transfers between devices, shards(): shares = lax.all_to_all(total_call(terms, scale), DP, 0, 0)  14.3 us
    ppermute x5, starting transfers between devices, sent(): return lax.ppermute(block, CTX, route)  7.74 us
    unnamed x21, local copies, waits for them, and re-layouts  5.82 us
    ppermute x5, waiting for transfers between devices, sent(): return lax.ppermute(block, CTX, route)  5.31 us
    ppermute x1, starting transfers between devices, shards(): cross = lax.ppermute(own, 'xh', [(0, 1)])  4.75 us
    all_to_all x1, starting transfers between devices, shards(): shares = lax.all_to_all(total_call(terms, scale), DP, 0, 0)  4.43 us
  transfers between devices with their start and end apart: 12, of which 4 were waited for; matrix products, arithmetic and copies ran while one was open for 2% of the time, Pallas kernels for 15%

profile of v4, /device:TPU:1, one launch (start us, length us, event | category | flops | bytes accessed | tf_op | source)
XLA Modules:
  0.0 108.7 jit_solution(16702257318685921738)
XLA Ops:
  0.6 1.5 %collective-permute-start.7 = (bf16[256,8192]{1,0:T(8,128)(2,1)}, bf16[256,8192]{1,0:T(8,128)(2,1)}, u32[]{:S(2)}, u32[]{:S(2)}) collective-permute-start(bf16[256,8192]{1,0:T(8,128)(2,1)} %bitcast.17), channel_id=1, source_target_pairs={{0,32},{32,0},{1,33},{33,1},{2,34},{34,2},{3,35},{35,3},{4,36},{36... | collective-permute-start | bytes 12582920 | tf_op jit(solution)/shard_map/ppermute | solution.py:415
  2.1 1.0 pad_maximum_fusion
  3.1 4.7 %collective-permute-start = (bf16[256,512]{1,0:T(8,128)(2,1)S(1)}, bf16[256,512]{1,0:T(8,128)(2,1)S(1)}, u32[]{:S(2)}, u32[]{:S(2)}) collective-permute-start(bf16[256,512]{1,0:T(8,128)(2,1)S(1)} %pad_maximum_fusion), channel_id=1, source_target_pairs={{0,64},{1,65},{2,66},{3,67},{4,68},{5,69},{6,70},{7,71},{8,72},{9,... | collective-permute-start | bytes 786440 | tf_op jit(solution)/shard_map/ppermute | solution.py:413
  7.9 0.4 collective-permute-start.2
  8.3 0.7 slice_bitcast_fusion
  9.0 1.9 %collective-permute-start.1 = (bf16[16,256]{1,0:T(8,128)(2,1)S(1)}, bf16[16,256]{1,0:T(8,128)(2,1)S(1)}, u32[]{:S(2)}, u32[]{:S(2)}) collective-permute-start(bf16[16,256]{1,0:T(8,128)(2,1)S(1)} %slice_bitcast_fusion), channel_id=1, source_target_pairs={{0,32},{32,64},{64,96},{1,33},{33,65},{65,97},{2,34},{34,66},{66,9... | collective-permute-start | bytes 24584 | tf_op jit(solution)/shard_map/ppermute | solution.py:393
  10.9 0.0 copy-start
  10.9 2.2 %copy-done = bf16[1,256,8192]{2,1,0:T(8,128)(2,1)S(1)} copy-done((bf16[1,256,8192]{2,1,0:T(8,128)(2,1)S(1)}, bf16[1,256,8192]{2,1,0:T(8,128)(2,1)}, u32[]{:S(2)}) %copy-start) | copy-done | bytes 4194328
  13.1 0.0 copy-start.2
  13.1 2.2 %copy-done.2 = bf16[8192,256]{1,0:T(8,128)(2,1)S(1)} copy-done((bf16[8192,256]{1,0:T(8,128)(2,1)S(1)}, bf16[8192,256]{1,0:T(8,128)(2,1)}, u32[]{:S(2)}) %copy-start.2) | copy-done | bytes 4194328
  15.2 0.0 copy-start.6
  15.3 0.8 copy-done.6
  16.0 0.0 copy-start.3
  16.0 0.0 copy-start.8
  16.0 0.0 copy-start.4
  16.0 0.0 copy-start.5
  16.0 0.0 copy-start.9
  16.0 4.1 %pre.1 = (bf16[256,256]{1,0:T(8,128)(2,1)S(1)}, bf16[512,1024]{1,0:T(8,128)(2,1)S(1)}) custom-call(bf16[256,8192]{1,0:T(8,128)(2,1)S(1)} %bitcast.18, bf16[8192,256]{1,0:T(8,128)(2,1)S(1)} %copy-done.2, bf16[16,1024]{1,0:T(8,128)(2,1)S(1)} %copy-done.6), custom_call_target="tpu_custom_call" | custom-call | flops 1073741824 | bytes 1024 | tf_op jit(solution)/shard_map/pre/pallas_call | solution.py:46
  20.2 0.0 collective-permute-done.1.tail_ref
  20.2 0.0 collective-permute-done.cross_ref
  20.2 0.6 collective-permute-start.3
  20.7 0.0 copy-done.3
  20.8 0.0 copy-done.8
  20.8 0.1 d_inner.1.d0_ref
  20.9 1.9 %collective-permute-start.4 = (bf16[256,256]{1,0:T(8,128)(2,1)S(1)}, bf16[256,256]{1,0:T(8,128)(2,1)S(1)}, u32[]{:S(2)}, u32[]{:S(2)}) collective-permute-start(bf16[256,256]{1,0:T(8,128)(2,1)S(1)} %d_inner.1.d0_ref), channel_id=1, source_target_pairs={{32,0},{64,32},{96,64},{33,1},{65,33},{97,65},{34,2},{66,34},{98,6... | collective-permute-start | bytes 393224 | tf_op jit(solution)/shard_map/ppermute | solution.py:393
  22.8 1.3 %collective-permute-start.5 = (bf16[256,256]{1,0:T(8,128)(2,1)S(1)}, bf16[256,256]{1,0:T(8,128)(2,1)S(1)}, u32[]{:S(2)}, u32[]{:S(2)}) collective-permute-start(bf16[256,256]{1,0:T(8,128)(2,1)S(1)} %d_inner.1.d0_ref), channel_id=1, source_target_pairs={{64,0},{96,32},{65,1},{97,33},{66,2},{98,34},{67,3},{99,35},{68,4}... | collective-permute-start | bytes 393224 | tf_op jit(solution)/shard_map/ppermute | solution.py:393
  24.1 0.0 collective-permute-done.2.pair_ref
  24.1 0.7 collective-permute-start.6
  24.8 0.0 collective-permute-done.3.cross_pair_ref
  24.8 0.0 copy-done.4
  24.8 0.0 copy-done.5
  24.8 0.0 copy-done.9
  24.9 0.0 copy-start.7
  24.9 0.0 copy-start.1
  24.9 2.7 %fwd.1 = (bf16[256,256]{1,0:T(8,128)(2,1)S(1)}, f32[256,256]{1,0:T(8,128)S(1)}, bf16[256,256]{1,0:T(8,128)(2,1)S(1)}) custom-call(s32[1]{0:T(128)} %bitcast.core_ref, bf16[512,1024]{1,0:T(8,128)(2,1)S(1)} %get-tuple-element.35.strips_ref, bf16[256,512]{1,0:T(8,128)(2,1)S(1)} %collective-permute-done.2.pair_ref, ...), custom_call_target="tpu_custom_call" | custom-call | flops 4294967296 | bytes 1024 | tf_op jit(solution)/shard_map/fwd/pallas_call | solution.py:46
  27.6 0.1 collective-permute-start.8
  27.6 1.0 collective-permute-done.4.d1_ref
  28.7 3.1 %collective-permute-done.5.d2_ref = bf16[256,256]{1,0:T(8,128)(2,1)S(1)} collective-permute-done((bf16[256,256]{1,0:T(8,128)(2,1)S(1)}, bf16[256,256]{1,0:T(8,128)(2,1)S(1)}, u32[]{:S(2)}, u32[]{:S(2)}) %collective-permute-start.5) | collective-permute-done | bytes 131104 | tf_op jit(solution)/shard_map/ppermute | solution.py:393
  31.7 0.0 collective-permute-done.6.d3_ref
  31.7 0.0 copy-done.7
  31.7 5.2 %bwd.1 = (f32[3,256,256]{2,1,0:T(8,128)S(1)}, f32[3,8,256]{2,1,0:T(8,128)S(1)}, f32[32,8,256]{2,1,0:T(8,128)S(1)}) custom-call(s32[1]{0:T(128)} %bitcast.core_ref, bf16[256,256]{1,0:T(8,128)(2,1)S(1)} %d_inner.1.d0_ref, bf16[256,256]{1,0:T(8,128)(2,1)S(1)} %collective-permute-done.4.d1_ref, bf16[256,256]{1,0:T(8,128)(2,1)S(1)} %collective-permute-done.5.d2_ref, ...), custom_call_target="tpu_custom_call" | custom-call | flops 1024 | bytes 1024 | tf_op jit(solution)/shard_map/bwd/pallas_call | solution.py:46
  36.9 0.0 collective-permute-done.8.other_gated_ref
  36.9 1.9 %collective-permute-start.9 = (f32[32,8,256]{2,1,0:T(8,128)S(1)}, f32[32,8,256]{2,1,0:T(8,128)S(1)}, u32[]{:S(2)}, u32[]{:S(2)}) collective-permute-start(f32[32,8,256]{2,1,0:T(8,128)S(1)} %get-tuple-element.46.small_ref), channel_id=1, source_target_pairs={{0,32},{32,0},{1,33},{33,1},{2,34},{34,2},{3,35},{35,3},{4,36},{36... | collective-permute-start | bytes 786440 | tf_op jit(solution)/shard_map/ppermute | solution.py:431
  38.8 1.9 %collective-permute-start.10 = (f32[3,8,256]{2,1,0:T(8,128)S(1)}, f32[3,8,256]{2,1,0:T(8,128)S(1)}, u32[]{:S(2)}, u32[]{:S(2)}) collective-permute-start(f32[3,8,256]{2,1,0:T(8,128)S(1)} %get-tuple-element.47), channel_id=1, source_target_pairs={{32,0},{64,32},{96,64},{33,1},{65,33},{97,65},{34,2},{66,34},{98,6... | collective-permute-start | bytes 73736 | tf_op jit(solution)/shard_map/ppermute | solution.py:393
  40.8 0.0 collective-permute-done.7.other_cot_ref
  40.8 0.0 copy-done.1
  40.8 3.5 %terms.1.terms_ref = bf16[2,256,2304]{2,1,0:T(8,128)(2,1)S(1)} custom-call(s32[1]{0:T(128)} %bitcast.core_ref, bf16[256,8192]{1,0:T(8,128)(2,1)S(1)} %bitcast.19, bf16[256,8192]{1,0:T(8,128)(2,1)} %collective-permute-done.7.other_cot_ref, bf16[256,256]{1,0:T(8,128)(2,1)S(1)} %get-tuple-element.38.gated_ref, ...), custom_call_target="tpu_custom_call" | custom-call | flops 1073741824 | bytes 1024 | tf_op jit(solution)/shard_map/terms/pallas_call | solution.py:46
  44.2 1.2 %collective-permute-done.10.next_ref = f32[3,8,256]{2,1,0:T(8,128)S(1)} collective-permute-done((f32[3,8,256]{2,1,0:T(8,128)S(1)}, f32[3,8,256]{2,1,0:T(8,128)S(1)}, u32[]{:S(2)}, u32[]{:S(2)}) %collective-permute-start.10) | collective-permute-done | bytes 24608 | tf_op jit(solution)/shard_map/ppermute | solution.py:393
  45.5 0.0 collective-permute-done.9.other_small_ref
  45.5 0.1 add_small.1
  45.5 39.3 %all_to_all.10.refs_0_ = bf16[64,8,2304]{2,1,0:T(8,128)(2,1)S(1)} all-to-all(bf16[64,8,2304]{2,1,0:T(8,128)(2,1)S(1)} %bitcast.16), channel_id=1, replica_groups=mesh['xh'=2,'co'=2,'y'=4,'xl'=2,'z'=4] {'xh','y','xl','z'}, dimensions={0} | all-to-all | bytes 4718592 | tf_op jit(solution)/shard_map/all_to_all | solution.py:437
  84.8 1.4 %total.1 = bf16[32,8,2304]{2,1,0:T(8,128)(2,1)} custom-call(bf16[64,8,2304]{2,1,0:T(8,128)(2,1)S(1)} %all_to_all.10.refs_0_), custom_call_target="tpu_custom_call" | custom-call | flops 1024 | bytes 1024 | tf_op jit(solution)/shard_map/total/pallas_call | solution.py:46
  86.2 4.4 %all-to-all-start.1 = ((bf16[32,8,2304]{2,1,0:T(8,128)(2,1)}), bf16[32,8,2304]{2,1,0:T(8,128)(2,1)S(1)}, u32[]{:S(2)}, u32[]{:S(2)}) async-start(bf16[32,8,2304]{2,1,0:T(8,128)(2,1)} %total.1), calls=%async_computation.1 | async-start | bytes 2359296 | tf_op jit(solution)/shard_map/all_to_all | solution.py:440
  90.7 0.7 copy.18
  91.3 0.9 input_grads.1
  92.2 14.3 %all-to-all-done.1 = bf16[32,8,2304]{2,1,0:T(8,128)(2,1)S(1)} async-done(((bf16[32,8,2304]{2,1,0:T(8,128)(2,1)}), bf16[32,8,2304]{2,1,0:T(8,128)(2,1)S(1)}, u32[]{:S(2)}, u32[]{:S(2)}) %all-to-all-start.1) | async-done | bytes 1179680 | tf_op jit(solution)/shard_map/all_to_all | solution.py:440
  106.6 2.1 %spread.1 = (f32[2048,256]{1,0:T(8,128)}, f32[3,3,256]{2,1,0:T(4,128)}, f32[16,1024]{1,0:T(8,128)}, f32[1,256]{1,0:T(1,128)}) custom-call(bf16[256,2304]{1,0:T(8,128)(2,1)S(1)} %bitcast.20), custom_call_target="tpu_custom_call" | custom-call | flops 1024 | bytes 1024 | tf_op jit(solution)/shard_map/spread/pallas_call | solution.py:46
Async XLA Ops:
  0.6 40.1 %collective-permute-start.7 = (bf16[256,8192]{1,0:T(8,128)(2,1)}, bf16[256,8192]{1,0:T(8,128)(2,1)}, u32[]{:S(2)}, u32[]{:S(2)}) collective-permute-start(bf16[256,8192]{1,0:T(8,128)(2,1)} %bitcast.17), channel_id=1, source_target_pairs={{0,32},{32,0},{1,33},{33,1},{2,34},{34,2},{3,35},{35,3},{4,36},{36... | collective-permute-start | bytes 12582920 | tf_op jit(solution)/shard_map/ppermute | solution.py:415
  3.1 17.0 %collective-permute-start = (bf16[256,512]{1,0:T(8,128)(2,1)S(1)}, bf16[256,512]{1,0:T(8,128)(2,1)S(1)}, u32[]{:S(2)}, u32[]{:S(2)}) collective-permute-start(bf16[256,512]{1,0:T(8,128)(2,1)S(1)} %pad_maximum_fusion), channel_id=1, source_target_pairs={{0,64},{1,65},{2,66},{3,67},{4,68},{5,69},{6,70},{7,71},{8,72},{9,... | collective-permute-start | bytes 786440 | tf_op jit(solution)/shard_map/ppermute | solution.py:413
  7.9 16.2 %collective-permute-start.2 = (bf16[256,512]{1,0:T(8,128)(2,1)S(1)}, bf16[256,512]{1,0:T(8,128)(2,1)S(1)}, u32[]{:S(2)}, u32[]{:S(2)}) collective-permute-start(bf16[256,512]{1,0:T(8,128)(2,1)S(1)} %pad_maximum_fusion), channel_id=1, source_target_pairs={{0,32},{32,0},{1,33},{33,1},{2,34},{34,2},{3,35},{35,3},{4,36},{36... | collective-permute-start | bytes 786440 | tf_op jit(solution)/shard_map/ppermute | solution.py:414
  9.0 11.2 %collective-permute-start.1 = (bf16[16,256]{1,0:T(8,128)(2,1)S(1)}, bf16[16,256]{1,0:T(8,128)(2,1)S(1)}, u32[]{:S(2)}, u32[]{:S(2)}) collective-permute-start(bf16[16,256]{1,0:T(8,128)(2,1)S(1)} %slice_bitcast_fusion), channel_id=1, source_target_pairs={{0,32},{32,64},{64,96},{1,33},{33,65},{65,97},{2,34},{34,66},{66,9... | collective-permute-start | bytes 24584 | tf_op jit(solution)/shard_map/ppermute | solution.py:393
  10.9 2.2 %copy-start = (bf16[1,256,8192]{2,1,0:T(8,128)(2,1)S(1)}, bf16[1,256,8192]{2,1,0:T(8,128)(2,1)}, u32[]{:S(2)}) copy-start(bf16[1,256,8192]{2,1,0:T(8,128)(2,1)} %param.15) | copy-start | bytes 12582916
  13.1 2.2 %copy-start.2 = (bf16[8192,256]{1,0:T(8,128)(2,1)S(1)}, bf16[8192,256]{1,0:T(8,128)(2,1)}, u32[]{:S(2)}) copy-start(bf16[8192,256]{1,0:T(8,128)(2,1)} %weight_ref.1) | copy-start | bytes 12582916
  15.2 0.8 copy-start.6
  16.0 4.7 %copy-start.3 = (bf16[1,256,256]{2,1,0:T(8,128)(2,1)S(1)}, bf16[1,256,256]{2,1,0:T(8,128)(2,1)}, u32[]{:S(2)}) copy-start(bf16[1,256,256]{2,1,0:T(8,128)(2,1)} %param.8) | copy-start | bytes 393220
  16.0 4.7 %copy-start.8 = (f32[3,3,256]{2,1,0:T(4,128)S(1)}, f32[3,3,256]{2,1,0:T(4,128)}, u32[]{:S(2)}) copy-start(f32[3,3,256]{2,1,0:T(4,128)} %taps_ref.7) | copy-start | bytes 27652
  16.0 8.8 %copy-start.4 = (bf16[1,256,256]{2,1,0:T(8,128)(2,1)S(1)}, bf16[1,256,256]{2,1,0:T(8,128)(2,1)}, u32[]{:S(2)}) copy-start(bf16[1,256,256]{2,1,0:T(8,128)(2,1)} %param.10) | copy-start | bytes 393220
  16.0 8.8 %copy-start.5 = (bf16[1,256,256]{2,1,0:T(8,128)(2,1)S(1)}, bf16[1,256,256]{2,1,0:T(8,128)(2,1)}, u32[]{:S(2)}) copy-start(bf16[1,256,256]{2,1,0:T(8,128)(2,1)} %param.9) | copy-start | bytes 393220
  16.0 8.8 %copy-start.9 = (f32[256]{0:T(256)S(1)}, f32[256]{0:T(256)}, u32[]{:S(2)}) copy-start(f32[256]{0:T(256)} %param.13) | copy-start | bytes 3076
  20.2 4.6 %collective-permute-start.3 = (bf16[256,512]{1,0:T(8,128)(2,1)S(1)}, bf16[256,512]{1,0:T(8,128)(2,1)S(1)}, u32[]{:S(2)}, u32[]{:S(2)}) collective-permute-start(bf16[256,512]{1,0:T(8,128)(2,1)S(1)} %collective-permute-done.cross_ref), channel_id=1, source_target_pairs={{0,32},{32,0},{1,33},{33,1},{2,34},{34,2},{3,35},{35,3},{4,36},{36... | collective-permute-start | bytes 786440 | tf_op jit(solution)/shard_map/ppermute | solution.py:419
  20.9 7.8 %collective-permute-start.4 = (bf16[256,256]{1,0:T(8,128)(2,1)S(1)}, bf16[256,256]{1,0:T(8,128)(2,1)S(1)}, u32[]{:S(2)}, u32[]{:S(2)}) collective-permute-start(bf16[256,256]{1,0:T(8,128)(2,1)S(1)} %d_inner.1.d0_ref), channel_id=1, source_target_pairs={{32,0},{64,32},{96,64},{33,1},{65,33},{97,65},{34,2},{66,34},{98,6... | collective-permute-start | bytes 393224 | tf_op jit(solution)/shard_map/ppermute | solution.py:393
  22.8 8.9 %collective-permute-start.5 = (bf16[256,256]{1,0:T(8,128)(2,1)S(1)}, bf16[256,256]{1,0:T(8,128)(2,1)S(1)}, u32[]{:S(2)}, u32[]{:S(2)}) collective-permute-start(bf16[256,256]{1,0:T(8,128)(2,1)S(1)} %d_inner.1.d0_ref), channel_id=1, source_target_pairs={{64,0},{96,32},{65,1},{97,33},{66,2},{98,34},{67,3},{99,35},{68,4}... | collective-permute-start | bytes 393224 | tf_op jit(solution)/shard_map/ppermute | solution.py:393
  24.1 7.6 %collective-permute-start.6 = (bf16[256,256]{1,0:T(8,128)(2,1)S(1)}, bf16[256,256]{1,0:T(8,128)(2,1)S(1)}, u32[]{:S(2)}, u32[]{:S(2)}) collective-permute-start(bf16[256,256]{1,0:T(8,128)(2,1)S(1)} %d_inner.1.d0_ref), channel_id=1, source_target_pairs={{96,0},{97,1},{98,2},{99,3},{100,4},{101,5},{102,6},{103,7},{104,8... | collective-permute-start | bytes 393224 | tf_op jit(solution)/shard_map/ppermute | solution.py:393
  24.9 6.9 %copy-start.7 = (bf16[16,1024]{1,0:T(8,128)(2,1)S(1)}, bf16[16,1024]{1,0:T(8,128)(2,1)}, u32[]{:S(2)}) copy-start(bf16[16,1024]{1,0:T(8,128)(2,1)} %lags_ref.1) | copy-start | bytes 98308
  24.9 15.9 %copy-start.1 = (bf16[1,256,8192]{2,1,0:T(8,128)(2,1)S(1)}, bf16[1,256,8192]{2,1,0:T(8,128)(2,1)}, u32[]{:S(2)}) copy-start(bf16[1,256,8192]{2,1,0:T(8,128)(2,1)} %param.15) | copy-start | bytes 12582916
  27.6 9.4 %collective-permute-start.8 = (bf16[256,256]{1,0:T(8,128)(2,1)S(1)}, bf16[256,256]{1,0:T(8,128)(2,1)S(1)}, u32[]{:S(2)}, u32[]{:S(2)}) collective-permute-start(bf16[256,256]{1,0:T(8,128)(2,1)S(1)} %get-tuple-element.38.gated_ref), channel_id=1, source_target_pairs={{0,32},{32,0},{1,33},{33,1},{2,34},{34,2},{3,35},{35,3},{4,36},{36... | collective-permute-start | bytes 393224 | tf_op jit(solution)/shard_map/ppermute | solution.py:425
  36.9 8.5 %collective-permute-start.9 = (f32[32,8,256]{2,1,0:T(8,128)S(1)}, f32[32,8,256]{2,1,0:T(8,128)S(1)}, u32[]{:S(2)}, u32[]{:S(2)}) collective-permute-start(f32[32,8,256]{2,1,0:T(8,128)S(1)} %get-tuple-element.46.small_ref), channel_id=1, source_target_pairs={{0,32},{32,0},{1,33},{33,1},{2,34},{34,2},{3,35},{35,3},{4,36},{36... | collective-permute-start | bytes 786440 | tf_op jit(solution)/shard_map/ppermute | solution.py:431
  38.8 6.6 %collective-permute-start.10 = (f32[3,8,256]{2,1,0:T(8,128)S(1)}, f32[3,8,256]{2,1,0:T(8,128)S(1)}, u32[]{:S(2)}, u32[]{:S(2)}) collective-permute-start(f32[3,8,256]{2,1,0:T(8,128)S(1)} %get-tuple-element.47), channel_id=1, source_target_pairs={{32,0},{64,32},{96,64},{33,1},{65,33},{97,65},{34,2},{66,34},{98,6... | collective-permute-start | bytes 73736 | tf_op jit(solution)/shard_map/ppermute | solution.py:393
  86.2 20.3 %all-to-all-start.1 = ((bf16[32,8,2304]{2,1,0:T(8,128)(2,1)}), bf16[32,8,2304]{2,1,0:T(8,128)(2,1)S(1)}, u32[]{:S(2)}, u32[]{:S(2)}) async-start(bf16[32,8,2304]{2,1,0:T(8,128)(2,1)} %total.1), calls=%async_computation.1 | async-start | bytes 2359296 | tf_op jit(solution)/shard_map/all_to_all | solution.py:440

commit v5 on v4

--- a/solution.py
+++ b/solution.py
@@ -40,7 +40,7 @@
     defaults = {"in_specs": in_specs, "out_specs": jax.tree.map(lambda _: spec, out_shape)}
     more = {**defaults, **more}
     placed = [
-        pltpu.with_memory_space_constraint(x, pltpu.VMEM) if s.memory_space == pltpu.VMEM else x
+        x if s.memory_space == pltpu.SMEM else pltpu.with_memory_space_constraint(x, s.memory_space)
         for x, s in zip(operands, more["in_specs"])
     ]
     return pl.pallas_call(
@@ -145,7 +145,7 @@
         pltpu.VMEM((PIECES, tile, CHANS), BF16),
         pltpu.SemaphoreType.DMA((2, PIECES)),
     ]
-    far = pl.BlockSpec(memory_space=pl.ANY)
+    far = pl.BlockSpec(memory_space=pltpu.HBM)
     in_specs = [far, far, pl.BlockSpec(memory_space=pltpu.VMEM)]
     return call(
         pre_kernel, "pre", out_shape, (cot, weight, lags), scratch, in_specs=in_specs, flops=1 << 30

time: 111 us -> 107 us (0.964)
  local copies, waits for them, and re-layouts: 6.52 us -> 2.14 us
    unnamed x21 -> x17, local copies, waits for them, and re-layouts: 5.82 us -> 1.44 us
  transfers between devices with their start and end apart: 12 -> 12, of which waited for: 4 -> 4; matrix products, arithmetic and copies ran while one was open for 2% -> 2% of each run, Pallas kernels for 15% -> 16%
where the time goes in v5:
time: 107 us; the launch traced here: 105 us
  blocking collectives  39.3 us (37%)
  starting transfers between devices  21.5 us (20%)
  Pallas kernels  20.7 us (19%)
  waiting for transfers between devices  19.7 us (18%)
  local copies, waits for them, and re-layouts  2.14 us (2%)
    all_to_all x1, blocking collectives, shards(): terms = lax.all_to_all(terms, CHIPS, 0, 0)  39.3 us
    pallas_call x9, Pallas kernels, call(): pl.pallas_call(kernel, out_shape=out_shape, scratch_shapes=list(scratch),...  20.7 us
    all_to_all x1, waiting for transfers between devices, shards(): shares = lax.all_to_all(total_call(terms, scale), DP, 0, 0)  14.3 us
    ppermute x5, starting transfers between devices, sent(): return lax.ppermute(block, CTX, route)  7.87 us
    ppermute x5, waiting for transfers between devices, sent(): return lax.ppermute(block, CTX, route)  5.32 us
    ppermute x1, starting transfers between devices, shards(): cross = lax.ppermute(own, 'xh', [(0, 1)])  4.75 us
    all_to_all x1, starting transfers between devices, shards(): shares = lax.all_to_all(total_call(terms, scale), DP, 0, 0)  4.41 us
  transfers between devices with their start and end apart: 12, of which 4 were waited for; matrix products, arithmetic and copies ran while one was open for 2% of the time, Pallas kernels for 16%

profile of v5, /device:TPU:1, one launch (start us, length us, event | category | flops | bytes accessed | tf_op | source)
XLA Modules:
  0.0 105.1 jit_solution(6142031195494354384)
XLA Ops:
  0.6 1.5 %collective-permute-start.7 = (bf16[256,8192]{1,0:T(8,128)(2,1)}, bf16[256,8192]{1,0:T(8,128)(2,1)}, u32[]{:S(2)}, u32[]{:S(2)}) collective-permute-start(bf16[256,8192]{1,0:T(8,128)(2,1)} %bitcast.17), channel_id=1, source_target_pairs={{0,32},{32,0},{1,33},{33,1},{2,34},{34,2},{3,35},{35,3},{4,36},{36... | collective-permute-start | bytes 12582920 | tf_op jit(solution)/shard_map/ppermute | solution.py:415
  2.1 1.0 pad_maximum_fusion
  3.1 4.7 %collective-permute-start = (bf16[256,512]{1,0:T(8,128)(2,1)S(1)}, bf16[256,512]{1,0:T(8,128)(2,1)S(1)}, u32[]{:S(2)}, u32[]{:S(2)}) collective-permute-start(bf16[256,512]{1,0:T(8,128)(2,1)S(1)} %pad_maximum_fusion), channel_id=1, source_target_pairs={{0,64},{1,65},{2,66},{3,67},{4,68},{5,69},{6,70},{7,71},{8,72},{9,... | collective-permute-start | bytes 786440 | tf_op jit(solution)/shard_map/ppermute | solution.py:413
  7.9 0.4 collective-permute-start.2
  8.3 0.7 slice_bitcast_fusion
  9.0 0.0 copy-start.1
  9.0 0.0 copy-start.2
  9.0 0.0 copy-start.3
  9.0 2.0 %collective-permute-start.1 = (bf16[16,256]{1,0:T(8,128)(2,1)S(1)}, bf16[16,256]{1,0:T(8,128)(2,1)S(1)}, u32[]{:S(2)}, u32[]{:S(2)}) collective-permute-start(bf16[16,256]{1,0:T(8,128)(2,1)S(1)} %slice_bitcast_fusion), channel_id=1, source_target_pairs={{0,32},{32,64},{64,96},{1,33},{33,65},{65,97},{2,34},{34,66},{66,9... | collective-permute-start | bytes 24584 | tf_op jit(solution)/shard_map/ppermute | solution.py:393
  11.0 0.0 copy-start.4
  11.0 0.7 copy-done.4
  11.8 0.0 copy-start.6
  11.8 0.0 copy-start.7
  11.8 4.8 %pre.1 = (bf16[256,256]{1,0:T(8,128)(2,1)S(1)}, bf16[512,1024]{1,0:T(8,128)(2,1)S(1)}) custom-call(bf16[256,8192]{1,0:T(8,128)(2,1)} %bitcast.18, bf16[8192,256]{1,0:T(8,128)(2,1)} %weight_ref.1, bf16[16,1024]{1,0:T(8,128)(2,1)S(1)} %copy-done.4), custom_call_target="tpu_custom_call" | custom-call | flops 1073741824 | bytes 1024 | tf_op jit(solution)/shard_map/pre/pallas_call | solution.py:46
  16.6 0.0 collective-permute-done.1.tail_ref
  16.6 0.0 collective-permute-done.cross_ref
  16.6 0.6 collective-permute-start.3
  17.2 0.0 copy-done.1
  17.2 0.0 copy-done.6
  17.2 0.1 d_inner.1.d0_ref
  17.3 1.9 %collective-permute-start.4 = (bf16[256,256]{1,0:T(8,128)(2,1)S(1)}, bf16[256,256]{1,0:T(8,128)(2,1)S(1)}, u32[]{:S(2)}, u32[]{:S(2)}) collective-permute-start(bf16[256,256]{1,0:T(8,128)(2,1)S(1)} %d_inner.1.d0_ref), channel_id=1, source_target_pairs={{32,0},{64,32},{96,64},{33,1},{65,33},{97,65},{34,2},{66,34},{98,6... | collective-permute-start | bytes 393224 | tf_op jit(solution)/shard_map/ppermute | solution.py:393
  19.3 1.3 %collective-permute-start.5 = (bf16[256,256]{1,0:T(8,128)(2,1)S(1)}, bf16[256,256]{1,0:T(8,128)(2,1)S(1)}, u32[]{:S(2)}, u32[]{:S(2)}) collective-permute-start(bf16[256,256]{1,0:T(8,128)(2,1)S(1)} %d_inner.1.d0_ref), channel_id=1, source_target_pairs={{64,0},{96,32},{65,1},{97,33},{66,2},{98,34},{67,3},{99,35},{68,4}... | collective-permute-start | bytes 393224 | tf_op jit(solution)/shard_map/ppermute | solution.py:393
  20.6 0.0 collective-permute-done.2.pair_ref
  20.6 0.7 collective-permute-start.6
  21.3 0.0 collective-permute-done.3.cross_pair_ref
  21.3 0.0 copy-done.2
  21.3 0.0 copy-done.3
  21.3 0.0 copy-done.7
  21.3 0.0 copy-start.5
  21.3 0.0 copy-start
  21.3 2.7 %fwd.1 = (bf16[256,256]{1,0:T(8,128)(2,1)S(1)}, f32[256,256]{1,0:T(8,128)S(1)}, bf16[256,256]{1,0:T(8,128)(2,1)S(1)}) custom-call(s32[1]{0:T(128)} %bitcast.core_ref, bf16[512,1024]{1,0:T(8,128)(2,1)S(1)} %get-tuple-element.35.strips_ref, bf16[256,512]{1,0:T(8,128)(2,1)S(1)} %collective-permute-done.2.pair_ref, ...), custom_call_target="tpu_custom_call" | custom-call | flops 4294967296 | bytes 1024 | tf_op jit(solution)/shard_map/fwd/pallas_call | solution.py:46
  24.0 0.1 collective-permute-start.8
  24.1 1.0 collective-permute-done.4.d1_ref
  25.1 3.1 %collective-permute-done.5.d2_ref = bf16[256,256]{1,0:T(8,128)(2,1)S(1)} collective-permute-done((bf16[256,256]{1,0:T(8,128)(2,1)S(1)}, bf16[256,256]{1,0:T(8,128)(2,1)S(1)}, u32[]{:S(2)}, u32[]{:S(2)}) %collective-permute-start.5) | collective-permute-done | bytes 131104 | tf_op jit(solution)/shard_map/ppermute | solution.py:393
  28.2 0.0 collective-permute-done.6.d3_ref
  28.2 0.0 copy-done.5
  28.2 5.2 %bwd.1 = (f32[3,256,256]{2,1,0:T(8,128)S(1)}, f32[3,8,256]{2,1,0:T(8,128)S(1)}, f32[32,8,256]{2,1,0:T(8,128)S(1)}) custom-call(s32[1]{0:T(128)} %bitcast.core_ref, bf16[256,256]{1,0:T(8,128)(2,1)S(1)} %d_inner.1.d0_ref, bf16[256,256]{1,0:T(8,128)(2,1)S(1)} %collective-permute-done.4.d1_ref, bf16[256,256]{1,0:T(8,128)(2,1)S(1)} %collective-permute-done.5.d2_ref, ...), custom_call_target="tpu_custom_call" | custom-call | flops 1024 | bytes 1024 | tf_op jit(solution)/shard_map/bwd/pallas_call | solution.py:46
  33.4 0.0 collective-permute-done.8.other_gated_ref
  33.4 1.9 %collective-permute-start.9 = (f32[32,8,256]{2,1,0:T(8,128)S(1)}, f32[32,8,256]{2,1,0:T(8,128)S(1)}, u32[]{:S(2)}, u32[]{:S(2)}) collective-permute-start(f32[32,8,256]{2,1,0:T(8,128)S(1)} %get-tuple-element.46.small_ref), channel_id=1, source_target_pairs={{0,32},{32,0},{1,33},{33,1},{2,34},{34,2},{3,35},{35,3},{4,36},{36... | collective-permute-start | bytes 786440 | tf_op jit(solution)/shard_map/ppermute | solution.py:431
  35.3 1.9 %collective-permute-start.10 = (f32[3,8,256]{2,1,0:T(8,128)S(1)}, f32[3,8,256]{2,1,0:T(8,128)S(1)}, u32[]{:S(2)}, u32[]{:S(2)}) collective-permute-start(f32[3,8,256]{2,1,0:T(8,128)S(1)} %get-tuple-element.47), channel_id=1, source_target_pairs={{32,0},{64,32},{96,64},{33,1},{65,33},{97,65},{34,2},{66,34},{98,6... | collective-permute-start | bytes 73736 | tf_op jit(solution)/shard_map/ppermute | solution.py:393
  37.2 0.0 collective-permute-done.7.other_cot_ref
  37.2 0.0 copy-done
  37.2 3.5 %terms.1.terms_ref = bf16[2,256,2304]{2,1,0:T(8,128)(2,1)S(1)} custom-call(s32[1]{0:T(128)} %bitcast.core_ref, bf16[256,8192]{1,0:T(8,128)(2,1)S(1)} %bitcast.19, bf16[256,8192]{1,0:T(8,128)(2,1)} %collective-permute-done.7.other_cot_ref, bf16[256,256]{1,0:T(8,128)(2,1)S(1)} %get-tuple-element.38.gated_ref, ...), custom_call_target="tpu_custom_call" | custom-call | flops 1073741824 | bytes 1024 | tf_op jit(solution)/shard_map/terms/pallas_call | solution.py:46
  40.7 1.2 %collective-permute-done.10.next_ref = f32[3,8,256]{2,1,0:T(8,128)S(1)} collective-permute-done((f32[3,8,256]{2,1,0:T(8,128)S(1)}, f32[3,8,256]{2,1,0:T(8,128)S(1)}, u32[]{:S(2)}, u32[]{:S(2)}) %collective-permute-start.10) | collective-permute-done | bytes 24608 | tf_op jit(solution)/shard_map/ppermute | solution.py:393
  41.9 0.0 collective-permute-done.9.other_small_ref
  41.9 0.1 add_small.1
  42.0 39.3 %all_to_all.10.refs_0_ = bf16[64,8,2304]{2,1,0:T(8,128)(2,1)S(1)} all-to-all(bf16[64,8,2304]{2,1,0:T(8,128)(2,1)S(1)} %bitcast.16), channel_id=1, replica_groups=mesh['xh'=2,'co'=2,'y'=4,'xl'=2,'z'=4] {'xh','y','xl','z'}, dimensions={0} | all-to-all | bytes 4718592 | tf_op jit(solution)/shard_map/all_to_all | solution.py:437
  81.3 1.4 %total.1 = bf16[32,8,2304]{2,1,0:T(8,128)(2,1)} custom-call(bf16[64,8,2304]{2,1,0:T(8,128)(2,1)S(1)} %all_to_all.10.refs_0_), custom_call_target="tpu_custom_call" | custom-call | flops 1024 | bytes 1024 | tf_op jit(solution)/shard_map/total/pallas_call | solution.py:46
  82.7 4.4 %all-to-all-start.1 = ((bf16[32,8,2304]{2,1,0:T(8,128)(2,1)}), bf16[32,8,2304]{2,1,0:T(8,128)(2,1)S(1)}, u32[]{:S(2)}, u32[]{:S(2)}) async-start(bf16[32,8,2304]{2,1,0:T(8,128)(2,1)} %total.1), calls=%async_computation.1 | async-start | bytes 2359296 | tf_op jit(solution)/shard_map/all_to_all | solution.py:440
  87.1 0.7 copy.18
  87.7 0.9 input_grads.1
  88.6 14.3 %all-to-all-done.1 = bf16[32,8,2304]{2,1,0:T(8,128)(2,1)S(1)} async-done(((bf16[32,8,2304]{2,1,0:T(8,128)(2,1)}), bf16[32,8,2304]{2,1,0:T(8,128)(2,1)S(1)}, u32[]{:S(2)}, u32[]{:S(2)}) %all-to-all-start.1) | async-done | bytes 1179680 | tf_op jit(solution)/shard_map/all_to_all | solution.py:440
  103.0 2.1 %spread.1 = (f32[2048,256]{1,0:T(8,128)}, f32[3,3,256]{2,1,0:T(4,128)}, f32[16,1024]{1,0:T(8,128)}, f32[1,256]{1,0:T(1,128)}) custom-call(bf16[256,2304]{1,0:T(8,128)(2,1)S(1)} %bitcast.20), custom_call_target="tpu_custom_call" | custom-call | flops 1024 | bytes 1024 | tf_op jit(solution)/shard_map/spread/pallas_call | solution.py:46
Async XLA Ops:
  0.6 36.6 %collective-permute-start.7 = (bf16[256,8192]{1,0:T(8,128)(2,1)}, bf16[256,8192]{1,0:T(8,128)(2,1)}, u32[]{:S(2)}, u32[]{:S(2)}) collective-permute-start(bf16[256,8192]{1,0:T(8,128)(2,1)} %bitcast.17), channel_id=1, source_target_pairs={{0,32},{32,0},{1,33},{33,1},{2,34},{34,2},{3,35},{35,3},{4,36},{36... | collective-permute-start | bytes 12582920 | tf_op jit(solution)/shard_map/ppermute | solution.py:415
  3.1 13.5 %collective-permute-start = (bf16[256,512]{1,0:T(8,128)(2,1)S(1)}, bf16[256,512]{1,0:T(8,128)(2,1)S(1)}, u32[]{:S(2)}, u32[]{:S(2)}) collective-permute-start(bf16[256,512]{1,0:T(8,128)(2,1)S(1)} %pad_maximum_fusion), channel_id=1, source_target_pairs={{0,64},{1,65},{2,66},{3,67},{4,68},{5,69},{6,70},{7,71},{8,72},{9,... | collective-permute-start | bytes 786440 | tf_op jit(solution)/shard_map/ppermute | solution.py:413
  7.9 12.7 %collective-permute-start.2 = (bf16[256,512]{1,0:T(8,128)(2,1)S(1)}, bf16[256,512]{1,0:T(8,128)(2,1)S(1)}, u32[]{:S(2)}, u32[]{:S(2)}) collective-permute-start(bf16[256,512]{1,0:T(8,128)(2,1)S(1)} %pad_maximum_fusion), channel_id=1, source_target_pairs={{0,32},{32,0},{1,33},{33,1},{2,34},{34,2},{3,35},{35,3},{4,36},{36... | collective-permute-start | bytes 786440 | tf_op jit(solution)/shard_map/ppermute | solution.py:414
  9.0 8.2 %copy-start.1 = (bf16[1,256,256]{2,1,0:T(8,128)(2,1)S(1)}, bf16[1,256,256]{2,1,0:T(8,128)(2,1)}, u32[]{:S(2)}) copy-start(bf16[1,256,256]{2,1,0:T(8,128)(2,1)} %param.8) | copy-start | bytes 393220
  9.0 12.3 %copy-start.2 = (bf16[1,256,256]{2,1,0:T(8,128)(2,1)S(1)}, bf16[1,256,256]{2,1,0:T(8,128)(2,1)}, u32[]{:S(2)}) copy-start(bf16[1,256,256]{2,1,0:T(8,128)(2,1)} %param.10) | copy-start | bytes 393220
  9.0 12.3 %copy-start.3 = (bf16[1,256,256]{2,1,0:T(8,128)(2,1)S(1)}, bf16[1,256,256]{2,1,0:T(8,128)(2,1)}, u32[]{:S(2)}) copy-start(bf16[1,256,256]{2,1,0:T(8,128)(2,1)} %param.9) | copy-start | bytes 393220
  9.0 7.6 %collective-permute-start.1 = (bf16[16,256]{1,0:T(8,128)(2,1)S(1)}, bf16[16,256]{1,0:T(8,128)(2,1)S(1)}, u32[]{:S(2)}, u32[]{:S(2)}) collective-permute-start(bf16[16,256]{1,0:T(8,128)(2,1)S(1)} %slice_bitcast_fusion), channel_id=1, source_target_pairs={{0,32},{32,64},{64,96},{1,33},{33,65},{65,97},{2,34},{34,66},{66,9... | collective-permute-start | bytes 24584 | tf_op jit(solution)/shard_map/ppermute | solution.py:393
  11.0 0.8 copy-start.4
  11.8 5.4 %copy-start.6 = (f32[3,3,256]{2,1,0:T(4,128)S(1)}, f32[3,3,256]{2,1,0:T(4,128)}, u32[]{:S(2)}) copy-start(f32[3,3,256]{2,1,0:T(4,128)} %taps_ref.7) | copy-start | bytes 27652
  11.8 9.5 %copy-start.7 = (f32[256]{0:T(256)S(1)}, f32[256]{0:T(256)}, u32[]{:S(2)}) copy-start(f32[256]{0:T(256)} %param.13) | copy-start | bytes 3076
  16.6 4.6 %collective-permute-start.3 = (bf16[256,512]{1,0:T(8,128)(2,1)S(1)}, bf16[256,512]{1,0:T(8,128)(2,1)S(1)}, u32[]{:S(2)}, u32[]{:S(2)}) collective-permute-start(bf16[256,512]{1,0:T(8,128)(2,1)S(1)} %collective-permute-done.cross_ref), channel_id=1, source_target_pairs={{0,32},{32,0},{1,33},{33,1},{2,34},{34,2},{3,35},{35,3},{4,36},{36... | collective-permute-start | bytes 786440 | tf_op jit(solution)/shard_map/ppermute | solution.py:419
  17.3 7.8 %collective-permute-start.4 = (bf16[256,256]{1,0:T(8,128)(2,1)S(1)}, bf16[256,256]{1,0:T(8,128)(2,1)S(1)}, u32[]{:S(2)}, u32[]{:S(2)}) collective-permute-start(bf16[256,256]{1,0:T(8,128)(2,1)S(1)} %d_inner.1.d0_ref), channel_id=1, source_target_pairs={{32,0},{64,32},{96,64},{33,1},{65,33},{97,65},{34,2},{66,34},{98,6... | collective-permute-start | bytes 393224 | tf_op jit(solution)/shard_map/ppermute | solution.py:393
  19.3 8.9 %collective-permute-start.5 = (bf16[256,256]{1,0:T(8,128)(2,1)S(1)}, bf16[256,256]{1,0:T(8,128)(2,1)S(1)}, u32[]{:S(2)}, u32[]{:S(2)}) collective-permute-start(bf16[256,256]{1,0:T(8,128)(2,1)S(1)} %d_inner.1.d0_ref), channel_id=1, source_target_pairs={{64,0},{96,32},{65,1},{97,33},{66,2},{98,34},{67,3},{99,35},{68,4}... | collective-permute-start | bytes 393224 | tf_op jit(solution)/shard_map/ppermute | solution.py:393
  20.6 7.6 %collective-permute-start.6 = (bf16[256,256]{1,0:T(8,128)(2,1)S(1)}, bf16[256,256]{1,0:T(8,128)(2,1)S(1)}, u32[]{:S(2)}, u32[]{:S(2)}) collective-permute-start(bf16[256,256]{1,0:T(8,128)(2,1)S(1)} %d_inner.1.d0_ref), channel_id=1, source_target_pairs={{96,0},{97,1},{98,2},{99,3},{100,4},{101,5},{102,6},{103,7},{104,8... | collective-permute-start | bytes 393224 | tf_op jit(solution)/shard_map/ppermute | solution.py:393
  21.3 6.9 %copy-start.5 = (bf16[16,1024]{1,0:T(8,128)(2,1)S(1)}, bf16[16,1024]{1,0:T(8,128)(2,1)}, u32[]{:S(2)}) copy-start(bf16[16,1024]{1,0:T(8,128)(2,1)} %lags_ref.1) | copy-start | bytes 98308
  21.3 15.9 %copy-start = (bf16[1,256,8192]{2,1,0:T(8,128)(2,1)S(1)}, bf16[1,256,8192]{2,1,0:T(8,128)(2,1)}, u32[]{:S(2)}) copy-start(bf16[1,256,8192]{2,1,0:T(8,128)(2,1)} %param.15) | copy-start | bytes 12582916
  24.0 9.4 %collective-permute-start.8 = (bf16[256,256]{1,0:T(8,128)(2,1)S(1)}, bf16[256,256]{1,0:T(8,128)(2,1)S(1)}, u32[]{:S(2)}, u32[]{:S(2)}) collective-permute-start(bf16[256,256]{1,0:T(8,128)(2,1)S(1)} %get-tuple-element.38.gated_ref), channel_id=1, source_target_pairs={{0,32},{32,0},{1,33},{33,1},{2,34},{34,2},{3,35},{35,3},{4,36},{36... | collective-permute-start | bytes 393224 | tf_op jit(solution)/shard_map/ppermute | solution.py:425
  33.4 8.5 %collective-permute-start.9 = (f32[32,8,256]{2,1,0:T(8,128)S(1)}, f32[32,8,256]{2,1,0:T(8,128)S(1)}, u32[]{:S(2)}, u32[]{:S(2)}) collective-permute-start(f32[32,8,256]{2,1,0:T(8,128)S(1)} %get-tuple-element.46.small_ref), channel_id=1, source_target_pairs={{0,32},{32,0},{1,33},{33,1},{2,34},{34,2},{3,35},{35,3},{4,36},{36... | collective-permute-start | bytes 786440 | tf_op jit(solution)/shard_map/ppermute | solution.py:431
  35.3 6.6 %collective-permute-start.10 = (f32[3,8,256]{2,1,0:T(8,128)S(1)}, f32[3,8,256]{2,1,0:T(8,128)S(1)}, u32[]{:S(2)}, u32[]{:S(2)}) collective-permute-start(f32[3,8,256]{2,1,0:T(8,128)S(1)} %get-tuple-element.47), channel_id=1, source_target_pairs={{32,0},{64,32},{96,64},{33,1},{65,33},{97,65},{34,2},{66,34},{98,6... | collective-permute-start | bytes 73736 | tf_op jit(solution)/shard_map/ppermute | solution.py:393
  82.7 20.3 %all-to-all-start.1 = ((bf16[32,8,2304]{2,1,0:T(8,128)(2,1)}), bf16[32,8,2304]{2,1,0:T(8,128)(2,1)S(1)}, u32[]{:S(2)}, u32[]{:S(2)}) async-start(bf16[32,8,2304]{2,1,0:T(8,128)(2,1)} %total.1), calls=%async_computation.1 | async-start | bytes 2359296 | tf_op jit(solution)/shard_map/all_to_all | solution.py:440

commit v6 on v5

--- a/solution.py
+++ b/solution.py
@@ -109,9 +109,7 @@
     return pltpu.roll(wide, WIDE - (STRIP - 1), 1)
 
 
-def pre_kernel(
-    cot_ref, weight_ref, filter_ref, d_gated_ref, strips_ref, cot_buffer, weight_buffer, sems
-):
+def d_gated_kernel(cot_ref, weight_ref, d_gated_ref, cot_buffer, weight_buffer, sems):
     tile = FEATS // PIECES
     copies = []
     for n in range(PIECES):
@@ -123,9 +121,6 @@
         for copy in pair:
             copy.start()
         copies.append(pair)
-    lines = lines_of(filter_ref, True)
-    for g in range(GROUPS):
-        strips_ref[g * STRIP : (g + 1) * STRIP, :] = strip_of(lines[g : g + 1])
     total = jnp.zeros((ROWS, CHANS), F32)
     for n in range(PIECES):
         for copy in copies[n]:
@@ -134,22 +129,31 @@
     d_gated_ref[...] = total.astype(BF16)
 
 
-def pre_call(cot, weight, lags):
-    out_shape = [
-        pltpu.VMEM((ROWS, CHANS), BF16),
-        pltpu.VMEM((GROUPS * STRIP, LENGTH), BF16),
-    ]
+def d_gated_call(cot, weight):
     tile = FEATS // PIECES
     scratch = [
         pltpu.VMEM((PIECES, ROWS, tile), BF16),
         pltpu.VMEM((PIECES, tile, CHANS), BF16),
         pltpu.SemaphoreType.DMA((2, PIECES)),
     ]
-    far = pl.BlockSpec(memory_space=pltpu.HBM)
-    in_specs = [far, far, pl.BlockSpec(memory_space=pltpu.VMEM)]
+    in_specs = [pl.BlockSpec(memory_space=pltpu.HBM)] * 2
+    out_shape = pltpu.VMEM((ROWS, CHANS), BF16)
     return call(
-        pre_kernel, "pre", out_shape, (cot, weight, lags), scratch, in_specs=in_specs, flops=1 << 30
+        d_gated_kernel, "d_gated", out_shape, (cot, weight), scratch, in_specs=in_specs,
+        flops=1 << 30,
     )
+
+
+def strips_kernel(filter_ref, strips_ref, back_strips_ref):
+    for ref, turned in ((strips_ref, True), (back_strips_ref, False)):
+        lines = lines_of(filter_ref, turned)
+        for g in range(GROUPS):
+            ref[g * STRIP : (g + 1) * STRIP, :] = strip_of(lines[g : g + 1])
+
+
+def strips_call(lags):
+    out_shape = [pltpu.VMEM((GROUPS * STRIP, LENGTH), BF16)] * 2
+    return call(strips_kernel, "strips", out_shape, (lags,))
 
 
 def d_inner_kernel(d_gated_ref, query_ref, tail_ref, taps_ref, out_ref):
@@ -237,17 +241,14 @@
 
 
 def bwd_kernel(
-    core_ref, d0_ref, d1_ref, d2_ref, d3_ref, lags_ref, mixed_ref, key_ref, value_ref, pair_ref,
+    core_ref, d0_ref, d1_ref, d2_ref, d3_ref, strips_ref, mixed_ref, key_ref, value_ref, pair_ref,
     cross_pair_ref, query_ref, tail_ref, inner_ref, d_gated_ref, taps_ref, skip_ref,
     d_short_ref, head_ref, small_ref,
-    strips_ref, ahead_ref, outer_ref, stack_ref,
+    ahead_ref, outer_ref, stack_ref,
 ):
     for n, ref in enumerate((d0_ref, d1_ref, d2_ref, d3_ref)):
         ahead_ref[n * ROWS : (n + 1) * ROWS, :] = ref[...]
     ahead_ref[LENGTH:, :] = jnp.zeros((ROWS, CHANS), BF16)
-    lines = lines_of(lags_ref, False)
-    for g in range(GROUPS):
-        strips_ref[g * STRIP : (g + 1) * STRIP, :] = strip_of(lines[g : g + 1])
     d_inner = d0_ref[...].astype(F32)
     mixed = mixed_ref[...]
     d_mixed = all_strips(strips_ref, ahead_ref) + skip_ref[...] * d_inner
@@ -306,7 +307,6 @@
         pltpu.VMEM((SHARES, SEGMENT, CHANS), F32),
     ]
     scratch = [
-        pltpu.VMEM((GROUPS * STRIP, LENGTH), BF16),
         pltpu.VMEM((LENGTH + ROWS, CHANS), BF16),
         pltpu.VMEM((GROUPS * SMALL, WIDE), F32),
         pltpu.VMEM((GROUPS * SMALL, CHANS), BF16),
@@ -414,25 +414,26 @@
     pair = lax.ppermute(own, "co", swap)
     other_cot = lax.ppermute(cot, "co", swap)
 
-    d_gated, strips = pre_call(cot, out_weight, long_filter)
-    cross, tail, d_gated, strips = lax.optimization_barrier((cross, tail, d_gated, strips))
+    d_gated = d_gated_call(cot, out_weight)
+    cross, tail, d_gated, lags = lax.optimization_barrier((cross, tail, d_gated, long_filter))
     cross_pair = lax.ppermute(cross, "co", swap)
+    strips, back_strips = strips_call(lags)
     d_inner = d_inner_call(d_gated, query, tail, taps)
     blocks = [d_inner] + [sent(d_inner, -distance) for distance in (1, 2, 3)]
     gated, inner, mixed = fwd_call(
         core, strips, pair, cross, cross_pair, key, value, query, tail, taps, skip
     )
     other_gated = lax.ppermute(gated, "co", swap)
+    terms = terms_call(core, cot, other_cot, gated, other_gated)
+    terms, inner, *blocks = lax.optimization_barrier((terms, inner, *blocks))
     d_short, head, small = bwd_call(
-        core, *blocks, long_filter, mixed, key, value, pair, cross_pair, query, tail, inner,
+        core, *blocks, back_strips, mixed, key, value, pair, cross_pair, query, tail, inner,
         d_gated, taps, skip,
     )
-    other_gated, head, small = lax.optimization_barrier((other_gated, head, small))
     other_small = lax.ppermute(small, "co", swap)
     following = sent(head, -1)
-    terms = terms_call(core, cot, other_cot, gated, other_gated)
-    terms, other_small, following = lax.optimization_barrier((terms, other_small, following))
     terms = add_small_call(terms, small, other_small)
+    terms, following = lax.optimization_barrier((terms, following))
     terms = terms.reshape(2 * SHARES, CHANS // SHARES, SHARE + CHANS)
     terms = lax.all_to_all(terms, CHIPS, 0, 0)
     grad_query, grad_key, grad_value = input_grad_call(d_short, following, taps)

time: 107 us -> 112 us (1.047)
  waiting for transfers between devices: 19.7 us -> 23.3 us
  blocking collectives: 39.3 us -> 41.5 us
    ppermute x5, waiting for transfers between devices: 5.32 us -> 7.86 us  [sent(): return lax.ppermute(block, CTX, route)]
    all_to_all x1, blocking collectives: 39.3 us -> 41.5 us  [shards(): terms = lax.all_to_all(terms, CHIPS, 0, 0)]
    pallas_call x9 -> x10, Pallas kernels: 20.7 us -> 21 us  [call(): pl.pallas_call(kernel, out_shape=out_shape, scratch_shapes=list(scratch),...]
  transfers between devices with their start and end apart: 12 -> 12, of which waited for: 4 -> 5; matrix products, arithmetic and copies ran while one was open for 2% -> 2% of each run, Pallas kernels for 16% -> 11%
where the time goes in v6:
time: 112 us; the launch traced here: 111 us
  blocking collectives  41.5 us (37%)
  waiting for transfers between devices  23.3 us (21%)
  starting transfers between devices  21.6 us (19%)
  Pallas kernels  21 us (19%)
  local copies, waits for them, and re-layouts  1.39 us (1%)
    all_to_all x1, blocking collectives, shards(): terms = lax.all_to_all(terms, CHIPS, 0, 0)  41.5 us
    pallas_call x10, Pallas kernels, call(): pl.pallas_call(kernel, out_shape=out_shape, scratch_shapes=list(scratch),...  21 us
    all_to_all x1, waiting for transfers between devices, shards(): shares = lax.all_to_all(total_call(terms, scale), DP, 0, 0)  15.2 us
    ppermute x5, starting transfers between devices, sent(): return lax.ppermute(block, CTX, route)  7.98 us
    ppermute x5, waiting for transfers between devices, sent(): return lax.ppermute(block, CTX, route)  7.86 us
    ppermute x1, starting transfers between devices, shards(): cross = lax.ppermute(own, 'xh', [(0, 1)])  4.75 us
    all_to_all x1, starting transfers between devices, shards(): shares = lax.all_to_all(total_call(terms, scale), DP, 0, 0)  3.94 us
  transfers between devices with their start and end apart: 12, of which 5 were waited for; matrix products, arithmetic and copies ran while one was open for 2% of the time, Pallas kernels for 11%

profile of v6, /device:TPU:1, one launch (start us, length us, event | category | flops | bytes accessed | tf_op | source)
XLA Modules:
  0.0 110.7 jit_solution(8388690031682250922)
XLA Ops:
  0.6 1.5 %collective-permute-start.4 = (bf16[256,8192]{1,0:T(8,128)(2,1)}, bf16[256,8192]{1,0:T(8,128)(2,1)}, u32[]{:S(2)}, u32[]{:S(2)}) collective-permute-start(bf16[256,8192]{1,0:T(8,128)(2,1)} %bitcast.17), channel_id=1, source_target_pairs={{0,32},{32,0},{1,33},{33,1},{2,34},{34,2},{3,35},{35,3},{4,36},{36... | collective-permute-start | bytes 12582920 | tf_op jit(solution)/shard_map/ppermute | solution.py:415
  2.1 1.0 pad_maximum_fusion
  3.1 4.7 %collective-permute-start = (bf16[256,512]{1,0:T(8,128)(2,1)S(1)}, bf16[256,512]{1,0:T(8,128)(2,1)S(1)}, u32[]{:S(2)}, u32[]{:S(2)}) collective-permute-start(bf16[256,512]{1,0:T(8,128)(2,1)S(1)} %pad_maximum_fusion), channel_id=1, source_target_pairs={{0,64},{1,65},{2,66},{3,67},{4,68},{5,69},{6,70},{7,71},{8,72},{9,... | collective-permute-start | bytes 786440 | tf_op jit(solution)/shard_map/ppermute | solution.py:413
  7.9 0.4 collective-permute-start.2
  8.3 0.7 slice_bitcast_fusion
  9.0 0.0 copy-start.5
  9.0 0.0 copy-start.1
  9.0 0.0 copy-start.2
  9.0 0.0 copy-start.3
  9.0 0.0 copy-start.4
  9.0 0.0 copy-start.6
  9.0 2.1 %collective-permute-start.1 = (bf16[16,256]{1,0:T(8,128)(2,1)S(1)}, bf16[16,256]{1,0:T(8,128)(2,1)S(1)}, u32[]{:S(2)}, u32[]{:S(2)}) collective-permute-start(bf16[16,256]{1,0:T(8,128)(2,1)S(1)} %slice_bitcast_fusion), channel_id=1, source_target_pairs={{0,32},{32,64},{64,96},{1,33},{33,65},{65,97},{2,34},{34,66},{66,9... | collective-permute-start | bytes 24584 | tf_op jit(solution)/shard_map/ppermute | solution.py:393
  11.0 4.3 %d_gated.1.d_gated_ref = bf16[256,256]{1,0:T(8,128)(2,1)S(1)} custom-call(bf16[256,8192]{1,0:T(8,128)(2,1)} %bitcast.18, bf16[8192,256]{1,0:T(8,128)(2,1)} %weight_ref.1), custom_call_target="tpu_custom_call" | custom-call | flops 1073741824 | bytes 1024 | tf_op jit(solution)/shard_map/d_gated/pallas_call | solution.py:46
  15.4 0.0 collective-permute-done.1.tail_ref
  15.4 0.0 collective-permute-done.cross_ref
  15.4 0.6 collective-permute-start.3
  16.0 0.0 copy-done.5
  16.0 0.9 strips.1
  16.8 0.0 collective-permute-done.2.pair_ref
  16.9 0.3 collective-permute-done.3.cross_pair_ref
  17.1 0.0 copy-done.1
  17.1 0.0 copy-done.2
  17.1 0.0 copy-done.3
  17.1 0.0 copy-done.4
  17.1 0.0 copy-done.6
  17.1 0.0 copy-start
  17.2 2.7 %fwd.1 = (bf16[256,256]{1,0:T(8,128)(2,1)S(1)}, f32[256,256]{1,0:T(8,128)S(1)}, bf16[256,256]{1,0:T(8,128)(2,1)S(1)}) custom-call(s32[1]{0:T(128)} %bitcast.core_ref, bf16[512,1024]{1,0:T(8,128)(2,1)S(1)} %get-tuple-element.36.strips_ref, bf16[256,512]{1,0:T(8,128)(2,1)S(1)} %collective-permute-done.2.pair_ref, ...), custom_call_target="tpu_custom_call" | custom-call | flops 4294967296 | bytes 1024 | tf_op jit(solution)/shard_map/fwd/pallas_call | solution.py:46
  19.8 0.5 collective-permute-start.5
  20.3 0.1 d_inner.1.d0_ref
  20.4 2.0 %collective-permute-start.6 = (bf16[256,256]{1,0:T(8,128)(2,1)S(1)}, bf16[256,256]{1,0:T(8,128)(2,1)S(1)}, u32[]{:S(2)}, u32[]{:S(2)}) collective-permute-start(bf16[256,256]{1,0:T(8,128)(2,1)S(1)} %d_inner.1.d0_ref), channel_id=1, source_target_pairs={{32,0},{64,32},{96,64},{33,1},{65,33},{97,65},{34,2},{66,34},{98,6... | collective-permute-start | bytes 393224 | tf_op jit(solution)/shard_map/ppermute | solution.py:393
  22.4 1.3 %collective-permute-start.7 = (bf16[256,256]{1,0:T(8,128)(2,1)S(1)}, bf16[256,256]{1,0:T(8,128)(2,1)S(1)}, u32[]{:S(2)}, u32[]{:S(2)}) collective-permute-start(bf16[256,256]{1,0:T(8,128)(2,1)S(1)} %d_inner.1.d0_ref), channel_id=1, source_target_pairs={{64,0},{96,32},{65,1},{97,33},{66,2},{98,34},{67,3},{99,35},{68,4}... | collective-permute-start | bytes 393224 | tf_op jit(solution)/shard_map/ppermute | solution.py:393
  23.7 0.7 collective-permute-start.8
  24.4 0.0 collective-permute-done.5.other_gated_ref
  24.4 0.0 collective-permute-done.4.other_cot_ref
  24.4 0.0 copy-done
  24.5 3.5 %terms.1.terms_ref = bf16[2,256,2304]{2,1,0:T(8,128)(2,1)S(1)} custom-call(s32[1]{0:T(128)} %bitcast.core_ref, bf16[256,8192]{1,0:T(8,128)(2,1)S(1)} %bitcast.19, bf16[256,8192]{1,0:T(8,128)(2,1)} %collective-permute-done.4.other_cot_ref, bf16[256,256]{1,0:T(8,128)(2,1)S(1)} %get-tuple-element.39.gated_ref, ...), custom_call_target="tpu_custom_call" | custom-call | flops 1073741824 | bytes 1024 | tf_op jit(solution)/shard_map/terms/pallas_call | solution.py:46
  27.9 0.3 collective-permute-done.6.d1_ref
  28.2 3.0 %collective-permute-done.7.d2_ref = bf16[256,256]{1,0:T(8,128)(2,1)S(1)} collective-permute-done((bf16[256,256]{1,0:T(8,128)(2,1)S(1)}, bf16[256,256]{1,0:T(8,128)(2,1)S(1)}, u32[]{:S(2)}, u32[]{:S(2)}) %collective-permute-start.7) | collective-permute-done | bytes 131104 | tf_op jit(solution)/shard_map/ppermute | solution.py:393
  31.1 0.0 collective-permute-done.8.d3_ref
  31.2 5.1 %bwd.1 = (f32[3,256,256]{2,1,0:T(8,128)S(1)}, f32[3,8,256]{2,1,0:T(8,128)S(1)}, f32[32,8,256]{2,1,0:T(8,128)S(1)}) custom-call(s32[1]{0:T(128)} %bitcast.core_ref, bf16[256,256]{1,0:T(8,128)(2,1)S(1)} %d_inner.1.d0_ref, bf16[256,256]{1,0:T(8,128)(2,1)S(1)} %collective-permute-done.6.d1_ref, bf16[256,256]{1,0:T(8,128)(2,1)S(1)} %collective-permute-done.7.d2_ref, ...), custom_call_target="tpu_custom_call" | custom-call | flops 1024 | bytes 1024 | tf_op jit(solution)/shard_map/bwd/pallas_call | solution.py:46
  36.3 2.0 %collective-permute-start.9 = (f32[32,8,256]{2,1,0:T(8,128)S(1)}, f32[32,8,256]{2,1,0:T(8,128)S(1)}, u32[]{:S(2)}, u32[]{:S(2)}) collective-permute-start(f32[32,8,256]{2,1,0:T(8,128)S(1)} %get-tuple-element.51.small_ref), channel_id=1, source_target_pairs={{0,32},{32,0},{1,33},{33,1},{2,34},{34,2},{3,35},{35,3},{4,36},{36... | collective-permute-start | bytes 786440 | tf_op jit(solution)/shard_map/ppermute | solution.py:433
  38.3 1.9 %collective-permute-start.10 = (f32[3,8,256]{2,1,0:T(8,128)S(1)}, f32[3,8,256]{2,1,0:T(8,128)S(1)}, u32[]{:S(2)}, u32[]{:S(2)}) collective-permute-start(f32[3,8,256]{2,1,0:T(8,128)S(1)} %get-tuple-element.52), channel_id=1, source_target_pairs={{32,0},{64,32},{96,64},{33,1},{65,33},{97,65},{34,2},{66,34},{98,6... | collective-permute-start | bytes 73736 | tf_op jit(solution)/shard_map/ppermute | solution.py:393
  40.2 0.0 collective-permute-done.9.other_small_ref
  40.2 0.1 add_small.1
  40.3 4.6 %collective-permute-done.10.next_ref = f32[3,8,256]{2,1,0:T(8,128)S(1)} collective-permute-done((f32[3,8,256]{2,1,0:T(8,128)S(1)}, f32[3,8,256]{2,1,0:T(8,128)S(1)}, u32[]{:S(2)}, u32[]{:S(2)}) %collective-permute-start.10) | collective-permute-done | bytes 24608 | tf_op jit(solution)/shard_map/ppermute | solution.py:393
  44.9 41.5 %all_to_all.10.refs_0_ = bf16[64,8,2304]{2,1,0:T(8,128)(2,1)S(1)} all-to-all(bf16[64,8,2304]{2,1,0:T(8,128)(2,1)S(1)} %bitcast.16), channel_id=1, replica_groups=mesh['xh'=2,'co'=2,'y'=4,'xl'=2,'z'=4] {'xh','y','xl','z'}, dimensions={0} | all-to-all | bytes 4718592 | tf_op jit(solution)/shard_map/all_to_all | solution.py:438
  86.5 1.4 %total.1 = bf16[32,8,2304]{2,1,0:T(8,128)(2,1)} custom-call(bf16[64,8,2304]{2,1,0:T(8,128)(2,1)S(1)} %all_to_all.10.refs_0_), custom_call_target="tpu_custom_call" | custom-call | flops 1024 | bytes 1024 | tf_op jit(solution)/shard_map/total/pallas_call | solution.py:46
  87.9 3.9 %all-to-all-start.1 = ((bf16[32,8,2304]{2,1,0:T(8,128)(2,1)}), bf16[32,8,2304]{2,1,0:T(8,128)(2,1)S(1)}, u32[]{:S(2)}, u32[]{:S(2)}) async-start(bf16[32,8,2304]{2,1,0:T(8,128)(2,1)} %total.1), calls=%async_computation.1 | async-start | bytes 2359296 | tf_op jit(solution)/shard_map/all_to_all | solution.py:441
  91.8 0.7 copy.18
  92.5 0.9 input_grads.1
  93.4 15.2 %all-to-all-done.1 = bf16[32,8,2304]{2,1,0:T(8,128)(2,1)S(1)} async-done(((bf16[32,8,2304]{2,1,0:T(8,128)(2,1)}), bf16[32,8,2304]{2,1,0:T(8,128)(2,1)S(1)}, u32[]{:S(2)}, u32[]{:S(2)}) %all-to-all-start.1) | async-done | bytes 1179680 | tf_op jit(solution)/shard_map/all_to_all | solution.py:441
  108.6 2.1 %spread.1 = (f32[2048,256]{1,0:T(8,128)}, f32[3,3,256]{2,1,0:T(4,128)}, f32[16,1024]{1,0:T(8,128)}, f32[1,256]{1,0:T(1,128)}) custom-call(bf16[256,2304]{1,0:T(8,128)(2,1)S(1)} %bitcast.20), custom_call_target="tpu_custom_call" | custom-call | flops 1024 | bytes 1024 | tf_op jit(solution)/shard_map/spread/pallas_call | solution.py:46
Async XLA Ops:
  0.6 23.8 %collective-permute-start.4 = (bf16[256,8192]{1,0:T(8,128)(2,1)}, bf16[256,8192]{1,0:T(8,128)(2,1)}, u32[]{:S(2)}, u32[]{:S(2)}) collective-permute-start(bf16[256,8192]{1,0:T(8,128)(2,1)} %bitcast.17), channel_id=1, source_target_pairs={{0,32},{32,0},{1,33},{33,1},{2,34},{34,2},{3,35},{35,3},{4,36},{36... | collective-permute-start | bytes 12582920 | tf_op jit(solution)/shard_map/ppermute | solution.py:415
  3.1 12.3 %collective-permute-start = (bf16[256,512]{1,0:T(8,128)(2,1)S(1)}, bf16[256,512]{1,0:T(8,128)(2,1)S(1)}, u32[]{:S(2)}, u32[]{:S(2)}) collective-permute-start(bf16[256,512]{1,0:T(8,128)(2,1)S(1)} %pad_maximum_fusion), channel_id=1, source_target_pairs={{0,64},{1,65},{2,66},{3,67},{4,68},{5,69},{6,70},{7,71},{8,72},{9,... | collective-permute-start | bytes 786440 | tf_op jit(solution)/shard_map/ppermute | solution.py:413
  7.9 9.0 %collective-permute-start.2 = (bf16[256,512]{1,0:T(8,128)(2,1)S(1)}, bf16[256,512]{1,0:T(8,128)(2,1)S(1)}, u32[]{:S(2)}, u32[]{:S(2)}) collective-permute-start(bf16[256,512]{1,0:T(8,128)(2,1)S(1)} %pad_maximum_fusion), channel_id=1, source_target_pairs={{0,32},{32,0},{1,33},{33,1},{2,34},{34,2},{3,35},{35,3},{4,36},{36... | collective-permute-start | bytes 786440 | tf_op jit(solution)/shard_map/ppermute | solution.py:414
  9.0 7.0 %copy-start.5 = (bf16[16,1024]{1,0:T(8,128)(2,1)S(1)}, bf16[16,1024]{1,0:T(8,128)(2,1)}, u32[]{:S(2)}) copy-start(bf16[16,1024]{1,0:T(8,128)(2,1)} %filter_ref) | copy-start | bytes 98308
  9.0 8.2 %copy-start.1 = (bf16[1,256,256]{2,1,0:T(8,128)(2,1)S(1)}, bf16[1,256,256]{2,1,0:T(8,128)(2,1)}, u32[]{:S(2)}) copy-start(bf16[1,256,256]{2,1,0:T(8,128)(2,1)} %param.8) | copy-start | bytes 393220
  9.0 8.2 %copy-start.2 = (bf16[1,256,256]{2,1,0:T(8,128)(2,1)S(1)}, bf16[1,256,256]{2,1,0:T(8,128)(2,1)}, u32[]{:S(2)}) copy-start(bf16[1,256,256]{2,1,0:T(8,128)(2,1)} %param.10) | copy-start | bytes 393220
  9.0 8.2 %copy-start.3 = (bf16[1,256,256]{2,1,0:T(8,128)(2,1)S(1)}, bf16[1,256,256]{2,1,0:T(8,128)(2,1)}, u32[]{:S(2)}) copy-start(bf16[1,256,256]{2,1,0:T(8,128)(2,1)} %param.9) | copy-start | bytes 393220
  9.0 8.2 %copy-start.4 = (f32[3,3,256]{2,1,0:T(4,128)S(1)}, f32[3,3,256]{2,1,0:T(4,128)}, u32[]{:S(2)}) copy-start(f32[3,3,256]{2,1,0:T(4,128)} %taps_ref.7) | copy-start | bytes 27652
  9.0 8.2 %copy-start.6 = (f32[256]{0:T(256)S(1)}, f32[256]{0:T(256)}, u32[]{:S(2)}) copy-start(f32[256]{0:T(256)} %param.13) | copy-start | bytes 3076
  9.0 6.4 %collective-permute-start.1 = (bf16[16,256]{1,0:T(8,128)(2,1)S(1)}, bf16[16,256]{1,0:T(8,128)(2,1)S(1)}, u32[]{:S(2)}, u32[]{:S(2)}) collective-permute-start(bf16[16,256]{1,0:T(8,128)(2,1)S(1)} %slice_bitcast_fusion), channel_id=1, source_target_pairs={{0,32},{32,64},{64,96},{1,33},{33,65},{65,97},{2,34},{34,66},{66,9... | collective-permute-start | bytes 24584 | tf_op jit(solution)/shard_map/ppermute | solution.py:393
  15.4 1.7 %collective-permute-start.3 = (bf16[256,512]{1,0:T(8,128)(2,1)S(1)}, bf16[256,512]{1,0:T(8,128)(2,1)S(1)}, u32[]{:S(2)}, u32[]{:S(2)}) collective-permute-start(bf16[256,512]{1,0:T(8,128)(2,1)S(1)} %collective-permute-done.cross_ref), channel_id=1, source_target_pairs={{0,32},{32,0},{1,33},{33,1},{2,34},{34,2},{3,35},{35,3},{4,36},{36... | collective-permute-start | bytes 786440 | tf_op jit(solution)/shard_map/ppermute | solution.py:419
  17.1 7.3 %copy-start = (bf16[1,256,8192]{2,1,0:T(8,128)(2,1)S(1)}, bf16[1,256,8192]{2,1,0:T(8,128)(2,1)}, u32[]{:S(2)}) copy-start(bf16[1,256,8192]{2,1,0:T(8,128)(2,1)} %param.15) | copy-start | bytes 12582916
  19.8 4.6 %collective-permute-start.5 = (bf16[256,256]{1,0:T(8,128)(2,1)S(1)}, bf16[256,256]{1,0:T(8,128)(2,1)S(1)}, u32[]{:S(2)}, u32[]{:S(2)}) collective-permute-start(bf16[256,256]{1,0:T(8,128)(2,1)S(1)} %get-tuple-element.39.gated_ref), channel_id=1, source_target_pairs={{0,32},{32,0},{1,33},{33,1},{2,34},{34,2},{3,35},{35,3},{4,36},{36... | collective-permute-start | bytes 393224 | tf_op jit(solution)/shard_map/ppermute | solution.py:426
  20.4 7.8 %collective-permute-start.6 = (bf16[256,256]{1,0:T(8,128)(2,1)S(1)}, bf16[256,256]{1,0:T(8,128)(2,1)S(1)}, u32[]{:S(2)}, u32[]{:S(2)}) collective-permute-start(bf16[256,256]{1,0:T(8,128)(2,1)S(1)} %d_inner.1.d0_ref), channel_id=1, source_target_pairs={{32,0},{64,32},{96,64},{33,1},{65,33},{97,65},{34,2},{66,34},{98,6... | collective-permute-start | bytes 393224 | tf_op jit(solution)/shard_map/ppermute | solution.py:393
  22.4 8.7 %collective-permute-start.7 = (bf16[256,256]{1,0:T(8,128)(2,1)S(1)}, bf16[256,256]{1,0:T(8,128)(2,1)S(1)}, u32[]{:S(2)}, u32[]{:S(2)}) collective-permute-start(bf16[256,256]{1,0:T(8,128)(2,1)S(1)} %d_inner.1.d0_ref), channel_id=1, source_target_pairs={{64,0},{96,32},{65,1},{97,33},{66,2},{98,34},{67,3},{99,35},{68,4}... | collective-permute-start | bytes 393224 | tf_op jit(solution)/shard_map/ppermute | solution.py:393
  23.7 7.4 %collective-permute-start.8 = (bf16[256,256]{1,0:T(8,128)(2,1)S(1)}, bf16[256,256]{1,0:T(8,128)(2,1)S(1)}, u32[]{:S(2)}, u32[]{:S(2)}) collective-permute-start(bf16[256,256]{1,0:T(8,128)(2,1)S(1)} %d_inner.1.d0_ref), channel_id=1, source_target_pairs={{96,0},{97,1},{98,2},{99,3},{100,4},{101,5},{102,6},{103,7},{104,8... | collective-permute-start | bytes 393224 | tf_op jit(solution)/shard_map/ppermute | solution.py:393
  36.3 3.9 %collective-permute-start.9 = (f32[32,8,256]{2,1,0:T(8,128)S(1)}, f32[32,8,256]{2,1,0:T(8,128)S(1)}, u32[]{:S(2)}, u32[]{:S(2)}) collective-permute-start(f32[32,8,256]{2,1,0:T(8,128)S(1)} %get-tuple-element.51.small_ref), channel_id=1, source_target_pairs={{0,32},{32,0},{1,33},{33,1},{2,34},{34,2},{3,35},{35,3},{4,36},{36... | collective-permute-start | bytes 786440 | tf_op jit(solution)/shard_map/ppermute | solution.py:433
  38.3 6.6 %collective-permute-start.10 = (f32[3,8,256]{2,1,0:T(8,128)S(1)}, f32[3,8,256]{2,1,0:T(8,128)S(1)}, u32[]{:S(2)}, u32[]{:S(2)}) collective-permute-start(f32[3,8,256]{2,1,0:T(8,128)S(1)} %get-tuple-element.52), channel_id=1, source_target_pairs={{32,0},{64,32},{96,64},{33,1},{65,33},{97,65},{34,2},{66,34},{98,6... | collective-permute-start | bytes 73736 | tf_op jit(solution)/shard_map/ppermute | solution.py:393
  87.9 20.7 %all-to-all-start.1 = ((bf16[32,8,2304]{2,1,0:T(8,128)(2,1)}), bf16[32,8,2304]{2,1,0:T(8,128)(2,1)S(1)}, u32[]{:S(2)}, u32[]{:S(2)}) async-start(bf16[32,8,2304]{2,1,0:T(8,128)(2,1)} %total.1), calls=%async_computation.1 | async-start | bytes 2359296 | tf_op jit(solution)/shard_map/all_to_all | solution.py:441

commit v7 on v6

--- a/solution.py
+++ b/solution.py
@@ -30,7 +30,7 @@
 SEGMENT = 8
 SPREAD = 4
 PIECES = 8
-VMEM_LIMIT = 24 * 1024 * 1024
+VMEM_LIMIT = 20 * 1024 * 1024
 
 
 def call(kernel, name, out_shape, operands, scratch=(), scalars=0, flops=1 << 10, **more):
@@ -109,7 +109,10 @@
     return pltpu.roll(wide, WIDE - (STRIP - 1), 1)
 
 
-def d_gated_kernel(cot_ref, weight_ref, d_gated_ref, cot_buffer, weight_buffer, sems):
+def pre_kernel(
+    cot_ref, weight_ref, filter_ref, d_gated_ref, strips_ref, back_strips_ref, cot_buffer,
+    weight_buffer, sems,
+):
     tile = FEATS // PIECES
     copies = []
     for n in range(PIECES):
@@ -121,6 +124,10 @@
         for copy in pair:
             copy.start()
         copies.append(pair)
+    for ref, turned in ((strips_ref, True), (back_strips_ref, False)):
+        lines = lines_of(filter_ref, turned)
+        for g in range(GROUPS):
+            ref[g * STRIP : (g + 1) * STRIP, :] = strip_of(lines[g : g + 1])
     total = jnp.zeros((ROWS, CHANS), F32)
     for n in range(PIECES):
         for copy in copies[n]:
@@ -129,31 +136,17 @@
     d_gated_ref[...] = total.astype(BF16)
 
 
-def d_gated_call(cot, weight):
+def pre_call(*operands):
     tile = FEATS // PIECES
     scratch = [
         pltpu.VMEM((PIECES, ROWS, tile), BF16),
         pltpu.VMEM((PIECES, tile, CHANS), BF16),
         pltpu.SemaphoreType.DMA((2, PIECES)),
     ]
-    in_specs = [pl.BlockSpec(memory_space=pltpu.HBM)] * 2
-    out_shape = pltpu.VMEM((ROWS, CHANS), BF16)
-    return call(
-        d_gated_kernel, "d_gated", out_shape, (cot, weight), scratch, in_specs=in_specs,
-        flops=1 << 30,
-    )
-
-
-def strips_kernel(filter_ref, strips_ref, back_strips_ref):
-    for ref, turned in ((strips_ref, True), (back_strips_ref, False)):
-        lines = lines_of(filter_ref, turned)
-        for g in range(GROUPS):
-            ref[g * STRIP : (g + 1) * STRIP, :] = strip_of(lines[g : g + 1])
-
-
-def strips_call(lags):
-    out_shape = [pltpu.VMEM((GROUPS * STRIP, LENGTH), BF16)] * 2
-    return call(strips_kernel, "strips", out_shape, (lags,))
+    in_specs = [pl.BlockSpec(memory_space=pltpu.HBM)] * 2 + [pl.BlockSpec(memory_space=pltpu.VMEM)]
+    out_shape = [pltpu.VMEM((ROWS, CHANS), BF16)]
+    out_shape += [pltpu.VMEM((GROUPS * STRIP, LENGTH), BF16)] * 2
+    return call(pre_kernel, "pre", out_shape, operands, scratch, in_specs=in_specs, flops=1 << 30)
 
 
 def d_inner_kernel(d_gated_ref, query_ref, tail_ref, taps_ref, out_ref):
@@ -223,16 +216,35 @@
     return (rounded + left).astype(BF16)
 
 
-def add_small_kernel(terms_ref, small_ref, other_small_ref, out_ref):
+def add_small_kernel(terms_ref, small_ref, other_small_ref, out_ref, parts_ref, sems):
     parts = two_parts(small_ref[...] + other_small_ref[...]).astype(F32)
-    parts = parts.reshape(CHANS, CHANS).astype(BF16)
-    for half in range(2):
-        out_ref[half, :, SHARE:] = parts
+    parts_ref[...] = parts.reshape(CHANS, CHANS).astype(BF16)
+    copies = [
+        pltpu.make_async_copy(parts_ref, out_ref.at[half, :, pl.ds(SHARE, CHANS)], sems.at[half])
+        for half in range(2)
+    ]
+    for copy in copies:
+        copy.start()
+    for copy in copies:
+        copy.wait()
 
 
 def add_small_call(*operands):
-    out_shape = pltpu.VMEM(operands[0].shape, BF16)
-    return call(add_small_kernel, "add_small", out_shape, operands, input_output_aliases={0: 0})
+    place = pl.BlockSpec(memory_space=pl.ANY)
+    spec = pl.BlockSpec(memory_space=pltpu.VMEM)
+    return pl.pallas_call(
+        add_small_kernel,
+        in_specs=[place, spec, spec],
+        out_specs=place,
+        out_shape=jax.ShapeDtypeStruct(operands[0].shape, BF16),
+        scratch_shapes=[pltpu.VMEM((CHANS, CHANS), BF16), pltpu.SemaphoreType.DMA((2,))],
+        input_output_aliases={0: 0},
+        compiler_params=pltpu.CompilerParams(vmem_limit_bytes=VMEM_LIMIT),
+        name="add_small",
+    )(
+        operands[0],
+        *(pltpu.with_memory_space_constraint(x, pltpu.VMEM) for x in operands[1:]),
+    )
 
 
 def place(g, n):
@@ -414,28 +426,28 @@
     pair = lax.ppermute(own, "co", swap)
     other_cot = lax.ppermute(cot, "co", swap)
 
-    d_gated = d_gated_call(cot, out_weight)
-    cross, tail, d_gated, lags = lax.optimization_barrier((cross, tail, d_gated, long_filter))
+    d_gated, strips, back_strips = pre_call(cot, out_weight, long_filter)
+    cross, tail, d_gated = lax.optimization_barrier((cross, tail, d_gated))
     cross_pair = lax.ppermute(cross, "co", swap)
-    strips, back_strips = strips_call(lags)
     d_inner = d_inner_call(d_gated, query, tail, taps)
     blocks = [d_inner] + [sent(d_inner, -distance) for distance in (1, 2, 3)]
     gated, inner, mixed = fwd_call(
         core, strips, pair, cross, cross_pair, key, value, query, tail, taps, skip
     )
     other_gated = lax.ppermute(gated, "co", swap)
-    terms = terms_call(core, cot, other_cot, gated, other_gated)
-    terms, inner, *blocks = lax.optimization_barrier((terms, inner, *blocks))
     d_short, head, small = bwd_call(
         core, *blocks, back_strips, mixed, key, value, pair, cross_pair, query, tail, inner,
         d_gated, taps, skip,
     )
+    other_gated, head, small = lax.optimization_barrier((other_gated, head, small))
     other_small = lax.ppermute(small, "co", swap)
-    following = sent(head, -1)
+    terms = terms_call(core, cot, other_cot, gated, other_gated)
+    terms, other_small = lax.optimization_barrier((terms, other_small))
     terms = add_small_call(terms, small, other_small)
-    terms, following = lax.optimization_barrier((terms, following))
+    terms, head = lax.optimization_barrier((terms, head))
     terms = terms.reshape(2 * SHARES, CHANS // SHARES, SHARE + CHANS)
     terms = lax.all_to_all(terms, CHIPS, 0, 0)
+    following = sent(head, -1)
     grad_query, grad_key, grad_value = input_grad_call(d_short, following, taps)
 
     shares = lax.all_to_all(total_call(terms, scale), DP, 0, 0)

time: 112 us -> 107 us (0.955)
  waiting for transfers between devices: 23.3 us -> 15.3 us
  local copies, waits for them, and re-layouts: 1.39 us -> 4.32 us
    all_to_all x1, waiting for transfers between devices: 15.2 us -> 0.01 us  [shards(): shares = lax.all_to_all(total_call(terms, scale), DP, 0, 0)]
    ppermute x5, waiting for transfers between devices: 7.86 us -> 15.3 us  [sent(): return lax.ppermute(block, CTX, route)]
    unnamed x15 -> x19, local copies, waits for them, and re-layouts: 0.69 us -> 3.62 us
    ppermute x5, starting transfers between devices: 7.98 us -> 9.26 us  [sent(): return lax.ppermute(block, CTX, route)]
    pallas_call x10 -> x8, Pallas kernels: 21 us -> 20.9 us  [call(): pl.pallas_call(kernel, out_shape=out_shape, scratch_shapes=list(scratch),...]
  transfers between devices with their start and end apart: 12 -> 12, of which waited for: 5 -> 2; matrix products, arithmetic and copies ran while one was open for 2% -> 2% of each run, Pallas kernels for 11% -> 16%
where the time goes in v7:
time: 107 us; the launch traced here: 106 us
  blocking collectives  41.2 us (39%)
  starting transfers between devices  22.3 us (21%)
  Pallas kernels  21 us (20%)
  waiting for transfers between devices  15.3 us (14%)
  local copies, waits for them, and re-layouts  4.32 us (4%)
    all_to_all x1, blocking collectives, shards(): terms = lax.all_to_all(terms, CHIPS, 0, 0)  41.2 us
    pallas_call x8, Pallas kernels, call(): pl.pallas_call(kernel, out_shape=out_shape, scratch_shapes=list(scratch),...  20.9 us
    ppermute x5, waiting for transfers between devices, sent(): return lax.ppermute(block, CTX, route)  15.3 us
    ppermute x5, starting transfers between devices, sent(): return lax.ppermute(block, CTX, route)  9.26 us
    ppermute x1, starting transfers between devices, shards(): cross = lax.ppermute(own, 'xh', [(0, 1)])  4.75 us
    all_to_all x1, starting transfers between devices, shards(): shares = lax.all_to_all(total_call(terms, scale), DP, 0, 0)  3.94 us
    unnamed x19, local copies, waits for them, and re-layouts  3.62 us
  transfers between devices with their start and end apart: 12, of which 2 were waited for; matrix products, arithmetic and copies ran while one was open for 2% of the time, Pallas kernels for 16%

profile of v7, /device:TPU:1, one launch (start us, length us, event | category | flops | bytes accessed | tf_op | source)
XLA Modules:
  0.0 105.9 jit_solution(16362208994075280563)
XLA Ops:
  0.6 1.5 %collective-permute-start.7 = (bf16[256,8192]{1,0:T(8,128)(2,1)}, bf16[256,8192]{1,0:T(8,128)(2,1)}, u32[]{:S(2)}, u32[]{:S(2)}) collective-permute-start(bf16[256,8192]{1,0:T(8,128)(2,1)} %bitcast.17), channel_id=1, source_target_pairs={{0,32},{32,0},{1,33},{33,1},{2,34},{34,2},{3,35},{35,3},{4,36},{36... | collective-permute-start | bytes 12582920 | tf_op jit(solution)/shard_map/ppermute | solution.py:427
  2.1 1.0 pad_maximum_fusion
  3.1 4.7 %collective-permute-start.1 = (bf16[256,512]{1,0:T(8,128)(2,1)S(1)}, bf16[256,512]{1,0:T(8,128)(2,1)S(1)}, u32[]{:S(2)}, u32[]{:S(2)}) collective-permute-start(bf16[256,512]{1,0:T(8,128)(2,1)S(1)} %pad_maximum_fusion), channel_id=1, source_target_pairs={{0,64},{1,65},{2,66},{3,67},{4,68},{5,69},{6,70},{7,71},{8,72},{9,... | collective-permute-start | bytes 786440 | tf_op jit(solution)/shard_map/ppermute | solution.py:425
  7.9 0.4 collective-permute-start
  8.3 0.7 slice_bitcast_fusion
  9.0 0.0 copy-start.1
  9.0 0.0 copy-start.4
  9.0 0.0 copy-start.2
  9.0 0.0 copy-start.3
  9.0 2.1 %collective-permute-start.2 = (bf16[16,256]{1,0:T(8,128)(2,1)S(1)}, bf16[16,256]{1,0:T(8,128)(2,1)S(1)}, u32[]{:S(2)}, u32[]{:S(2)}) collective-permute-start(bf16[16,256]{1,0:T(8,128)(2,1)S(1)} %slice_bitcast_fusion), channel_id=1, source_target_pairs={{0,32},{32,64},{64,96},{1,33},{33,65},{65,97},{2,34},{34,66},{66,9... | collective-permute-start | bytes 24584 | tf_op jit(solution)/shard_map/ppermute | solution.py:405
  11.0 0.0 copy-start.5
  11.0 0.7 copy-done.5
  11.8 0.0 copy-start.6
  11.8 5.1 %pre.1 = (bf16[256,256]{1,0:T(8,128)(2,1)S(1)}, bf16[512,1024]{1,0:T(8,128)(2,1)S(1)}, bf16[512,1024]{1,0:T(8,128)(2,1)S(1)}) custom-call(bf16[256,8192]{1,0:T(8,128)(2,1)} %bitcast.18, bf16[8192,256]{1,0:T(8,128)(2,1)} %weight_ref.1, bf16[16,1024]{1,0:T(8,128)(2,1)S(1)} %copy-done.5), custom_call_target="tpu_custom_call" | custom-call | flops 1073741824 | bytes 1024 | tf_op jit(solution)/shard_map/pre/pallas_call | solution.py:46
  16.9 0.0 copy-start.7
  16.9 1.0 copy-done.7
  17.9 0.0 collective-permute-done.2.tail_ref
  17.9 0.0 collective-permute-done.1.cross_ref
  17.9 0.5 collective-permute-start.3
  18.4 0.0 copy-done.1
  18.4 0.0 copy-done.4
  18.4 0.1 d_inner.1.d0_ref
  18.5 1.9 %collective-permute-start.4 = (bf16[256,256]{1,0:T(8,128)(2,1)S(1)}, bf16[256,256]{1,0:T(8,128)(2,1)S(1)}, u32[]{:S(2)}, u32[]{:S(2)}) collective-permute-start(bf16[256,256]{1,0:T(8,128)(2,1)S(1)} %d_inner.1.d0_ref), channel_id=1, source_target_pairs={{32,0},{64,32},{96,64},{33,1},{65,33},{97,65},{34,2},{66,34},{98,6... | collective-permute-start | bytes 393224 | tf_op jit(solution)/shard_map/ppermute | solution.py:405
  20.4 1.3 %collective-permute-start.5 = (bf16[256,256]{1,0:T(8,128)(2,1)S(1)}, bf16[256,256]{1,0:T(8,128)(2,1)S(1)}, u32[]{:S(2)}, u32[]{:S(2)}) collective-permute-start(bf16[256,256]{1,0:T(8,128)(2,1)S(1)} %d_inner.1.d0_ref), channel_id=1, source_target_pairs={{64,0},{96,32},{65,1},{97,33},{66,2},{98,34},{67,3},{99,35},{68,4}... | collective-permute-start | bytes 393224 | tf_op jit(solution)/shard_map/ppermute | solution.py:405
  21.7 0.0 collective-permute-done.pair_ref
  21.8 0.7 collective-permute-start.6
  22.4 0.0 collective-permute-done.3.cross_pair_ref
  22.4 0.0 copy-done.2
  22.5 0.0 copy-done.3
  22.5 0.0 copy-done.6
  22.5 0.0 copy-start.8
  22.5 1.2 %copy-done.8 = bf16[512,1024]{1,0:T(8,128)(2,1)S(1)} copy-done((bf16[512,1024]{1,0:T(8,128)(2,1)S(1)}, bf16[512,1024]{1,0:T(8,128)(2,1)}, u32[]{:S(2)}) %copy-start.8) | copy-done | bytes 1048600
  23.7 0.0 copy-start
  23.7 2.7 %fwd.1 = (bf16[256,256]{1,0:T(8,128)(2,1)S(1)}, f32[256,256]{1,0:T(8,128)S(1)}, bf16[256,256]{1,0:T(8,128)(2,1)S(1)}) custom-call(s32[1]{0:T(128)} %bitcast.core_ref, bf16[512,1024]{1,0:T(8,128)(2,1)S(1)} %copy-done.8, bf16[256,512]{1,0:T(8,128)(2,1)S(1)} %collective-permute-done.pair_ref, bf16[256,512]{1,0:T(8,128)(2,1)S(1)} %collective-permute-done.1.cross_ref, ...), custom_call_target="tpu_custom_call" | custom-call | flops 4294967296 | bytes 1024 | tf_op jit(solution)/shard_map/fwd/pallas_call | solution.py:46
  26.4 0.1 collective-permute-start.8
  26.5 0.0 collective-permute-done.4.d1_ref
  26.5 2.9 %collective-permute-done.5.d2_ref = bf16[256,256]{1,0:T(8,128)(2,1)S(1)} collective-permute-done((bf16[256,256]{1,0:T(8,128)(2,1)S(1)}, bf16[256,256]{1,0:T(8,128)(2,1)S(1)}, u32[]{:S(2)}, u32[]{:S(2)}) %collective-permute-start.5) | collective-permute-done | bytes 131104 | tf_op jit(solution)/shard_map/ppermute | solution.py:405
  29.4 0.0 collective-permute-done.6.d3_ref
  29.4 5.1 %bwd.1 = (f32[3,256,256]{2,1,0:T(8,128)S(1)}, f32[3,8,256]{2,1,0:T(8,128)S(1)}, f32[32,8,256]{2,1,0:T(8,128)S(1)}) custom-call(s32[1]{0:T(128)} %bitcast.core_ref, bf16[256,256]{1,0:T(8,128)(2,1)S(1)} %d_inner.1.d0_ref, bf16[256,256]{1,0:T(8,128)(2,1)S(1)} %collective-permute-done.4.d1_ref, bf16[256,256]{1,0:T(8,128)(2,1)S(1)} %collective-permute-done.5.d2_ref, ...), custom_call_target="tpu_custom_call" | custom-call | flops 1024 | bytes 1024 | tf_op jit(solution)/shard_map/bwd/pallas_call | solution.py:46
  34.5 0.0 collective-permute-done.8.other_gated_ref
  34.5 1.9 %collective-permute-start.9 = (f32[32,8,256]{2,1,0:T(8,128)S(1)}, f32[32,8,256]{2,1,0:T(8,128)S(1)}, u32[]{:S(2)}, u32[]{:S(2)}) collective-permute-start(f32[32,8,256]{2,1,0:T(8,128)S(1)} %get-tuple-element.47.small_ref), channel_id=1, source_target_pairs={{0,32},{32,0},{1,33},{33,1},{2,34},{34,2},{3,35},{35,3},{4,36},{36... | collective-permute-start | bytes 786440 | tf_op jit(solution)/shard_map/ppermute | solution.py:443
  36.4 0.0 collective-permute-done.7.other_cot_ref
  36.4 0.0 copy-done
  36.4 3.5 %terms.1.terms_ref = bf16[2,256,2304]{2,1,0:T(8,128)(2,1)S(1)} custom-call(s32[1]{0:T(128)} %bitcast.core_ref, bf16[256,8192]{1,0:T(8,128)(2,1)S(1)} %bitcast.19, bf16[256,8192]{1,0:T(8,128)(2,1)} %collective-permute-done.7.other_cot_ref, bf16[256,256]{1,0:T(8,128)(2,1)S(1)} %get-tuple-element.38.gated_ref, ...), custom_call_target="tpu_custom_call" | custom-call | flops 1073741824 | bytes 1024 | tf_op jit(solution)/shard_map/terms/pallas_call | solution.py:46
  39.9 0.0 collective-permute-done.9.other_small_ref
  39.9 0.1 add_small.1
  40.0 41.2 %all_to_all.10.refs_0_ = bf16[64,8,2304]{2,1,0:T(8,128)(2,1)S(1)} all-to-all(bf16[64,8,2304]{2,1,0:T(8,128)(2,1)S(1)} %bitcast.16), channel_id=1, replica_groups=mesh['xh'=2,'co'=2,'y'=4,'xl'=2,'z'=4] {'xh','y','xl','z'}, dimensions={0} | all-to-all | bytes 4718592 | tf_op jit(solution)/shard_map/all_to_all | solution.py:449
  81.2 1.4 %total.1 = bf16[32,8,2304]{2,1,0:T(8,128)(2,1)} custom-call(bf16[64,8,2304]{2,1,0:T(8,128)(2,1)S(1)} %all_to_all.10.refs_0_), custom_call_target="tpu_custom_call" | custom-call | flops 1024 | bytes 1024 | tf_op jit(solution)/shard_map/total/pallas_call | solution.py:46
  82.6 3.9 %all-to-all-start.1 = ((bf16[32,8,2304]{2,1,0:T(8,128)(2,1)}), bf16[32,8,2304]{2,1,0:T(8,128)(2,1)S(1)}, u32[]{:S(2)}, u32[]{:S(2)}) async-start(bf16[32,8,2304]{2,1,0:T(8,128)(2,1)} %total.1), calls=%async_computation.1 | async-start | bytes 2359296 | tf_op jit(solution)/shard_map/all_to_all | solution.py:453
  86.5 3.3 %collective-permute-start.10 = (f32[3,8,256]{2,1,0:T(8,128)S(1)}, f32[3,8,256]{2,1,0:T(8,128)S(1)}, u32[]{:S(2)}, u32[]{:S(2)}) collective-permute-start(f32[3,8,256]{2,1,0:T(8,128)S(1)} %get-tuple-element.51), channel_id=1, source_target_pairs={{32,0},{64,32},{96,64},{33,1},{65,33},{97,65},{34,2},{66,34},{98,6... | collective-permute-start | bytes 73736 | tf_op jit(solution)/shard_map/ppermute | solution.py:405
  89.9 0.7 copy.18
  90.5 12.4 %collective-permute-done.10.next_ref = f32[3,8,256]{2,1,0:T(8,128)S(1)} collective-permute-done((f32[3,8,256]{2,1,0:T(8,128)S(1)}, f32[3,8,256]{2,1,0:T(8,128)S(1)}, u32[]{:S(2)}, u32[]{:S(2)}) %collective-permute-start.10) | collective-permute-done | bytes 24608 | tf_op jit(solution)/shard_map/ppermute | solution.py:405
  102.9 0.9 input_grads.1
  103.8 0.0 all-to-all-done.1
  103.8 2.1 %spread.1 = (f32[2048,256]{1,0:T(8,128)}, f32[3,3,256]{2,1,0:T(4,128)}, f32[16,1024]{1,0:T(8,128)}, f32[1,256]{1,0:T(1,128)}) custom-call(bf16[256,2304]{1,0:T(8,128)(2,1)S(1)} %bitcast.20), custom_call_target="tpu_custom_call" | custom-call | flops 1024 | bytes 1024 | tf_op jit(solution)/shard_map/spread/pallas_call | solution.py:46
Async XLA Ops:
  0.6 35.8 %collective-permute-start.7 = (bf16[256,8192]{1,0:T(8,128)(2,1)}, bf16[256,8192]{1,0:T(8,128)(2,1)}, u32[]{:S(2)}, u32[]{:S(2)}) collective-permute-start(bf16[256,8192]{1,0:T(8,128)(2,1)} %bitcast.17), channel_id=1, source_target_pairs={{0,32},{32,0},{1,33},{33,1},{2,34},{34,2},{3,35},{35,3},{4,36},{36... | collective-permute-start | bytes 12582920 | tf_op jit(solution)/shard_map/ppermute | solution.py:427
  3.1 14.8 %collective-permute-start.1 = (bf16[256,512]{1,0:T(8,128)(2,1)S(1)}, bf16[256,512]{1,0:T(8,128)(2,1)S(1)}, u32[]{:S(2)}, u32[]{:S(2)}) collective-permute-start(bf16[256,512]{1,0:T(8,128)(2,1)S(1)} %pad_maximum_fusion), channel_id=1, source_target_pairs={{0,64},{1,65},{2,66},{3,67},{4,68},{5,69},{6,70},{7,71},{8,72},{9,... | collective-permute-start | bytes 786440 | tf_op jit(solution)/shard_map/ppermute | solution.py:425
  7.9 13.9 %collective-permute-start = (bf16[256,512]{1,0:T(8,128)(2,1)S(1)}, bf16[256,512]{1,0:T(8,128)(2,1)S(1)}, u32[]{:S(2)}, u32[]{:S(2)}) collective-permute-start(bf16[256,512]{1,0:T(8,128)(2,1)S(1)} %pad_maximum_fusion), channel_id=1, source_target_pairs={{0,32},{32,0},{1,33},{33,1},{2,34},{34,2},{3,35},{35,3},{4,36},{36... | collective-permute-start | bytes 786440 | tf_op jit(solution)/shard_map/ppermute | solution.py:426
  9.0 9.4 %copy-start.1 = (bf16[1,256,256]{2,1,0:T(8,128)(2,1)S(1)}, bf16[1,256,256]{2,1,0:T(8,128)(2,1)}, u32[]{:S(2)}) copy-start(bf16[1,256,256]{2,1,0:T(8,128)(2,1)} %param.8) | copy-start | bytes 393220
  9.0 9.4 %copy-start.4 = (f32[3,3,256]{2,1,0:T(4,128)S(1)}, f32[3,3,256]{2,1,0:T(4,128)}, u32[]{:S(2)}) copy-start(f32[3,3,256]{2,1,0:T(4,128)} %taps_ref.7) | copy-start | bytes 27652
  9.0 13.5 %copy-start.2 = (bf16[1,256,256]{2,1,0:T(8,128)(2,1)S(1)}, bf16[1,256,256]{2,1,0:T(8,128)(2,1)}, u32[]{:S(2)}) copy-start(bf16[1,256,256]{2,1,0:T(8,128)(2,1)} %param.10) | copy-start | bytes 393220
  9.0 13.5 %copy-start.3 = (bf16[1,256,256]{2,1,0:T(8,128)(2,1)S(1)}, bf16[1,256,256]{2,1,0:T(8,128)(2,1)}, u32[]{:S(2)}) copy-start(bf16[1,256,256]{2,1,0:T(8,128)(2,1)} %param.9) | copy-start | bytes 393220
  9.0 8.9 %collective-permute-start.2 = (bf16[16,256]{1,0:T(8,128)(2,1)S(1)}, bf16[16,256]{1,0:T(8,128)(2,1)S(1)}, u32[]{:S(2)}, u32[]{:S(2)}) collective-permute-start(bf16[16,256]{1,0:T(8,128)(2,1)S(1)} %slice_bitcast_fusion), channel_id=1, source_target_pairs={{0,32},{32,64},{64,96},{1,33},{33,65},{65,97},{2,34},{34,66},{66,9... | collective-permute-start | bytes 24584 | tf_op jit(solution)/shard_map/ppermute | solution.py:405
  11.0 0.8 copy-start.5
  11.8 10.7 %copy-start.6 = (f32[256]{0:T(256)S(1)}, f32[256]{0:T(256)}, u32[]{:S(2)}) copy-start(f32[256]{0:T(256)} %param.13) | copy-start | bytes 3076
  16.9 1.0 copy-start.7
  17.9 4.6 %collective-permute-start.3 = (bf16[256,512]{1,0:T(8,128)(2,1)S(1)}, bf16[256,512]{1,0:T(8,128)(2,1)S(1)}, u32[]{:S(2)}, u32[]{:S(2)}) collective-permute-start(bf16[256,512]{1,0:T(8,128)(2,1)S(1)} %collective-permute-done.1.cross_ref), channel_id=1, source_target_pairs={{0,32},{32,0},{1,33},{33,1},{2,34},{34,2},{3,35},{35,3},{4,36},{36... | collective-permute-start | bytes 786440 | tf_op jit(solution)/shard_map/ppermute | solution.py:431
  18.5 8.0 %collective-permute-start.4 = (bf16[256,256]{1,0:T(8,128)(2,1)S(1)}, bf16[256,256]{1,0:T(8,128)(2,1)S(1)}, u32[]{:S(2)}, u32[]{:S(2)}) collective-permute-start(bf16[256,256]{1,0:T(8,128)(2,1)S(1)} %d_inner.1.d0_ref), channel_id=1, source_target_pairs={{32,0},{64,32},{96,64},{33,1},{65,33},{97,65},{34,2},{66,34},{98,6... | collective-permute-start | bytes 393224 | tf_op jit(solution)/shard_map/ppermute | solution.py:405
  20.4 8.9 %collective-permute-start.5 = (bf16[256,256]{1,0:T(8,128)(2,1)S(1)}, bf16[256,256]{1,0:T(8,128)(2,1)S(1)}, u32[]{:S(2)}, u32[]{:S(2)}) collective-permute-start(bf16[256,256]{1,0:T(8,128)(2,1)S(1)} %d_inner.1.d0_ref), channel_id=1, source_target_pairs={{64,0},{96,32},{65,1},{97,33},{66,2},{98,34},{67,3},{99,35},{68,4}... | collective-permute-start | bytes 393224 | tf_op jit(solution)/shard_map/ppermute | solution.py:405
  21.8 7.6 %collective-permute-start.6 = (bf16[256,256]{1,0:T(8,128)(2,1)S(1)}, bf16[256,256]{1,0:T(8,128)(2,1)S(1)}, u32[]{:S(2)}, u32[]{:S(2)}) collective-permute-start(bf16[256,256]{1,0:T(8,128)(2,1)S(1)} %d_inner.1.d0_ref), channel_id=1, source_target_pairs={{96,0},{97,1},{98,2},{99,3},{100,4},{101,5},{102,6},{103,7},{104,8... | collective-permute-start | bytes 393224 | tf_op jit(solution)/shard_map/ppermute | solution.py:405
  22.5 1.2 %copy-start.8 = (bf16[512,1024]{1,0:T(8,128)(2,1)S(1)}, bf16[512,1024]{1,0:T(8,128)(2,1)}, u32[]{:S(2)}) copy-start(bf16[512,1024]{1,0:T(8,128)(2,1)} %copy-done.7) | copy-start | bytes 3145732
  23.7 12.7 %copy-start = (bf16[1,256,8192]{2,1,0:T(8,128)(2,1)S(1)}, bf16[1,256,8192]{2,1,0:T(8,128)(2,1)}, u32[]{:S(2)}) copy-start(bf16[1,256,8192]{2,1,0:T(8,128)(2,1)} %param.15) | copy-start | bytes 12582916
  26.4 8.1 %collective-permute-start.8 = (bf16[256,256]{1,0:T(8,128)(2,1)S(1)}, bf16[256,256]{1,0:T(8,128)(2,1)S(1)}, u32[]{:S(2)}, u32[]{:S(2)}) collective-permute-start(bf16[256,256]{1,0:T(8,128)(2,1)S(1)} %get-tuple-element.38.gated_ref), channel_id=1, source_target_pairs={{0,32},{32,0},{1,33},{33,1},{2,34},{34,2},{3,35},{35,3},{4,36},{36... | collective-permute-start | bytes 393224 | tf_op jit(solution)/shard_map/ppermute | solution.py:437
  34.5 5.4 %collective-permute-start.9 = (f32[32,8,256]{2,1,0:T(8,128)S(1)}, f32[32,8,256]{2,1,0:T(8,128)S(1)}, u32[]{:S(2)}, u32[]{:S(2)}) collective-permute-start(f32[32,8,256]{2,1,0:T(8,128)S(1)} %get-tuple-element.47.small_ref), channel_id=1, source_target_pairs={{0,32},{32,0},{1,33},{33,1},{2,34},{34,2},{3,35},{35,3},{4,36},{36... | collective-permute-start | bytes 786440 | tf_op jit(solution)/shard_map/ppermute | solution.py:443
  82.6 21.2 %all-to-all-start.1 = ((bf16[32,8,2304]{2,1,0:T(8,128)(2,1)}), bf16[32,8,2304]{2,1,0:T(8,128)(2,1)S(1)}, u32[]{:S(2)}, u32[]{:S(2)}) async-start(bf16[32,8,2304]{2,1,0:T(8,128)(2,1)} %total.1), calls=%async_computation.1 | async-start | bytes 2359296 | tf_op jit(solution)/shard_map/all_to_all | solution.py:453
  86.5 16.4 %collective-permute-start.10 = (f32[3,8,256]{2,1,0:T(8,128)S(1)}, f32[3,8,256]{2,1,0:T(8,128)S(1)}, u32[]{:S(2)}, u32[]{:S(2)}) collective-permute-start(f32[3,8,256]{2,1,0:T(8,128)S(1)} %get-tuple-element.51), channel_id=1, source_target_pairs={{32,0},{64,32},{96,64},{33,1},{65,33},{97,65},{34,2},{66,34},{98,6... | collective-permute-start | bytes 73736 | tf_op jit(solution)/shard_map/ppermute | solution.py:405

commit v8 on v7

--- a/solution.py
+++ b/solution.py
@@ -23,7 +23,6 @@
 PAD = 128
 WIDE = LENGTH + PAD
 FEATS = 8192
-SMALL = 32
 TAIL = 16
 SHARES = 32
 SHARE = FEATS // 4
@@ -110,10 +109,12 @@
 
 
 def pre_kernel(
-    cot_ref, weight_ref, filter_ref, d_gated_ref, strips_ref, back_strips_ref, cot_buffer,
-    weight_buffer, sems,
+    cot_ref, weight_ref, lags_ref, d_gated_ref, strips_ref, cot_buffer, weight_buffer, filter_ref,
+    sems, lags_sem,
 ):
     tile = FEATS // PIECES
+    lags_copy = pltpu.make_async_copy(lags_ref, filter_ref, lags_sem)
+    lags_copy.start()
     copies = []
     for n in range(PIECES):
         piece = slice(n * tile, (n + 1) * tile)
@@ -124,10 +125,10 @@
         for copy in pair:
             copy.start()
         copies.append(pair)
-    for ref, turned in ((strips_ref, True), (back_strips_ref, False)):
-        lines = lines_of(filter_ref, turned)
-        for g in range(GROUPS):
-            ref[g * STRIP : (g + 1) * STRIP, :] = strip_of(lines[g : g + 1])
+    lags_copy.wait()
+    lines = lines_of(filter_ref, True)
+    for g in range(GROUPS):
+        strips_ref[g * STRIP : (g + 1) * STRIP, :] = strip_of(lines[g : g + 1])
     total = jnp.zeros((ROWS, CHANS), F32)
     for n in range(PIECES):
         for copy in copies[n]:
@@ -141,11 +142,15 @@
     scratch = [
         pltpu.VMEM((PIECES, ROWS, tile), BF16),
         pltpu.VMEM((PIECES, tile, CHANS), BF16),
+        pltpu.VMEM((GROUPS, LENGTH), BF16),
         pltpu.SemaphoreType.DMA((2, PIECES)),
-    ]
-    in_specs = [pl.BlockSpec(memory_space=pltpu.HBM)] * 2 + [pl.BlockSpec(memory_space=pltpu.VMEM)]
-    out_shape = [pltpu.VMEM((ROWS, CHANS), BF16)]
-    out_shape += [pltpu.VMEM((GROUPS * STRIP, LENGTH), BF16)] * 2
+        pltpu.SemaphoreType.DMA,
+    ]
+    in_specs = [pl.BlockSpec(memory_space=pltpu.HBM)] * 3
+    out_shape = [
+        pltpu.VMEM((ROWS, CHANS), BF16),
+        pltpu.VMEM((GROUPS * STRIP, LENGTH), BF16),
+    ]
     return call(pre_kernel, "pre", out_shape, operands, scratch, in_specs=in_specs, flops=1 << 30)
 
 
@@ -161,8 +166,7 @@
 def fwd_kernel(
     core_ref, strips_ref, pair_ref, cross_ref, cross_pair_ref, key_ref, value_ref, query_ref,
     tail_ref, taps_ref, skip_ref,
-    gated_ref, inner_ref, mixed_ref,
-    signal_ref,
+    gated_ref, inner_ref, signal_ref,
 ):
     upper = core_ref[0] == 1
     pair = pair_ref[...].astype(F32)
@@ -175,7 +179,6 @@
     k_short = short_sum(taps_ref, 1, [part[:, :CHANS] for part in shifted])
     v_short = short_sum(taps_ref, 2, [part[:, CHANS:] for part in shifted])
     mixed = (k_short * v_short).astype(BF16)
-    mixed_ref[...] = mixed[LENGTH - ROWS :]
     signal_ref[: ROWS - STRIP, :] = jnp.zeros((ROWS - STRIP, CHANS), BF16)
     signal_ref[ROWS - STRIP :, :] = mixed
     inner = all_strips(strips_ref, signal_ref) + skip_ref[...] * mixed[LENGTH - ROWS :].astype(F32)
@@ -188,10 +191,9 @@
     out_shape = [
         pltpu.VMEM((ROWS, CHANS), BF16),
         pltpu.VMEM((ROWS, CHANS), F32),
-        pltpu.VMEM((ROWS, CHANS), BF16),
-    ]
-    scratch = [pltpu.VMEM((LENGTH + ROWS - STRIP, CHANS), BF16)]
-    return call(fwd_kernel, "fwd", out_shape, operands, scratch, 1, 4 << 30)
+        pltpu.VMEM((LENGTH + ROWS - STRIP, CHANS), BF16),
+    ]
+    return call(fwd_kernel, "fwd", out_shape, operands, (), 1, 4 << 30)
 
 
 def terms_kernel(core_ref, own_cot_ref, other_cot_ref, gated_ref, other_gated_ref, out_ref):
@@ -252,17 +254,70 @@
     return row % SHARES, row // SHARES
 
 
+def turn_matrix(size, block):
+    row = lax.broadcasted_iota(jnp.int32, (size, size), 0)
+    col = lax.broadcasted_iota(jnp.int32, (size, size), 1)
+    return ((row // block) * block + (block - 1 - row % block) == col).astype(F32)
+
+
+def lag_kernel(d_inner_ref, signal_ref, filter_ref, outer_ref, stack_ref, sums_ref):
+    turn = turn_matrix(ROWS, STRIP).astype(BF16)
+    turned = jnp.dot(turn, d_inner_ref[...], preferred_element_type=F32)
+    ids = lane_groups(STRIP)
+    outer_ref[:, LENGTH:] = jnp.zeros((GROUPS * STRIP, PAD), F32)
+    for n in range(ROWS // STRIP):
+        piece = turned[n * STRIP : (n + 1) * STRIP]
+        for g in range(GROUPS):
+            stack_ref[g * STRIP : (g + 1) * STRIP, :] = jnp.where(ids == g, piece, 0.0).astype(BF16)
+        term = lax.dot_general(
+            stack_ref[...],
+            signal_ref[n * STRIP : n * STRIP + LENGTH, :],
+            (((1,), (1,)), ((), ())),
+            preferred_element_type=F32,
+        )
+        if n == 0:
+            outer_ref[:, :LENGTH] = term
+        else:
+            outer_ref[:, :LENGTH] += term
+    for g in range(GROUPS):
+        rows = outer_ref[g * STRIP : (g + 1) * STRIP, :]
+        skewed = pltpu.roll(rows, WIDE - (STRIP - 1), 1, stride=1, stride_axis=0)
+        sums_ref[g : g + 1, :] = jnp.sum(skewed, axis=0, keepdims=True)
+    sums = pltpu.roll(sums_ref[...], STRIP - 1, 1)
+    turn = turn_matrix(CHANS, CHANS)
+    last = LENGTH // CHANS - 1
+    for n in range(LENGTH // CHANS):
+        filter_ref[:, n * CHANS : (n + 1) * CHANS] = jnp.dot(
+            sums[:, (last - n) * CHANS : (last - n + 1) * CHANS],
+            turn,
+            precision=lax.Precision.HIGHEST,
+            preferred_element_type=F32,
+        )
+
+
+def lag_call(*operands):
+    scratch = [
+        pltpu.VMEM((GROUPS * STRIP, WIDE), F32),
+        pltpu.VMEM((GROUPS * STRIP, CHANS), BF16),
+        pltpu.VMEM((GROUPS, WIDE), F32),
+    ]
+    return call(lag_kernel, "lag_sums", pltpu.VMEM((GROUPS, LENGTH), F32), operands, scratch)
+
+
 def bwd_kernel(
-    core_ref, d0_ref, d1_ref, d2_ref, d3_ref, strips_ref, mixed_ref, key_ref, value_ref, pair_ref,
-    cross_pair_ref, query_ref, tail_ref, inner_ref, d_gated_ref, taps_ref, skip_ref,
+    core_ref, d0_ref, d1_ref, d2_ref, d3_ref, lags_ref, filter_ref, signal_ref, key_ref, value_ref,
+    pair_ref, cross_pair_ref, query_ref, tail_ref, inner_ref, d_gated_ref, taps_ref, skip_ref,
     d_short_ref, head_ref, small_ref,
-    ahead_ref, outer_ref, stack_ref,
+    strips_ref, ahead_ref,
 ):
     for n, ref in enumerate((d0_ref, d1_ref, d2_ref, d3_ref)):
         ahead_ref[n * ROWS : (n + 1) * ROWS, :] = ref[...]
     ahead_ref[LENGTH:, :] = jnp.zeros((ROWS, CHANS), BF16)
+    lines = lines_of(lags_ref, False)
+    for g in range(GROUPS):
+        strips_ref[g * STRIP : (g + 1) * STRIP, :] = strip_of(lines[g : g + 1])
     d_inner = d0_ref[...].astype(F32)
-    mixed = mixed_ref[...]
+    mixed = signal_ref[LENGTH - STRIP :, :]
     d_mixed = all_strips(strips_ref, ahead_ref) + skip_ref[...] * d_inner
 
     upper = core_ref[0] == 1
@@ -282,34 +337,10 @@
             small_ref[3 * i + j, 2:3, :] = jnp.sum(grad * parts[j], axis=0, keepdims=True)
     small_ref[9, 2:3, :] = jnp.sum(d_inner * mixed.astype(F32), axis=0, keepdims=True)
 
-    row = lax.broadcasted_iota(jnp.int32, (ROWS, ROWS), 0)
-    col = lax.broadcasted_iota(jnp.int32, (ROWS, ROWS), 1)
-    turn = ((row // SMALL) * SMALL + (SMALL - 1 - row % SMALL) == col).astype(F32).astype(BF16)
-    turned = jnp.dot(turn, mixed, preferred_element_type=F32)
-    ids = lane_groups(SMALL)
-    for part in range(ROWS // SMALL):
-        piece = turned[part * SMALL : (part + 1) * SMALL]
-        for g in range(GROUPS):
-            stack_ref[g * SMALL : (g + 1) * SMALL, :] = jnp.where(ids == g, piece, 0.0).astype(BF16)
-        term = lax.dot_general(
-            stack_ref[...],
-            ahead_ref[part * SMALL : part * SMALL + LENGTH, :],
-            (((1,), (1,)), ((), ())),
-            preferred_element_type=F32,
-        )
-        if part == 0:
-            outer_ref[:, :LENGTH] = term
-        else:
-            outer_ref[:, :LENGTH] += term
-    outer_ref[:, LENGTH:] = jnp.zeros((GROUPS * SMALL, PAD), F32)
     for g in range(GROUPS):
-        skewed = pltpu.roll(
-            outer_ref[g * SMALL : (g + 1) * SMALL, :], WIDE - (SMALL - 1), 1, stride=1, stride_axis=0
-        )
-        sums = jnp.sum(skewed[:, :LENGTH], axis=0, keepdims=True)
         for n in range(LENGTH // CHANS):
             share, slot = place(g, n)
-            small_ref[share, slot : slot + 1, :] = sums[:, n * CHANS : (n + 1) * CHANS]
+            small_ref[share, slot : slot + 1, :] = filter_ref[g : g + 1, n * CHANS : (n + 1) * CHANS]
 
 
 def bwd_call(*operands):
@@ -319,9 +350,8 @@
         pltpu.VMEM((SHARES, SEGMENT, CHANS), F32),
     ]
     scratch = [
+        pltpu.VMEM((GROUPS * STRIP, LENGTH), BF16),
         pltpu.VMEM((LENGTH + ROWS, CHANS), BF16),
-        pltpu.VMEM((GROUPS * SMALL, WIDE), F32),
-        pltpu.VMEM((GROUPS * SMALL, CHANS), BF16),
     ]
     return call(bwd_kernel, "bwd", out_shape, operands, scratch, 1)
 
@@ -426,18 +456,19 @@
     pair = lax.ppermute(own, "co", swap)
     other_cot = lax.ppermute(cot, "co", swap)
 
-    d_gated, strips, back_strips = pre_call(cot, out_weight, long_filter)
+    d_gated, strips = pre_call(cot, out_weight, long_filter)
     cross, tail, d_gated = lax.optimization_barrier((cross, tail, d_gated))
     cross_pair = lax.ppermute(cross, "co", swap)
     d_inner = d_inner_call(d_gated, query, tail, taps)
     blocks = [d_inner] + [sent(d_inner, -distance) for distance in (1, 2, 3)]
-    gated, inner, mixed = fwd_call(
+    gated, inner, signal = fwd_call(
         core, strips, pair, cross, cross_pair, key, value, query, tail, taps, skip
     )
     other_gated = lax.ppermute(gated, "co", swap)
+    lag_sums = lag_call(d_inner, signal)
     d_short, head, small = bwd_call(
-        core, *blocks, back_strips, mixed, key, value, pair, cross_pair, query, tail, inner,
-        d_gated, taps, skip,
+        core, *blocks, long_filter, lag_sums, signal, key, value, pair, cross_pair, query, tail,
+        inner, d_gated, taps, skip,
     )
     other_gated, head, small = lax.optimization_barrier((other_gated, head, small))
     other_small = lax.ppermute(small, "co", swap)

time: 107 us -> 106 us (level)
  local copies, waits for them, and re-layouts: 4.32 us -> 1.39 us
  Pallas kernels: 21 us -> 23.4 us
  blocking collectives: 41.2 us -> 43.1 us
  waiting for transfers between devices: 15.3 us -> 13.6 us
    unnamed x19 -> x15, local copies, waits for them, and re-layouts: 3.62 us -> 0.69 us
    pallas_call x8 -> x9, Pallas kernels: 20.9 us -> 23.3 us  [call(): pl.pallas_call(kernel, out_shape=out_shape, scratch_shapes=list(scratch),...]
    all_to_all x1, blocking collectives: 41.2 us -> 43.1 us  [shards(): terms = lax.all_to_all(terms, CHIPS, 0, 0)]
    ppermute x5, waiting for transfers between devices: 15.3 us -> 13.6 us  [sent(): return lax.ppermute(block, CTX, route)]
  transfers between devices with their start and end apart: 12 -> 12, of which waited for: 2 -> 2; matrix products, arithmetic and copies ran while one was open for 2% -> 2% of each run, Pallas kernels for 16% -> 19%
where the time goes in v8:
time: 106 us
  blocking collectives  43.1 us (41%)
  Pallas kernels  23.4 us (22%)
  starting transfers between devices  22.4 us (21%)
  waiting for transfers between devices  13.6 us (13%)
  local copies, waits for them, and re-layouts  1.39 us (1%)
    all_to_all x1, blocking collectives, shards(): terms = lax.all_to_all(terms, CHIPS, 0, 0)  43.1 us
    pallas_call x9, Pallas kernels, call(): pl.pallas_call(kernel, out_shape=out_shape, scratch_shapes=list(scratch),...  23.3 us
    ppermute x5, waiting for transfers between devices, sent(): return lax.ppermute(block, CTX, route)  13.6 us
    ppermute x5, starting transfers between devices, sent(): return lax.ppermute(block, CTX, route)  9.27 us
    ppermute x1, starting transfers between devices, shards(): cross = lax.ppermute(own, 'xh', [(0, 1)])  4.75 us
    all_to_all x1, starting transfers between devices, shards(): shares = lax.all_to_all(total_call(terms, scale), DP, 0, 0)  3.94 us
  transfers between devices with their start and end apart: 12, of which 2 were waited for; matrix products, arithmetic and copies ran while one was open for 2% of the time, Pallas kernels for 19%

profile of v8, /device:TPU:1, one launch (start us, length us, event | category | flops | bytes accessed | tf_op | source)
XLA Modules:
  0.0 105.8 jit_solution(8512023935479374882)
XLA Ops:
  0.6 1.5 %collective-permute-start.7 = (bf16[256,8192]{1,0:T(8,128)(2,1)}, bf16[256,8192]{1,0:T(8,128)(2,1)}, u32[]{:S(2)}, u32[]{:S(2)}) collective-permute-start(bf16[256,8192]{1,0:T(8,128)(2,1)} %bitcast.17), channel_id=1, source_target_pairs={{0,32},{32,0},{1,33},{33,1},{2,34},{34,2},{3,35},{35,3},{4,36},{36... | collective-permute-start | bytes 12582920 | tf_op jit(solution)/shard_map/ppermute | solution.py:457
  2.1 1.0 pad_maximum_fusion
  3.1 4.7 %collective-permute-start.1 = (bf16[256,512]{1,0:T(8,128)(2,1)S(1)}, bf16[256,512]{1,0:T(8,128)(2,1)S(1)}, u32[]{:S(2)}, u32[]{:S(2)}) collective-permute-start(bf16[256,512]{1,0:T(8,128)(2,1)S(1)} %pad_maximum_fusion), channel_id=1, source_target_pairs={{0,64},{1,65},{2,66},{3,67},{4,68},{5,69},{6,70},{7,71},{8,72},{9,... | collective-permute-start | bytes 786440 | tf_op jit(solution)/shard_map/ppermute | solution.py:455
  7.9 0.4 collective-permute-start
  8.3 0.7 slice_bitcast_fusion
  9.0 0.0 copy-start.1
  9.0 0.0 copy-start.5
  9.0 0.0 copy-start.2
  9.0 0.0 copy-start.3
  9.0 0.0 copy-start.6
  9.0 2.1 %collective-permute-start.2 = (bf16[16,256]{1,0:T(8,128)(2,1)S(1)}, bf16[16,256]{1,0:T(8,128)(2,1)S(1)}, u32[]{:S(2)}, u32[]{:S(2)}) collective-permute-start(bf16[16,256]{1,0:T(8,128)(2,1)S(1)} %slice_bitcast_fusion), channel_id=1, source_target_pairs={{0,32},{32,64},{64,96},{1,33},{33,65},{65,97},{2,34},{34,66},{66,9... | collective-permute-start | bytes 24584 | tf_op jit(solution)/shard_map/ppermute | solution.py:435
  11.0 6.6 %pre.1 = (bf16[256,256]{1,0:T(8,128)(2,1)S(1)}, bf16[512,1024]{1,0:T(8,128)(2,1)S(1)}) custom-call(bf16[256,8192]{1,0:T(8,128)(2,1)} %bitcast.18, bf16[8192,256]{1,0:T(8,128)(2,1)} %weight_ref.1, bf16[16,1024]{1,0:T(8,128)(2,1)} %lags_ref.3), custom_call_target="tpu_custom_call" | custom-call | flops 1073741824 | bytes 1024 | tf_op jit(solution)/shard_map/pre/pallas_call | solution.py:45
  17.6 0.0 collective-permute-done.2.tail_ref
  17.6 0.0 collective-permute-done.1.cross_ref
  17.6 0.6 collective-permute-start.3
  18.2 0.0 copy-done.1
  18.2 0.0 copy-done.5
  18.2 0.1 d_inner.1.d_inner_ref.d0_ref
  18.3 1.9 %collective-permute-start.4 = (bf16[256,256]{1,0:T(8,128)(2,1)S(1)}, bf16[256,256]{1,0:T(8,128)(2,1)S(1)}, u32[]{:S(2)}, u32[]{:S(2)}) collective-permute-start(bf16[256,256]{1,0:T(8,128)(2,1)S(1)} %d_inner.1.d_inner_ref.d0_ref), channel_id=1, source_target_pairs={{32,0},{64,32},{96,64},{33,1},{65,33},{97,65},{34,2},{66,34},{98,6... | collective-permute-start | bytes 393224 | tf_op jit(solution)/shard_map/ppermute | solution.py:435
  20.3 1.3 %collective-permute-start.5 = (bf16[256,256]{1,0:T(8,128)(2,1)S(1)}, bf16[256,256]{1,0:T(8,128)(2,1)S(1)}, u32[]{:S(2)}, u32[]{:S(2)}) collective-permute-start(bf16[256,256]{1,0:T(8,128)(2,1)S(1)} %d_inner.1.d_inner_ref.d0_ref), channel_id=1, source_target_pairs={{64,0},{96,32},{65,1},{97,33},{66,2},{98,34},{67,3},{99,35},{68,4}... | collective-permute-start | bytes 393224 | tf_op jit(solution)/shard_map/ppermute | solution.py:435
  21.6 0.0 collective-permute-done.pair_ref
  21.6 0.7 collective-permute-start.6
  22.3 0.0 collective-permute-done.3.cross_pair_ref
  22.3 0.0 copy-done.2
  22.3 0.0 copy-done.3
  22.3 0.0 copy-done.6
  22.3 0.0 copy-start.4
  22.3 0.0 copy-start
  22.3 2.7 %fwd.1 = (bf16[256,256]{1,0:T(8,128)(2,1)S(1)}, f32[256,256]{1,0:T(8,128)S(1)}, bf16[1248,256]{1,0:T(8,128)(2,1)S(1)}) custom-call(s32[1]{0:T(128)} %bitcast.core_ref, bf16[512,1024]{1,0:T(8,128)(2,1)S(1)} %get-tuple-element.33.strips_ref, bf16[256,512]{1,0:T(8,128)(2,1)S(1)} %collective-permute-done.pair_ref, ...), custom_call_target="tpu_custom_call" | custom-call | flops 4294967296 | bytes 1024 | tf_op jit(solution)/shard_map/fwd/pallas_call | solution.py:45
  25.0 0.1 collective-permute-start.8
  25.1 3.4 %lag_sums.1.filter_ref = f32[16,1024]{1,0:T(8,128)S(1)} custom-call(bf16[256,256]{1,0:T(8,128)(2,1)S(1)} %d_inner.1.d_inner_ref.d0_ref, bf16[1248,256]{1,0:T(8,128)(2,1)S(1)} %get-tuple-element.39.signal_ref), custom_call_target="tpu_custom_call" | custom-call | flops 1024 | bytes 1024 | tf_op jit(solution)/shard_map/lag_sums/pallas_call | solution.py:45
  28.5 0.0 collective-permute-done.4.d1_ref
  28.5 0.7 collective-permute-done.5.d2_ref
  29.2 0.0 collective-permute-done.6.d3_ref
  29.2 0.0 copy-done.4
  29.2 2.7 %bwd.1 = (f32[3,256,256]{2,1,0:T(8,128)S(1)}, f32[3,8,256]{2,1,0:T(8,128)S(1)}, f32[32,8,256]{2,1,0:T(8,128)S(1)}) custom-call(s32[1]{0:T(128)} %bitcast.core_ref, bf16[256,256]{1,0:T(8,128)(2,1)S(1)} %d_inner.1.d_inner_ref.d0_ref, bf16[256,256]{1,0:T(8,128)(2,1)S(1)} %collective-permute-done.4.d1_ref, bf16[256,256]{1,0:T(8,128)(2,1)S(1)} %collective-permute-done.5.d2_ref, ...), custom_call_target="tpu_custom_call" | custom-call | flops 1024 | bytes 1024 | tf_op jit(solution)/shard_map/bwd/pallas_call | solution.py:45
  31.9 0.0 collective-permute-done.8.other_gated_ref
  31.9 1.9 %collective-permute-start.9 = (f32[32,8,256]{2,1,0:T(8,128)S(1)}, f32[32,8,256]{2,1,0:T(8,128)S(1)}, u32[]{:S(2)}, u32[]{:S(2)}) collective-permute-start(f32[32,8,256]{2,1,0:T(8,128)S(1)} %get-tuple-element.45.small_ref), channel_id=1, source_target_pairs={{0,32},{32,0},{1,33},{33,1},{2,34},{34,2},{3,35},{35,3},{4,36},{36... | collective-permute-start | bytes 786440 | tf_op jit(solution)/shard_map/ppermute | solution.py:474
  33.8 0.0 collective-permute-done.7.other_cot_ref
  33.8 0.0 copy-done
  33.9 3.5 %terms.1.terms_ref = bf16[2,256,2304]{2,1,0:T(8,128)(2,1)S(1)} custom-call(s32[1]{0:T(128)} %bitcast.core_ref, bf16[256,8192]{1,0:T(8,128)(2,1)S(1)} %bitcast.19, bf16[256,8192]{1,0:T(8,128)(2,1)} %collective-permute-done.7.other_cot_ref, bf16[256,256]{1,0:T(8,128)(2,1)S(1)} %get-tuple-element.37.gated_ref, ...), custom_call_target="tpu_custom_call" | custom-call | flops 1073741824 | bytes 1024 | tf_op jit(solution)/shard_map/terms/pallas_call | solution.py:45
  37.3 0.0 collective-permute-done.9.other_small_ref
  37.3 0.1 add_small.1
  37.4 43.1 %all_to_all.10.refs_0_ = bf16[64,8,2304]{2,1,0:T(8,128)(2,1)S(1)} all-to-all(bf16[64,8,2304]{2,1,0:T(8,128)(2,1)S(1)} %bitcast.16), channel_id=1, replica_groups=mesh['xh'=2,'co'=2,'y'=4,'xl'=2,'z'=4] {'xh','y','xl','z'}, dimensions={0} | all-to-all | bytes 4718592 | tf_op jit(solution)/shard_map/all_to_all | solution.py:480
  80.6 1.4 %total.1 = bf16[32,8,2304]{2,1,0:T(8,128)(2,1)} custom-call(bf16[64,8,2304]{2,1,0:T(8,128)(2,1)S(1)} %all_to_all.10.refs_0_), custom_call_target="tpu_custom_call" | custom-call | flops 1024 | bytes 1024 | tf_op jit(solution)/shard_map/total/pallas_call | solution.py:45
  81.9 3.9 %all-to-all-start.1 = ((bf16[32,8,2304]{2,1,0:T(8,128)(2,1)}), bf16[32,8,2304]{2,1,0:T(8,128)(2,1)S(1)}, u32[]{:S(2)}, u32[]{:S(2)}) async-start(bf16[32,8,2304]{2,1,0:T(8,128)(2,1)} %total.1), calls=%async_computation.1 | async-start | bytes 2359296 | tf_op jit(solution)/shard_map/all_to_all | solution.py:484
  85.9 3.3 %collective-permute-start.10 = (f32[3,8,256]{2,1,0:T(8,128)S(1)}, f32[3,8,256]{2,1,0:T(8,128)S(1)}, u32[]{:S(2)}, u32[]{:S(2)}) collective-permute-start(f32[3,8,256]{2,1,0:T(8,128)S(1)} %get-tuple-element.49), channel_id=1, source_target_pairs={{32,0},{64,32},{96,64},{33,1},{65,33},{97,65},{34,2},{66,34},{98,6... | collective-permute-start | bytes 73736 | tf_op jit(solution)/shard_map/ppermute | solution.py:435
  89.2 0.7 copy.18
  89.9 12.9 %collective-permute-done.10.next_ref = f32[3,8,256]{2,1,0:T(8,128)S(1)} collective-permute-done((f32[3,8,256]{2,1,0:T(8,128)S(1)}, f32[3,8,256]{2,1,0:T(8,128)S(1)}, u32[]{:S(2)}, u32[]{:S(2)}) %collective-permute-start.10) | collective-permute-done | bytes 24608 | tf_op jit(solution)/shard_map/ppermute | solution.py:435
  102.8 0.9 input_grads.1
  103.7 0.0 all-to-all-done.1
  103.7 2.1 %spread.1 = (f32[2048,256]{1,0:T(8,128)}, f32[3,3,256]{2,1,0:T(4,128)}, f32[16,1024]{1,0:T(8,128)}, f32[1,256]{1,0:T(1,128)}) custom-call(bf16[256,2304]{1,0:T(8,128)(2,1)S(1)} %bitcast.20), custom_call_target="tpu_custom_call" | custom-call | flops 1024 | bytes 1024 | tf_op jit(solution)/shard_map/spread/pallas_call | solution.py:45
Async XLA Ops:
  0.6 33.2 %collective-permute-start.7 = (bf16[256,8192]{1,0:T(8,128)(2,1)}, bf16[256,8192]{1,0:T(8,128)(2,1)}, u32[]{:S(2)}, u32[]{:S(2)}) collective-permute-start(bf16[256,8192]{1,0:T(8,128)(2,1)} %bitcast.17), channel_id=1, source_target_pairs={{0,32},{32,0},{1,33},{33,1},{2,34},{34,2},{3,35},{35,3},{4,36},{36... | collective-permute-start | bytes 12582920 | tf_op jit(solution)/shard_map/ppermute | solution.py:457
  3.1 14.5 %collective-permute-start.1 = (bf16[256,512]{1,0:T(8,128)(2,1)S(1)}, bf16[256,512]{1,0:T(8,128)(2,1)S(1)}, u32[]{:S(2)}, u32[]{:S(2)}) collective-permute-start(bf16[256,512]{1,0:T(8,128)(2,1)S(1)} %pad_maximum_fusion), channel_id=1, source_target_pairs={{0,64},{1,65},{2,66},{3,67},{4,68},{5,69},{6,70},{7,71},{8,72},{9,... | collective-permute-start | bytes 786440 | tf_op jit(solution)/shard_map/ppermute | solution.py:455
  7.9 13.7 %collective-permute-start = (bf16[256,512]{1,0:T(8,128)(2,1)S(1)}, bf16[256,512]{1,0:T(8,128)(2,1)S(1)}, u32[]{:S(2)}, u32[]{:S(2)}) collective-permute-start(bf16[256,512]{1,0:T(8,128)(2,1)S(1)} %pad_maximum_fusion), channel_id=1, source_target_pairs={{0,32},{32,0},{1,33},{33,1},{2,34},{34,2},{3,35},{35,3},{4,36},{36... | collective-permute-start | bytes 786440 | tf_op jit(solution)/shard_map/ppermute | solution.py:456
  9.0 9.2 %copy-start.1 = (bf16[1,256,256]{2,1,0:T(8,128)(2,1)S(1)}, bf16[1,256,256]{2,1,0:T(8,128)(2,1)}, u32[]{:S(2)}) copy-start(bf16[1,256,256]{2,1,0:T(8,128)(2,1)} %param.8) | copy-start | bytes 393220
  9.0 9.2 %copy-start.5 = (f32[3,3,256]{2,1,0:T(4,128)S(1)}, f32[3,3,256]{2,1,0:T(4,128)}, u32[]{:S(2)}) copy-start(f32[3,3,256]{2,1,0:T(4,128)} %taps_ref.7) | copy-start | bytes 27652
  9.0 13.3 %copy-start.2 = (bf16[1,256,256]{2,1,0:T(8,128)(2,1)S(1)}, bf16[1,256,256]{2,1,0:T(8,128)(2,1)}, u32[]{:S(2)}) copy-start(bf16[1,256,256]{2,1,0:T(8,128)(2,1)} %param.10) | copy-start | bytes 393220
  9.0 13.3 %copy-start.3 = (bf16[1,256,256]{2,1,0:T(8,128)(2,1)S(1)}, bf16[1,256,256]{2,1,0:T(8,128)(2,1)}, u32[]{:S(2)}) copy-start(bf16[1,256,256]{2,1,0:T(8,128)(2,1)} %param.9) | copy-start | bytes 393220
  9.0 13.3 %copy-start.6 = (f32[256]{0:T(256)S(1)}, f32[256]{0:T(256)}, u32[]{:S(2)}) copy-start(f32[256]{0:T(256)} %param.13) | copy-start | bytes 3076
  9.0 8.6 %collective-permute-start.2 = (bf16[16,256]{1,0:T(8,128)(2,1)S(1)}, bf16[16,256]{1,0:T(8,128)(2,1)S(1)}, u32[]{:S(2)}, u32[]{:S(2)}) collective-permute-start(bf16[16,256]{1,0:T(8,128)(2,1)S(1)} %slice_bitcast_fusion), channel_id=1, source_target_pairs={{0,32},{32,64},{64,96},{1,33},{33,65},{65,97},{2,34},{34,66},{66,9... | collective-permute-start | bytes 24584 | tf_op jit(solution)/shard_map/ppermute | solution.py:435
  17.6 4.6 %collective-permute-start.3 = (bf16[256,512]{1,0:T(8,128)(2,1)S(1)}, bf16[256,512]{1,0:T(8,128)(2,1)S(1)}, u32[]{:S(2)}, u32[]{:S(2)}) collective-permute-start(bf16[256,512]{1,0:T(8,128)(2,1)S(1)} %collective-permute-done.1.cross_ref), channel_id=1, source_target_pairs={{0,32},{32,0},{1,33},{33,1},{2,34},{34,2},{3,35},{35,3},{4,36},{36... | collective-permute-start | bytes 786440 | tf_op jit(solution)/shard_map/ppermute | solution.py:461
  18.3 10.2 %collective-permute-start.4 = (bf16[256,256]{1,0:T(8,128)(2,1)S(1)}, bf16[256,256]{1,0:T(8,128)(2,1)S(1)}, u32[]{:S(2)}, u32[]{:S(2)}) collective-permute-start(bf16[256,256]{1,0:T(8,128)(2,1)S(1)} %d_inner.1.d_inner_ref.d0_ref), channel_id=1, source_target_pairs={{32,0},{64,32},{96,64},{33,1},{65,33},{97,65},{34,2},{66,34},{98,6... | collective-permute-start | bytes 393224 | tf_op jit(solution)/shard_map/ppermute | solution.py:435
  20.3 8.9 %collective-permute-start.5 = (bf16[256,256]{1,0:T(8,128)(2,1)S(1)}, bf16[256,256]{1,0:T(8,128)(2,1)S(1)}, u32[]{:S(2)}, u32[]{:S(2)}) collective-permute-start(bf16[256,256]{1,0:T(8,128)(2,1)S(1)} %d_inner.1.d_inner_ref.d0_ref), channel_id=1, source_target_pairs={{64,0},{96,32},{65,1},{97,33},{66,2},{98,34},{67,3},{99,35},{68,4}... | collective-permute-start | bytes 393224 | tf_op jit(solution)/shard_map/ppermute | solution.py:435
  21.6 7.6 %collective-permute-start.6 = (bf16[256,256]{1,0:T(8,128)(2,1)S(1)}, bf16[256,256]{1,0:T(8,128)(2,1)S(1)}, u32[]{:S(2)}, u32[]{:S(2)}) collective-permute-start(bf16[256,256]{1,0:T(8,128)(2,1)S(1)} %d_inner.1.d_inner_ref.d0_ref), channel_id=1, source_target_pairs={{96,0},{97,1},{98,2},{99,3},{100,4},{101,5},{102,6},{103,7},{104,8... | collective-permute-start | bytes 393224 | tf_op jit(solution)/shard_map/ppermute | solution.py:435
  22.3 6.9 %copy-start.4 = (bf16[16,1024]{1,0:T(8,128)(2,1)S(1)}, bf16[16,1024]{1,0:T(8,128)(2,1)}, u32[]{:S(2)}) copy-start(bf16[16,1024]{1,0:T(8,128)(2,1)} %lags_ref.3) | copy-start | bytes 98308
  22.3 11.5 %copy-start = (bf16[1,256,8192]{2,1,0:T(8,128)(2,1)S(1)}, bf16[1,256,8192]{2,1,0:T(8,128)(2,1)}, u32[]{:S(2)}) copy-start(bf16[1,256,8192]{2,1,0:T(8,128)(2,1)} %param.15) | copy-start | bytes 12582916
  25.0 6.9 %collective-permute-start.8 = (bf16[256,256]{1,0:T(8,128)(2,1)S(1)}, bf16[256,256]{1,0:T(8,128)(2,1)S(1)}, u32[]{:S(2)}, u32[]{:S(2)}) collective-permute-start(bf16[256,256]{1,0:T(8,128)(2,1)S(1)} %get-tuple-element.37.gated_ref), channel_id=1, source_target_pairs={{0,32},{32,0},{1,33},{33,1},{2,34},{34,2},{3,35},{35,3},{4,36},{36... | collective-permute-start | bytes 393224 | tf_op jit(solution)/shard_map/ppermute | solution.py:467
  31.9 5.4 %collective-permute-start.9 = (f32[32,8,256]{2,1,0:T(8,128)S(1)}, f32[32,8,256]{2,1,0:T(8,128)S(1)}, u32[]{:S(2)}, u32[]{:S(2)}) collective-permute-start(f32[32,8,256]{2,1,0:T(8,128)S(1)} %get-tuple-element.45.small_ref), channel_id=1, source_target_pairs={{0,32},{32,0},{1,33},{33,1},{2,34},{34,2},{3,35},{35,3},{4,36},{36... | collective-permute-start | bytes 786440 | tf_op jit(solution)/shard_map/ppermute | solution.py:474
  81.9 21.7 %all-to-all-start.1 = ((bf16[32,8,2304]{2,1,0:T(8,128)(2,1)}), bf16[32,8,2304]{2,1,0:T(8,128)(2,1)S(1)}, u32[]{:S(2)}, u32[]{:S(2)}) async-start(bf16[32,8,2304]{2,1,0:T(8,128)(2,1)} %total.1), calls=%async_computation.1 | async-start | bytes 2359296 | tf_op jit(solution)/shard_map/all_to_all | solution.py:484
  85.9 16.9 %collective-permute-start.10 = (f32[3,8,256]{2,1,0:T(8,128)S(1)}, f32[3,8,256]{2,1,0:T(8,128)S(1)}, u32[]{:S(2)}, u32[]{:S(2)}) collective-permute-start(f32[3,8,256]{2,1,0:T(8,128)S(1)} %get-tuple-element.49), channel_id=1, source_target_pairs={{32,0},{64,32},{96,64},{33,1},{65,33},{97,65},{34,2},{66,34},{98,6... | collective-permute-start | bytes 73736 | tf_op jit(solution)/shard_map/ppermute | solution.py:435

commit v9 on v8

--- a/solution.py
+++ b/solution.py
@@ -17,6 +17,7 @@
 
 ROWS = 256
 CHANS = 256
+HALF = CHANS // 2
 GROUPS = 16
 LENGTH = 1024
 STRIP = 32
@@ -53,8 +54,8 @@
     )(*placed)
 
 
-def lane_groups(rows):
-    return lax.broadcasted_iota(jnp.int32, (rows, CHANS), 1) // (CHANS // GROUPS)
+def lane_groups():
+    return lax.broadcasted_iota(jnp.int32, (STRIP, HALF), 1) // (CHANS // GROUPS)
 
 
 def later(x, count):
@@ -67,20 +68,32 @@
     return pltpu.roll(wide, 0, 1, stride=1, stride_axis=0)[:, :LENGTH].astype(BF16)
 
 
-def pick_groups(result):
-    ids = lane_groups(STRIP)
-    out = jnp.zeros((STRIP, CHANS), F32)
-    for g in range(GROUPS):
-        out = jnp.where(ids == g, result[g * STRIP : (g + 1) * STRIP], out)
-    return out
+def two_windows(signal_ref, n, half):
+    lanes = slice(half * HALF, (half + 1) * HALF)
+    windows = [signal_ref[m * STRIP : m * STRIP + LENGTH, lanes] for m in (n, n + 1)]
+    return jnp.concatenate(windows, axis=1)
 
 
 def all_strips(strips_ref, signal_ref):
-    parts = []
-    for n in range(ROWS // STRIP):
-        window = signal_ref[n * STRIP : n * STRIP + LENGTH, :]
-        parts.append(pick_groups(jnp.dot(strips_ref[...], window, preferred_element_type=F32)))
-    return jnp.concatenate(parts, axis=0)
+    ids = lane_groups()
+    rows = GROUPS * STRIP // 2
+    columns = []
+    for half in range(2):
+        parts = []
+        for n in range(0, ROWS // STRIP, 2):
+            result = jnp.dot(
+                strips_ref[half * rows : (half + 1) * rows, :],
+                two_windows(signal_ref, n, half),
+                preferred_element_type=F32,
+            )
+            for m in range(2):
+                out = jnp.zeros((STRIP, HALF), F32)
+                for g in range(GROUPS // 2):
+                    piece = result[g * STRIP : (g + 1) * STRIP, m * HALF : (m + 1) * HALF]
+                    out = jnp.where(ids == g, piece, out)
+                parts.append(out)
+        columns.append(jnp.concatenate(parts, axis=0))
+    return jnp.concatenate(columns, axis=1)
 
 
 def with_tail(tail, block):
@@ -263,22 +276,29 @@
 def lag_kernel(d_inner_ref, signal_ref, filter_ref, outer_ref, stack_ref, sums_ref):
     turn = turn_matrix(ROWS, STRIP).astype(BF16)
     turned = jnp.dot(turn, d_inner_ref[...], preferred_element_type=F32)
-    ids = lane_groups(STRIP)
+    ids = lane_groups()
+    count = GROUPS * STRIP // 2
     outer_ref[:, LENGTH:] = jnp.zeros((GROUPS * STRIP, PAD), F32)
-    for n in range(ROWS // STRIP):
-        piece = turned[n * STRIP : (n + 1) * STRIP]
-        for g in range(GROUPS):
-            stack_ref[g * STRIP : (g + 1) * STRIP, :] = jnp.where(ids == g, piece, 0.0).astype(BF16)
-        term = lax.dot_general(
-            stack_ref[...],
-            signal_ref[n * STRIP : n * STRIP + LENGTH, :],
-            (((1,), (1,)), ((), ())),
-            preferred_element_type=F32,
-        )
-        if n == 0:
-            outer_ref[:, :LENGTH] = term
-        else:
-            outer_ref[:, :LENGTH] += term
+    for half in range(2):
+        rows = slice(half * count, (half + 1) * count)
+        for n in range(0, ROWS // STRIP, 2):
+            for m in range(2):
+                start = (n + m) * STRIP
+                piece = turned[start : start + STRIP, half * HALF : (half + 1) * HALF]
+                for g in range(GROUPS // 2):
+                    stack_ref[g * STRIP : (g + 1) * STRIP, m * HALF : (m + 1) * HALF] = jnp.where(
+                        ids == g, piece, 0.0
+                    ).astype(BF16)
+            term = lax.dot_general(
+                stack_ref[...],
+                two_windows(signal_ref, n, half),
+                (((1,), (1,)), ((), ())),
+                preferred_element_type=F32,
+            )
+            if n == 0:
+                outer_ref[rows, :LENGTH] = term
+            else:
+                outer_ref[rows, :LENGTH] += term
     for g in range(GROUPS):
         rows = outer_ref[g * STRIP : (g + 1) * STRIP, :]
         skewed = pltpu.roll(rows, WIDE - (STRIP - 1), 1, stride=1, stride_axis=0)
@@ -298,7 +318,7 @@
 def lag_call(*operands):
     scratch = [
         pltpu.VMEM((GROUPS * STRIP, WIDE), F32),
-        pltpu.VMEM((GROUPS * STRIP, CHANS), BF16),
+        pltpu.VMEM((GROUPS * STRIP // 2, CHANS), BF16),
         pltpu.VMEM((GROUPS, WIDE), F32),
     ]
     return call(lag_kernel, "lag_sums", pltpu.VMEM((GROUPS, LENGTH), F32), operands, scratch)

time: 106 us -> 103 us (0.972)
  Pallas kernels: 23.4 us -> 20.6 us
  blocking collectives: 43.1 us -> 41.3 us
  waiting for transfers between devices: 13.6 us -> 14.9 us
    pallas_call x9, Pallas kernels: 23.3 us -> 20.5 us  [call(): pl.pallas_call(kernel, out_shape=out_shape, scratch_shapes=list(scratch),...]
    all_to_all x1, blocking collectives: 43.1 us -> 41.3 us  [shards(): terms = lax.all_to_all(terms, CHIPS, 0, 0)]
    ppermute x5, waiting for transfers between devices: 13.6 us -> 14.8 us  [sent(): return lax.ppermute(block, CTX, route)]
  transfers between devices with their start and end apart: 12 -> 12, of which waited for: 2 -> 2; matrix products, arithmetic and copies ran while one was open for 2% -> 2% of each run, Pallas kernels for 19% -> 17%
where the time goes in v9:
time: 103 us; the launch traced here: 102 us
  blocking collectives  41.3 us (40%)
  starting transfers between devices  22.4 us (22%)
  Pallas kernels  20.6 us (20%)
  waiting for transfers between devices  14.9 us (14%)
  local copies, waits for them, and re-layouts  1.39 us (1%)
    all_to_all x1, blocking collectives, shards(): terms = lax.all_to_all(terms, CHIPS, 0, 0)  41.3 us
    pallas_call x9, Pallas kernels, call(): pl.pallas_call(kernel, out_shape=out_shape, scratch_shapes=list(scratch),...  20.5 us
    ppermute x5, waiting for transfers between devices, sent(): return lax.ppermute(block, CTX, route)  14.8 us
    ppermute x5, starting transfers between devices, sent(): return lax.ppermute(block, CTX, route)  9.27 us
    ppermute x1, starting transfers between devices, shards(): cross = lax.ppermute(own, 'xh', [(0, 1)])  4.75 us
    all_to_all x1, starting transfers between devices, shards(): shares = lax.all_to_all(total_call(terms, scale), DP, 0, 0)  3.94 us
  transfers between devices with their start and end apart: 12, of which 2 were waited for; matrix products, arithmetic and copies ran while one was open for 2% of the time, Pallas kernels for 17%

profile of v9, /device:TPU:1, one launch (start us, length us, event | category | flops | bytes accessed | tf_op | source)
XLA Modules:
  0.0 102.4 jit_solution(5562204502773758367)
XLA Ops:
  0.6 1.5 %collective-permute-start.7 = (bf16[256,8192]{1,0:T(8,128)(2,1)}, bf16[256,8192]{1,0:T(8,128)(2,1)}, u32[]{:S(2)}, u32[]{:S(2)}) collective-permute-start(bf16[256,8192]{1,0:T(8,128)(2,1)} %bitcast.17), channel_id=1, source_target_pairs={{0,32},{32,0},{1,33},{33,1},{2,34},{34,2},{3,35},{35,3},{4,36},{36... | collective-permute-start | bytes 12582920 | tf_op jit(solution)/shard_map/ppermute | solution.py:477
  2.1 1.0 pad_maximum_fusion
  3.1 4.7 %collective-permute-start.1 = (bf16[256,512]{1,0:T(8,128)(2,1)S(1)}, bf16[256,512]{1,0:T(8,128)(2,1)S(1)}, u32[]{:S(2)}, u32[]{:S(2)}) collective-permute-start(bf16[256,512]{1,0:T(8,128)(2,1)S(1)} %pad_maximum_fusion), channel_id=1, source_target_pairs={{0,64},{1,65},{2,66},{3,67},{4,68},{5,69},{6,70},{7,71},{8,72},{9,... | collective-permute-start | bytes 786440 | tf_op jit(solution)/shard_map/ppermute | solution.py:475
  7.9 0.4 collective-permute-start
  8.3 0.7 slice_bitcast_fusion
  9.0 0.0 copy-start.1
  9.0 0.0 copy-start.5
  9.0 0.0 copy-start.2
  9.0 0.0 copy-start.3
  9.0 0.0 copy-start.6
  9.0 2.1 %collective-permute-start.2 = (bf16[16,256]{1,0:T(8,128)(2,1)S(1)}, bf16[16,256]{1,0:T(8,128)(2,1)S(1)}, u32[]{:S(2)}, u32[]{:S(2)}) collective-permute-start(bf16[16,256]{1,0:T(8,128)(2,1)S(1)} %slice_bitcast_fusion), channel_id=1, source_target_pairs={{0,32},{32,64},{64,96},{1,33},{33,65},{65,97},{2,34},{34,66},{66,9... | collective-permute-start | bytes 24584 | tf_op jit(solution)/shard_map/ppermute | solution.py:455
  11.0 6.6 %pre.1 = (bf16[256,256]{1,0:T(8,128)(2,1)S(1)}, bf16[512,1024]{1,0:T(8,128)(2,1)S(1)}) custom-call(bf16[256,8192]{1,0:T(8,128)(2,1)} %bitcast.18, bf16[8192,256]{1,0:T(8,128)(2,1)} %weight_ref.1, bf16[16,1024]{1,0:T(8,128)(2,1)} %lags_ref.3), custom_call_target="tpu_custom_call" | custom-call | flops 1073741824 | bytes 1024 | tf_op jit(solution)/shard_map/pre/pallas_call | solution.py:46
  17.6 0.0 collective-permute-done.2.tail_ref
  17.6 0.0 collective-permute-done.1.cross_ref
  17.6 0.6 collective-permute-start.3
  18.2 0.0 copy-done.1
  18.2 0.0 copy-done.5
  18.2 0.1 d_inner.1.d_inner_ref.d0_ref
  18.3 1.9 %collective-permute-start.4 = (bf16[256,256]{1,0:T(8,128)(2,1)S(1)}, bf16[256,256]{1,0:T(8,128)(2,1)S(1)}, u32[]{:S(2)}, u32[]{:S(2)}) collective-permute-start(bf16[256,256]{1,0:T(8,128)(2,1)S(1)} %d_inner.1.d_inner_ref.d0_ref), channel_id=1, source_target_pairs={{32,0},{64,32},{96,64},{33,1},{65,33},{97,65},{34,2},{66,34},{98,6... | collective-permute-start | bytes 393224 | tf_op jit(solution)/shard_map/ppermute | solution.py:455
  20.3 1.3 %collective-permute-start.5 = (bf16[256,256]{1,0:T(8,128)(2,1)S(1)}, bf16[256,256]{1,0:T(8,128)(2,1)S(1)}, u32[]{:S(2)}, u32[]{:S(2)}) collective-permute-start(bf16[256,256]{1,0:T(8,128)(2,1)S(1)} %d_inner.1.d_inner_ref.d0_ref), channel_id=1, source_target_pairs={{64,0},{96,32},{65,1},{97,33},{66,2},{98,34},{67,3},{99,35},{68,4}... | collective-permute-start | bytes 393224 | tf_op jit(solution)/shard_map/ppermute | solution.py:455
  21.6 0.0 collective-permute-done.pair_ref
  21.6 0.7 collective-permute-start.6
  22.3 0.0 collective-permute-done.3.cross_pair_ref
  22.3 0.0 copy-done.2
  22.3 0.0 copy-done.3
  22.3 0.0 copy-done.6
  22.3 0.0 copy-start.4
  22.3 0.0 copy-start
  22.3 1.9 %fwd.1 = (bf16[256,256]{1,0:T(8,128)(2,1)S(1)}, f32[256,256]{1,0:T(8,128)S(1)}, bf16[1248,256]{1,0:T(8,128)(2,1)S(1)}) custom-call(s32[1]{0:T(128)} %bitcast.core_ref, bf16[512,1024]{1,0:T(8,128)(2,1)S(1)} %get-tuple-element.33.strips_ref, bf16[256,512]{1,0:T(8,128)(2,1)S(1)} %collective-permute-done.pair_ref, ...), custom_call_target="tpu_custom_call" | custom-call | flops 4294967296 | bytes 1024 | tf_op jit(solution)/shard_map/fwd/pallas_call | solution.py:46
  24.3 0.1 collective-permute-start.8
  24.4 2.4 %lag_sums.1.filter_ref = f32[16,1024]{1,0:T(8,128)S(1)} custom-call(bf16[256,256]{1,0:T(8,128)(2,1)S(1)} %d_inner.1.d_inner_ref.d0_ref, bf16[1248,256]{1,0:T(8,128)(2,1)S(1)} %get-tuple-element.39.signal_ref), custom_call_target="tpu_custom_call" | custom-call | flops 1024 | bytes 1024 | tf_op jit(solution)/shard_map/lag_sums/pallas_call | solution.py:46
  26.8 0.0 collective-permute-done.4.d1_ref
  26.8 2.4 %collective-permute-done.5.d2_ref = bf16[256,256]{1,0:T(8,128)(2,1)S(1)} collective-permute-done((bf16[256,256]{1,0:T(8,128)(2,1)S(1)}, bf16[256,256]{1,0:T(8,128)(2,1)S(1)}, u32[]{:S(2)}, u32[]{:S(2)}) %collective-permute-start.5) | collective-permute-done | bytes 131104 | tf_op jit(solution)/shard_map/ppermute | solution.py:455
  29.2 0.0 collective-permute-done.6.d3_ref
  29.2 0.0 copy-done.4
  29.2 1.6 %bwd.1 = (f32[3,256,256]{2,1,0:T(8,128)S(1)}, f32[3,8,256]{2,1,0:T(8,128)S(1)}, f32[32,8,256]{2,1,0:T(8,128)S(1)}) custom-call(s32[1]{0:T(128)} %bitcast.core_ref, bf16[256,256]{1,0:T(8,128)(2,1)S(1)} %d_inner.1.d_inner_ref.d0_ref, bf16[256,256]{1,0:T(8,128)(2,1)S(1)} %collective-permute-done.4.d1_ref, bf16[256,256]{1,0:T(8,128)(2,1)S(1)} %collective-permute-done.5.d2_ref, ...), custom_call_target="tpu_custom_call" | custom-call | flops 1024 | bytes 1024 | tf_op jit(solution)/shard_map/bwd/pallas_call | solution.py:46
  30.8 0.0 collective-permute-done.8.other_gated_ref
  30.8 1.9 %collective-permute-start.9 = (f32[32,8,256]{2,1,0:T(8,128)S(1)}, f32[32,8,256]{2,1,0:T(8,128)S(1)}, u32[]{:S(2)}, u32[]{:S(2)}) collective-permute-start(f32[32,8,256]{2,1,0:T(8,128)S(1)} %get-tuple-element.45.small_ref), channel_id=1, source_target_pairs={{0,32},{32,0},{1,33},{33,1},{2,34},{34,2},{3,35},{35,3},{4,36},{36... | collective-permute-start | bytes 786440 | tf_op jit(solution)/shard_map/ppermute | solution.py:494
  32.7 0.0 collective-permute-done.7.other_cot_ref
  32.7 0.0 copy-done
  32.8 3.5 %terms.1.terms_ref = bf16[2,256,2304]{2,1,0:T(8,128)(2,1)S(1)} custom-call(s32[1]{0:T(128)} %bitcast.core_ref, bf16[256,8192]{1,0:T(8,128)(2,1)S(1)} %bitcast.19, bf16[256,8192]{1,0:T(8,128)(2,1)} %collective-permute-done.7.other_cot_ref, bf16[256,256]{1,0:T(8,128)(2,1)S(1)} %get-tuple-element.37.gated_ref, ...), custom_call_target="tpu_custom_call" | custom-call | flops 1073741824 | bytes 1024 | tf_op jit(solution)/shard_map/terms/pallas_call | solution.py:46
  36.2 0.0 collective-permute-done.9.other_small_ref
  36.2 0.1 add_small.1
  36.3 41.3 %all_to_all.10.refs_0_ = bf16[64,8,2304]{2,1,0:T(8,128)(2,1)S(1)} all-to-all(bf16[64,8,2304]{2,1,0:T(8,128)(2,1)S(1)} %bitcast.16), channel_id=1, replica_groups=mesh['xh'=2,'co'=2,'y'=4,'xl'=2,'z'=4] {'xh','y','xl','z'}, dimensions={0} | all-to-all | bytes 4718592 | tf_op jit(solution)/shard_map/all_to_all | solution.py:500
  77.7 1.4 %total.1 = bf16[32,8,2304]{2,1,0:T(8,128)(2,1)} custom-call(bf16[64,8,2304]{2,1,0:T(8,128)(2,1)S(1)} %all_to_all.10.refs_0_), custom_call_target="tpu_custom_call" | custom-call | flops 1024 | bytes 1024 | tf_op jit(solution)/shard_map/total/pallas_call | solution.py:46
  79.1 3.9 %all-to-all-start.1 = ((bf16[32,8,2304]{2,1,0:T(8,128)(2,1)}), bf16[32,8,2304]{2,1,0:T(8,128)(2,1)S(1)}, u32[]{:S(2)}, u32[]{:S(2)}) async-start(bf16[32,8,2304]{2,1,0:T(8,128)(2,1)} %total.1), calls=%async_computation.1 | async-start | bytes 2359296 | tf_op jit(solution)/shard_map/all_to_all | solution.py:504
  83.0 3.3 %collective-permute-start.10 = (f32[3,8,256]{2,1,0:T(8,128)S(1)}, f32[3,8,256]{2,1,0:T(8,128)S(1)}, u32[]{:S(2)}, u32[]{:S(2)}) collective-permute-start(f32[3,8,256]{2,1,0:T(8,128)S(1)} %get-tuple-element.49), channel_id=1, source_target_pairs={{32,0},{64,32},{96,64},{33,1},{65,33},{97,65},{34,2},{66,34},{98,6... | collective-permute-start | bytes 73736 | tf_op jit(solution)/shard_map/ppermute | solution.py:455
  86.3 0.7 copy.18
  87.0 12.4 %collective-permute-done.10.next_ref = f32[3,8,256]{2,1,0:T(8,128)S(1)} collective-permute-done((f32[3,8,256]{2,1,0:T(8,128)S(1)}, f32[3,8,256]{2,1,0:T(8,128)S(1)}, u32[]{:S(2)}, u32[]{:S(2)}) %collective-permute-start.10) | collective-permute-done | bytes 24608 | tf_op jit(solution)/shard_map/ppermute | solution.py:455
  99.4 0.9 input_grads.1
  100.3 0.0 all-to-all-done.1
  100.3 2.1 %spread.1 = (f32[2048,256]{1,0:T(8,128)}, f32[3,3,256]{2,1,0:T(4,128)}, f32[16,1024]{1,0:T(8,128)}, f32[1,256]{1,0:T(1,128)}) custom-call(bf16[256,2304]{1,0:T(8,128)(2,1)S(1)} %bitcast.20), custom_call_target="tpu_custom_call" | custom-call | flops 1024 | bytes 1024 | tf_op jit(solution)/shard_map/spread/pallas_call | solution.py:46
Async XLA Ops:
  0.6 32.1 %collective-permute-start.7 = (bf16[256,8192]{1,0:T(8,128)(2,1)}, bf16[256,8192]{1,0:T(8,128)(2,1)}, u32[]{:S(2)}, u32[]{:S(2)}) collective-permute-start(bf16[256,8192]{1,0:T(8,128)(2,1)} %bitcast.17), channel_id=1, source_target_pairs={{0,32},{32,0},{1,33},{33,1},{2,34},{34,2},{3,35},{35,3},{4,36},{36... | collective-permute-start | bytes 12582920 | tf_op jit(solution)/shard_map/ppermute | solution.py:477
  3.1 14.5 %collective-permute-start.1 = (bf16[256,512]{1,0:T(8,128)(2,1)S(1)}, bf16[256,512]{1,0:T(8,128)(2,1)S(1)}, u32[]{:S(2)}, u32[]{:S(2)}) collective-permute-start(bf16[256,512]{1,0:T(8,128)(2,1)S(1)} %pad_maximum_fusion), channel_id=1, source_target_pairs={{0,64},{1,65},{2,66},{3,67},{4,68},{5,69},{6,70},{7,71},{8,72},{9,... | collective-permute-start | bytes 786440 | tf_op jit(solution)/shard_map/ppermute | solution.py:475
  7.9 13.7 %collective-permute-start = (bf16[256,512]{1,0:T(8,128)(2,1)S(1)}, bf16[256,512]{1,0:T(8,128)(2,1)S(1)}, u32[]{:S(2)}, u32[]{:S(2)}) collective-permute-start(bf16[256,512]{1,0:T(8,128)(2,1)S(1)} %pad_maximum_fusion), channel_id=1, source_target_pairs={{0,32},{32,0},{1,33},{33,1},{2,34},{34,2},{3,35},{35,3},{4,36},{36... | collective-permute-start | bytes 786440 | tf_op jit(solution)/shard_map/ppermute | solution.py:476
  9.0 9.2 %copy-start.1 = (bf16[1,256,256]{2,1,0:T(8,128)(2,1)S(1)}, bf16[1,256,256]{2,1,0:T(8,128)(2,1)}, u32[]{:S(2)}) copy-start(bf16[1,256,256]{2,1,0:T(8,128)(2,1)} %param.8) | copy-start | bytes 393220
  9.0 9.2 %copy-start.5 = (f32[3,3,256]{2,1,0:T(4,128)S(1)}, f32[3,3,256]{2,1,0:T(4,128)}, u32[]{:S(2)}) copy-start(f32[3,3,256]{2,1,0:T(4,128)} %taps_ref.7) | copy-start | bytes 27652
  9.0 13.3 %copy-start.2 = (bf16[1,256,256]{2,1,0:T(8,128)(2,1)S(1)}, bf16[1,256,256]{2,1,0:T(8,128)(2,1)}, u32[]{:S(2)}) copy-start(bf16[1,256,256]{2,1,0:T(8,128)(2,1)} %param.10) | copy-start | bytes 393220
  9.0 13.3 %copy-start.3 = (bf16[1,256,256]{2,1,0:T(8,128)(2,1)S(1)}, bf16[1,256,256]{2,1,0:T(8,128)(2,1)}, u32[]{:S(2)}) copy-start(bf16[1,256,256]{2,1,0:T(8,128)(2,1)} %param.9) | copy-start | bytes 393220
  9.0 13.3 %copy-start.6 = (f32[256]{0:T(256)S(1)}, f32[256]{0:T(256)}, u32[]{:S(2)}) copy-start(f32[256]{0:T(256)} %param.13) | copy-start | bytes 3076
  9.0 8.6 %collective-permute-start.2 = (bf16[16,256]{1,0:T(8,128)(2,1)S(1)}, bf16[16,256]{1,0:T(8,128)(2,1)S(1)}, u32[]{:S(2)}, u32[]{:S(2)}) collective-permute-start(bf16[16,256]{1,0:T(8,128)(2,1)S(1)} %slice_bitcast_fusion), channel_id=1, source_target_pairs={{0,32},{32,64},{64,96},{1,33},{33,65},{65,97},{2,34},{34,66},{66,9... | collective-permute-start | bytes 24584 | tf_op jit(solution)/shard_map/ppermute | solution.py:455
  17.6 4.6 %collective-permute-start.3 = (bf16[256,512]{1,0:T(8,128)(2,1)S(1)}, bf16[256,512]{1,0:T(8,128)(2,1)S(1)}, u32[]{:S(2)}, u32[]{:S(2)}) collective-permute-start(bf16[256,512]{1,0:T(8,128)(2,1)S(1)} %collective-permute-done.1.cross_ref), channel_id=1, source_target_pairs={{0,32},{32,0},{1,33},{33,1},{2,34},{34,2},{3,35},{35,3},{4,36},{36... | collective-permute-start | bytes 786440 | tf_op jit(solution)/shard_map/ppermute | solution.py:481
  18.3 8.4 %collective-permute-start.4 = (bf16[256,256]{1,0:T(8,128)(2,1)S(1)}, bf16[256,256]{1,0:T(8,128)(2,1)S(1)}, u32[]{:S(2)}, u32[]{:S(2)}) collective-permute-start(bf16[256,256]{1,0:T(8,128)(2,1)S(1)} %d_inner.1.d_inner_ref.d0_ref), channel_id=1, source_target_pairs={{32,0},{64,32},{96,64},{33,1},{65,33},{97,65},{34,2},{66,34},{98,6... | collective-permute-start | bytes 393224 | tf_op jit(solution)/shard_map/ppermute | solution.py:455
  20.3 8.9 %collective-permute-start.5 = (bf16[256,256]{1,0:T(8,128)(2,1)S(1)}, bf16[256,256]{1,0:T(8,128)(2,1)S(1)}, u32[]{:S(2)}, u32[]{:S(2)}) collective-permute-start(bf16[256,256]{1,0:T(8,128)(2,1)S(1)} %d_inner.1.d_inner_ref.d0_ref), channel_id=1, source_target_pairs={{64,0},{96,32},{65,1},{97,33},{66,2},{98,34},{67,3},{99,35},{68,4}... | collective-permute-start | bytes 393224 | tf_op jit(solution)/shard_map/ppermute | solution.py:455
  21.6 7.6 %collective-permute-start.6 = (bf16[256,256]{1,0:T(8,128)(2,1)S(1)}, bf16[256,256]{1,0:T(8,128)(2,1)S(1)}, u32[]{:S(2)}, u32[]{:S(2)}) collective-permute-start(bf16[256,256]{1,0:T(8,128)(2,1)S(1)} %d_inner.1.d_inner_ref.d0_ref), channel_id=1, source_target_pairs={{96,0},{97,1},{98,2},{99,3},{100,4},{101,5},{102,6},{103,7},{104,8... | collective-permute-start | bytes 393224 | tf_op jit(solution)/shard_map/ppermute | solution.py:455
  22.3 6.9 %copy-start.4 = (bf16[16,1024]{1,0:T(8,128)(2,1)S(1)}, bf16[16,1024]{1,0:T(8,128)(2,1)}, u32[]{:S(2)}) copy-start(bf16[16,1024]{1,0:T(8,128)(2,1)} %lags_ref.3) | copy-start | bytes 98308
  22.3 10.4 %copy-start = (bf16[1,256,8192]{2,1,0:T(8,128)(2,1)S(1)}, bf16[1,256,8192]{2,1,0:T(8,128)(2,1)}, u32[]{:S(2)}) copy-start(bf16[1,256,8192]{2,1,0:T(8,128)(2,1)} %param.15) | copy-start | bytes 12582916
  24.3 6.6 %collective-permute-start.8 = (bf16[256,256]{1,0:T(8,128)(2,1)S(1)}, bf16[256,256]{1,0:T(8,128)(2,1)S(1)}, u32[]{:S(2)}, u32[]{:S(2)}) collective-permute-start(bf16[256,256]{1,0:T(8,128)(2,1)S(1)} %get-tuple-element.37.gated_ref), channel_id=1, source_target_pairs={{0,32},{32,0},{1,33},{33,1},{2,34},{34,2},{3,35},{35,3},{4,36},{36... | collective-permute-start | bytes 393224 | tf_op jit(solution)/shard_map/ppermute | solution.py:487
  30.8 5.4 %collective-permute-start.9 = (f32[32,8,256]{2,1,0:T(8,128)S(1)}, f32[32,8,256]{2,1,0:T(8,128)S(1)}, u32[]{:S(2)}, u32[]{:S(2)}) collective-permute-start(f32[32,8,256]{2,1,0:T(8,128)S(1)} %get-tuple-element.45.small_ref), channel_id=1, source_target_pairs={{0,32},{32,0},{1,33},{33,1},{2,34},{34,2},{3,35},{35,3},{4,36},{36... | collective-permute-start | bytes 786440 | tf_op jit(solution)/shard_map/ppermute | solution.py:494
  79.1 21.2 %all-to-all-start.1 = ((bf16[32,8,2304]{2,1,0:T(8,128)(2,1)}), bf16[32,8,2304]{2,1,0:T(8,128)(2,1)S(1)}, u32[]{:S(2)}, u32[]{:S(2)}) async-start(bf16[32,8,2304]{2,1,0:T(8,128)(2,1)} %total.1), calls=%async_computation.1 | async-start | bytes 2359296 | tf_op jit(solution)/shard_map/all_to_all | solution.py:504
  83.0 16.4 %collective-permute-start.10 = (f32[3,8,256]{2,1,0:T(8,128)S(1)}, f32[3,8,256]{2,1,0:T(8,128)S(1)}, u32[]{:S(2)}, u32[]{:S(2)}) collective-permute-start(f32[3,8,256]{2,1,0:T(8,128)S(1)} %get-tuple-element.49), channel_id=1, source_target_pairs={{32,0},{64,32},{96,64},{33,1},{65,33},{97,65},{34,2},{66,34},{98,6... | collective-permute-start | bytes 73736 | tf_op jit(solution)/shard_map/ppermute | solution.py:455

commit v10 on v9

--- a/solution.py
+++ b/solution.py
@@ -138,12 +138,13 @@
         for copy in pair:
             copy.start()
         copies.append(pair)
-    lags_copy.wait()
-    lines = lines_of(filter_ref, True)
-    for g in range(GROUPS):
-        strips_ref[g * STRIP : (g + 1) * STRIP, :] = strip_of(lines[g : g + 1])
     total = jnp.zeros((ROWS, CHANS), F32)
     for n in range(PIECES):
+        if n == PIECES // 2:
+            lags_copy.wait()
+            lines = lines_of(filter_ref, True)
+            for g in range(GROUPS):
+                strips_ref[g * STRIP : (g + 1) * STRIP, :] = strip_of(lines[g : g + 1])
         for copy in copies[n]:
             copy.wait()
         total += jnp.dot(cot_buffer[n], weight_buffer[n], preferred_element_type=F32)
@@ -221,21 +222,15 @@
 
 
 def terms_call(*operands):
-    out_shape = pltpu.VMEM((2, CHANS, SHARE + CHANS), BF16)
+    out_shape = pltpu.VMEM((2, CHANS, SHARE + HALF), BF16)
     return call(terms_kernel, "terms", out_shape, operands, scalars=1, flops=1 << 30)
 
 
-def two_parts(total):
-    rounded = total.astype(BF16).astype(F32)
-    left = pltpu.roll(total - rounded, SEGMENT // 2, total.ndim - 2)
-    return (rounded + left).astype(BF16)
-
-
 def add_small_kernel(terms_ref, small_ref, other_small_ref, out_ref, parts_ref, sems):
-    parts = two_parts(small_ref[...] + other_small_ref[...]).astype(F32)
-    parts_ref[...] = parts.reshape(CHANS, CHANS).astype(BF16)
+    total = small_ref[...] + other_small_ref[...]
+    parts_ref[...] = total.reshape(CHANS, HALF).astype(BF16)
     copies = [
-        pltpu.make_async_copy(parts_ref, out_ref.at[half, :, pl.ds(SHARE, CHANS)], sems.at[half])
+        pltpu.make_async_copy(parts_ref, out_ref.at[half, :, pl.ds(SHARE, HALF)], sems.at[half])
         for half in range(2)
     ]
     for copy in copies:
@@ -252,7 +247,7 @@
         in_specs=[place, spec, spec],
         out_specs=place,
         out_shape=jax.ShapeDtypeStruct(operands[0].shape, BF16),
-        scratch_shapes=[pltpu.VMEM((CHANS, CHANS), BF16), pltpu.SemaphoreType.DMA((2,))],
+        scratch_shapes=[pltpu.VMEM((CHANS, HALF), BF16), pltpu.SemaphoreType.DMA((2,))],
         input_output_aliases={0: 0},
         compiler_params=pltpu.CompilerParams(vmem_limit_bytes=VMEM_LIMIT),
         name="add_small",
@@ -262,9 +257,12 @@
     )
 
 
-def place(g, n):
-    row = g * (LENGTH // CHANS) + n
+def place(row):
     return row % SHARES, row // SHARES
+
+
+def tap_place(n, half):
+    return place(GROUPS * LENGTH // HALF + 2 * n + half)
 
 
 def turn_matrix(size, block):
@@ -347,6 +345,7 @@
     v_parts = with_tail(near[:, CHANS:], value_ref[...])
     q_parts = with_tail(tail_ref[...], query_ref[...])
     small_ref[...] = jnp.zeros_like(small_ref)
+    sums = []
     d_qs = d_gated_ref[...].astype(F32) * inner_ref[...]
     d_ks = d_mixed * short_sum(taps_ref, 2, v_parts)
     d_vs = d_mixed * short_sum(taps_ref, 1, k_parts)
@@ -354,20 +353,24 @@
         d_short_ref[i] = grad
         head_ref[i] = grad[:8]
         for j in range(3):
-            small_ref[3 * i + j, 2:3, :] = jnp.sum(grad * parts[j], axis=0, keepdims=True)
-    small_ref[9, 2:3, :] = jnp.sum(d_inner * mixed.astype(F32), axis=0, keepdims=True)
+            sums.append(jnp.sum(grad * parts[j], axis=0, keepdims=True))
+    sums.append(jnp.sum(d_inner * mixed.astype(F32), axis=0, keepdims=True))
+    for n, row in enumerate(sums):
+        for half in range(2):
+            share, slot = tap_place(n, half)
+            small_ref[share, slot : slot + 1, :] = row[:, half * HALF : (half + 1) * HALF]
 
     for g in range(GROUPS):
-        for n in range(LENGTH // CHANS):
-            share, slot = place(g, n)
-            small_ref[share, slot : slot + 1, :] = filter_ref[g : g + 1, n * CHANS : (n + 1) * CHANS]
+        for n in range(LENGTH // HALF):
+            share, slot = place(g * (LENGTH // HALF) + n)
+            small_ref[share, slot : slot + 1, :] = filter_ref[g : g + 1, n * HALF : (n + 1) * HALF]
 
 
 def bwd_call(*operands):
     out_shape = [
         pltpu.VMEM((3, ROWS, CHANS), F32),
         pltpu.VMEM((3, 8, CHANS), F32),
-        pltpu.VMEM((SHARES, SEGMENT, CHANS), F32),
+        pltpu.VMEM((SHARES, SEGMENT, HALF), F32),
     ]
     scratch = [
         pltpu.VMEM((GROUPS * STRIP, LENGTH), BF16),
@@ -394,11 +397,7 @@
 
 
 def total_kernel(scale, terms_ref, out_ref):
-    total = jnp.sum(terms_ref[...].astype(F32), axis=0) * scale
-    small = total[:, SHARE:]
-    row = lax.broadcasted_iota(jnp.int32, small.shape, 0)
-    small = jnp.where(row < SEGMENT // 2, small + pltpu.roll(small, SEGMENT // 2, 0), 0.0)
-    total = jnp.concatenate([total[:, :SHARE].astype(BF16), two_parts(small)], axis=1)
+    total = (jnp.sum(terms_ref[...].astype(F32), axis=0) * scale).astype(BF16)
     out_ref[...] = jnp.broadcast_to(total[None], out_ref.shape)
 
 
@@ -419,18 +418,20 @@
             pltpu.make_async_copy(turned_ref.at[piece, :], weight_ref.at[piece, :], sems.at[n])
         )
         copies[-1].start()
-    for share in range(SHARES):
-        segment = shares_ref[share * SEGMENT : (share + 1) * SEGMENT, SHARE:].astype(F32)
-        segment = segment + pltpu.roll(segment, SEGMENT // 2, 0)
-        for g in range(GROUPS):
-            for n in range(LENGTH // CHANS):
-                if place(g, n)[0] == share:
-                    slot = place(g, n)[1]
-                    filter_ref[g : g + 1, n * CHANS : (n + 1) * CHANS] = segment[slot : slot + 1]
-        if share < 9:
-            taps_ref[share // 3, share % 3 : share % 3 + 1, :] = segment[2:3]
-        if share == 9:
-            skip_ref[...] = segment[2:3]
+    small = shares_ref[:, SHARE:].astype(F32)
+
+    def part(share, slot):
+        return small[share * SEGMENT + slot : share * SEGMENT + slot + 1]
+
+    for g in range(GROUPS):
+        for n in range(LENGTH // HALF):
+            piece = part(*place(g * (LENGTH // HALF) + n))
+            filter_ref[g : g + 1, n * HALF : (n + 1) * HALF] = piece
+    for half in range(2):
+        lanes = slice(half * HALF, (half + 1) * HALF)
+        for n in range(9):
+            taps_ref[n // 3, n % 3 : n % 3 + 1, lanes] = part(*tap_place(n, half))
+        skip_ref[:, lanes] = part(*tap_place(9, half))
     for copy in copies:
         copy.wait()
 
@@ -445,7 +446,7 @@
     scratch = [pltpu.VMEM((SHARE, CHANS), F32), pltpu.SemaphoreType.DMA((SPREAD,))]
     out_specs = [pl.BlockSpec(memory_space=pl.ANY)]
     out_specs += [pl.BlockSpec(memory_space=pltpu.VMEM)] * 3
-    shares = shares.reshape(CHANS, SHARE + CHANS)
+    shares = shares.reshape(CHANS, SHARE + HALF)
     return call(spread_kernel, "spread", out_shape, (shares,), scratch, out_specs=out_specs)
 
 
@@ -496,7 +497,7 @@
     terms, other_small = lax.optimization_barrier((terms, other_small))
     terms = add_small_call(terms, small, other_small)
     terms, head = lax.optimization_barrier((terms, head))
-    terms = terms.reshape(2 * SHARES, CHANS // SHARES, SHARE + CHANS)
+    terms = terms.reshape(2 * SHARES, CHANS // SHARES, SHARE + HALF)
     terms = lax.all_to_all(terms, CHIPS, 0, 0)
     following = sent(head, -1)
     grad_query, grad_key, grad_value = input_grad_call(d_short, following, taps)

time: 103 us -> 99.6 us (0.967)
  Pallas kernels: 20.6 us -> 19.1 us
  blocking collectives: 41.3 us -> 40.2 us
    pallas_call x9, Pallas kernels: 20.5 us -> 19.1 us  [call(): pl.pallas_call(kernel, out_shape=out_shape, scratch_shapes=list(scratch),...]
    all_to_all x1, blocking collectives: 41.3 us -> 40.2 us  [shards(): terms = lax.all_to_all(terms, CHIPS, 0, 0)]
  transfers between devices with their start and end apart: 12 -> 12, of which waited for: 2 -> 2; matrix products, arithmetic and copies ran while one was open for 2% -> 2% of each run, Pallas kernels for 17% -> 16%
where the time goes in v10:
time: 99.6 us; the launch traced here: 99.1 us
  blocking collectives  40.2 us (40%)
  starting transfers between devices  22.3 us (22%)
  Pallas kernels  19.1 us (19%)
  waiting for transfers between devices  14.3 us (14%)
  local copies, waits for them, and re-layouts  1.39 us (1%)
    all_to_all x1, blocking collectives, shards(): terms = lax.all_to_all(terms, CHIPS, 0, 0)  40.2 us
    pallas_call x9, Pallas kernels, call(): pl.pallas_call(kernel, out_shape=out_shape, scratch_shapes=list(scratch),...  19.1 us
    ppermute x5, waiting for transfers between devices, sent(): return lax.ppermute(block, CTX, route)  14.3 us
    ppermute x5, starting transfers between devices, sent(): return lax.ppermute(block, CTX, route)  9.13 us
    ppermute x1, starting transfers between devices, shards(): cross = lax.ppermute(own, 'xh', [(0, 1)])  4.75 us
    all_to_all x1, starting transfers between devices, shards(): shares = lax.all_to_all(total_call(terms, scale), DP, 0, 0)  3.94 us
  transfers between devices with their start and end apart: 12, of which 2 were waited for; matrix products, arithmetic and copies ran while one was open for 2% of the time, Pallas kernels for 16%

profile of v10, /device:TPU:1, one launch (start us, length us, event | category | flops | bytes accessed | tf_op | source)
XLA Modules:
  0.0 99.1 jit_solution(3137527020624397438)
XLA Ops:
  0.6 1.5 %collective-permute-start.7 = (bf16[256,8192]{1,0:T(8,128)(2,1)}, bf16[256,8192]{1,0:T(8,128)(2,1)}, u32[]{:S(2)}, u32[]{:S(2)}) collective-permute-start(bf16[256,8192]{1,0:T(8,128)(2,1)} %bitcast.17), channel_id=1, source_target_pairs={{0,32},{32,0},{1,33},{33,1},{2,34},{34,2},{3,35},{35,3},{4,36},{36... | collective-permute-start | bytes 12582920 | tf_op jit(solution)/shard_map/ppermute | solution.py:478
  2.1 1.0 pad_maximum_fusion
  3.1 4.7 %collective-permute-start.1 = (bf16[256,512]{1,0:T(8,128)(2,1)S(1)}, bf16[256,512]{1,0:T(8,128)(2,1)S(1)}, u32[]{:S(2)}, u32[]{:S(2)}) collective-permute-start(bf16[256,512]{1,0:T(8,128)(2,1)S(1)} %pad_maximum_fusion), channel_id=1, source_target_pairs={{0,64},{1,65},{2,66},{3,67},{4,68},{5,69},{6,70},{7,71},{8,72},{9,... | collective-permute-start | bytes 786440 | tf_op jit(solution)/shard_map/ppermute | solution.py:476
  7.9 0.4 collective-permute-start
  8.3 0.7 slice_bitcast_fusion
  9.0 0.0 copy-start.1
  9.0 0.0 copy-start.5
  9.0 0.0 copy-start.2
  9.0 0.0 copy-start.3
  9.0 0.0 copy-start.6
  9.0 2.1 %collective-permute-start.2 = (bf16[16,256]{1,0:T(8,128)(2,1)S(1)}, bf16[16,256]{1,0:T(8,128)(2,1)S(1)}, u32[]{:S(2)}, u32[]{:S(2)}) collective-permute-start(bf16[16,256]{1,0:T(8,128)(2,1)S(1)} %slice_bitcast_fusion), channel_id=1, source_target_pairs={{0,32},{32,64},{64,96},{1,33},{33,65},{65,97},{2,34},{34,66},{66,9... | collective-permute-start | bytes 24584 | tf_op jit(solution)/shard_map/ppermute | solution.py:456
  11.0 5.2 %pre.1 = (bf16[256,256]{1,0:T(8,128)(2,1)S(1)}, bf16[512,1024]{1,0:T(8,128)(2,1)S(1)}) custom-call(bf16[256,8192]{1,0:T(8,128)(2,1)} %bitcast.18, bf16[8192,256]{1,0:T(8,128)(2,1)} %weight_ref.1, bf16[16,1024]{1,0:T(8,128)(2,1)} %lags_ref.3), custom_call_target="tpu_custom_call" | custom-call | flops 1073741824 | bytes 1024 | tf_op jit(solution)/shard_map/pre/pallas_call | solution.py:46
  16.2 0.0 collective-permute-done.2.tail_ref
  16.2 0.0 collective-permute-done.1.cross_ref
  16.3 0.6 collective-permute-start.3
  16.8 0.0 copy-done.1
  16.8 0.0 copy-done.5
  16.8 0.1 d_inner.1.d_inner_ref.d0_ref
  17.0 1.9 %collective-permute-start.4 = (bf16[256,256]{1,0:T(8,128)(2,1)S(1)}, bf16[256,256]{1,0:T(8,128)(2,1)S(1)}, u32[]{:S(2)}, u32[]{:S(2)}) collective-permute-start(bf16[256,256]{1,0:T(8,128)(2,1)S(1)} %d_inner.1.d_inner_ref.d0_ref), channel_id=1, source_target_pairs={{32,0},{64,32},{96,64},{33,1},{65,33},{97,65},{34,2},{66,34},{98,6... | collective-permute-start | bytes 393224 | tf_op jit(solution)/shard_map/ppermute | solution.py:456
  18.9 1.3 %collective-permute-start.5 = (bf16[256,256]{1,0:T(8,128)(2,1)S(1)}, bf16[256,256]{1,0:T(8,128)(2,1)S(1)}, u32[]{:S(2)}, u32[]{:S(2)}) collective-permute-start(bf16[256,256]{1,0:T(8,128)(2,1)S(1)} %d_inner.1.d_inner_ref.d0_ref), channel_id=1, source_target_pairs={{64,0},{96,32},{65,1},{97,33},{66,2},{98,34},{67,3},{99,35},{68,4}... | collective-permute-start | bytes 393224 | tf_op jit(solution)/shard_map/ppermute | solution.py:456
  20.2 0.0 collective-permute-done.pair_ref
  20.2 0.7 collective-permute-start.6
  20.9 0.0 collective-permute-done.3.cross_pair_ref
  20.9 0.0 copy-done.2
  20.9 0.0 copy-done.3
  20.9 0.0 copy-done.6
  20.9 0.0 copy-start.4
  20.9 0.0 copy-start
  21.0 1.9 %fwd.1 = (bf16[256,256]{1,0:T(8,128)(2,1)S(1)}, f32[256,256]{1,0:T(8,128)S(1)}, bf16[1248,256]{1,0:T(8,128)(2,1)S(1)}) custom-call(s32[1]{0:T(128)} %bitcast.core_ref, bf16[512,1024]{1,0:T(8,128)(2,1)S(1)} %get-tuple-element.33.strips_ref, bf16[256,512]{1,0:T(8,128)(2,1)S(1)} %collective-permute-done.pair_ref, ...), custom_call_target="tpu_custom_call" | custom-call | flops 4294967296 | bytes 1024 | tf_op jit(solution)/shard_map/fwd/pallas_call | solution.py:46
  22.9 0.1 collective-permute-start.8
  23.0 2.4 %lag_sums.1.filter_ref = f32[16,1024]{1,0:T(8,128)S(1)} custom-call(bf16[256,256]{1,0:T(8,128)(2,1)S(1)} %d_inner.1.d_inner_ref.d0_ref, bf16[1248,256]{1,0:T(8,128)(2,1)S(1)} %get-tuple-element.39.signal_ref), custom_call_target="tpu_custom_call" | custom-call | flops 1024 | bytes 1024 | tf_op jit(solution)/shard_map/lag_sums/pallas_call | solution.py:46
  25.4 0.0 collective-permute-done.4.d1_ref
  25.4 2.4 %collective-permute-done.5.d2_ref = bf16[256,256]{1,0:T(8,128)(2,1)S(1)} collective-permute-done((bf16[256,256]{1,0:T(8,128)(2,1)S(1)}, bf16[256,256]{1,0:T(8,128)(2,1)S(1)}, u32[]{:S(2)}, u32[]{:S(2)}) %collective-permute-start.5) | collective-permute-done | bytes 131104 | tf_op jit(solution)/shard_map/ppermute | solution.py:456
  27.8 0.0 collective-permute-done.6.d3_ref
  27.8 0.0 copy-done.4
  27.8 1.6 %bwd.1 = (f32[3,256,256]{2,1,0:T(8,128)S(1)}, f32[3,8,256]{2,1,0:T(8,128)S(1)}, f32[32,8,128]{2,1,0:T(8,128)S(1)}) custom-call(s32[1]{0:T(128)} %bitcast.core_ref, bf16[256,256]{1,0:T(8,128)(2,1)S(1)} %d_inner.1.d_inner_ref.d0_ref, bf16[256,256]{1,0:T(8,128)(2,1)S(1)} %collective-permute-done.4.d1_ref, bf16[256,256]{1,0:T(8,128)(2,1)S(1)} %collective-permute-done.5.d2_ref, ...), custom_call_target="tpu_custom_call" | custom-call | flops 1024 | bytes 1024 | tf_op jit(solution)/shard_map/bwd/pallas_call | solution.py:46
  29.5 0.0 collective-permute-done.8.other_gated_ref
  29.5 1.9 %collective-permute-start.9 = (f32[32,8,128]{2,1,0:T(8,128)S(1)}, f32[32,8,128]{2,1,0:T(8,128)S(1)}, u32[]{:S(2)}, u32[]{:S(2)}) collective-permute-start(f32[32,8,128]{2,1,0:T(8,128)S(1)} %get-tuple-element.45.small_ref), channel_id=1, source_target_pairs={{0,32},{32,0},{1,33},{33,1},{2,34},{34,2},{3,35},{35,3},{4,36},{36... | collective-permute-start | bytes 393224 | tf_op jit(solution)/shard_map/ppermute | solution.py:495
  31.4 0.0 collective-permute-done.7.other_cot_ref
  31.4 0.0 copy-done
  31.4 3.5 %terms.1.terms_ref = bf16[2,256,2176]{2,1,0:T(8,128)(2,1)S(1)} custom-call(s32[1]{0:T(128)} %bitcast.core_ref, bf16[256,8192]{1,0:T(8,128)(2,1)S(1)} %bitcast.19, bf16[256,8192]{1,0:T(8,128)(2,1)} %collective-permute-done.7.other_cot_ref, bf16[256,256]{1,0:T(8,128)(2,1)S(1)} %get-tuple-element.37.gated_ref, ...), custom_call_target="tpu_custom_call" | custom-call | flops 1073741824 | bytes 1024 | tf_op jit(solution)/shard_map/terms/pallas_call | solution.py:46
  34.8 0.0 collective-permute-done.9.other_small_ref
  34.8 0.1 add_small.1
  34.9 40.2 %all_to_all.10.refs_0_ = bf16[64,8,2176]{2,1,0:T(8,128)(2,1)S(1)} all-to-all(bf16[64,8,2176]{2,1,0:T(8,128)(2,1)S(1)} %bitcast.16), channel_id=1, replica_groups=mesh['xh'=2,'co'=2,'y'=4,'xl'=2,'z'=4] {'xh','y','xl','z'}, dimensions={0} | all-to-all | bytes 4456448 | tf_op jit(solution)/shard_map/all_to_all | solution.py:501
  75.1 1.4 %total.1 = bf16[32,8,2176]{2,1,0:T(8,128)(2,1)} custom-call(bf16[64,8,2176]{2,1,0:T(8,128)(2,1)S(1)} %all_to_all.10.refs_0_), custom_call_target="tpu_custom_call" | custom-call | flops 1024 | bytes 1024 | tf_op jit(solution)/shard_map/total/pallas_call | solution.py:46
  76.5 3.9 %all-to-all-start.1 = ((bf16[32,8,2176]{2,1,0:T(8,128)(2,1)}), bf16[32,8,2176]{2,1,0:T(8,128)(2,1)S(1)}, u32[]{:S(2)}, u32[]{:S(2)}) async-start(bf16[32,8,2176]{2,1,0:T(8,128)(2,1)} %total.1), calls=%async_computation.1 | async-start | bytes 2228224 | tf_op jit(solution)/shard_map/all_to_all | solution.py:505
  80.4 3.2 %collective-permute-start.10 = (f32[3,8,256]{2,1,0:T(8,128)S(1)}, f32[3,8,256]{2,1,0:T(8,128)S(1)}, u32[]{:S(2)}, u32[]{:S(2)}) collective-permute-start(f32[3,8,256]{2,1,0:T(8,128)S(1)} %get-tuple-element.49), channel_id=1, source_target_pairs={{32,0},{64,32},{96,64},{33,1},{65,33},{97,65},{34,2},{66,34},{98,6... | collective-permute-start | bytes 73736 | tf_op jit(solution)/shard_map/ppermute | solution.py:456
  83.6 0.7 copy.18
  84.3 11.8 %collective-permute-done.10.next_ref = f32[3,8,256]{2,1,0:T(8,128)S(1)} collective-permute-done((f32[3,8,256]{2,1,0:T(8,128)S(1)}, f32[3,8,256]{2,1,0:T(8,128)S(1)}, u32[]{:S(2)}, u32[]{:S(2)}) %collective-permute-start.10) | collective-permute-done | bytes 24608 | tf_op jit(solution)/shard_map/ppermute | solution.py:456
  96.1 0.9 input_grads.1
  97.0 0.0 all-to-all-done.1
  97.0 2.1 %spread.1 = (f32[2048,256]{1,0:T(8,128)}, f32[3,3,256]{2,1,0:T(4,128)}, f32[16,1024]{1,0:T(8,128)}, f32[1,256]{1,0:T(1,128)}) custom-call(bf16[256,2176]{1,0:T(8,128)(2,1)S(1)} %bitcast.20), custom_call_target="tpu_custom_call" | custom-call | flops 1024 | bytes 1024 | tf_op jit(solution)/shard_map/spread/pallas_call | solution.py:46
Async XLA Ops:
  0.6 30.7 %collective-permute-start.7 = (bf16[256,8192]{1,0:T(8,128)(2,1)}, bf16[256,8192]{1,0:T(8,128)(2,1)}, u32[]{:S(2)}, u32[]{:S(2)}) collective-permute-start(bf16[256,8192]{1,0:T(8,128)(2,1)} %bitcast.17), channel_id=1, source_target_pairs={{0,32},{32,0},{1,33},{33,1},{2,34},{34,2},{3,35},{35,3},{4,36},{36... | collective-permute-start | bytes 12582920 | tf_op jit(solution)/shard_map/ppermute | solution.py:478
  3.1 13.1 %collective-permute-start.1 = (bf16[256,512]{1,0:T(8,128)(2,1)S(1)}, bf16[256,512]{1,0:T(8,128)(2,1)S(1)}, u32[]{:S(2)}, u32[]{:S(2)}) collective-permute-start(bf16[256,512]{1,0:T(8,128)(2,1)S(1)} %pad_maximum_fusion), channel_id=1, source_target_pairs={{0,64},{1,65},{2,66},{3,67},{4,68},{5,69},{6,70},{7,71},{8,72},{9,... | collective-permute-start | bytes 786440 | tf_op jit(solution)/shard_map/ppermute | solution.py:476
  7.9 12.3 %collective-permute-start = (bf16[256,512]{1,0:T(8,128)(2,1)S(1)}, bf16[256,512]{1,0:T(8,128)(2,1)S(1)}, u32[]{:S(2)}, u32[]{:S(2)}) collective-permute-start(bf16[256,512]{1,0:T(8,128)(2,1)S(1)} %pad_maximum_fusion), channel_id=1, source_target_pairs={{0,32},{32,0},{1,33},{33,1},{2,34},{34,2},{3,35},{35,3},{4,36},{36... | collective-permute-start | bytes 786440 | tf_op jit(solution)/shard_map/ppermute | solution.py:477
  9.0 7.9 %copy-start.1 = (bf16[1,256,256]{2,1,0:T(8,128)(2,1)S(1)}, bf16[1,256,256]{2,1,0:T(8,128)(2,1)}, u32[]{:S(2)}) copy-start(bf16[1,256,256]{2,1,0:T(8,128)(2,1)} %param.8) | copy-start | bytes 393220
  9.0 7.9 %copy-start.5 = (f32[3,3,256]{2,1,0:T(4,128)S(1)}, f32[3,3,256]{2,1,0:T(4,128)}, u32[]{:S(2)}) copy-start(f32[3,3,256]{2,1,0:T(4,128)} %taps_ref.7) | copy-start | bytes 27652
  9.0 12.0 %copy-start.2 = (bf16[1,256,256]{2,1,0:T(8,128)(2,1)S(1)}, bf16[1,256,256]{2,1,0:T(8,128)(2,1)}, u32[]{:S(2)}) copy-start(bf16[1,256,256]{2,1,0:T(8,128)(2,1)} %param.10) | copy-start | bytes 393220
  9.0 12.0 %copy-start.3 = (bf16[1,256,256]{2,1,0:T(8,128)(2,1)S(1)}, bf16[1,256,256]{2,1,0:T(8,128)(2,1)}, u32[]{:S(2)}) copy-start(bf16[1,256,256]{2,1,0:T(8,128)(2,1)} %param.9) | copy-start | bytes 393220
  9.0 12.0 %copy-start.6 = (f32[256]{0:T(256)S(1)}, f32[256]{0:T(256)}, u32[]{:S(2)}) copy-start(f32[256]{0:T(256)} %param.13) | copy-start | bytes 3076
  9.0 7.3 %collective-permute-start.2 = (bf16[16,256]{1,0:T(8,128)(2,1)S(1)}, bf16[16,256]{1,0:T(8,128)(2,1)S(1)}, u32[]{:S(2)}, u32[]{:S(2)}) collective-permute-start(bf16[16,256]{1,0:T(8,128)(2,1)S(1)} %slice_bitcast_fusion), channel_id=1, source_target_pairs={{0,32},{32,64},{64,96},{1,33},{33,65},{65,97},{2,34},{34,66},{66,9... | collective-permute-start | bytes 24584 | tf_op jit(solution)/shard_map/ppermute | solution.py:456
  16.3 4.6 %collective-permute-start.3 = (bf16[256,512]{1,0:T(8,128)(2,1)S(1)}, bf16[256,512]{1,0:T(8,128)(2,1)S(1)}, u32[]{:S(2)}, u32[]{:S(2)}) collective-permute-start(bf16[256,512]{1,0:T(8,128)(2,1)S(1)} %collective-permute-done.1.cross_ref), channel_id=1, source_target_pairs={{0,32},{32,0},{1,33},{33,1},{2,34},{34,2},{3,35},{35,3},{4,36},{36... | collective-permute-start | bytes 786440 | tf_op jit(solution)/shard_map/ppermute | solution.py:482
  17.0 8.4 %collective-permute-start.4 = (bf16[256,256]{1,0:T(8,128)(2,1)S(1)}, bf16[256,256]{1,0:T(8,128)(2,1)S(1)}, u32[]{:S(2)}, u32[]{:S(2)}) collective-permute-start(bf16[256,256]{1,0:T(8,128)(2,1)S(1)} %d_inner.1.d_inner_ref.d0_ref), channel_id=1, source_target_pairs={{32,0},{64,32},{96,64},{33,1},{65,33},{97,65},{34,2},{66,34},{98,6... | collective-permute-start | bytes 393224 | tf_op jit(solution)/shard_map/ppermute | solution.py:456
  18.9 8.9 %collective-permute-start.5 = (bf16[256,256]{1,0:T(8,128)(2,1)S(1)}, bf16[256,256]{1,0:T(8,128)(2,1)S(1)}, u32[]{:S(2)}, u32[]{:S(2)}) collective-permute-start(bf16[256,256]{1,0:T(8,128)(2,1)S(1)} %d_inner.1.d_inner_ref.d0_ref), channel_id=1, source_target_pairs={{64,0},{96,32},{65,1},{97,33},{66,2},{98,34},{67,3},{99,35},{68,4}... | collective-permute-start | bytes 393224 | tf_op jit(solution)/shard_map/ppermute | solution.py:456
  20.2 7.6 %collective-permute-start.6 = (bf16[256,256]{1,0:T(8,128)(2,1)S(1)}, bf16[256,256]{1,0:T(8,128)(2,1)S(1)}, u32[]{:S(2)}, u32[]{:S(2)}) collective-permute-start(bf16[256,256]{1,0:T(8,128)(2,1)S(1)} %d_inner.1.d_inner_ref.d0_ref), channel_id=1, source_target_pairs={{96,0},{97,1},{98,2},{99,3},{100,4},{101,5},{102,6},{103,7},{104,8... | collective-permute-start | bytes 393224 | tf_op jit(solution)/shard_map/ppermute | solution.py:456
  20.9 6.9 %copy-start.4 = (bf16[16,1024]{1,0:T(8,128)(2,1)S(1)}, bf16[16,1024]{1,0:T(8,128)(2,1)}, u32[]{:S(2)}) copy-start(bf16[16,1024]{1,0:T(8,128)(2,1)} %lags_ref.3) | copy-start | bytes 98308
  20.9 10.4 %copy-start = (bf16[1,256,8192]{2,1,0:T(8,128)(2,1)S(1)}, bf16[1,256,8192]{2,1,0:T(8,128)(2,1)}, u32[]{:S(2)}) copy-start(bf16[1,256,8192]{2,1,0:T(8,128)(2,1)} %param.15) | copy-start | bytes 12582916
  22.9 6.6 %collective-permute-start.8 = (bf16[256,256]{1,0:T(8,128)(2,1)S(1)}, bf16[256,256]{1,0:T(8,128)(2,1)S(1)}, u32[]{:S(2)}, u32[]{:S(2)}) collective-permute-start(bf16[256,256]{1,0:T(8,128)(2,1)S(1)} %get-tuple-element.37.gated_ref), channel_id=1, source_target_pairs={{0,32},{32,0},{1,33},{33,1},{2,34},{34,2},{3,35},{35,3},{4,36},{36... | collective-permute-start | bytes 393224 | tf_op jit(solution)/shard_map/ppermute | solution.py:488
  29.5 5.4 %collective-permute-start.9 = (f32[32,8,128]{2,1,0:T(8,128)S(1)}, f32[32,8,128]{2,1,0:T(8,128)S(1)}, u32[]{:S(2)}, u32[]{:S(2)}) collective-permute-start(f32[32,8,128]{2,1,0:T(8,128)S(1)} %get-tuple-element.45.small_ref), channel_id=1, source_target_pairs={{0,32},{32,0},{1,33},{33,1},{2,34},{34,2},{3,35},{35,3},{4,36},{36... | collective-permute-start | bytes 393224 | tf_op jit(solution)/shard_map/ppermute | solution.py:495
  76.5 20.5 %all-to-all-start.1 = ((bf16[32,8,2176]{2,1,0:T(8,128)(2,1)}), bf16[32,8,2176]{2,1,0:T(8,128)(2,1)S(1)}, u32[]{:S(2)}, u32[]{:S(2)}) async-start(bf16[32,8,2176]{2,1,0:T(8,128)(2,1)} %total.1), calls=%async_computation.1 | async-start | bytes 2228224 | tf_op jit(solution)/shard_map/all_to_all | solution.py:505
  80.4 15.7 %collective-permute-start.10 = (f32[3,8,256]{2,1,0:T(8,128)S(1)}, f32[3,8,256]{2,1,0:T(8,128)S(1)}, u32[]{:S(2)}, u32[]{:S(2)}) collective-permute-start(f32[3,8,256]{2,1,0:T(8,128)S(1)} %get-tuple-element.49), channel_id=1, source_target_pairs={{32,0},{64,32},{96,64},{33,1},{65,33},{97,65},{34,2},{66,34},{98,6... | collective-permute-start | bytes 73736 | tf_op jit(solution)/shard_map/ppermute | solution.py:456

commit v11 on v10

--- a/solution.py
+++ b/solution.py
@@ -215,9 +215,8 @@
     for half in range(2):
         start = pl.multiple_of((2 * half + core_ref[0]) * SHARE, SHARE)
         own_cot = own_cot_ref[:, pl.ds(start, SHARE)]
-        other_cot = other_cot_ref[:, pl.ds(start, SHARE)]
         total = lax.dot_general(gated_ref[...], own_cot, dims, preferred_element_type=F32)
-        total += lax.dot_general(other_gated_ref[...], other_cot, dims, preferred_element_type=F32)
+        total += lax.dot_general(other_gated_ref[...], other_cot_ref[half], dims, preferred_element_type=F32)
         out_ref[half, :, :SHARE] = total.astype(BF16)
 
 
@@ -271,7 +270,20 @@
     return ((row // block) * block + (block - 1 - row % block) == col).astype(F32)
 
 
-def lag_kernel(d_inner_ref, signal_ref, filter_ref, outer_ref, stack_ref, sums_ref):
+def lag_kernel(
+    core_ref, cot_ref, d_inner_ref, signal_ref,
+    filter_ref, part_ref,
+    outer_ref, stack_ref, sums_ref, sems,
+):
+    copies = []
+    for half in range(2):
+        start = pl.multiple_of((2 * half + core_ref[0]) * SHARE, SHARE)
+        copies.append(
+            pltpu.make_async_copy(
+                cot_ref.at[:, pl.ds(start, SHARE)], part_ref.at[half], sems.at[half]
+            )
+        )
+        copies[-1].start()
     turn = turn_matrix(ROWS, STRIP).astype(BF16)
     turned = jnp.dot(turn, d_inner_ref[...], preferred_element_type=F32)
     ids = lane_groups()
@@ -311,6 +323,8 @@
             precision=lax.Precision.HIGHEST,
             preferred_element_type=F32,
         )
+    for copy in copies:
+        copy.wait()
 
 
 def lag_call(*operands):
@@ -318,8 +332,12 @@
         pltpu.VMEM((GROUPS * STRIP, WIDE), F32),
         pltpu.VMEM((GROUPS * STRIP // 2, CHANS), BF16),
         pltpu.VMEM((GROUPS, WIDE), F32),
-    ]
-    return call(lag_kernel, "lag_sums", pltpu.VMEM((GROUPS, LENGTH), F32), operands, scratch)
+        pltpu.SemaphoreType.DMA((2,)),
+    ]
+    out_shape = [pltpu.VMEM((GROUPS, LENGTH), F32), pltpu.VMEM((2, ROWS, SHARE), BF16)]
+    in_specs = [pl.BlockSpec(memory_space=pltpu.SMEM), pl.BlockSpec(memory_space=pltpu.HBM)]
+    in_specs += [pl.BlockSpec(memory_space=pltpu.VMEM)] * 2
+    return call(lag_kernel, "lag_sums", out_shape, operands, scratch, in_specs=in_specs)
 
 
 def bwd_kernel(
@@ -379,8 +397,8 @@
     return call(bwd_kernel, "bwd", out_shape, operands, scratch, 1)
 
 
-def input_grad_kernel(d_short_ref, next_ref, taps_ref, query_ref, key_ref, value_ref):
-    for i, out_ref in enumerate((query_ref, key_ref, value_ref)):
+def input_grads(d_short_ref, next_ref, taps_ref, out_refs):
+    for i, out_ref in enumerate(out_refs):
         joined = jnp.concatenate([d_short_ref[i], next_ref[i]], axis=0)
         rows = joined.shape[0]
         parts = (
@@ -391,11 +409,6 @@
         out_ref[...] = short_sum(taps_ref, i, parts).astype(BF16)
 
 
-def input_grad_call(*operands):
-    out_shape = [jax.ShapeDtypeStruct((ROWS, CHANS), BF16)] * 3
-    return call(input_grad_kernel, "input_grads", out_shape, operands)
-
-
 def total_kernel(scale, terms_ref, out_ref):
     total = (jnp.sum(terms_ref[...].astype(F32), axis=0) * scale).astype(BF16)
     out_ref[...] = jnp.broadcast_to(total[None], out_ref.shape)
@@ -407,7 +420,9 @@
 
 
 def spread_kernel(
-    shares_ref, weight_ref, taps_ref, filter_ref, skip_ref, turned_ref, sems
+    shares_ref, d_short_ref, next_ref, short_taps_ref,
+    weight_ref, taps_ref, filter_ref, skip_ref, query_ref, key_ref, value_ref,
+    turned_ref, sems,
 ):
     tile = SHARE // SPREAD
     copies = []
@@ -418,6 +433,7 @@
             pltpu.make_async_copy(turned_ref.at[piece, :], weight_ref.at[piece, :], sems.at[n])
         )
         copies[-1].start()
+    input_grads(d_short_ref, next_ref, short_taps_ref, (query_ref, key_ref, value_ref))
     small = shares_ref[:, SHARE:].astype(F32)
 
     def part(share, slot):
@@ -436,18 +452,20 @@
         copy.wait()
 
 
-def spread_call(shares):
+def spread_call(shares, *operands):
     out_shape = [
         jax.ShapeDtypeStruct((SHARE, CHANS), F32),
         jax.ShapeDtypeStruct((3, 3, CHANS), F32),
         jax.ShapeDtypeStruct((GROUPS, LENGTH), F32),
         jax.ShapeDtypeStruct((1, CHANS), F32),
+        *[jax.ShapeDtypeStruct((ROWS, CHANS), BF16)] * 3,
     ]
     scratch = [pltpu.VMEM((SHARE, CHANS), F32), pltpu.SemaphoreType.DMA((SPREAD,))]
     out_specs = [pl.BlockSpec(memory_space=pl.ANY)]
-    out_specs += [pl.BlockSpec(memory_space=pltpu.VMEM)] * 3
+    out_specs += [pl.BlockSpec(memory_space=pltpu.VMEM)] * 6
     shares = shares.reshape(CHANS, SHARE + HALF)
-    return call(spread_kernel, "spread", out_shape, (shares,), scratch, out_specs=out_specs)
+    operands = (shares, *operands)
+    return call(spread_kernel, "spread", out_shape, operands, scratch, out_specs=out_specs)
 
 
 def sent(block, distance):
@@ -486,29 +504,28 @@
         core, strips, pair, cross, cross_pair, key, value, query, tail, taps, skip
     )
     other_gated = lax.ppermute(gated, "co", swap)
-    lag_sums = lag_call(d_inner, signal)
+    lag_sums, other_part = lag_call(core, other_cot, d_inner, signal)
     d_short, head, small = bwd_call(
         core, *blocks, long_filter, lag_sums, signal, key, value, pair, cross_pair, query, tail,
         inner, d_gated, taps, skip,
     )
     other_gated, head, small = lax.optimization_barrier((other_gated, head, small))
     other_small = lax.ppermute(small, "co", swap)
-    terms = terms_call(core, cot, other_cot, gated, other_gated)
+    terms = terms_call(core, cot, other_part, gated, other_gated)
     terms, other_small = lax.optimization_barrier((terms, other_small))
     terms = add_small_call(terms, small, other_small)
     terms, head = lax.optimization_barrier((terms, head))
     terms = terms.reshape(2 * SHARES, CHANS // SHARES, SHARE + HALF)
     terms = lax.all_to_all(terms, CHIPS, 0, 0)
     following = sent(head, -1)
-    grad_query, grad_key, grad_value = input_grad_call(d_short, following, taps)
 
     shares = lax.all_to_all(total_call(terms, scale), DP, 0, 0)
-    grad_weight, grad_taps, grad_filter, grad_skip = spread_call(shares)
+    grad_weight, grad_taps, grad_filter, grad_skip, *input_grad = spread_call(
+        shares, d_short, following, taps
+    )
     return (
         gated[None],
-        grad_query[None],
-        grad_key[None],
-        grad_value[None],
+        *(grad[None] for grad in input_grad),
         grad_taps,
         grad_filter,
         grad_skip.reshape(CHANS),

time: 99.6 us -> 98.5 us (0.989)
  Pallas kernels: 19.1 us -> 17.2 us
  blocking collectives: 40.2 us -> 41.2 us
  waiting for transfers between devices: 14.3 us -> 13.3 us
    pallas_call x9 -> x8, Pallas kernels: 19.1 us -> 17.1 us  [call(): pl.pallas_call(kernel, out_shape=out_shape, scratch_shapes=list(scratch),...]
    ppermute x5, waiting for transfers between devices: 14.3 us -> 13.2 us  [sent(): return lax.ppermute(block, CTX, route)]
  transfers between devices with their start and end apart: 12 -> 12, of which waited for: 2 -> 3; matrix products, arithmetic and copies ran while one was open for 2% -> 2% of each run, Pallas kernels for 16% -> 14%
where the time goes in v11:
time: 98.5 us; the launch traced here: 97.3 us
  blocking collectives  41.2 us (42%)
  starting transfers between devices  22.3 us (23%)
  Pallas kernels  17.2 us (17%)
  waiting for transfers between devices  13.3 us (14%)
  local copies, waits for them, and re-layouts  1.39 us (1%)
  other arithmetic  0.99 us (1%)
    all_to_all x1, blocking collectives, shards(): terms = lax.all_to_all(terms, CHIPS, 0, 0)  41.2 us
    pallas_call x8, Pallas kernels, call(): pl.pallas_call(kernel, out_shape=out_shape, scratch_shapes=list(scratch),...  17.1 us
    ppermute x5, waiting for transfers between devices, sent(): return lax.ppermute(block, CTX, route)  13.2 us
    ppermute x5, starting transfers between devices, sent(): return lax.ppermute(block, CTX, route)  9.16 us
    ppermute x1, starting transfers between devices, shards(): cross = lax.ppermute(own, 'xh', [(0, 1)])  4.75 us
    all_to_all x1, starting transfers between devices, shards(): shares = lax.all_to_all(total_call(terms, scale), DP, 0, 0)  3.94 us
  transfers between devices with their start and end apart: 12, of which 3 were waited for; matrix products, arithmetic and copies ran while one was open for 2% of the time, Pallas kernels for 14%

profile of v11, /device:TPU:1, one launch (start us, length us, event | category | flops | bytes accessed | tf_op | source)
XLA Modules:
  0.0 97.3 jit_solution(3693257965168337925)
XLA Ops:
  0.6 1.5 %collective-permute-start.4 = (bf16[256,8192]{1,0:T(8,128)(2,1)}, bf16[256,8192]{1,0:T(8,128)(2,1)}, u32[]{:S(2)}, u32[]{:S(2)}) collective-permute-start(bf16[256,8192]{1,0:T(8,128)(2,1)} %bitcast.17), channel_id=1, source_target_pairs={{0,32},{32,0},{1,33},{33,1},{2,34},{34,2},{3,35},{35,3},{4,36},{36... | collective-permute-start | bytes 12582920 | tf_op jit(solution)/shard_map/ppermute | solution.py:496
  2.1 1.0 %pad_maximum_fusion = bf16[256,512]{1,0:T(8,128)(2,1)S(1)} fusion(bf16[256,256]{1,0:T(8,128)(2,1)} %bitcast.24, bf16[256,256]{1,0:T(8,128)(2,1)} %bitcast.27), kind=kLoop, calls=%fused_computation | loop fusion | flops 524288 | bytes 524288 | tf_op jit(solution)/shard_map/concatenate | solution.py:492
  3.1 4.7 %collective-permute-start.1 = (bf16[256,512]{1,0:T(8,128)(2,1)S(1)}, bf16[256,512]{1,0:T(8,128)(2,1)S(1)}, u32[]{:S(2)}, u32[]{:S(2)}) collective-permute-start(bf16[256,512]{1,0:T(8,128)(2,1)S(1)} %pad_maximum_fusion), channel_id=1, source_target_pairs={{0,64},{1,65},{2,66},{3,67},{4,68},{5,69},{6,70},{7,71},{8,72},{9,... | collective-permute-start | bytes 786440 | tf_op jit(solution)/shard_map/ppermute | solution.py:494
  7.9 0.4 collective-permute-start
  8.3 0.7 slice_bitcast_fusion
  9.0 0.0 copy-start.1
  9.0 0.0 copy-start.5
  9.0 0.0 copy-start.2
  9.0 0.0 copy-start.3
  9.0 0.0 copy-start.6
  9.0 2.1 %collective-permute-start.2 = (bf16[16,256]{1,0:T(8,128)(2,1)S(1)}, bf16[16,256]{1,0:T(8,128)(2,1)S(1)}, u32[]{:S(2)}, u32[]{:S(2)}) collective-permute-start(bf16[16,256]{1,0:T(8,128)(2,1)S(1)} %slice_bitcast_fusion), channel_id=1, source_target_pairs={{0,32},{32,64},{64,96},{1,33},{33,65},{65,97},{2,34},{34,66},{66,9... | collective-permute-start | bytes 24584 | tf_op jit(solution)/shard_map/ppermute | solution.py:474
  11.0 5.2 %pre.1 = (bf16[256,256]{1,0:T(8,128)(2,1)S(1)}, bf16[512,1024]{1,0:T(8,128)(2,1)S(1)}) custom-call(bf16[256,8192]{1,0:T(8,128)(2,1)} %bitcast.18, bf16[8192,256]{1,0:T(8,128)(2,1)} %weight_ref.1, bf16[16,1024]{1,0:T(8,128)(2,1)} %lags_ref.3), custom_call_target="tpu_custom_call" | custom-call | flops 1073741824 | bytes 1024 | tf_op jit(solution)/shard_map/pre/pallas_call | solution.py:46
  16.2 0.0 collective-permute-done.2.tail_ref
  16.2 0.0 collective-permute-done.1.cross_ref
  16.3 0.6 collective-permute-start.3
  16.8 0.0 copy-done.1
  16.8 0.0 copy-done.5
  16.8 0.1 d_inner.1.d_inner_ref.d0_ref
  17.0 1.9 %collective-permute-start.6 = (bf16[256,256]{1,0:T(8,128)(2,1)S(1)}, bf16[256,256]{1,0:T(8,128)(2,1)S(1)}, u32[]{:S(2)}, u32[]{:S(2)}) collective-permute-start(bf16[256,256]{1,0:T(8,128)(2,1)S(1)} %d_inner.1.d_inner_ref.d0_ref), channel_id=1, source_target_pairs={{32,0},{64,32},{96,64},{33,1},{65,33},{97,65},{34,2},{66,34},{98,6... | collective-permute-start | bytes 393224 | tf_op jit(solution)/shard_map/ppermute | solution.py:474
  18.9 1.3 %collective-permute-start.7 = (bf16[256,256]{1,0:T(8,128)(2,1)S(1)}, bf16[256,256]{1,0:T(8,128)(2,1)S(1)}, u32[]{:S(2)}, u32[]{:S(2)}) collective-permute-start(bf16[256,256]{1,0:T(8,128)(2,1)S(1)} %d_inner.1.d_inner_ref.d0_ref), channel_id=1, source_target_pairs={{64,0},{96,32},{65,1},{97,33},{66,2},{98,34},{67,3},{99,35},{68,4}... | collective-permute-start | bytes 393224 | tf_op jit(solution)/shard_map/ppermute | solution.py:474
  20.2 0.0 collective-permute-done.pair_ref
  20.2 0.7 collective-permute-start.8
  20.9 0.0 collective-permute-done.3.cross_pair_ref
  20.9 0.0 copy-done.2
  20.9 0.0 copy-done.3
  20.9 0.0 copy-done.6
  20.9 1.9 %fwd.1 = (bf16[256,256]{1,0:T(8,128)(2,1)S(1)}, f32[256,256]{1,0:T(8,128)S(1)}, bf16[1248,256]{1,0:T(8,128)(2,1)S(1)}) custom-call(s32[1]{0:T(128)} %bitcast.core_ref, bf16[512,1024]{1,0:T(8,128)(2,1)S(1)} %get-tuple-element.35.strips_ref, bf16[256,512]{1,0:T(8,128)(2,1)S(1)} %collective-permute-done.pair_ref, ...), custom_call_target="tpu_custom_call" | custom-call | flops 4294967296 | bytes 1024 | tf_op jit(solution)/shard_map/fwd/pallas_call | solution.py:46
  22.9 0.1 collective-permute-start.5
  23.0 0.0 collective-permute-done.4.cot_ref
  23.0 0.0 copy-start.4
  23.0 0.0 copy-start
  23.0 3.4 %lag_sums.1 = (f32[16,1024]{1,0:T(8,128)S(1)}, bf16[2,256,2048]{2,1,0:T(8,128)(2,1)S(1)}) custom-call(s32[1]{0:T(128)} %bitcast.core_ref, bf16[256,8192]{1,0:T(8,128)(2,1)} %collective-permute-done.4.cot_ref, bf16[256,256]{1,0:T(8,128)(2,1)S(1)} %d_inner.1.d_inner_ref.d0_ref, bf16[1248,256]{1,0:T(8,128)(2,1)S(1)} %get-tuple-element.41.signal_ref), custom_call_target="tpu_custom_call" | custom-call | flops 1024 | bytes 1024 | tf_op jit(solution)/shard_map/lag_sums/pallas_call | solution.py:46
  26.4 0.0 collective-permute-done.6.d1_ref
  26.4 1.4 %collective-permute-done.7.d2_ref = bf16[256,256]{1,0:T(8,128)(2,1)S(1)} collective-permute-done((bf16[256,256]{1,0:T(8,128)(2,1)S(1)}, bf16[256,256]{1,0:T(8,128)(2,1)S(1)}, u32[]{:S(2)}, u32[]{:S(2)}) %collective-permute-start.7) | collective-permute-done | bytes 131104 | tf_op jit(solution)/shard_map/ppermute | solution.py:474
  27.8 0.0 collective-permute-done.8.d3_ref
  27.8 0.0 copy-done.4
  27.8 1.6 %bwd.1 = (f32[3,256,256]{2,1,0:T(8,128)S(1)}, f32[3,8,256]{2,1,0:T(8,128)S(1)}, f32[32,8,128]{2,1,0:T(8,128)S(1)}) custom-call(s32[1]{0:T(128)} %bitcast.core_ref, bf16[256,256]{1,0:T(8,128)(2,1)S(1)} %d_inner.1.d_inner_ref.d0_ref, bf16[256,256]{1,0:T(8,128)(2,1)S(1)} %collective-permute-done.6.d1_ref, bf16[256,256]{1,0:T(8,128)(2,1)S(1)} %collective-permute-done.7.d2_ref, ...), custom_call_target="tpu_custom_call" | custom-call | flops 1024 | bytes 1024 | tf_op jit(solution)/shard_map/bwd/pallas_call | solution.py:46
  29.5 0.0 collective-permute-done.5.other_gated_ref
  29.5 1.9 %collective-permute-start.9 = (f32[32,8,128]{2,1,0:T(8,128)S(1)}, f32[32,8,128]{2,1,0:T(8,128)S(1)}, u32[]{:S(2)}, u32[]{:S(2)}) collective-permute-start(f32[32,8,128]{2,1,0:T(8,128)S(1)} %get-tuple-element.48.small_ref), channel_id=1, source_target_pairs={{0,32},{32,0},{1,33},{33,1},{2,34},{34,2},{3,35},{35,3},{4,36},{36... | collective-permute-start | bytes 393224 | tf_op jit(solution)/shard_map/ppermute | solution.py:513
  31.4 0.0 copy-done
  31.4 1.3 %terms.1.terms_ref = bf16[2,256,2176]{2,1,0:T(8,128)(2,1)S(1)} custom-call(s32[1]{0:T(128)} %bitcast.core_ref, bf16[256,8192]{1,0:T(8,128)(2,1)S(1)} %bitcast.19, bf16[2,256,2048]{2,1,0:T(8,128)(2,1)S(1)} %get-tuple-element.42.other_cot_ref, bf16[256,256]{1,0:T(8,128)(2,1)S(1)} %get-tuple-element.39.gated_ref, ...), custom_call_target="tpu_custom_call" | custom-call | flops 1073741824 | bytes 1024 | tf_op jit(solution)/shard_map/terms/pallas_call | solution.py:46
  32.6 0.0 collective-permute-done.9.other_small_ref
  32.7 0.1 add_small.1
  32.7 41.2 %all_to_all.10.refs_0_ = bf16[64,8,2176]{2,1,0:T(8,128)(2,1)S(1)} all-to-all(bf16[64,8,2176]{2,1,0:T(8,128)(2,1)S(1)} %bitcast.16), channel_id=1, replica_groups=mesh['xh'=2,'co'=2,'y'=4,'xl'=2,'z'=4] {'xh','y','xl','z'}, dimensions={0} | all-to-all | bytes 4456448 | tf_op jit(solution)/shard_map/all_to_all | solution.py:519
  73.9 1.4 %total.1 = bf16[32,8,2176]{2,1,0:T(8,128)(2,1)} custom-call(bf16[64,8,2176]{2,1,0:T(8,128)(2,1)S(1)} %all_to_all.10.refs_0_), custom_call_target="tpu_custom_call" | custom-call | flops 1024 | bytes 1024 | tf_op jit(solution)/shard_map/total/pallas_call | solution.py:46
  75.3 3.9 %all-to-all-start.1 = ((bf16[32,8,2176]{2,1,0:T(8,128)(2,1)}), bf16[32,8,2176]{2,1,0:T(8,128)(2,1)S(1)}, u32[]{:S(2)}, u32[]{:S(2)}) async-start(bf16[32,8,2176]{2,1,0:T(8,128)(2,1)} %total.1), calls=%async_computation.1 | async-start | bytes 2228224 | tf_op jit(solution)/shard_map/all_to_all | solution.py:522
  79.2 3.2 %collective-permute-start.10 = (f32[3,8,256]{2,1,0:T(8,128)S(1)}, f32[3,8,256]{2,1,0:T(8,128)S(1)}, u32[]{:S(2)}, u32[]{:S(2)}) collective-permute-start(f32[3,8,256]{2,1,0:T(8,128)S(1)} %get-tuple-element.54), channel_id=1, source_target_pairs={{32,0},{64,32},{96,64},{33,1},{65,33},{97,65},{34,2},{66,34},{98,6... | collective-permute-start | bytes 73736 | tf_op jit(solution)/shard_map/ppermute | solution.py:474
  82.4 0.7 copy.18
  83.1 11.8 %collective-permute-done.10.next_ref = f32[3,8,256]{2,1,0:T(8,128)S(1)} collective-permute-done((f32[3,8,256]{2,1,0:T(8,128)S(1)}, f32[3,8,256]{2,1,0:T(8,128)S(1)}, u32[]{:S(2)}, u32[]{:S(2)}) %collective-permute-start.10) | collective-permute-done | bytes 24608 | tf_op jit(solution)/shard_map/ppermute | solution.py:474
  94.9 0.1 all-to-all-done.1
  95.0 2.3 %spread.1 = (f32[2048,256]{1,0:T(8,128)}, f32[3,3,256]{2,1,0:T(4,128)}, f32[16,1024]{1,0:T(8,128)}, f32[1,256]{1,0:T(1,128)}, bf16[256,256]{1,0:T(8,128)(2,1)}, ...) custom-call(bf16[256,2176]{1,0:T(8,128)(2,1)S(1)} %bitcast.20, f32[3,256,256]{2,1,0:T(8,128)S(1)} %get-tuple-element.53.d_short_ref, ...), custom_call_target="tpu_custom_call" | custom-call | flops 1024 | bytes 1024 | tf_op jit(solution)/shard_map/spread/pallas_call | solution.py:46
Async XLA Ops:
  0.6 22.3 %collective-permute-start.4 = (bf16[256,8192]{1,0:T(8,128)(2,1)}, bf16[256,8192]{1,0:T(8,128)(2,1)}, u32[]{:S(2)}, u32[]{:S(2)}) collective-permute-start(bf16[256,8192]{1,0:T(8,128)(2,1)} %bitcast.17), channel_id=1, source_target_pairs={{0,32},{32,0},{1,33},{33,1},{2,34},{34,2},{3,35},{35,3},{4,36},{36... | collective-permute-start | bytes 12582920 | tf_op jit(solution)/shard_map/ppermute | solution.py:496
  3.1 13.1 %collective-permute-start.1 = (bf16[256,512]{1,0:T(8,128)(2,1)S(1)}, bf16[256,512]{1,0:T(8,128)(2,1)S(1)}, u32[]{:S(2)}, u32[]{:S(2)}) collective-permute-start(bf16[256,512]{1,0:T(8,128)(2,1)S(1)} %pad_maximum_fusion), channel_id=1, source_target_pairs={{0,64},{1,65},{2,66},{3,67},{4,68},{5,69},{6,70},{7,71},{8,72},{9,... | collective-permute-start | bytes 786440 | tf_op jit(solution)/shard_map/ppermute | solution.py:494
  7.9 12.3 %collective-permute-start = (bf16[256,512]{1,0:T(8,128)(2,1)S(1)}, bf16[256,512]{1,0:T(8,128)(2,1)S(1)}, u32[]{:S(2)}, u32[]{:S(2)}) collective-permute-start(bf16[256,512]{1,0:T(8,128)(2,1)S(1)} %pad_maximum_fusion), channel_id=1, source_target_pairs={{0,32},{32,0},{1,33},{33,1},{2,34},{34,2},{3,35},{35,3},{4,36},{36... | collective-permute-start | bytes 786440 | tf_op jit(solution)/shard_map/ppermute | solution.py:495
  9.0 7.9 %copy-start.1 = (bf16[1,256,256]{2,1,0:T(8,128)(2,1)S(1)}, bf16[1,256,256]{2,1,0:T(8,128)(2,1)}, u32[]{:S(2)}) copy-start(bf16[1,256,256]{2,1,0:T(8,128)(2,1)} %param.8) | copy-start | bytes 393220
  9.0 7.9 %copy-start.5 = (f32[3,3,256]{2,1,0:T(4,128)S(1)}, f32[3,3,256]{2,1,0:T(4,128)}, u32[]{:S(2)}) copy-start(f32[3,3,256]{2,1,0:T(4,128)} %short_taps_ref.1) | copy-start | bytes 27652
  9.0 12.0 %copy-start.2 = (bf16[1,256,256]{2,1,0:T(8,128)(2,1)S(1)}, bf16[1,256,256]{2,1,0:T(8,128)(2,1)}, u32[]{:S(2)}) copy-start(bf16[1,256,256]{2,1,0:T(8,128)(2,1)} %param.10) | copy-start | bytes 393220
  9.0 12.0 %copy-start.3 = (bf16[1,256,256]{2,1,0:T(8,128)(2,1)S(1)}, bf16[1,256,256]{2,1,0:T(8,128)(2,1)}, u32[]{:S(2)}) copy-start(bf16[1,256,256]{2,1,0:T(8,128)(2,1)} %param.9) | copy-start | bytes 393220
  9.0 12.0 %copy-start.6 = (f32[256]{0:T(256)S(1)}, f32[256]{0:T(256)}, u32[]{:S(2)}) copy-start(f32[256]{0:T(256)} %param.13) | copy-start | bytes 3076
  9.0 7.3 %collective-permute-start.2 = (bf16[16,256]{1,0:T(8,128)(2,1)S(1)}, bf16[16,256]{1,0:T(8,128)(2,1)S(1)}, u32[]{:S(2)}, u32[]{:S(2)}) collective-permute-start(bf16[16,256]{1,0:T(8,128)(2,1)S(1)} %slice_bitcast_fusion), channel_id=1, source_target_pairs={{0,32},{32,64},{64,96},{1,33},{33,65},{65,97},{2,34},{34,66},{66,9... | collective-permute-start | bytes 24584 | tf_op jit(solution)/shard_map/ppermute | solution.py:474
  16.3 4.6 %collective-permute-start.3 = (bf16[256,512]{1,0:T(8,128)(2,1)S(1)}, bf16[256,512]{1,0:T(8,128)(2,1)S(1)}, u32[]{:S(2)}, u32[]{:S(2)}) collective-permute-start(bf16[256,512]{1,0:T(8,128)(2,1)S(1)} %collective-permute-done.1.cross_ref), channel_id=1, source_target_pairs={{0,32},{32,0},{1,33},{33,1},{2,34},{34,2},{3,35},{35,3},{4,36},{36... | collective-permute-start | bytes 786440 | tf_op jit(solution)/shard_map/ppermute | solution.py:500
  17.0 9.5 %collective-permute-start.6 = (bf16[256,256]{1,0:T(8,128)(2,1)S(1)}, bf16[256,256]{1,0:T(8,128)(2,1)S(1)}, u32[]{:S(2)}, u32[]{:S(2)}) collective-permute-start(bf16[256,256]{1,0:T(8,128)(2,1)S(1)} %d_inner.1.d_inner_ref.d0_ref), channel_id=1, source_target_pairs={{32,0},{64,32},{96,64},{33,1},{65,33},{97,65},{34,2},{66,34},{98,6... | collective-permute-start | bytes 393224 | tf_op jit(solution)/shard_map/ppermute | solution.py:474
  18.9 8.9 %collective-permute-start.7 = (bf16[256,256]{1,0:T(8,128)(2,1)S(1)}, bf16[256,256]{1,0:T(8,128)(2,1)S(1)}, u32[]{:S(2)}, u32[]{:S(2)}) collective-permute-start(bf16[256,256]{1,0:T(8,128)(2,1)S(1)} %d_inner.1.d_inner_ref.d0_ref), channel_id=1, source_target_pairs={{64,0},{96,32},{65,1},{97,33},{66,2},{98,34},{67,3},{99,35},{68,4}... | collective-permute-start | bytes 393224 | tf_op jit(solution)/shard_map/ppermute | solution.py:474
  20.2 7.6 %collective-permute-start.8 = (bf16[256,256]{1,0:T(8,128)(2,1)S(1)}, bf16[256,256]{1,0:T(8,128)(2,1)S(1)}, u32[]{:S(2)}, u32[]{:S(2)}) collective-permute-start(bf16[256,256]{1,0:T(8,128)(2,1)S(1)} %d_inner.1.d_inner_ref.d0_ref), channel_id=1, source_target_pairs={{96,0},{97,1},{98,2},{99,3},{100,4},{101,5},{102,6},{103,7},{104,8... | collective-permute-start | bytes 393224 | tf_op jit(solution)/shard_map/ppermute | solution.py:474
  22.9 6.6 %collective-permute-start.5 = (bf16[256,256]{1,0:T(8,128)(2,1)S(1)}, bf16[256,256]{1,0:T(8,128)(2,1)S(1)}, u32[]{:S(2)}, u32[]{:S(2)}) collective-permute-start(bf16[256,256]{1,0:T(8,128)(2,1)S(1)} %get-tuple-element.39.gated_ref), channel_id=1, source_target_pairs={{0,32},{32,0},{1,33},{33,1},{2,34},{34,2},{3,35},{35,3},{4,36},{36... | collective-permute-start | bytes 393224 | tf_op jit(solution)/shard_map/ppermute | solution.py:506
  23.0 4.9 %copy-start.4 = (bf16[16,1024]{1,0:T(8,128)(2,1)S(1)}, bf16[16,1024]{1,0:T(8,128)(2,1)}, u32[]{:S(2)}) copy-start(bf16[16,1024]{1,0:T(8,128)(2,1)} %lags_ref.3) | copy-start | bytes 98308
  23.0 8.4 %copy-start = (bf16[1,256,8192]{2,1,0:T(8,128)(2,1)S(1)}, bf16[1,256,8192]{2,1,0:T(8,128)(2,1)}, u32[]{:S(2)}) copy-start(bf16[1,256,8192]{2,1,0:T(8,128)(2,1)} %param.15) | copy-start | bytes 12582916
  29.5 3.2 %collective-permute-start.9 = (f32[32,8,128]{2,1,0:T(8,128)S(1)}, f32[32,8,128]{2,1,0:T(8,128)S(1)}, u32[]{:S(2)}, u32[]{:S(2)}) collective-permute-start(f32[32,8,128]{2,1,0:T(8,128)S(1)} %get-tuple-element.48.small_ref), channel_id=1, source_target_pairs={{0,32},{32,0},{1,33},{33,1},{2,34},{34,2},{3,35},{35,3},{4,36},{36... | collective-permute-start | bytes 393224 | tf_op jit(solution)/shard_map/ppermute | solution.py:513
  75.3 19.7 %all-to-all-start.1 = ((bf16[32,8,2176]{2,1,0:T(8,128)(2,1)}), bf16[32,8,2176]{2,1,0:T(8,128)(2,1)S(1)}, u32[]{:S(2)}, u32[]{:S(2)}) async-start(bf16[32,8,2176]{2,1,0:T(8,128)(2,1)} %total.1), calls=%async_computation.1 | async-start | bytes 2228224 | tf_op jit(solution)/shard_map/all_to_all | solution.py:522
  79.2 15.6 %collective-permute-start.10 = (f32[3,8,256]{2,1,0:T(8,128)S(1)}, f32[3,8,256]{2,1,0:T(8,128)S(1)}, u32[]{:S(2)}, u32[]{:S(2)}) collective-permute-start(f32[3,8,256]{2,1,0:T(8,128)S(1)} %get-tuple-element.54), channel_id=1, source_target_pairs={{32,0},{64,32},{96,64},{33,1},{65,33},{97,65},{34,2},{66,34},{98,6... | collective-permute-start | bytes 73736 | tf_op jit(solution)/shard_map/ppermute | solution.py:474

commit v12 on v11

--- a/solution.py
+++ b/solution.py
@@ -341,13 +341,22 @@
 
 
 def bwd_kernel(
-    core_ref, d0_ref, d1_ref, d2_ref, d3_ref, lags_ref, filter_ref, signal_ref, key_ref, value_ref,
+    core_ref, d0_ref, d_pair_ref, d_cross_ref, d_cross_pair_ref, lags_ref, filter_ref, signal_ref, key_ref, value_ref,
     pair_ref, cross_pair_ref, query_ref, tail_ref, inner_ref, d_gated_ref, taps_ref, skip_ref,
     d_short_ref, head_ref, small_ref,
     strips_ref, ahead_ref,
 ):
-    for n, ref in enumerate((d0_ref, d1_ref, d2_ref, d3_ref)):
-        ahead_ref[n * ROWS : (n + 1) * ROWS, :] = ref[...]
+    upper = core_ref[0] == 1
+    d_pair = d_pair_ref[...].astype(F32)
+    d_cross_pair = d_cross_pair_ref[...].astype(F32)
+    later_blocks = (
+        d0_ref[...],
+        jnp.where(upper, d_cross_pair, d_pair).astype(BF16),
+        d_cross_ref[...],
+        jnp.where(upper, 0.0, d_cross_pair).astype(BF16),
+    )
+    for n, block in enumerate(later_blocks):
+        ahead_ref[n * ROWS : (n + 1) * ROWS, :] = block
     ahead_ref[LENGTH:, :] = jnp.zeros((ROWS, CHANS), BF16)
     lines = lines_of(lags_ref, False)
     for g in range(GROUPS):
@@ -356,7 +365,6 @@
     mixed = signal_ref[LENGTH - STRIP :, :]
     d_mixed = all_strips(strips_ref, ahead_ref) + skip_ref[...] * d_inner
 
-    upper = core_ref[0] == 1
     last = slice(ROWS - TAIL, ROWS)
     near = jnp.where(upper, pair_ref[last, :].astype(F32), cross_pair_ref[last, :].astype(F32))
     k_parts = with_tail(near[:, :CHANS], key_ref[...])
@@ -499,14 +507,17 @@
     cross, tail, d_gated = lax.optimization_barrier((cross, tail, d_gated))
     cross_pair = lax.ppermute(cross, "co", swap)
     d_inner = d_inner_call(d_gated, query, tail, taps)
-    blocks = [d_inner] + [sent(d_inner, -distance) for distance in (1, 2, 3)]
+    d_cross = lax.ppermute(d_inner, "xh", [(1, 0)])
+    d_pair = lax.ppermute(d_inner, "co", swap)
     gated, inner, signal = fwd_call(
         core, strips, pair, cross, cross_pair, key, value, query, tail, taps, skip
     )
     other_gated = lax.ppermute(gated, "co", swap)
+    d_cross, signal = lax.optimization_barrier((d_cross, signal))
+    d_cross_pair = lax.ppermute(d_cross, "co", swap)
     lag_sums, other_part = lag_call(core, other_cot, d_inner, signal)
     d_short, head, small = bwd_call(
-        core, *blocks, long_filter, lag_sums, signal, key, value, pair, cross_pair, query, tail,
+        core, d_inner, d_pair, d_cross, d_cross_pair, long_filter, lag_sums, signal, key, value, pair, cross_pair, query, tail,
         inner, d_gated, taps, skip,
     )
     other_gated, head, small = lax.optimization_barrier((other_gated, head, small))

time: 98.5 us -> 97.9 us (level)
  waiting for transfers between devices: 13.3 us -> 17 us
  starting transfers between devices: 22.3 us -> 19.2 us
  blocking collectives: 41.2 us -> 40 us
    ppermute x0 -> x3, waiting for transfers between devices: none -> 5.11 us  [the longest x1 5.1 us: shards(): d_cross = lax.ppermute(d_inner, 'xh', [(1, 0)])]
    ppermute x5 -> x2, starting transfers between devices: 9.16 us -> 5.25 us  [sent(): return lax.ppermute(block, CTX, route)]
    ppermute x0 -> x3, starting transfers between devices: none -> 2.23 us  [the longest x1 1.29 us: shards(): d_cross = lax.ppermute(d_inner, 'xh', [(1, 0)])]
    ppermute x5 -> x2, waiting for transfers between devices: 13.2 us -> 11.8 us  [sent(): return lax.ppermute(block, CTX, route)]
    ppermute x1, starting transfers between devices: 1.89 us -> 0.57 us  [shards(): other_small = lax.ppermute(small, 'co', swap)]
    all_to_all x1, blocking collectives: 41.2 us -> 40 us  [shards(): terms = lax.all_to_all(terms, CHIPS, 0, 0)]
where the time goes in v12:
time: 97.9 us; the launch traced here: 96.7 us
  blocking collectives  40 us (41%)
  starting transfers between devices  19.2 us (20%)
  Pallas kernels  17.2 us (18%)
  waiting for transfers between devices  17 us (17%)
  local copies, waits for them, and re-layouts  1.39 us (1%)
  other arithmetic  0.99 us (1%)
    all_to_all x1, blocking collectives, shards(): terms = lax.all_to_all(terms, CHIPS, 0, 0)  40 us
    pallas_call x8, Pallas kernels, call(): pl.pallas_call(kernel, out_shape=out_shape, scratch_shapes=list(scratch),...  17.2 us
    ppermute x2, waiting for transfers between devices, sent(): return lax.ppermute(block, CTX, route)  11.8 us
    ppermute x2, starting transfers between devices, sent(): return lax.ppermute(block, CTX, route)  5.25 us
    ppermute x1, waiting for transfers between devices, shards(): d_cross = lax.ppermute(d_inner, 'xh', [(1, 0)])  5.1 us
    ppermute x1, starting transfers between devices, shards(): cross = lax.ppermute(own, 'xh', [(0, 1)])  4.75 us
    all_to_all x1, starting transfers between devices, shards(): shares = lax.all_to_all(total_call(terms, scale), DP, 0, 0)  3.94 us
  transfers between devices with their start and end apart: 12, of which 3 were waited for; matrix products, arithmetic and copies ran while one was open for 2% of the time, Pallas kernels for 14%

profile of v12, /device:TPU:1, one launch (start us, length us, event | category | flops | bytes accessed | tf_op | source)
XLA Modules:
  0.0 96.7 jit_solution(15170258830153205819)
XLA Ops:
  0.6 1.5 %collective-permute-start.4 = (bf16[256,8192]{1,0:T(8,128)(2,1)}, bf16[256,8192]{1,0:T(8,128)(2,1)}, u32[]{:S(2)}, u32[]{:S(2)}) collective-permute-start(bf16[256,8192]{1,0:T(8,128)(2,1)} %bitcast.17), channel_id=1, source_target_pairs={{0,32},{32,0},{1,33},{33,1},{2,34},{34,2},{3,35},{35,3},{4,36},{36... | collective-permute-start | bytes 12582920 | tf_op jit(solution)/shard_map/ppermute | solution.py:504
  2.1 1.0 %pad_maximum_fusion = bf16[256,512]{1,0:T(8,128)(2,1)S(1)} fusion(bf16[256,256]{1,0:T(8,128)(2,1)} %bitcast.24, bf16[256,256]{1,0:T(8,128)(2,1)} %bitcast.27), kind=kLoop, calls=%fused_computation | loop fusion | flops 524288 | bytes 524288 | tf_op jit(solution)/shard_map/concatenate | solution.py:500
  3.1 4.7 %collective-permute-start.1 = (bf16[256,512]{1,0:T(8,128)(2,1)S(1)}, bf16[256,512]{1,0:T(8,128)(2,1)S(1)}, u32[]{:S(2)}, u32[]{:S(2)}) collective-permute-start(bf16[256,512]{1,0:T(8,128)(2,1)S(1)} %pad_maximum_fusion), channel_id=1, source_target_pairs={{0,64},{1,65},{2,66},{3,67},{4,68},{5,69},{6,70},{7,71},{8,72},{9,... | collective-permute-start | bytes 786440 | tf_op jit(solution)/shard_map/ppermute | solution.py:502
  7.9 0.4 collective-permute-start
  8.3 0.7 slice_bitcast_fusion
  9.0 0.0 copy-start.1
  9.0 0.0 copy-start.5
  9.0 0.0 copy-start.2
  9.0 0.0 copy-start.3
  9.0 0.0 copy-start.6
  9.0 2.1 %collective-permute-start.2 = (bf16[16,256]{1,0:T(8,128)(2,1)S(1)}, bf16[16,256]{1,0:T(8,128)(2,1)S(1)}, u32[]{:S(2)}, u32[]{:S(2)}) collective-permute-start(bf16[16,256]{1,0:T(8,128)(2,1)S(1)} %slice_bitcast_fusion), channel_id=1, source_target_pairs={{0,32},{32,64},{64,96},{1,33},{33,65},{65,97},{2,34},{34,66},{66,9... | collective-permute-start | bytes 24584 | tf_op jit(solution)/shard_map/ppermute | solution.py:482
  11.0 5.2 %pre.1 = (bf16[256,256]{1,0:T(8,128)(2,1)S(1)}, bf16[512,1024]{1,0:T(8,128)(2,1)S(1)}) custom-call(bf16[256,8192]{1,0:T(8,128)(2,1)} %bitcast.18, bf16[8192,256]{1,0:T(8,128)(2,1)} %weight_ref.1, bf16[16,1024]{1,0:T(8,128)(2,1)} %lags_ref.3), custom_call_target="tpu_custom_call" | custom-call | flops 1073741824 | bytes 1024 | tf_op jit(solution)/shard_map/pre/pallas_call | solution.py:46
  16.2 0.0 collective-permute-done.2.tail_ref
  16.2 0.0 collective-permute-done.1.cross_ref
  16.3 0.6 collective-permute-start.3
  16.8 0.0 copy-done.1
  16.8 0.0 copy-done.5
  16.8 0.1 d_inner.1.d_inner_ref.d0_ref
  17.0 1.3 %collective-permute-start.5 = (bf16[256,256]{1,0:T(8,128)(2,1)S(1)}, bf16[256,256]{1,0:T(8,128)(2,1)S(1)}, u32[]{:S(2)}, u32[]{:S(2)}) collective-permute-start(bf16[256,256]{1,0:T(8,128)(2,1)S(1)} %d_inner.1.d_inner_ref.d0_ref), channel_id=1, source_target_pairs={{64,0},{65,1},{66,2},{67,3},{68,4},{69,5},{70,6},{71,7},{72,8},{73... | collective-permute-start | bytes 393224 | tf_op jit(solution)/shard_map/ppermute | solution.py:510
  18.3 0.1 collective-permute-start.7
  18.4 0.0 collective-permute-done.pair_ref
  18.4 0.0 collective-permute-done.3.cross_pair_ref
  18.4 0.0 copy-done.2
  18.4 0.0 copy-done.3
  18.4 0.0 copy-done.6
  18.4 1.9 %fwd.1 = (bf16[256,256]{1,0:T(8,128)(2,1)S(1)}, f32[256,256]{1,0:T(8,128)S(1)}, bf16[1248,256]{1,0:T(8,128)(2,1)S(1)}) custom-call(s32[1]{0:T(128)} %bitcast.core_ref, bf16[512,1024]{1,0:T(8,128)(2,1)S(1)} %get-tuple-element.37.strips_ref, bf16[256,512]{1,0:T(8,128)(2,1)S(1)} %collective-permute-done.pair_ref, ...), custom_call_target="tpu_custom_call" | custom-call | flops 4294967296 | bytes 1024 | tf_op jit(solution)/shard_map/fwd/pallas_call | solution.py:46
  20.3 5.1 %collective-permute-done.5.d_cross_ref = bf16[256,256]{1,0:T(8,128)(2,1)S(1)} collective-permute-done((bf16[256,256]{1,0:T(8,128)(2,1)S(1)}, bf16[256,256]{1,0:T(8,128)(2,1)S(1)}, u32[]{:S(2)}, u32[]{:S(2)}) %collective-permute-start.5) | collective-permute-done | bytes 131104 | tf_op jit(solution)/shard_map/ppermute | solution.py:510
  25.4 0.8 collective-permute-start.8
  26.3 0.0 copy-start.4
  26.3 0.0 collective-permute-start.6
  26.3 0.0 collective-permute-done.4.cot_ref
  26.3 0.0 copy-start
  26.3 3.4 %lag_sums.1 = (f32[16,1024]{1,0:T(8,128)S(1)}, bf16[2,256,2048]{2,1,0:T(8,128)(2,1)S(1)}) custom-call(s32[1]{0:T(128)} %bitcast.core_ref, bf16[256,8192]{1,0:T(8,128)(2,1)} %collective-permute-done.4.cot_ref, bf16[256,256]{1,0:T(8,128)(2,1)S(1)} %d_inner.1.d_inner_ref.d0_ref, bf16[1248,256]{1,0:T(8,128)(2,1)S(1)} %get-tuple-element.44.signal_ref), custom_call_target="tpu_custom_call" | custom-call | flops 1024 | bytes 1024 | tf_op jit(solution)/shard_map/lag_sums/pallas_call | solution.py:46
  29.7 0.0 collective-permute-done.7.d_pair_ref
  29.7 0.0 collective-permute-done.8.d_cross_pair_ref
  29.7 0.0 copy-done.4
  29.7 1.6 %bwd.1 = (f32[3,256,256]{2,1,0:T(8,128)S(1)}, f32[3,8,256]{2,1,0:T(8,128)S(1)}, f32[32,8,128]{2,1,0:T(8,128)S(1)}) custom-call(s32[1]{0:T(128)} %bitcast.core_ref, bf16[256,256]{1,0:T(8,128)(2,1)S(1)} %d_inner.1.d_inner_ref.d0_ref, bf16[256,256]{1,0:T(8,128)(2,1)S(1)} %collective-permute-done.7.d_pair_ref, ...), custom_call_target="tpu_custom_call" | custom-call | flops 1024 | bytes 1024 | tf_op jit(solution)/shard_map/bwd/pallas_call | solution.py:46
  31.4 0.0 collective-permute-done.6.other_gated_ref
  31.4 0.6 collective-permute-start.9
  32.0 0.0 copy-done
  32.0 1.3 %terms.1.terms_ref = bf16[2,256,2176]{2,1,0:T(8,128)(2,1)S(1)} custom-call(s32[1]{0:T(128)} %bitcast.core_ref, bf16[256,8192]{1,0:T(8,128)(2,1)S(1)} %bitcast.19, bf16[2,256,2048]{2,1,0:T(8,128)(2,1)S(1)} %get-tuple-element.45.other_cot_ref, bf16[256,256]{1,0:T(8,128)(2,1)S(1)} %get-tuple-element.41.gated_ref, ...), custom_call_target="tpu_custom_call" | custom-call | flops 1073741824 | bytes 1024 | tf_op jit(solution)/shard_map/terms/pallas_call | solution.py:46
  33.2 0.0 collective-permute-done.9.other_small_ref
  33.3 0.1 add_small.1
  33.3 40.0 %all_to_all.10.refs_0_ = bf16[64,8,2176]{2,1,0:T(8,128)(2,1)S(1)} all-to-all(bf16[64,8,2176]{2,1,0:T(8,128)(2,1)S(1)} %bitcast.16), channel_id=1, replica_groups=mesh['xh'=2,'co'=2,'y'=4,'xl'=2,'z'=4] {'xh','y','xl','z'}, dimensions={0} | all-to-all | bytes 4456448 | tf_op jit(solution)/shard_map/all_to_all | solution.py:530
  73.3 1.4 %total.1 = bf16[32,8,2176]{2,1,0:T(8,128)(2,1)} custom-call(bf16[64,8,2176]{2,1,0:T(8,128)(2,1)S(1)} %all_to_all.10.refs_0_), custom_call_target="tpu_custom_call" | custom-call | flops 1024 | bytes 1024 | tf_op jit(solution)/shard_map/total/pallas_call | solution.py:46
  74.7 3.9 %all-to-all-start.1 = ((bf16[32,8,2176]{2,1,0:T(8,128)(2,1)}), bf16[32,8,2176]{2,1,0:T(8,128)(2,1)S(1)}, u32[]{:S(2)}, u32[]{:S(2)}) async-start(bf16[32,8,2176]{2,1,0:T(8,128)(2,1)} %total.1), calls=%async_computation.1 | async-start | bytes 2228224 | tf_op jit(solution)/shard_map/all_to_all | solution.py:533
  78.6 3.2 %collective-permute-start.10 = (f32[3,8,256]{2,1,0:T(8,128)S(1)}, f32[3,8,256]{2,1,0:T(8,128)S(1)}, u32[]{:S(2)}, u32[]{:S(2)}) collective-permute-start(f32[3,8,256]{2,1,0:T(8,128)S(1)} %get-tuple-element.58), channel_id=1, source_target_pairs={{32,0},{64,32},{96,64},{33,1},{65,33},{97,65},{34,2},{66,34},{98,6... | collective-permute-start | bytes 73736 | tf_op jit(solution)/shard_map/ppermute | solution.py:482
  81.8 0.7 copy.18
  82.5 11.8 %collective-permute-done.10.next_ref = f32[3,8,256]{2,1,0:T(8,128)S(1)} collective-permute-done((f32[3,8,256]{2,1,0:T(8,128)S(1)}, f32[3,8,256]{2,1,0:T(8,128)S(1)}, u32[]{:S(2)}, u32[]{:S(2)}) %collective-permute-start.10) | collective-permute-done | bytes 24608 | tf_op jit(solution)/shard_map/ppermute | solution.py:482
  94.3 0.1 all-to-all-done.1
  94.4 2.3 %spread.1 = (f32[2048,256]{1,0:T(8,128)}, f32[3,3,256]{2,1,0:T(4,128)}, f32[16,1024]{1,0:T(8,128)}, f32[1,256]{1,0:T(1,128)}, bf16[256,256]{1,0:T(8,128)(2,1)}, ...) custom-call(bf16[256,2176]{1,0:T(8,128)(2,1)S(1)} %bitcast.20, f32[3,256,256]{2,1,0:T(8,128)S(1)} %get-tuple-element.57.d_short_ref, ...), custom_call_target="tpu_custom_call" | custom-call | flops 1024 | bytes 1024 | tf_op jit(solution)/shard_map/spread/pallas_call | solution.py:46
Async XLA Ops:
  0.6 25.6 %collective-permute-start.4 = (bf16[256,8192]{1,0:T(8,128)(2,1)}, bf16[256,8192]{1,0:T(8,128)(2,1)}, u32[]{:S(2)}, u32[]{:S(2)}) collective-permute-start(bf16[256,8192]{1,0:T(8,128)(2,1)} %bitcast.17), channel_id=1, source_target_pairs={{0,32},{32,0},{1,33},{33,1},{2,34},{34,2},{3,35},{35,3},{4,36},{36... | collective-permute-start | bytes 12582920 | tf_op jit(solution)/shard_map/ppermute | solution.py:504
  3.1 13.1 %collective-permute-start.1 = (bf16[256,512]{1,0:T(8,128)(2,1)S(1)}, bf16[256,512]{1,0:T(8,128)(2,1)S(1)}, u32[]{:S(2)}, u32[]{:S(2)}) collective-permute-start(bf16[256,512]{1,0:T(8,128)(2,1)S(1)} %pad_maximum_fusion), channel_id=1, source_target_pairs={{0,64},{1,65},{2,66},{3,67},{4,68},{5,69},{6,70},{7,71},{8,72},{9,... | collective-permute-start | bytes 786440 | tf_op jit(solution)/shard_map/ppermute | solution.py:502
  7.9 10.5 %collective-permute-start = (bf16[256,512]{1,0:T(8,128)(2,1)S(1)}, bf16[256,512]{1,0:T(8,128)(2,1)S(1)}, u32[]{:S(2)}, u32[]{:S(2)}) collective-permute-start(bf16[256,512]{1,0:T(8,128)(2,1)S(1)} %pad_maximum_fusion), channel_id=1, source_target_pairs={{0,32},{32,0},{1,33},{33,1},{2,34},{34,2},{3,35},{35,3},{4,36},{36... | collective-permute-start | bytes 786440 | tf_op jit(solution)/shard_map/ppermute | solution.py:503
  9.0 7.9 %copy-start.1 = (bf16[1,256,256]{2,1,0:T(8,128)(2,1)S(1)}, bf16[1,256,256]{2,1,0:T(8,128)(2,1)}, u32[]{:S(2)}) copy-start(bf16[1,256,256]{2,1,0:T(8,128)(2,1)} %param.8) | copy-start | bytes 393220
  9.0 7.9 %copy-start.5 = (f32[3,3,256]{2,1,0:T(4,128)S(1)}, f32[3,3,256]{2,1,0:T(4,128)}, u32[]{:S(2)}) copy-start(f32[3,3,256]{2,1,0:T(4,128)} %short_taps_ref.1) | copy-start | bytes 27652
  9.0 9.4 %copy-start.2 = (bf16[1,256,256]{2,1,0:T(8,128)(2,1)S(1)}, bf16[1,256,256]{2,1,0:T(8,128)(2,1)}, u32[]{:S(2)}) copy-start(bf16[1,256,256]{2,1,0:T(8,128)(2,1)} %param.10) | copy-start | bytes 393220
  9.0 9.4 %copy-start.3 = (bf16[1,256,256]{2,1,0:T(8,128)(2,1)S(1)}, bf16[1,256,256]{2,1,0:T(8,128)(2,1)}, u32[]{:S(2)}) copy-start(bf16[1,256,256]{2,1,0:T(8,128)(2,1)} %param.9) | copy-start | bytes 393220
  9.0 9.4 %copy-start.6 = (f32[256]{0:T(256)S(1)}, f32[256]{0:T(256)}, u32[]{:S(2)}) copy-start(f32[256]{0:T(256)} %param.13) | copy-start | bytes 3076
  9.0 7.3 %collective-permute-start.2 = (bf16[16,256]{1,0:T(8,128)(2,1)S(1)}, bf16[16,256]{1,0:T(8,128)(2,1)S(1)}, u32[]{:S(2)}, u32[]{:S(2)}) collective-permute-start(bf16[16,256]{1,0:T(8,128)(2,1)S(1)} %slice_bitcast_fusion), channel_id=1, source_target_pairs={{0,32},{32,64},{64,96},{1,33},{33,65},{65,97},{2,34},{34,66},{66,9... | collective-permute-start | bytes 24584 | tf_op jit(solution)/shard_map/ppermute | solution.py:482
  16.3 2.1 %collective-permute-start.3 = (bf16[256,512]{1,0:T(8,128)(2,1)S(1)}, bf16[256,512]{1,0:T(8,128)(2,1)S(1)}, u32[]{:S(2)}, u32[]{:S(2)}) collective-permute-start(bf16[256,512]{1,0:T(8,128)(2,1)S(1)} %collective-permute-done.1.cross_ref), channel_id=1, source_target_pairs={{0,32},{32,0},{1,33},{33,1},{2,34},{34,2},{3,35},{35,3},{4,36},{36... | collective-permute-start | bytes 786440 | tf_op jit(solution)/shard_map/ppermute | solution.py:508
  17.0 8.5 %collective-permute-start.5 = (bf16[256,256]{1,0:T(8,128)(2,1)S(1)}, bf16[256,256]{1,0:T(8,128)(2,1)S(1)}, u32[]{:S(2)}, u32[]{:S(2)}) collective-permute-start(bf16[256,256]{1,0:T(8,128)(2,1)S(1)} %d_inner.1.d_inner_ref.d0_ref), channel_id=1, source_target_pairs={{64,0},{65,1},{66,2},{67,3},{68,4},{69,5},{70,6},{71,7},{72,8},{73... | collective-permute-start | bytes 393224 | tf_op jit(solution)/shard_map/ppermute | solution.py:510
  18.3 11.5 %collective-permute-start.7 = (bf16[256,256]{1,0:T(8,128)(2,1)S(1)}, bf16[256,256]{1,0:T(8,128)(2,1)S(1)}, u32[]{:S(2)}, u32[]{:S(2)}) collective-permute-start(bf16[256,256]{1,0:T(8,128)(2,1)S(1)} %d_inner.1.d_inner_ref.d0_ref), channel_id=1, source_target_pairs={{0,32},{32,0},{1,33},{33,1},{2,34},{34,2},{3,35},{35,3},{4,36},{36... | collective-permute-start | bytes 393224 | tf_op jit(solution)/shard_map/ppermute | solution.py:511
  25.4 4.3 %collective-permute-start.8 = (bf16[256,256]{1,0:T(8,128)(2,1)S(1)}, bf16[256,256]{1,0:T(8,128)(2,1)S(1)}, u32[]{:S(2)}, u32[]{:S(2)}) collective-permute-start(bf16[256,256]{1,0:T(8,128)(2,1)S(1)} %collective-permute-done.5.d_cross_ref), channel_id=1, source_target_pairs={{0,32},{32,0},{1,33},{33,1},{2,34},{34,2},{3,35},{35,3},{4,36},{36... | collective-permute-start | bytes 393224 | tf_op jit(solution)/shard_map/ppermute | solution.py:517
  26.3 3.5 %copy-start.4 = (bf16[16,1024]{1,0:T(8,128)(2,1)S(1)}, bf16[16,1024]{1,0:T(8,128)(2,1)}, u32[]{:S(2)}) copy-start(bf16[16,1024]{1,0:T(8,128)(2,1)} %lags_ref.3) | copy-start | bytes 98308
  26.3 5.1 %collective-permute-start.6 = (bf16[256,256]{1,0:T(8,128)(2,1)S(1)}, bf16[256,256]{1,0:T(8,128)(2,1)S(1)}, u32[]{:S(2)}, u32[]{:S(2)}) collective-permute-start(bf16[256,256]{1,0:T(8,128)(2,1)S(1)} %get-tuple-element.41.gated_ref), channel_id=1, source_target_pairs={{0,32},{32,0},{1,33},{33,1},{2,34},{34,2},{3,35},{35,3},{4,36},{36... | collective-permute-start | bytes 393224 | tf_op jit(solution)/shard_map/ppermute | solution.py:515
  26.3 5.7 %copy-start = (bf16[1,256,8192]{2,1,0:T(8,128)(2,1)S(1)}, bf16[1,256,8192]{2,1,0:T(8,128)(2,1)}, u32[]{:S(2)}) copy-start(bf16[1,256,8192]{2,1,0:T(8,128)(2,1)} %param.15) | copy-start | bytes 12582916
  31.4 1.9 %collective-permute-start.9 = (f32[32,8,128]{2,1,0:T(8,128)S(1)}, f32[32,8,128]{2,1,0:T(8,128)S(1)}, u32[]{:S(2)}, u32[]{:S(2)}) collective-permute-start(f32[32,8,128]{2,1,0:T(8,128)S(1)} %get-tuple-element.52.small_ref), channel_id=1, source_target_pairs={{0,32},{32,0},{1,33},{33,1},{2,34},{34,2},{3,35},{35,3},{4,36},{36... | collective-permute-start | bytes 393224 | tf_op jit(solution)/shard_map/ppermute | solution.py:524
  74.7 19.7 %all-to-all-start.1 = ((bf16[32,8,2176]{2,1,0:T(8,128)(2,1)}), bf16[32,8,2176]{2,1,0:T(8,128)(2,1)S(1)}, u32[]{:S(2)}, u32[]{:S(2)}) async-start(bf16[32,8,2176]{2,1,0:T(8,128)(2,1)} %total.1), calls=%async_computation.1 | async-start | bytes 2228224 | tf_op jit(solution)/shard_map/all_to_all | solution.py:533
  78.6 15.6 %collective-permute-start.10 = (f32[3,8,256]{2,1,0:T(8,128)S(1)}, f32[3,8,256]{2,1,0:T(8,128)S(1)}, u32[]{:S(2)}, u32[]{:S(2)}) collective-permute-start(f32[3,8,256]{2,1,0:T(8,128)S(1)} %get-tuple-element.58), channel_id=1, source_target_pairs={{32,0},{64,32},{96,64},{33,1},{65,33},{97,65},{34,2},{66,34},{98,6... | collective-permute-start | bytes 73736 | tf_op jit(solution)/shard_map/ppermute | solution.py:482

commit v13 on v12

--- a/solution.py
+++ b/solution.py
@@ -513,9 +513,9 @@
         core, strips, pair, cross, cross_pair, key, value, query, tail, taps, skip
     )
     other_gated = lax.ppermute(gated, "co", swap)
-    d_cross, signal = lax.optimization_barrier((d_cross, signal))
+    lag_sums, other_part = lag_call(core, other_cot, d_inner, signal)
+    d_cross, lag_sums = lax.optimization_barrier((d_cross, lag_sums))
     d_cross_pair = lax.ppermute(d_cross, "co", swap)
-    lag_sums, other_part = lag_call(core, other_cot, d_inner, signal)
     d_short, head, small = bwd_call(
         core, d_inner, d_pair, d_cross, d_cross_pair, long_filter, lag_sums, signal, key, value, pair, cross_pair, query, tail,
         inner, d_gated, taps, skip,

time: 97.9 us -> 96.3 us (0.984)
  waiting for transfers between devices: 17 us -> 14.3 us
    ppermute x1, waiting for transfers between devices: 5.1 us -> 1.64 us  [shards(): d_cross = lax.ppermute(d_inner, 'xh', [(1, 0)])]
where the time goes in v13:
time: 96.3 us; the launch traced here: 95 us
  blocking collectives  40.7 us (42%)
  starting transfers between devices  19.7 us (20%)
  Pallas kernels  17.2 us (18%)
  waiting for transfers between devices  14.3 us (15%)
  local copies, waits for them, and re-layouts  1.39 us (1%)
  other arithmetic  0.99 us (1%)
    all_to_all x1, blocking collectives, shards(): terms = lax.all_to_all(terms, CHIPS, 0, 0)  40.7 us
    pallas_call x8, Pallas kernels, call(): pl.pallas_call(kernel, out_shape=out_shape, scratch_shapes=list(scratch),...  17.1 us
    ppermute x2, waiting for transfers between devices, sent(): return lax.ppermute(block, CTX, route)  11.6 us
    ppermute x2, starting transfers between devices, sent(): return lax.ppermute(block, CTX, route)  5.56 us
    ppermute x1, starting transfers between devices, shards(): cross = lax.ppermute(own, 'xh', [(0, 1)])  4.75 us
    all_to_all x1, starting transfers between devices, shards(): shares = lax.all_to_all(total_call(terms, scale), DP, 0, 0)  4.25 us
  transfers between devices with their start and end apart: 12, of which 3 were waited for; matrix products, arithmetic and copies ran while one was open for 2% of the time, Pallas kernels for 14%

profile of v13, /device:TPU:1, one launch (start us, length us, event | category | flops | bytes accessed | tf_op | source)
XLA Modules:
  0.0 95.0 jit_solution(7498981676186227668)
XLA Ops:
  0.6 1.5 %collective-permute-start.4 = (bf16[256,8192]{1,0:T(8,128)(2,1)}, bf16[256,8192]{1,0:T(8,128)(2,1)}, u32[]{:S(2)}, u32[]{:S(2)}) collective-permute-start(bf16[256,8192]{1,0:T(8,128)(2,1)} %bitcast.17), channel_id=1, source_target_pairs={{0,32},{32,0},{1,33},{33,1},{2,34},{34,2},{3,35},{35,3},{4,36},{36... | collective-permute-start | bytes 12582920 | tf_op jit(solution)/shard_map/ppermute | solution.py:504
  2.1 1.0 %pad_maximum_fusion = bf16[256,512]{1,0:T(8,128)(2,1)S(1)} fusion(bf16[256,256]{1,0:T(8,128)(2,1)} %bitcast.24, bf16[256,256]{1,0:T(8,128)(2,1)} %bitcast.27), kind=kLoop, calls=%fused_computation | loop fusion | flops 524288 | bytes 524288 | tf_op jit(solution)/shard_map/concatenate | solution.py:500
  3.1 4.7 %collective-permute-start.1 = (bf16[256,512]{1,0:T(8,128)(2,1)S(1)}, bf16[256,512]{1,0:T(8,128)(2,1)S(1)}, u32[]{:S(2)}, u32[]{:S(2)}) collective-permute-start(bf16[256,512]{1,0:T(8,128)(2,1)S(1)} %pad_maximum_fusion), channel_id=1, source_target_pairs={{0,64},{1,65},{2,66},{3,67},{4,68},{5,69},{6,70},{7,71},{8,72},{9,... | collective-permute-start | bytes 786440 | tf_op jit(solution)/shard_map/ppermute | solution.py:502
  7.9 0.4 collective-permute-start
  8.3 0.7 slice_bitcast_fusion
  9.0 0.0 copy-start.1
  9.0 0.0 copy-start.5
  9.0 0.0 copy-start.2
  9.0 0.0 copy-start.3
  9.0 0.0 copy-start.6
  9.0 2.1 %collective-permute-start.2 = (bf16[16,256]{1,0:T(8,128)(2,1)S(1)}, bf16[16,256]{1,0:T(8,128)(2,1)S(1)}, u32[]{:S(2)}, u32[]{:S(2)}) collective-permute-start(bf16[16,256]{1,0:T(8,128)(2,1)S(1)} %slice_bitcast_fusion), channel_id=1, source_target_pairs={{0,32},{32,64},{64,96},{1,33},{33,65},{65,97},{2,34},{34,66},{66,9... | collective-permute-start | bytes 24584 | tf_op jit(solution)/shard_map/ppermute | solution.py:482
  11.0 5.2 %pre.1 = (bf16[256,256]{1,0:T(8,128)(2,1)S(1)}, bf16[512,1024]{1,0:T(8,128)(2,1)S(1)}) custom-call(bf16[256,8192]{1,0:T(8,128)(2,1)} %bitcast.18, bf16[8192,256]{1,0:T(8,128)(2,1)} %weight_ref.1, bf16[16,1024]{1,0:T(8,128)(2,1)} %lags_ref.3), custom_call_target="tpu_custom_call" | custom-call | flops 1073741824 | bytes 1024 | tf_op jit(solution)/shard_map/pre/pallas_call | solution.py:46
  16.2 0.0 collective-permute-done.2.tail_ref
  16.2 0.0 collective-permute-done.1.cross_ref
  16.3 0.6 collective-permute-start.3
  16.8 0.0 copy-done.1
  16.8 0.0 copy-done.5
  16.8 0.1 d_inner.1.d_inner_ref.d0_ref
  17.0 1.3 %collective-permute-start.7 = (bf16[256,256]{1,0:T(8,128)(2,1)S(1)}, bf16[256,256]{1,0:T(8,128)(2,1)S(1)}, u32[]{:S(2)}, u32[]{:S(2)}) collective-permute-start(bf16[256,256]{1,0:T(8,128)(2,1)S(1)} %d_inner.1.d_inner_ref.d0_ref), channel_id=1, source_target_pairs={{64,0},{65,1},{66,2},{67,3},{68,4},{69,5},{70,6},{71,7},{72,8},{73... | collective-permute-start | bytes 393224 | tf_op jit(solution)/shard_map/ppermute | solution.py:510
  18.3 0.1 collective-permute-start.6
  18.4 0.0 collective-permute-done.pair_ref
  18.4 0.0 collective-permute-done.3.cross_pair_ref
  18.4 0.0 copy-done.2
  18.4 0.0 copy-done.3
  18.4 0.0 copy-done.6
  18.4 1.9 %fwd.1 = (bf16[256,256]{1,0:T(8,128)(2,1)S(1)}, f32[256,256]{1,0:T(8,128)S(1)}, bf16[1248,256]{1,0:T(8,128)(2,1)S(1)}) custom-call(s32[1]{0:T(128)} %bitcast.core_ref, bf16[512,1024]{1,0:T(8,128)(2,1)S(1)} %get-tuple-element.37.strips_ref, bf16[256,512]{1,0:T(8,128)(2,1)S(1)} %collective-permute-done.pair_ref, ...), custom_call_target="tpu_custom_call" | custom-call | flops 4294967296 | bytes 1024 | tf_op jit(solution)/shard_map/fwd/pallas_call | solution.py:46
  20.3 0.0 collective-permute-done.4.cot_ref
  20.4 0.0 copy-start.4
  20.4 0.0 copy-start
  20.4 3.4 %lag_sums.1 = (f32[16,1024]{1,0:T(8,128)S(1)}, bf16[2,256,2048]{2,1,0:T(8,128)(2,1)S(1)}) custom-call(s32[1]{0:T(128)} %bitcast.core_ref, bf16[256,8192]{1,0:T(8,128)(2,1)} %collective-permute-done.4.cot_ref, bf16[256,256]{1,0:T(8,128)(2,1)S(1)} %d_inner.1.d_inner_ref.d0_ref, bf16[1248,256]{1,0:T(8,128)(2,1)S(1)} %get-tuple-element.43.signal_ref), custom_call_target="tpu_custom_call" | custom-call | flops 1024 | bytes 1024 | tf_op jit(solution)/shard_map/lag_sums/pallas_call | solution.py:46
  23.8 1.6 %collective-permute-done.7.d_cross_ref = bf16[256,256]{1,0:T(8,128)(2,1)S(1)} collective-permute-done((bf16[256,256]{1,0:T(8,128)(2,1)S(1)}, bf16[256,256]{1,0:T(8,128)(2,1)S(1)}, u32[]{:S(2)}, u32[]{:S(2)}) %collective-permute-start.7) | collective-permute-done | bytes 131104 | tf_op jit(solution)/shard_map/ppermute | solution.py:510
  25.4 0.8 collective-permute-start.8
  26.3 0.0 collective-permute-start.5
  26.3 0.0 collective-permute-done.6.d_pair_ref
  26.3 1.0 %collective-permute-done.8.d_cross_pair_ref = bf16[256,256]{1,0:T(8,128)(2,1)S(1)} collective-permute-done((bf16[256,256]{1,0:T(8,128)(2,1)S(1)}, bf16[256,256]{1,0:T(8,128)(2,1)S(1)}, u32[]{:S(2)}, u32[]{:S(2)}) %collective-permute-start.8) | collective-permute-done | bytes 131104 | tf_op jit(solution)/shard_map/ppermute | solution.py:518
  27.3 0.0 copy-done.4
  27.3 1.6 %bwd.1 = (f32[3,256,256]{2,1,0:T(8,128)S(1)}, f32[3,8,256]{2,1,0:T(8,128)S(1)}, f32[32,8,128]{2,1,0:T(8,128)S(1)}) custom-call(s32[1]{0:T(128)} %bitcast.core_ref, bf16[256,256]{1,0:T(8,128)(2,1)S(1)} %d_inner.1.d_inner_ref.d0_ref, bf16[256,256]{1,0:T(8,128)(2,1)S(1)} %collective-permute-done.6.d_pair_ref, ...), custom_call_target="tpu_custom_call" | custom-call | flops 1024 | bytes 1024 | tf_op jit(solution)/shard_map/bwd/pallas_call | solution.py:46
  28.9 0.0 collective-permute-done.5.other_gated_ref
  28.9 0.4 collective-permute-start.9
  29.3 0.0 copy-done
  29.3 1.3 %terms.1.terms_ref = bf16[2,256,2176]{2,1,0:T(8,128)(2,1)S(1)} custom-call(s32[1]{0:T(128)} %bitcast.core_ref, bf16[256,8192]{1,0:T(8,128)(2,1)S(1)} %bitcast.19, bf16[2,256,2048]{2,1,0:T(8,128)(2,1)S(1)} %get-tuple-element.44.other_cot_ref, bf16[256,256]{1,0:T(8,128)(2,1)S(1)} %get-tuple-element.41.gated_ref, ...), custom_call_target="tpu_custom_call" | custom-call | flops 1073741824 | bytes 1024 | tf_op jit(solution)/shard_map/terms/pallas_call | solution.py:46
  30.6 0.0 collective-permute-done.9.other_small_ref
  30.6 0.1 add_small.1
  30.7 40.7 %all_to_all.10.refs_0_ = bf16[64,8,2176]{2,1,0:T(8,128)(2,1)S(1)} all-to-all(bf16[64,8,2176]{2,1,0:T(8,128)(2,1)S(1)} %bitcast.16), channel_id=1, replica_groups=mesh['xh'=2,'co'=2,'y'=4,'xl'=2,'z'=4] {'xh','y','xl','z'}, dimensions={0} | all-to-all | bytes 4456448 | tf_op jit(solution)/shard_map/all_to_all | solution.py:530
  71.4 1.4 %total.1 = bf16[32,8,2176]{2,1,0:T(8,128)(2,1)} custom-call(bf16[64,8,2176]{2,1,0:T(8,128)(2,1)S(1)} %all_to_all.10.refs_0_), custom_call_target="tpu_custom_call" | custom-call | flops 1024 | bytes 1024 | tf_op jit(solution)/shard_map/total/pallas_call | solution.py:46
  72.7 4.3 %all-to-all-start.1 = ((bf16[32,8,2176]{2,1,0:T(8,128)(2,1)}), bf16[32,8,2176]{2,1,0:T(8,128)(2,1)S(1)}, u32[]{:S(2)}, u32[]{:S(2)}) async-start(bf16[32,8,2176]{2,1,0:T(8,128)(2,1)} %total.1), calls=%async_computation.1 | async-start | bytes 2228224 | tf_op jit(solution)/shard_map/all_to_all | solution.py:533
  77.0 3.5 %collective-permute-start.10 = (f32[3,8,256]{2,1,0:T(8,128)S(1)}, f32[3,8,256]{2,1,0:T(8,128)S(1)}, u32[]{:S(2)}, u32[]{:S(2)}) collective-permute-start(f32[3,8,256]{2,1,0:T(8,128)S(1)} %get-tuple-element.58), channel_id=1, source_target_pairs={{32,0},{64,32},{96,64},{33,1},{65,33},{97,65},{34,2},{66,34},{98,6... | collective-permute-start | bytes 73736 | tf_op jit(solution)/shard_map/ppermute | solution.py:482
  80.5 0.7 copy.18
  81.1 11.6 %collective-permute-done.10.next_ref = f32[3,8,256]{2,1,0:T(8,128)S(1)} collective-permute-done((f32[3,8,256]{2,1,0:T(8,128)S(1)}, f32[3,8,256]{2,1,0:T(8,128)S(1)}, u32[]{:S(2)}, u32[]{:S(2)}) %collective-permute-start.10) | collective-permute-done | bytes 24608 | tf_op jit(solution)/shard_map/ppermute | solution.py:482
  92.8 0.0 all-to-all-done.1
  92.8 2.3 %spread.1 = (f32[2048,256]{1,0:T(8,128)}, f32[3,3,256]{2,1,0:T(4,128)}, f32[16,1024]{1,0:T(8,128)}, f32[1,256]{1,0:T(1,128)}, bf16[256,256]{1,0:T(8,128)(2,1)}, ...) custom-call(bf16[256,2176]{1,0:T(8,128)(2,1)S(1)} %bitcast.20, f32[3,256,256]{2,1,0:T(8,128)S(1)} %get-tuple-element.57.d_short_ref, ...), custom_call_target="tpu_custom_call" | custom-call | flops 1024 | bytes 1024 | tf_op jit(solution)/shard_map/spread/pallas_call | solution.py:46
Async XLA Ops:
  0.6 19.7 %collective-permute-start.4 = (bf16[256,8192]{1,0:T(8,128)(2,1)}, bf16[256,8192]{1,0:T(8,128)(2,1)}, u32[]{:S(2)}, u32[]{:S(2)}) collective-permute-start(bf16[256,8192]{1,0:T(8,128)(2,1)} %bitcast.17), channel_id=1, source_target_pairs={{0,32},{32,0},{1,33},{33,1},{2,34},{34,2},{3,35},{35,3},{4,36},{36... | collective-permute-start | bytes 12582920 | tf_op jit(solution)/shard_map/ppermute | solution.py:504
  3.1 13.1 %collective-permute-start.1 = (bf16[256,512]{1,0:T(8,128)(2,1)S(1)}, bf16[256,512]{1,0:T(8,128)(2,1)S(1)}, u32[]{:S(2)}, u32[]{:S(2)}) collective-permute-start(bf16[256,512]{1,0:T(8,128)(2,1)S(1)} %pad_maximum_fusion), channel_id=1, source_target_pairs={{0,64},{1,65},{2,66},{3,67},{4,68},{5,69},{6,70},{7,71},{8,72},{9,... | collective-permute-start | bytes 786440 | tf_op jit(solution)/shard_map/ppermute | solution.py:502
  7.9 10.5 %collective-permute-start = (bf16[256,512]{1,0:T(8,128)(2,1)S(1)}, bf16[256,512]{1,0:T(8,128)(2,1)S(1)}, u32[]{:S(2)}, u32[]{:S(2)}) collective-permute-start(bf16[256,512]{1,0:T(8,128)(2,1)S(1)} %pad_maximum_fusion), channel_id=1, source_target_pairs={{0,32},{32,0},{1,33},{33,1},{2,34},{34,2},{3,35},{35,3},{4,36},{36... | collective-permute-start | bytes 786440 | tf_op jit(solution)/shard_map/ppermute | solution.py:503
  9.0 7.9 %copy-start.1 = (bf16[1,256,256]{2,1,0:T(8,128)(2,1)S(1)}, bf16[1,256,256]{2,1,0:T(8,128)(2,1)}, u32[]{:S(2)}) copy-start(bf16[1,256,256]{2,1,0:T(8,128)(2,1)} %param.8) | copy-start | bytes 393220
  9.0 7.9 %copy-start.5 = (f32[3,3,256]{2,1,0:T(4,128)S(1)}, f32[3,3,256]{2,1,0:T(4,128)}, u32[]{:S(2)}) copy-start(f32[3,3,256]{2,1,0:T(4,128)} %short_taps_ref.1) | copy-start | bytes 27652
  9.0 9.4 %copy-start.2 = (bf16[1,256,256]{2,1,0:T(8,128)(2,1)S(1)}, bf16[1,256,256]{2,1,0:T(8,128)(2,1)}, u32[]{:S(2)}) copy-start(bf16[1,256,256]{2,1,0:T(8,128)(2,1)} %param.10) | copy-start | bytes 393220
  9.0 9.4 %copy-start.3 = (bf16[1,256,256]{2,1,0:T(8,128)(2,1)S(1)}, bf16[1,256,256]{2,1,0:T(8,128)(2,1)}, u32[]{:S(2)}) copy-start(bf16[1,256,256]{2,1,0:T(8,128)(2,1)} %param.9) | copy-start | bytes 393220
  9.0 9.4 %copy-start.6 = (f32[256]{0:T(256)S(1)}, f32[256]{0:T(256)}, u32[]{:S(2)}) copy-start(f32[256]{0:T(256)} %param.13) | copy-start | bytes 3076
  9.0 7.3 %collective-permute-start.2 = (bf16[16,256]{1,0:T(8,128)(2,1)S(1)}, bf16[16,256]{1,0:T(8,128)(2,1)S(1)}, u32[]{:S(2)}, u32[]{:S(2)}) collective-permute-start(bf16[16,256]{1,0:T(8,128)(2,1)S(1)} %slice_bitcast_fusion), channel_id=1, source_target_pairs={{0,32},{32,64},{64,96},{1,33},{33,65},{65,97},{2,34},{34,66},{66,9... | collective-permute-start | bytes 24584 | tf_op jit(solution)/shard_map/ppermute | solution.py:482
  16.3 2.1 %collective-permute-start.3 = (bf16[256,512]{1,0:T(8,128)(2,1)S(1)}, bf16[256,512]{1,0:T(8,128)(2,1)S(1)}, u32[]{:S(2)}, u32[]{:S(2)}) collective-permute-start(bf16[256,512]{1,0:T(8,128)(2,1)S(1)} %collective-permute-done.1.cross_ref), channel_id=1, source_target_pairs={{0,32},{32,0},{1,33},{33,1},{2,34},{34,2},{3,35},{35,3},{4,36},{36... | collective-permute-start | bytes 786440 | tf_op jit(solution)/shard_map/ppermute | solution.py:508
  17.0 8.5 %collective-permute-start.7 = (bf16[256,256]{1,0:T(8,128)(2,1)S(1)}, bf16[256,256]{1,0:T(8,128)(2,1)S(1)}, u32[]{:S(2)}, u32[]{:S(2)}) collective-permute-start(bf16[256,256]{1,0:T(8,128)(2,1)S(1)} %d_inner.1.d_inner_ref.d0_ref), channel_id=1, source_target_pairs={{64,0},{65,1},{66,2},{67,3},{68,4},{69,5},{70,6},{71,7},{72,8},{73... | collective-permute-start | bytes 393224 | tf_op jit(solution)/shard_map/ppermute | solution.py:510
  18.3 8.0 %collective-permute-start.6 = (bf16[256,256]{1,0:T(8,128)(2,1)S(1)}, bf16[256,256]{1,0:T(8,128)(2,1)S(1)}, u32[]{:S(2)}, u32[]{:S(2)}) collective-permute-start(bf16[256,256]{1,0:T(8,128)(2,1)S(1)} %d_inner.1.d_inner_ref.d0_ref), channel_id=1, source_target_pairs={{0,32},{32,0},{1,33},{33,1},{2,34},{34,2},{3,35},{35,3},{4,36},{36... | collective-permute-start | bytes 393224 | tf_op jit(solution)/shard_map/ppermute | solution.py:511
  20.4 6.9 %copy-start.4 = (bf16[16,1024]{1,0:T(8,128)(2,1)S(1)}, bf16[16,1024]{1,0:T(8,128)(2,1)}, u32[]{:S(2)}) copy-start(bf16[16,1024]{1,0:T(8,128)(2,1)} %lags_ref.3) | copy-start | bytes 98308
  20.4 9.0 %copy-start = (bf16[1,256,8192]{2,1,0:T(8,128)(2,1)S(1)}, bf16[1,256,8192]{2,1,0:T(8,128)(2,1)}, u32[]{:S(2)}) copy-start(bf16[1,256,8192]{2,1,0:T(8,128)(2,1)} %param.15) | copy-start | bytes 12582916
  25.4 1.8 %collective-permute-start.8 = (bf16[256,256]{1,0:T(8,128)(2,1)S(1)}, bf16[256,256]{1,0:T(8,128)(2,1)S(1)}, u32[]{:S(2)}, u32[]{:S(2)}) collective-permute-start(bf16[256,256]{1,0:T(8,128)(2,1)S(1)} %collective-permute-done.7.d_cross_ref), channel_id=1, source_target_pairs={{0,32},{32,0},{1,33},{33,1},{2,34},{34,2},{3,35},{35,3},{4,36},{36... | collective-permute-start | bytes 393224 | tf_op jit(solution)/shard_map/ppermute | solution.py:518
  26.3 2.6 %collective-permute-start.5 = (bf16[256,256]{1,0:T(8,128)(2,1)S(1)}, bf16[256,256]{1,0:T(8,128)(2,1)S(1)}, u32[]{:S(2)}, u32[]{:S(2)}) collective-permute-start(bf16[256,256]{1,0:T(8,128)(2,1)S(1)} %get-tuple-element.41.gated_ref), channel_id=1, source_target_pairs={{0,32},{32,0},{1,33},{33,1},{2,34},{34,2},{3,35},{35,3},{4,36},{36... | collective-permute-start | bytes 393224 | tf_op jit(solution)/shard_map/ppermute | solution.py:515
  28.9 1.7 %collective-permute-start.9 = (f32[32,8,128]{2,1,0:T(8,128)S(1)}, f32[32,8,128]{2,1,0:T(8,128)S(1)}, u32[]{:S(2)}, u32[]{:S(2)}) collective-permute-start(f32[32,8,128]{2,1,0:T(8,128)S(1)} %get-tuple-element.52.small_ref), channel_id=1, source_target_pairs={{0,32},{32,0},{1,33},{33,1},{2,34},{34,2},{3,35},{35,3},{4,36},{36... | collective-permute-start | bytes 393224 | tf_op jit(solution)/shard_map/ppermute | solution.py:524
  72.7 20.0 %all-to-all-start.1 = ((bf16[32,8,2176]{2,1,0:T(8,128)(2,1)}), bf16[32,8,2176]{2,1,0:T(8,128)(2,1)S(1)}, u32[]{:S(2)}, u32[]{:S(2)}) async-start(bf16[32,8,2176]{2,1,0:T(8,128)(2,1)} %total.1), calls=%async_computation.1 | async-start | bytes 2228224 | tf_op jit(solution)/shard_map/all_to_all | solution.py:533
  77.0 15.8 %collective-permute-start.10 = (f32[3,8,256]{2,1,0:T(8,128)S(1)}, f32[3,8,256]{2,1,0:T(8,128)S(1)}, u32[]{:S(2)}, u32[]{:S(2)}) collective-permute-start(f32[3,8,256]{2,1,0:T(8,128)S(1)} %get-tuple-element.58), channel_id=1, source_target_pairs={{32,0},{64,32},{96,64},{33,1},{65,33},{97,65},{34,2},{66,34},{98,6... | collective-permute-start | bytes 73736 | tf_op jit(solution)/shard_map/ppermute | solution.py:482

commit v14 on v13

--- a/solution.py
+++ b/solution.py
@@ -210,19 +210,17 @@
     return call(fwd_kernel, "fwd", out_shape, operands, (), 1, 4 << 30)
 
 
-def terms_kernel(core_ref, own_cot_ref, other_cot_ref, gated_ref, other_gated_ref, out_ref):
+def terms_kernel(own_cot_ref, other_cot_ref, gated_ref, other_gated_ref, out_ref):
     dims = (((0,), (0,)), ((), ()))
     for half in range(2):
-        start = pl.multiple_of((2 * half + core_ref[0]) * SHARE, SHARE)
-        own_cot = own_cot_ref[:, pl.ds(start, SHARE)]
-        total = lax.dot_general(gated_ref[...], own_cot, dims, preferred_element_type=F32)
+        total = lax.dot_general(gated_ref[...], own_cot_ref[half], dims, preferred_element_type=F32)
         total += lax.dot_general(other_gated_ref[...], other_cot_ref[half], dims, preferred_element_type=F32)
         out_ref[half, :, :SHARE] = total.astype(BF16)
 
 
 def terms_call(*operands):
     out_shape = pltpu.VMEM((2, CHANS, SHARE + HALF), BF16)
-    return call(terms_kernel, "terms", out_shape, operands, scalars=1, flops=1 << 30)
+    return call(terms_kernel, "terms", out_shape, operands, flops=1 << 30)
 
 
 def add_small_kernel(terms_ref, small_ref, other_small_ref, out_ref, parts_ref, sems):
@@ -271,19 +269,21 @@
 
 
 def lag_kernel(
-    core_ref, cot_ref, d_inner_ref, signal_ref,
-    filter_ref, part_ref,
+    core_ref, own_cot_ref, other_cot_ref, d_inner_ref, signal_ref,
+    filter_ref, own_part_ref, other_part_ref,
     outer_ref, stack_ref, sums_ref, sems,
 ):
     copies = []
     for half in range(2):
         start = pl.multiple_of((2 * half + core_ref[0]) * SHARE, SHARE)
-        copies.append(
-            pltpu.make_async_copy(
-                cot_ref.at[:, pl.ds(start, SHARE)], part_ref.at[half], sems.at[half]
+        pairs = ((own_cot_ref, own_part_ref), (other_cot_ref, other_part_ref))
+        for n, (cot_ref, part_ref) in enumerate(pairs):
+            copies.append(
+                pltpu.make_async_copy(
+                    cot_ref.at[:, pl.ds(start, SHARE)], part_ref.at[half], sems.at[n, half]
+                )
             )
-        )
-        copies[-1].start()
+            copies[-1].start()
     turn = turn_matrix(ROWS, STRIP).astype(BF16)
     turned = jnp.dot(turn, d_inner_ref[...], preferred_element_type=F32)
     ids = lane_groups()
@@ -332,10 +332,10 @@
         pltpu.VMEM((GROUPS * STRIP, WIDE), F32),
         pltpu.VMEM((GROUPS * STRIP // 2, CHANS), BF16),
         pltpu.VMEM((GROUPS, WIDE), F32),
-        pltpu.SemaphoreType.DMA((2,)),
-    ]
-    out_shape = [pltpu.VMEM((GROUPS, LENGTH), F32), pltpu.VMEM((2, ROWS, SHARE), BF16)]
-    in_specs = [pl.BlockSpec(memory_space=pltpu.SMEM), pl.BlockSpec(memory_space=pltpu.HBM)]
+        pltpu.SemaphoreType.DMA((2, 2)),
+    ]
+    out_shape = [pltpu.VMEM((GROUPS, LENGTH), F32)] + [pltpu.VMEM((2, ROWS, SHARE), BF16)] * 2
+    in_specs = [pl.BlockSpec(memory_space=pltpu.SMEM)] + [pl.BlockSpec(memory_space=pltpu.HBM)] * 2
     in_specs += [pl.BlockSpec(memory_space=pltpu.VMEM)] * 2
     return call(lag_kernel, "lag_sums", out_shape, operands, scratch, in_specs=in_specs)
 
@@ -513,7 +513,7 @@
         core, strips, pair, cross, cross_pair, key, value, query, tail, taps, skip
     )
     other_gated = lax.ppermute(gated, "co", swap)
-    lag_sums, other_part = lag_call(core, other_cot, d_inner, signal)
+    lag_sums, own_part, other_part = lag_call(core, cot, other_cot, d_inner, signal)
     d_cross, lag_sums = lax.optimization_barrier((d_cross, lag_sums))
     d_cross_pair = lax.ppermute(d_cross, "co", swap)
     d_short, head, small = bwd_call(
@@ -522,7 +522,7 @@
     )
     other_gated, head, small = lax.optimization_barrier((other_gated, head, small))
     other_small = lax.ppermute(small, "co", swap)
-    terms = terms_call(core, cot, other_part, gated, other_gated)
+    terms = terms_call(own_part, other_part, gated, other_gated)
     terms, other_small = lax.optimization_barrier((terms, other_small))
     terms = add_small_call(terms, small, other_small)
     terms, head = lax.optimization_barrier((terms, head))

time: 96.3 us -> 96.8 us (level)
  transfers between devices with their start and end apart: 12 -> 12, of which waited for: 3 -> 3; matrix products, arithmetic and copies ran while one was open for 2% -> 2% of each run, Pallas kernels for 14% -> 15%
where the time goes in v14:
time: 96.8 us; the launch traced here: 95.5 us
  blocking collectives  41.2 us (43%)
  starting transfers between devices  19.6 us (20%)
  Pallas kernels  17.7 us (18%)
  waiting for transfers between devices  13.8 us (14%)
  local copies, waits for them, and re-layouts  1.38 us (1%)
  other arithmetic  0.99 us (1%)
    all_to_all x1, blocking collectives, shards(): terms = lax.all_to_all(terms, CHIPS, 0, 0)  41.2 us
    pallas_call x8, Pallas kernels, call(): pl.pallas_call(kernel, out_shape=out_shape, scratch_shapes=list(scratch),...  17.7 us
    ppermute x2, waiting for transfers between devices, sent(): return lax.ppermute(block, CTX, route)  11.6 us
    ppermute x2, starting transfers between devices, sent(): return lax.ppermute(block, CTX, route)  5.5 us
    ppermute x1, starting transfers between devices, shards(): cross = lax.ppermute(own, 'xh', [(0, 1)])  4.75 us
    all_to_all x1, starting transfers between devices, shards(): shares = lax.all_to_all(total_call(terms, scale), DP, 0, 0)  4.24 us
  transfers between devices with their start and end apart: 12, of which 3 were waited for; matrix products, arithmetic and copies ran while one was open for 2% of the time, Pallas kernels for 15%

profile of v14, /device:TPU:1, one launch (start us, length us, event | category | flops | bytes accessed | tf_op | source)
XLA Modules:
  0.0 95.5 jit_solution(16329145051825244448)
XLA Ops:
  0.6 1.5 %collective-permute-start.4 = (bf16[256,8192]{1,0:T(8,128)(2,1)}, bf16[256,8192]{1,0:T(8,128)(2,1)}, u32[]{:S(2)}, u32[]{:S(2)}) collective-permute-start(bf16[256,8192]{1,0:T(8,128)(2,1)} %bitcast.29), channel_id=1, source_target_pairs={{0,32},{32,0},{1,33},{33,1},{2,34},{34,2},{3,35},{35,3},{4,36},{36... | collective-permute-start | bytes 12582920 | tf_op jit(solution)/shard_map/ppermute | solution.py:504
  2.1 1.0 %pad_maximum_fusion = bf16[256,512]{1,0:T(8,128)(2,1)S(1)} fusion(bf16[256,256]{1,0:T(8,128)(2,1)} %bitcast.21, bf16[256,256]{1,0:T(8,128)(2,1)} %bitcast.24), kind=kLoop, calls=%fused_computation | loop fusion | flops 524288 | bytes 524288 | tf_op jit(solution)/shard_map/concatenate | solution.py:500
  3.1 4.7 %collective-permute-start.1 = (bf16[256,512]{1,0:T(8,128)(2,1)S(1)}, bf16[256,512]{1,0:T(8,128)(2,1)S(1)}, u32[]{:S(2)}, u32[]{:S(2)}) collective-permute-start(bf16[256,512]{1,0:T(8,128)(2,1)S(1)} %pad_maximum_fusion), channel_id=1, source_target_pairs={{0,64},{1,65},{2,66},{3,67},{4,68},{5,69},{6,70},{7,71},{8,72},{9,... | collective-permute-start | bytes 786440 | tf_op jit(solution)/shard_map/ppermute | solution.py:502
  7.9 0.4 collective-permute-start
  8.3 0.7 slice_bitcast_fusion
  9.0 0.0 copy-start
  9.0 0.0 copy-start.4
  9.0 0.0 copy-start.1
  9.0 0.0 copy-start.2
  9.0 0.0 copy-start.5
  9.0 2.1 %collective-permute-start.2 = (bf16[16,256]{1,0:T(8,128)(2,1)S(1)}, bf16[16,256]{1,0:T(8,128)(2,1)S(1)}, u32[]{:S(2)}, u32[]{:S(2)}) collective-permute-start(bf16[16,256]{1,0:T(8,128)(2,1)S(1)} %slice_bitcast_fusion), channel_id=1, source_target_pairs={{0,32},{32,64},{64,96},{1,33},{33,65},{65,97},{2,34},{34,66},{66,9... | collective-permute-start | bytes 24584 | tf_op jit(solution)/shard_map/ppermute | solution.py:482
  11.0 5.2 %pre.1 = (bf16[256,256]{1,0:T(8,128)(2,1)S(1)}, bf16[512,1024]{1,0:T(8,128)(2,1)S(1)}) custom-call(bf16[256,8192]{1,0:T(8,128)(2,1)} %bitcast.30, bf16[8192,256]{1,0:T(8,128)(2,1)} %weight_ref.1, bf16[16,1024]{1,0:T(8,128)(2,1)} %lags_ref.3), custom_call_target="tpu_custom_call" | custom-call | flops 1073741824 | bytes 1024 | tf_op jit(solution)/shard_map/pre/pallas_call | solution.py:46
  16.2 0.0 collective-permute-done.2.tail_ref
  16.2 0.0 collective-permute-done.1.cross_ref
  16.3 0.6 collective-permute-start.3
  16.8 0.0 copy-done
  16.8 0.0 copy-done.4
  16.8 0.1 d_inner.1.d_inner_ref.d0_ref
  17.0 1.3 %collective-permute-start.7 = (bf16[256,256]{1,0:T(8,128)(2,1)S(1)}, bf16[256,256]{1,0:T(8,128)(2,1)S(1)}, u32[]{:S(2)}, u32[]{:S(2)}) collective-permute-start(bf16[256,256]{1,0:T(8,128)(2,1)S(1)} %d_inner.1.d_inner_ref.d0_ref), channel_id=1, source_target_pairs={{64,0},{65,1},{66,2},{67,3},{68,4},{69,5},{70,6},{71,7},{72,8},{73... | collective-permute-start | bytes 393224 | tf_op jit(solution)/shard_map/ppermute | solution.py:510
  18.3 0.1 collective-permute-start.6
  18.4 0.0 collective-permute-done.pair_ref
  18.4 0.0 collective-permute-done.3.cross_pair_ref
  18.4 0.0 copy-done.1
  18.4 0.0 copy-done.2
  18.4 0.0 copy-done.5
  18.4 1.9 %fwd.1 = (bf16[256,256]{1,0:T(8,128)(2,1)S(1)}, f32[256,256]{1,0:T(8,128)S(1)}, bf16[1248,256]{1,0:T(8,128)(2,1)S(1)}) custom-call(s32[1]{0:T(128)} %bitcast.core_ref, bf16[512,1024]{1,0:T(8,128)(2,1)S(1)} %get-tuple-element.38.strips_ref, bf16[256,512]{1,0:T(8,128)(2,1)S(1)} %collective-permute-done.pair_ref, ...), custom_call_target="tpu_custom_call" | custom-call | flops 4294967296 | bytes 1024 | tf_op jit(solution)/shard_map/fwd/pallas_call | solution.py:46
  20.3 0.0 collective-permute-done.4.other_cot_ref
  20.4 0.0 copy-start.3
  20.4 3.9 %lag_sums.1 = (f32[16,1024]{1,0:T(8,128)S(1)}, bf16[2,256,2048]{2,1,0:T(8,128)(2,1)S(1)}, bf16[2,256,2048]{2,1,0:T(8,128)(2,1)S(1)}) custom-call(s32[1]{0:T(128)} %bitcast.core_ref, bf16[256,8192]{1,0:T(8,128)(2,1)} %bitcast.31, bf16[256,8192]{1,0:T(8,128)(2,1)} %collective-permute-done.4.other_cot_ref, bf16[256,256]{1,0:T(8,128)(2,1)S(1)} %d_inner.1.d_inner_ref.d0_ref, ...), custom_call_target="tpu_custom_call" | custom-call | flops 1024 | bytes 1024 | tf_op jit(solution)/shard_map/lag_sums/pallas_call | solution.py:46
  24.3 1.1 %collective-permute-done.7.d_cross_ref = bf16[256,256]{1,0:T(8,128)(2,1)S(1)} collective-permute-done((bf16[256,256]{1,0:T(8,128)(2,1)S(1)}, bf16[256,256]{1,0:T(8,128)(2,1)S(1)}, u32[]{:S(2)}, u32[]{:S(2)}) %collective-permute-start.7) | collective-permute-done | bytes 131104 | tf_op jit(solution)/shard_map/ppermute | solution.py:510
  25.4 0.8 collective-permute-start.8
  26.3 0.0 collective-permute-start.5
  26.3 0.0 collective-permute-done.6.d_pair_ref
  26.3 1.0 %collective-permute-done.8.d_cross_pair_ref = bf16[256,256]{1,0:T(8,128)(2,1)S(1)} collective-permute-done((bf16[256,256]{1,0:T(8,128)(2,1)S(1)}, bf16[256,256]{1,0:T(8,128)(2,1)S(1)}, u32[]{:S(2)}, u32[]{:S(2)}) %collective-permute-start.8) | collective-permute-done | bytes 131104 | tf_op jit(solution)/shard_map/ppermute | solution.py:518
  27.3 0.0 copy-done.3
  27.3 1.6 %bwd.1 = (f32[3,256,256]{2,1,0:T(8,128)S(1)}, f32[3,8,256]{2,1,0:T(8,128)S(1)}, f32[32,8,128]{2,1,0:T(8,128)S(1)}) custom-call(s32[1]{0:T(128)} %bitcast.core_ref, bf16[256,256]{1,0:T(8,128)(2,1)S(1)} %d_inner.1.d_inner_ref.d0_ref, bf16[256,256]{1,0:T(8,128)(2,1)S(1)} %collective-permute-done.6.d_pair_ref, ...), custom_call_target="tpu_custom_call" | custom-call | flops 1024 | bytes 1024 | tf_op jit(solution)/shard_map/bwd/pallas_call | solution.py:46
  28.9 0.0 collective-permute-done.5.other_gated_ref
  28.9 0.4 collective-permute-start.9
  29.3 1.3 %terms.1.terms_ref = bf16[2,256,2176]{2,1,0:T(8,128)(2,1)S(1)} custom-call(bf16[2,256,2048]{2,1,0:T(8,128)(2,1)S(1)} %get-tuple-element.45.own_cot_ref, bf16[2,256,2048]{2,1,0:T(8,128)(2,1)S(1)} %get-tuple-element.46.other_cot_ref, bf16[256,256]{1,0:T(8,128)(2,1)S(1)} %get-tuple-element.42.gated_ref, bf16[256,256]{1,0:T(8,128)(2,1)S(1)} %collective-permute-done.5.other_gated_ref), custom_call_target="tpu_custom_call" | custom-call | flops 1073741824 | bytes 1024 | tf_op jit(solution)/shard_map/terms/pallas_call | solution.py:46
  30.6 0.0 collective-permute-done.9.other_small_ref
  30.6 0.1 add_small.1
  30.7 41.2 %all_to_all.10.refs_0_ = bf16[64,8,2176]{2,1,0:T(8,128)(2,1)S(1)} all-to-all(bf16[64,8,2176]{2,1,0:T(8,128)(2,1)S(1)} %bitcast.16), channel_id=1, replica_groups=mesh['xh'=2,'co'=2,'y'=4,'xl'=2,'z'=4] {'xh','y','xl','z'}, dimensions={0} | all-to-all | bytes 4456448 | tf_op jit(solution)/shard_map/all_to_all | solution.py:530
  71.9 1.4 %total.1 = bf16[32,8,2176]{2,1,0:T(8,128)(2,1)} custom-call(bf16[64,8,2176]{2,1,0:T(8,128)(2,1)S(1)} %all_to_all.10.refs_0_), custom_call_target="tpu_custom_call" | custom-call | flops 1024 | bytes 1024 | tf_op jit(solution)/shard_map/total/pallas_call | solution.py:46
  73.3 4.2 %all-to-all-start.1 = ((bf16[32,8,2176]{2,1,0:T(8,128)(2,1)}), bf16[32,8,2176]{2,1,0:T(8,128)(2,1)S(1)}, u32[]{:S(2)}, u32[]{:S(2)}) async-start(bf16[32,8,2176]{2,1,0:T(8,128)(2,1)} %total.1), calls=%async_computation.1 | async-start | bytes 2228224 | tf_op jit(solution)/shard_map/all_to_all | solution.py:533
  77.5 3.5 %collective-permute-start.10 = (f32[3,8,256]{2,1,0:T(8,128)S(1)}, f32[3,8,256]{2,1,0:T(8,128)S(1)}, u32[]{:S(2)}, u32[]{:S(2)}) collective-permute-start(f32[3,8,256]{2,1,0:T(8,128)S(1)} %get-tuple-element.60), channel_id=1, source_target_pairs={{32,0},{64,32},{96,64},{33,1},{65,33},{97,65},{34,2},{66,34},{98,6... | collective-permute-start | bytes 73736 | tf_op jit(solution)/shard_map/ppermute | solution.py:482
  81.0 0.7 copy.18
  81.6 11.6 %collective-permute-done.10.next_ref = f32[3,8,256]{2,1,0:T(8,128)S(1)} collective-permute-done((f32[3,8,256]{2,1,0:T(8,128)S(1)}, f32[3,8,256]{2,1,0:T(8,128)S(1)}, u32[]{:S(2)}, u32[]{:S(2)}) %collective-permute-start.10) | collective-permute-done | bytes 24608 | tf_op jit(solution)/shard_map/ppermute | solution.py:482
  93.3 0.0 all-to-all-done.1
  93.3 2.3 %spread.1 = (f32[2048,256]{1,0:T(8,128)}, f32[3,3,256]{2,1,0:T(4,128)}, f32[16,1024]{1,0:T(8,128)}, f32[1,256]{1,0:T(1,128)}, bf16[256,256]{1,0:T(8,128)(2,1)}, ...) custom-call(bf16[256,2176]{1,0:T(8,128)(2,1)S(1)} %bitcast.17, f32[3,256,256]{2,1,0:T(8,128)S(1)} %get-tuple-element.59.d_short_ref, ...), custom_call_target="tpu_custom_call" | custom-call | flops 1024 | bytes 1024 | tf_op jit(solution)/shard_map/spread/pallas_call | solution.py:46
Async XLA Ops:
  0.6 19.7 %collective-permute-start.4 = (bf16[256,8192]{1,0:T(8,128)(2,1)}, bf16[256,8192]{1,0:T(8,128)(2,1)}, u32[]{:S(2)}, u32[]{:S(2)}) collective-permute-start(bf16[256,8192]{1,0:T(8,128)(2,1)} %bitcast.29), channel_id=1, source_target_pairs={{0,32},{32,0},{1,33},{33,1},{2,34},{34,2},{3,35},{35,3},{4,36},{36... | collective-permute-start | bytes 12582920 | tf_op jit(solution)/shard_map/ppermute | solution.py:504
  3.1 13.1 %collective-permute-start.1 = (bf16[256,512]{1,0:T(8,128)(2,1)S(1)}, bf16[256,512]{1,0:T(8,128)(2,1)S(1)}, u32[]{:S(2)}, u32[]{:S(2)}) collective-permute-start(bf16[256,512]{1,0:T(8,128)(2,1)S(1)} %pad_maximum_fusion), channel_id=1, source_target_pairs={{0,64},{1,65},{2,66},{3,67},{4,68},{5,69},{6,70},{7,71},{8,72},{9,... | collective-permute-start | bytes 786440 | tf_op jit(solution)/shard_map/ppermute | solution.py:502
  7.9 10.5 %collective-permute-start = (bf16[256,512]{1,0:T(8,128)(2,1)S(1)}, bf16[256,512]{1,0:T(8,128)(2,1)S(1)}, u32[]{:S(2)}, u32[]{:S(2)}) collective-permute-start(bf16[256,512]{1,0:T(8,128)(2,1)S(1)} %pad_maximum_fusion), channel_id=1, source_target_pairs={{0,32},{32,0},{1,33},{33,1},{2,34},{34,2},{3,35},{35,3},{4,36},{36... | collective-permute-start | bytes 786440 | tf_op jit(solution)/shard_map/ppermute | solution.py:503
  9.0 7.9 %copy-start = (bf16[1,256,256]{2,1,0:T(8,128)(2,1)S(1)}, bf16[1,256,256]{2,1,0:T(8,128)(2,1)}, u32[]{:S(2)}) copy-start(bf16[1,256,256]{2,1,0:T(8,128)(2,1)} %param.8) | copy-start | bytes 393220
  9.0 7.9 %copy-start.4 = (f32[3,3,256]{2,1,0:T(4,128)S(1)}, f32[3,3,256]{2,1,0:T(4,128)}, u32[]{:S(2)}) copy-start(f32[3,3,256]{2,1,0:T(4,128)} %short_taps_ref.1) | copy-start | bytes 27652
  9.0 9.4 %copy-start.1 = (bf16[1,256,256]{2,1,0:T(8,128)(2,1)S(1)}, bf16[1,256,256]{2,1,0:T(8,128)(2,1)}, u32[]{:S(2)}) copy-start(bf16[1,256,256]{2,1,0:T(8,128)(2,1)} %param.10) | copy-start | bytes 393220
  9.0 9.4 %copy-start.2 = (bf16[1,256,256]{2,1,0:T(8,128)(2,1)S(1)}, bf16[1,256,256]{2,1,0:T(8,128)(2,1)}, u32[]{:S(2)}) copy-start(bf16[1,256,256]{2,1,0:T(8,128)(2,1)} %param.9) | copy-start | bytes 393220
  9.0 9.4 %copy-start.5 = (f32[256]{0:T(256)S(1)}, f32[256]{0:T(256)}, u32[]{:S(2)}) copy-start(f32[256]{0:T(256)} %param.13) | copy-start | bytes 3076
  9.0 7.3 %collective-permute-start.2 = (bf16[16,256]{1,0:T(8,128)(2,1)S(1)}, bf16[16,256]{1,0:T(8,128)(2,1)S(1)}, u32[]{:S(2)}, u32[]{:S(2)}) collective-permute-start(bf16[16,256]{1,0:T(8,128)(2,1)S(1)} %slice_bitcast_fusion), channel_id=1, source_target_pairs={{0,32},{32,64},{64,96},{1,33},{33,65},{65,97},{2,34},{34,66},{66,9... | collective-permute-start | bytes 24584 | tf_op jit(solution)/shard_map/ppermute | solution.py:482
  16.3 2.1 %collective-permute-start.3 = (bf16[256,512]{1,0:T(8,128)(2,1)S(1)}, bf16[256,512]{1,0:T(8,128)(2,1)S(1)}, u32[]{:S(2)}, u32[]{:S(2)}) collective-permute-start(bf16[256,512]{1,0:T(8,128)(2,1)S(1)} %collective-permute-done.1.cross_ref), channel_id=1, source_target_pairs={{0,32},{32,0},{1,33},{33,1},{2,34},{34,2},{3,35},{35,3},{4,36},{36... | collective-permute-start | bytes 786440 | tf_op jit(solution)/shard_map/ppermute | solution.py:508
  17.0 8.5 %collective-permute-start.7 = (bf16[256,256]{1,0:T(8,128)(2,1)S(1)}, bf16[256,256]{1,0:T(8,128)(2,1)S(1)}, u32[]{:S(2)}, u32[]{:S(2)}) collective-permute-start(bf16[256,256]{1,0:T(8,128)(2,1)S(1)} %d_inner.1.d_inner_ref.d0_ref), channel_id=1, source_target_pairs={{64,0},{65,1},{66,2},{67,3},{68,4},{69,5},{70,6},{71,7},{72,8},{73... | collective-permute-start | bytes 393224 | tf_op jit(solution)/shard_map/ppermute | solution.py:510
  18.3 8.0 %collective-permute-start.6 = (bf16[256,256]{1,0:T(8,128)(2,1)S(1)}, bf16[256,256]{1,0:T(8,128)(2,1)S(1)}, u32[]{:S(2)}, u32[]{:S(2)}) collective-permute-start(bf16[256,256]{1,0:T(8,128)(2,1)S(1)} %d_inner.1.d_inner_ref.d0_ref), channel_id=1, source_target_pairs={{0,32},{32,0},{1,33},{33,1},{2,34},{34,2},{3,35},{35,3},{4,36},{36... | collective-permute-start | bytes 393224 | tf_op jit(solution)/shard_map/ppermute | solution.py:511
  20.4 6.9 %copy-start.3 = (bf16[16,1024]{1,0:T(8,128)(2,1)S(1)}, bf16[16,1024]{1,0:T(8,128)(2,1)}, u32[]{:S(2)}) copy-start(bf16[16,1024]{1,0:T(8,128)(2,1)} %lags_ref.3) | copy-start | bytes 98308
  25.4 1.8 %collective-permute-start.8 = (bf16[256,256]{1,0:T(8,128)(2,1)S(1)}, bf16[256,256]{1,0:T(8,128)(2,1)S(1)}, u32[]{:S(2)}, u32[]{:S(2)}) collective-permute-start(bf16[256,256]{1,0:T(8,128)(2,1)S(1)} %collective-permute-done.7.d_cross_ref), channel_id=1, source_target_pairs={{0,32},{32,0},{1,33},{33,1},{2,34},{34,2},{3,35},{35,3},{4,36},{36... | collective-permute-start | bytes 393224 | tf_op jit(solution)/shard_map/ppermute | solution.py:518
  26.3 2.6 %collective-permute-start.5 = (bf16[256,256]{1,0:T(8,128)(2,1)S(1)}, bf16[256,256]{1,0:T(8,128)(2,1)S(1)}, u32[]{:S(2)}, u32[]{:S(2)}) collective-permute-start(bf16[256,256]{1,0:T(8,128)(2,1)S(1)} %get-tuple-element.42.gated_ref), channel_id=1, source_target_pairs={{0,32},{32,0},{1,33},{33,1},{2,34},{34,2},{3,35},{35,3},{4,36},{36... | collective-permute-start | bytes 393224 | tf_op jit(solution)/shard_map/ppermute | solution.py:515
  28.9 1.7 %collective-permute-start.9 = (f32[32,8,128]{2,1,0:T(8,128)S(1)}, f32[32,8,128]{2,1,0:T(8,128)S(1)}, u32[]{:S(2)}, u32[]{:S(2)}) collective-permute-start(f32[32,8,128]{2,1,0:T(8,128)S(1)} %get-tuple-element.54.small_ref), channel_id=1, source_target_pairs={{0,32},{32,0},{1,33},{33,1},{2,34},{34,2},{3,35},{35,3},{4,36},{36... | collective-permute-start | bytes 393224 | tf_op jit(solution)/shard_map/ppermute | solution.py:524
  73.3 20.0 %all-to-all-start.1 = ((bf16[32,8,2176]{2,1,0:T(8,128)(2,1)}), bf16[32,8,2176]{2,1,0:T(8,128)(2,1)S(1)}, u32[]{:S(2)}, u32[]{:S(2)}) async-start(bf16[32,8,2176]{2,1,0:T(8,128)(2,1)} %total.1), calls=%async_computation.1 | async-start | bytes 2228224 | tf_op jit(solution)/shard_map/all_to_all | solution.py:533
  77.5 15.8 %collective-permute-start.10 = (f32[3,8,256]{2,1,0:T(8,128)S(1)}, f32[3,8,256]{2,1,0:T(8,128)S(1)}, u32[]{:S(2)}, u32[]{:S(2)}) collective-permute-start(f32[3,8,256]{2,1,0:T(8,128)S(1)} %get-tuple-element.60), channel_id=1, source_target_pairs={{32,0},{64,32},{96,64},{33,1},{65,33},{97,65},{34,2},{66,34},{98,6... | collective-permute-start | bytes 73736 | tf_op jit(solution)/shard_map/ppermute | solution.py:482
